TPU v7x, 256 devices: a whole 4x4x8 slice. The times are simulated.
256 devices in a mesh: segment: 2 (over core), et: 128 (over x, y, z).
Axes of the slice: x: 4, y: 4, z: 8, core: 2. Of those that a mesh axis runs over, the one named last changes fastest.
Arguments:
- inputs: bfloat16 [1, 128, 6144], P(None, 'et'), may hold values from -6 to 6
- cotangent: bfloat16 [1, 128, 6144], P(None, 'et'), may hold values from -6 to 6
- gate_weight: bfloat16 [2, 6144, 16384], P('segment', None, 'et'), may hold values from -0.078125 to 0.078125
- up_weight: bfloat16 [2, 6144, 16384], P('segment', None, 'et'), may hold values from -0.078125 to 0.078125
- down_weight: bfloat16 [2, 16384, 6144], P('segment', 'et'), may hold values from -0.0625 to 0.0625
- route_rows: int32 [2, 1, 128], P('segment'), may hold values from 0 to 127, as said below
- route_count: int32 [2, 1], P('segment'), may hold values from 32 to 128, as said below
- route_weight: float32 [2, 1, 128], P('segment'), may hold values from 0.05 to 1
- width_mask: int32 [2, 128], P('segment', 'et'), may hold values from 0 to 1, as said below
Outputs:
- section_output: bfloat16 [2, 1, 128, 6144], P('segment', None, 'et')
- grad_input: bfloat16 [2, 1, 128, 6144], P('segment', None, 'et')
- grad_gate: bfloat16 [2, 6144, 16384], P('segment', None, 'et')
- grad_up: bfloat16 [2, 6144, 16384], P('segment', None, 'et')
- grad_down: bfloat16 [2, 16384, 6144], P('segment', 'et')
Inputs may be any that keep to these rules, and one draw needn't show every extreme that they name: `route_rows`: each list names every one of the 128 tokens once; its first route_count entries are the slots routed to the expert. `route_count`: 128 in at least one entry. `width_mask`: the kept tiles of each section are its first ones, at least 32 of them and never all.
All inputs are finite; a program needn't handle non-finite values.
Results may differ from a plain program's by a relative error of at most 0.015.
Values may be sent and summed in bfloat16 or wider, within the bound.
No kernel may reach another device: no remote copies, remote signals or barrier semaphores. Data moves between devices by JAX's collectives and lax.ppermute only.
A program may use at most 128 MiB of HBM per device.

v0:
```python
import jax
import jax.numpy as jnp
from jax import lax
from jax.sharding import PartitionSpec as P


def shifted(value, axis, by):
    size = lax.axis_size(axis)
    pairs = [(i, i + by) for i in range(size) if 0 <= i + by < size]
    return lax.ppermute(value, axis, pairs)


def expert_hidden(picked, gate_w, up_w, keep):
    gate_value = jnp.dot(picked, gate_w, preferred_element_type=jnp.float32)
    up_value = jnp.dot(picked, up_w, preferred_element_type=jnp.float32)
    hidden = (gate_value * jax.nn.sigmoid(gate_value) * up_value * keep).astype(jnp.bfloat16)
    return (gate_value, up_value, hidden)


def expert_deltas(picked, slot_grad_in, gate_value, up_value, hidden, down_w, keep):
    contract_last = (((1,), (1,)), ((), ()))
    contract_first = (((0,), (0,)), ((), ()))
    hidden_delta = lax.dot_general(
        slot_grad_in, down_w, contract_last, preferred_element_type=jnp.float32
    )
    sig_gate = jax.nn.sigmoid(gate_value)
    gate_delta = (
        hidden_delta * keep * up_value * sig_gate * (1.0 + gate_value * (1.0 - sig_gate))
    ).astype(jnp.bfloat16)
    up_delta = (hidden_delta * keep * gate_value * sig_gate).astype(jnp.bfloat16)
    grad_gate = lax.dot_general(
        picked, gate_delta, contract_first, preferred_element_type=jnp.float32
    )
    grad_up = lax.dot_general(picked, up_delta, contract_first, preferred_element_type=jnp.float32)
    grad_down = lax.dot_general(
        hidden, slot_grad_in, contract_first, preferred_element_type=jnp.float32
    )
    return (gate_delta, up_delta, grad_gate, grad_up, grad_down)


def slot_gradient(gate_delta, up_delta, gate_w, up_w):
    contract_last = (((1,), (1,)), ((), ()))
    slot_grad = lax.dot_general(
        gate_delta, gate_w, contract_last, preferred_element_type=jnp.float32
    )
    return slot_grad + lax.dot_general(
        up_delta, up_w, contract_last, preferred_element_type=jnp.float32
    )


def take_micro(buffer, micro_index):
    return lax.dynamic_index_in_dim(buffer, micro_index, 0, keepdims=False)


def store_micro(buffer, micro_index, value):
    return lax.dynamic_update_index_in_dim(buffer, value, micro_index, 0)


def pick_route(route_rows, route_count, route_weight, micro_index):
    slot_rows = take_micro(route_rows[0], micro_index)
    live_count = take_micro(route_count[0], micro_index)
    slot_weight = take_micro(route_weight[0], micro_index)
    slot_total = slot_rows.shape[0]
    positions = jnp.arange(slot_total, dtype=jnp.int32)
    live = positions < live_count
    inverse = jnp.zeros((slot_total,), jnp.int32).at[slot_rows].set(positions)
    return (slot_rows, jnp.where(live, slot_weight, 0.0), inverse)


def per_device(
    inputs,
    cotangent,
    gate_weight,
    up_weight,
    down_weight,
    route_rows,
    route_count,
    route_weight,
    width_mask,
):
    micro_count = inputs.shape[0]
    token_rows = inputs.shape[1]
    width = inputs.shape[2]
    segment_count = lax.axis_size("segment")
    segment_index = lax.axis_index("segment")
    total_rows = token_rows * lax.axis_size("et")
    slot_count = route_rows.shape[2]
    gate_w = gate_weight[0]
    up_w = up_weight[0]
    down_w = down_weight[0]
    hidden_cols = gate_w.shape[1]
    keep = jnp.repeat(width_mask[0].astype(jnp.float32), hidden_cols // width_mask.shape[1])
    phases = micro_count + segment_count - 1
    saved_input = jnp.zeros((micro_count, token_rows, width), jnp.bfloat16)
    saved_whole = jnp.zeros((micro_count, total_rows, width), jnp.bfloat16)
    saved_gate = jnp.zeros((micro_count, slot_count, hidden_cols), jnp.float32)
    saved_up = jnp.zeros((micro_count, slot_count, hidden_cols), jnp.float32)
    saved_hidden = jnp.zeros((micro_count, slot_count, hidden_cols), jnp.bfloat16)
    outputs = jnp.zeros((micro_count, token_rows, width), jnp.bfloat16)
    incoming = jnp.zeros((token_rows, width), jnp.bfloat16)
    for phase in range(phases):
        micro_raw = phase - segment_index
        valid = (micro_raw >= 0) & (micro_raw < micro_count)
        micro_index = jnp.clip(micro_raw, 0, micro_count - 1)
        current = jnp.where(segment_index == 0, take_micro(inputs, micro_index), incoming)
        gathered = lax.all_gather(current, "et", axis=0, tiled=True)
        slot_rows, slot_scale, inverse = pick_route(
            route_rows, route_count, route_weight, micro_index
        )
        picked = jnp.take(gathered, slot_rows, axis=0)
        gate_value, up_value, hidden = expert_hidden(picked, gate_w, up_w, keep)
        outcome = jnp.dot(hidden, down_w, preferred_element_type=jnp.float32)
        added = jnp.take(slot_scale[:, None] * outcome, inverse, axis=0)
        mine = lax.psum_scatter(added, "et", scatter_dimension=0, tiled=True)
        result = (current.astype(jnp.float32) + mine).astype(jnp.bfloat16)
        late = micro_raw >= 0
        stored = jnp.where(late, micro_index, micro_count - 1)
        saved_input = store_micro(saved_input, stored, current)
        saved_whole = store_micro(saved_whole, stored, gathered)
        saved_gate = store_micro(saved_gate, stored, gate_value)
        saved_up = store_micro(saved_up, stored, up_value)
        saved_hidden = store_micro(saved_hidden, stored, hidden)
        outputs = jnp.where(valid, store_micro(outputs, micro_index, result), outputs)
        if phase + 1 < phases:
            incoming = shifted(result, "segment", 1)
    acc_gate = jnp.zeros((width, hidden_cols), jnp.float32)
    acc_up = jnp.zeros((width, hidden_cols), jnp.float32)
    acc_down = jnp.zeros((hidden_cols, width), jnp.float32)
    grad_inputs = jnp.zeros((micro_count, token_rows, width), jnp.bfloat16)
    incoming = jnp.zeros((token_rows, width), jnp.bfloat16)
    for phase in range(phases):
        micro_raw = phase - (segment_count - 1 - segment_index)
        valid = (micro_raw >= 0) & (micro_raw < micro_count)
        micro_index = jnp.clip(micro_raw, 0, micro_count - 1)
        upstream = jnp.where(
            segment_index == segment_count - 1, take_micro(cotangent, micro_index), incoming
        )
        grad_gathered = lax.all_gather(upstream, "et", axis=0, tiled=True)
        gathered = take_micro(saved_whole, micro_index)
        slot_rows, slot_scale, inverse = pick_route(
            route_rows, route_count, route_weight, micro_index
        )
        slot_scale = jnp.where(valid, slot_scale, 0.0)
        picked = jnp.take(gathered, slot_rows, axis=0)
        grad_picked = jnp.take(grad_gathered, slot_rows, axis=0)
        slot_grad_in = (slot_scale[:, None] * grad_picked.astype(jnp.float32)).astype(jnp.bfloat16)
        gate_delta, up_delta, part_gate, part_up, part_down = expert_deltas(
            picked,
            slot_grad_in,
            take_micro(saved_gate, micro_index),
            take_micro(saved_up, micro_index),
            take_micro(saved_hidden, micro_index),
            down_w,
            keep,
        )
        acc_gate = acc_gate + part_gate
        acc_up = acc_up + part_up
        acc_down = acc_down + part_down
        slot_grad = slot_gradient(gate_delta, up_delta, gate_w, up_w)
        added = jnp.take(slot_grad, inverse, axis=0)
        mine = lax.psum_scatter(added, "et", scatter_dimension=0, tiled=True)
        result = (upstream.astype(jnp.float32) + mine).astype(jnp.bfloat16)
        grad_inputs = jnp.where(valid, store_micro(grad_inputs, micro_index, result), grad_inputs)
        if phase + 1 < phases:
            incoming = shifted(result, "segment", -1)
    return (
        outputs[None],
        grad_inputs[None],
        acc_gate.astype(jnp.bfloat16)[None],
        acc_up.astype(jnp.bfloat16)[None],
        acc_down.astype(jnp.bfloat16)[None],
    )


def solution(mesh):
    return jax.shard_map(
        per_device,
        mesh=mesh,
        in_specs=(
            P(None, "et", None),
            P(None, "et", None),
            P("segment", None, "et"),
            P("segment", None, "et"),
            P("segment", "et", None),
            P("segment", None, None),
            P("segment", None),
            P("segment", None, None),
            P("segment", "et"),
        ),
        out_specs=(
            P("segment", None, "et", None),
            P("segment", None, "et", None),
            P("segment", None, "et"),
            P("segment", None, "et"),
            P("segment", "et", None),
        ),
        check_vma=False,
    )
```

profile of v0, /device:TPU:1, one launch (start us, length us, event | category | flops | bytes accessed | tf_op | source)
XLA Modules:
  0.0 1269.1 jit_solution(9324662932709823214)
XLA Ops:
  7.2 1.5 fusion.56
  10.8 1.0 scatter_custom_fusion
  13.8 113.3 %all-gather.9.cloned.1.call-done = bf16[128,1,6144]{2,1,0:T(2,128)(2,1)} async-done(((bf16[1,1,6144]{2,1,0:T(2,128)(2,1)}), bf16[128,1,6144]{2,1,0:T(2,128)(2,1)}) %all-gather.9.cloned.1.call-update) | async-done | bytes 1572880 | tf_op jit(solution)/shard_map/all_gather | solution.py:106
  127.1 2.8 copy.25
  129.9 2.6 gather_fusion
  132.5 2.6 fusion.24
  135.2 4.2 convolution_multiply_fusion.1
  139.3 6.5 gather_fusion.1
  145.8 4.0 broadcast_select_fusion.3
  151.8 226.9 %all-reduce.9.cloned.1.call-done = f32[128,6144]{1,0:T(8,128)} async-done(((f32[128,6144]{1,0:T(8,128)}), f32[128,6144]{1,0:T(8,128)}) %all-reduce.9.cloned.1.call-update) | async-done | bytes 3145744
  378.7 1.5 fusion.55
  380.3 1.3 collective-permute-start
  381.6 4.8 collective-permute-done
  387.3 108.1 %all-gather.13.cloned.1.call-done = bf16[128,1,6144]{2,1,0:T(2,128)(2,1)} async-done(((bf16[1,1,6144]{2,1,0:T(2,128)(2,1)}), bf16[128,1,6144]{2,1,0:T(2,128)(2,1)}) %all-gather.13.cloned.1.call-update) | async-done | bytes 1572880 | tf_op jit(solution)/shard_map/all_gather | solution.py:138
  495.4 2.8 copy.23
  498.2 2.6 gather_fusion.4
  500.8 111.6 %all-gather.11.cloned.1.call-done = bf16[128,1,6144]{2,1,0:T(2,128)(2,1)} async-done(((bf16[1,1,6144]{2,1,0:T(2,128)(2,1)}), bf16[128,1,6144]{2,1,0:T(2,128)(2,1)}) %all-gather.11.cloned.1.call-update) | async-done | bytes 1572880 | tf_op jit(solution)/shard_map/all_gather | solution.py:106
  612.5 2.8 copy.24
  615.3 2.6 gather_fusion.2
  617.9 2.2 fusion.14
  620.9 0.8 copy-done.4
  623.4 2.3 convolution_add_fusion.4
  625.7 6.5 gather_fusion.5
  632.2 4.0 broadcast_select_fusion.1
  636.2 228.8 %all-reduce.11.cloned.1.call-done = f32[128,6144]{1,0:T(8,128)} async-done(((f32[128,6144]{1,0:T(8,128)}), f32[128,6144]{1,0:T(8,128)}) %all-reduce.11.cloned.1.call-update) | async-done | bytes 3145744
  865.0 1.5 fusion.53
  866.5 6.0 collective-permute-start.1
  872.6 0.8 collective-permute-done.1
  874.3 107.9 %all-gather.15.cloned.1.call-done = bf16[128,1,6144]{2,1,0:T(2,128)(2,1)} async-done(((bf16[1,1,6144]{2,1,0:T(2,128)(2,1)}), bf16[128,1,6144]{2,1,0:T(2,128)(2,1)}) %all-gather.15.cloned.1.call-update) | async-done | bytes 1572880 | tf_op jit(solution)/shard_map/all_gather | solution.py:138
  982.2 2.8 copy.22
  985.0 2.6 gather_fusion.6
  987.7 2.6 multiply_convert_fusion.2
  990.3 2.3 convolution_multiply_fusion
  992.6 6.5 gather_fusion.3
  999.7 2.3 convolution_add_fusion.3
  1002.0 6.4 gather_fusion.7
  1008.4 6.4 broadcast_select_fusion
  1014.8 1.4 copy-done.2
  1016.2 0.7 fusion.68
  1016.9 0.7 fusion.69
  1017.6 0.7 copy-done.9
  1018.3 0.7 fusion.67
  1018.9 0.7 copy-done.10
  1019.7 1.9 fusion.3
  1021.6 1.8 fusion.5
  1023.5 1.9 fusion.4
  1025.3 234.4 %all-reduce.13.cloned.1.call-done = (f32[128,6144]{1,0:T(8,128)}, f32[128,6144]{1,0:T(8,128)}) async-done(((f32[128,6144]{1,0:T(8,128)}, f32[128,6144]{1,0:T(8,128)}), (f32[128,6144]{1,0:T(8,128)}, f32[128,6144]{1,0:T(8,128)})) %all-reduce.13.cloned.1.call-update) | async-done | bytes 6291472
  1259.7 2.6 fusion.50
  (58 shorter events, 9.8 us)
Async XLA Ops:
  7.2 128.0 %copy-start = (bf16[1,6144,128]{2,1,0:T(8,128)(2,1)S(1)}, bf16[1,6144,128]{2,1,0:T(8,128)(2,1)}, u32[]{:S(2)}) copy-start(bf16[1,6144,128]{2,1,0:T(8,128)(2,1)} %param.16) | copy-start | bytes 4718596
  7.2 119.9 %all-gather.9.cloned.1.call-start = ((), (), s32[]{:S(2)}) async-start(), calls=%async_computation | async-start | bytes 3170304 | tf_op jit(solution)/shard_map/all_gather | solution.py:106
  8.7 370.0 %all-reduce.9.cloned.1.call-start = ((), (), s32[]{:S(2)}) async-start(), calls=%async_computation.4 | async-start | bytes 6291456
  132.5 2.6 copy-start.3
  149.8 0.7 copy-start.12
  149.8 1.5 copy-start.13
  149.8 229.0 %copy-start.11 = (bf16[1,1,6144]{2,1,0:T(2,128)(2,1)S(1)}, bf16[1,1,6144]{2,1,0:T(2,128)(2,1)}, u32[]{:S(2)}) copy-start(bf16[1,1,6144]{2,1,0:T(2,128)(2,1)} %param.13) | copy-start | bytes 36868
  149.8 345.6 %all-gather.13.cloned.1.call-start = ((), (), s32[]{:S(2)}) async-start(), calls=%async_computation.2 | async-start | bytes 3170304 | tf_op jit(solution)/shard_map/all_gather | solution.py:138
  151.2 461.3 %all-gather.11.cloned.1.call-start = ((), (), s32[]{:S(2)}) async-start(), calls=%async_computation.1 | async-start | bytes 3170304 | tf_op jit(solution)/shard_map/all_gather | solution.py:106
  380.3 6.1 collective-permute-start
  387.0 478.0 %all-reduce.11.cloned.1.call-start = ((), (), s32[]{:S(2)}) async-start(), calls=%async_computation.5 | async-start | bytes 6291456
  617.9 2.2 copy-start.1
  617.9 2.4 copy-start.6
  620.3 1.4 copy-start.4
  620.3 1.9 copy-start.8
  622.1 0.7 copy-start.14
  636.2 346.1 %all-gather.15.cloned.1.call-start = ((), (), s32[]{:S(2)}) async-start(), calls=%async_computation.3 | async-start | bytes 3170304 | tf_op jit(solution)/shard_map/all_gather | solution.py:138
  866.5 6.9 collective-permute-start.1
  874.1 385.7 %all-reduce.13.cloned.1.call-start = ((), (), s32[]{:S(2)}) async-start(), calls=%async_computation.6 | async-start | bytes 12582912
  987.7 2.7 copy-start.5
  992.6 6.5 copy-start.7
  1014.8 1.4 copy-start.2
  1016.9 1.4 copy-start.9
  1018.3 1.4 copy-start.10
Sparse Core Ops, SparseCore 0:
  12.2 114.7 all-gather.8
  149.9 228.7 all-reduce.8
  383.6 111.7 all-gather.12
  500.1 112.3 all-gather.10
  636.3 228.6 all-reduce.10
  874.2 108.0 all-gather.14
  1014.9 244.7 all-reduce.12
where the time goes:
time: 1270 us
  waiting for transfers between devices  1140 us (90%)
  local copies, waits for them, and re-layouts  54 us (4%)
  matrix products  28.6 us (2%)
  other arithmetic  26 us (2%)
  between operations  15.7 us (1%)
    unnamed x10, waiting for transfers between devices  690 us
    all_gather x2, waiting for transfers between devices, per_device(): gathered = lax.all_gather(current, 'et', axis=0, tiled=True)  225 us
    all_gather x2, waiting for transfers between devices, per_device(): grad_gathered = lax.all_gather(upstream, 'et', axis=0, tiled=True)  216 us
  transfers between devices with their start and end apart: 9, of which 9 were waited for; matrix products, arithmetic and copies ran while one was open for 2% of the time, Pallas kernels for 0%

commit v1 on v0

v1 whole, which is shorter than its diff:
```python
import jax
import jax.numpy as jnp
from jax import lax
from jax.sharding import PartitionSpec as P

LANES = 128
CONTRACT_LAST = (((1,), (1,)), ((), ()))
CONTRACT_FIRST = (((0,), (0,)), ((), ()))


def exchange(value):
    return lax.all_to_all(value, "et", 0, 0, tiled=True)


def spread(row):
    size = lax.axis_size("et")
    return exchange(jnp.broadcast_to(row[None], (size, *row.shape)))


def collect(parts):
    size = lax.axis_size("et")
    tiles = parts.reshape(size, -1, LANES).astype(jnp.bfloat16)
    return jnp.sum(exchange(tiles).astype(jnp.float32), axis=0)


def across(value, pairs):
    return lax.ppermute(value, "segment", pairs)


def dot_f32(a, b):
    return jnp.dot(a, b, preferred_element_type=jnp.float32)


def per_device(
    inputs,
    cotangent,
    gate_weight,
    up_weight,
    down_weight,
    route_rows,
    route_count,
    route_weight,
    width_mask,
):
    width = inputs.shape[2]
    half = width // 2
    tokens = lax.axis_size("et")
    first = lax.axis_index("segment") == 0
    gate_w = gate_weight[0]
    up_w = up_weight[0]
    down_w = down_weight[0]
    keep = width_mask[0, 0].astype(jnp.float32)
    to_one, to_zero, both = [(0, 1)], [(1, 0)], [(0, 1), (1, 0)]

    slots = route_rows.shape[2]
    live = jnp.arange(slots, dtype=jnp.int32) < route_count[0, 0]
    slot_scale = jnp.where(live, route_weight[0, 0], 0.0)
    chosen = route_rows[0, 0][None, :] == jnp.arange(tokens, dtype=jnp.int32)[:, None]
    scale = jnp.sum(jnp.where(chosen, slot_scale[None, :], 0.0), axis=1, keepdims=True)

    in_rows = inputs[0].reshape(2, half // LANES, LANES)
    in_half = jnp.where(first, in_rows[0], in_rows[1])
    cot_rows = cotangent[0].reshape(2, half // LANES, LANES)
    cot_half = jnp.where(first, cot_rows[0], cot_rows[1])
    cot_all = lax.all_gather(cotangent[0], "et", axis=0, tiled=True)

    mine = spread(in_half).reshape(tokens, half)
    tokens_in = jnp.concatenate([mine, across(mine, to_zero)], axis=1)
    gate_value = dot_f32(tokens_in, gate_w)
    up_value = dot_f32(tokens_in, up_w)
    hidden = (gate_value * jax.nn.sigmoid(gate_value) * up_value * keep).astype(jnp.bfloat16)
    outcome = (scale * dot_f32(hidden, down_w)).astype(jnp.bfloat16)
    other = across(outcome[:, half:], to_one)
    total = collect(jnp.where(first, outcome[:, :half], other))
    mid_half = (in_half.astype(jnp.float32) + total).astype(jnp.bfloat16)
    mine = spread(mid_half).reshape(tokens, half)
    tokens_mid = jnp.concatenate([across(mine, to_one), mine], axis=1)
    picked = jnp.where(first, tokens_in, tokens_mid)

    gate_value = dot_f32(picked, gate_w)
    up_value = dot_f32(picked, up_w)
    sig = jax.nn.sigmoid(gate_value)
    hidden = (gate_value * sig * up_value * keep).astype(jnp.bfloat16)
    outcome = (scale * dot_f32(hidden, down_w)).astype(jnp.bfloat16)
    gate_slope = keep * up_value * sig * (1.0 + gate_value * (1.0 - sig))
    up_slope = keep * gate_value * sig

    def backward(upstream):
        slot_grad_in = (scale * upstream.astype(jnp.float32)).astype(jnp.bfloat16)
        hidden_delta = lax.dot_general(
            slot_grad_in, down_w, CONTRACT_LAST, preferred_element_type=jnp.float32
        )
        gate_delta = (hidden_delta * gate_slope).astype(jnp.bfloat16)
        up_delta = (hidden_delta * up_slope).astype(jnp.bfloat16)
        slot_grad = lax.dot_general(
            gate_delta, gate_w, CONTRACT_LAST, preferred_element_type=jnp.float32
        ) + lax.dot_general(up_delta, up_w, CONTRACT_LAST, preferred_element_type=jnp.float32)
        return slot_grad_in, gate_delta, up_delta, slot_grad.astype(jnp.bfloat16)

    _, _, _, slot_grad = backward(cot_all)
    other = across(slot_grad[:, :half], to_zero)
    total = collect(jnp.where(first, other, slot_grad[:, half:]))
    back_half = (cot_half.astype(jnp.float32) + total).astype(jnp.bfloat16)
    mine = spread(back_half).reshape(tokens, half)
    back_all = jnp.concatenate([mine, across(mine, to_zero)], axis=1)
    upstream = jnp.where(first, back_all, cot_all)

    slot_grad_in, gate_delta, up_delta, slot_grad = backward(upstream)
    total = collect(jnp.where(first, slot_grad, outcome))

    def whole(piece):
        other_piece = across(piece, both)
        low = jnp.where(first, piece, other_piece)
        high = jnp.where(first, other_piece, piece)
        return jnp.concatenate([low, high], axis=0)

    mid_row = whole(mid_half)
    back_row = whole(back_half)
    last = (jnp.where(first, back_row, mid_row).astype(jnp.float32) + total).astype(jnp.bfloat16)
    section_output = jnp.where(first, mid_row, last)
    grad_input = jnp.where(first, last, back_row)

    grad_gate = lax.dot_general(
        picked, gate_delta, CONTRACT_FIRST, preferred_element_type=jnp.float32
    )
    grad_up = lax.dot_general(picked, up_delta, CONTRACT_FIRST, preferred_element_type=jnp.float32)
    grad_down = lax.dot_general(
        hidden, slot_grad_in, CONTRACT_FIRST, preferred_element_type=jnp.float32
    )
    return (
        section_output.reshape(1, 1, 1, width),
        grad_input.reshape(1, 1, 1, width),
        grad_gate.astype(jnp.bfloat16)[None],
        grad_up.astype(jnp.bfloat16)[None],
        grad_down.astype(jnp.bfloat16)[None],
    )


def solution(mesh):
    return jax.shard_map(
        per_device,
        mesh=mesh,
        in_specs=(
            P(None, "et", None),
            P(None, "et", None),
            P("segment", None, "et"),
            P("segment", None, "et"),
            P("segment", "et", None),
            P("segment", None, None),
            P("segment", None),
            P("segment", None, None),
            P("segment", "et"),
        ),
        out_specs=(
            P("segment", None, "et", None),
            P("segment", None, "et", None),
            P("segment", None, "et"),
            P("segment", None, "et"),
            P("segment", "et", None),
        ),
        check_vma=False,
    )
```

time: 1270 us -> 346 us (0.27)
  waiting for transfers between devices: 1140 us -> 173 us
  blocking collectives: 0 us -> 59 us
  starting transfers between devices: 8.01 us -> 61.6 us
  local copies, waits for them, and re-layouts: 54 us -> 9.64 us
  other arithmetic: 26 us -> 8.39 us
    unnamed x10 -> x1, waiting for transfers between devices: 690 us -> 0.68 us
    all_gather x4 -> x1, waiting for transfers between devices: 441 us -> 58.8 us  [per_device(): cot_all = lax.all_gather(cotangent[0], 'et', axis=0, tiled=True)]
    all_to_all x0 -> x4, waiting for transfers between devices: none -> 105 us  [exchange(): return lax.all_to_all(value, 'et', 0, 0, tiled=True)]
    all_to_all x0 -> x2, blocking collectives: none -> 59 us  [exchange(): return lax.all_to_all(value, 'et', 0, 0, tiled=True)]
    all_to_all x0 -> x4, starting transfers between devices: none -> 40.2 us  [exchange(): return lax.all_to_all(value, 'et', 0, 0, tiled=True)]
    gather x8 -> x0, local copies, waits for them, and re-layouts: 36.4 us -> none  [the longest x2 13 us: per_device(): added = jnp.take(slot_scale[:, None] * outcome, inverse, axis=0)]
    select_n x9 -> x6, other arithmetic: 18.9 us -> 3.46 us  [the longest x1 1.86 us: per_device(): picked = jnp.where(first, tokens_in, tokens_mid)]
    ppermute x2 -> x7, starting transfers between devices: 7.31 us -> 21.4 us  [across(): return lax.ppermute(value, 'segment', pairs)]
  transfers between devices with their start and end apart: 9 -> 12, of which waited for: 9 -> 11; matrix products, arithmetic and copies ran while one was open for 2% -> 4% of each run, Pallas kernels for 0% -> 0%
where the time goes in v1:
time: 346 us
  waiting for transfers between devices  173 us (50%)
  starting transfers between devices  61.6 us (18%)
  blocking collectives  59 us (17%)
  matrix products  17.9 us (5%)
  between operations  15.7 us (5%)
  local copies, waits for them, and re-layouts  9.64 us (3%)
  other arithmetic  8.39 us (2%)
    all_to_all x4, waiting for transfers between devices, exchange(): return lax.all_to_all(value, 'et', 0, 0, tiled=True)  105 us
    all_to_all x2, blocking collectives, exchange(): return lax.all_to_all(value, 'et', 0, 0, tiled=True)  59 us
    all_gather x1, waiting for transfers between devices, per_device(): cot_all = lax.all_gather(cotangent[0], 'et', axis=0, tiled=True)  58.8 us
    all_to_all x4, starting transfers between devices, exchange(): return lax.all_to_all(value, 'et', 0, 0, tiled=True)  40.2 us
    ppermute x7, starting transfers between devices, across(): return lax.ppermute(value, 'segment', pairs)  21.4 us
    ppermute x7, waiting for transfers between devices, across(): return lax.ppermute(value, 'segment', pairs)  8.33 us
    unnamed x33, local copies, waits for them, and re-layouts  8.25 us
  transfers between devices with their start and end apart: 12, of which 11 were waited for; matrix products, arithmetic and copies ran while one was open for 4% of the time, Pallas kernels for 0%

profile of v1, /device:TPU:1, one launch (start us, length us, event | category | flops | bytes accessed | tf_op | source)
XLA Modules:
  0.0 345.5 jit_solution(17823842290551725506)
XLA Ops:
  7.2 0.9 fusion.45
  8.1 1.0 broadcast_in_dim.49
  9.1 16.5 %all-to-all-start = ((bf16[128,24,128]{2,1,0:T(8,128)(2,1)}), bf16[128,24,128]{2,1,0:T(8,128)(2,1)S(1)}, u32[]{:S(2)}, u32[]{:S(2)}) async-start(bf16[128,24,128]{2,1,0:T(8,128)(2,1)} %broadcast_in_dim.49), calls=%async_computation | async-start | bytes 1572864 | tf_op jit(solution)/shard_map/all_to_all | solution.py:12
  26.9 23.4 %all-to-all-done = bf16[128,24,128]{2,1,0:T(8,128)(2,1)S(1)} async-done(((bf16[128,24,128]{2,1,0:T(8,128)(2,1)}), bf16[128,24,128]{2,1,0:T(8,128)(2,1)S(1)}, u32[]{:S(2)}, u32[]{:S(2)}) %all-to-all-start) | async-done | bytes 786464 | tf_op jit(solution)/shard_map/all_to_all | solution.py:12
  50.4 4.5 %collective-permute-start = (bf16[128,3072]{1,0:T(8,128)(2,1)S(1)}, bf16[128,3072]{1,0:T(8,128)(2,1)S(1)}, u32[]{:S(2)}, u32[]{:S(2)}) collective-permute-start(bf16[128,3072]{1,0:T(8,128)(2,1)S(1)} %bitcast.104), channel_id=1, source_target_pairs={{128,0},{129,1},{130,2},{131,3},{132,4},{133,5},{134,6},{135,7},{1... | collective-permute-start | bytes 2359304 | tf_op jit(solution)/shard_map/ppermute | solution.py:27
  55.1 1.4 constant_dynamic-update-slice_fusion.1
  57.4 0.6 copy-done.4
  58.0 3.0 fusion
  61.0 1.3 collective-permute-start.1
  62.3 2.9 collective-permute-done.1
  65.3 1.0 copy.17
  66.3 6.2 %all-to-all-start.1 = ((bf16[128,24,128]{2,1,0:T(8,128)(2,1)}), bf16[128,24,128]{2,1,0:T(8,128)(2,1)S(1)}, u32[]{:S(2)}, u32[]{:S(2)}) async-start(bf16[128,24,128]{2,1,0:T(8,128)(2,1)} %bitcast.17), calls=%async_computation.1 | async-start | bytes 1572864 | tf_op jit(solution)/shard_map/all_to_all | solution.py:12
  72.6 0.7 all-gather.3.cloned.1.call-update
  73.3 24.8 %all-to-all-done.1 = bf16[128,24,128]{2,1,0:T(8,128)(2,1)S(1)} async-done(((bf16[128,24,128]{2,1,0:T(8,128)(2,1)}), bf16[128,24,128]{2,1,0:T(8,128)(2,1)S(1)}, u32[]{:S(2)}, u32[]{:S(2)}) %all-to-all-start.1) | async-done | bytes 786464 | tf_op jit(solution)/shard_map/all_to_all | solution.py:12
  98.4 29.6 %all_to_all.30 = bf16[128,24,128]{2,1,0:T(8,128)(2,1)S(1)} all-to-all(bf16[128,24,128]{2,1,0:T(8,128)(2,1)S(1)} %broadcast_in_dim.50), channel_id=1, replica_groups=mesh['segment'=2,'et'=128] {'et'}, dimensions={0} | all-to-all | bytes 1572864 | tf_op jit(solution)/shard_map/all_to_all | solution.py:12
  128.0 1.0 copy.33
  129.1 1.5 collective-permute-start.3
  130.5 58.8 %all-gather.3.cloned.1.call-done = bf16[128,1,6144]{2,1,0:T(2,128)(2,1)} async-done(((bf16[1,1,6144]{2,1,0:T(2,128)(2,1)}), bf16[128,1,6144]{2,1,0:T(2,128)(2,1)}) %all-gather.3.cloned.1.call-update) | async-done | bytes 1572880 | tf_op jit(solution)/shard_map/all_gather | solution.py:65
  189.3 3.0 fusion.8
  192.4 1.9 maximum_select_fusion
  194.2 0.6 fusion.17
  195.4 0.6 fusion.23
  196.0 0.6 fusion.1
  196.6 7.1 %collective-permute-start.4 = (bf16[128,3072]{1,0:T(8,128)(2,1)S(1)}, bf16[128,3072]{1,0:T(8,128)(2,1)S(1)}, u32[]{:S(2)}, u32[]{:S(2)}) collective-permute-start(bf16[128,3072]{1,0:T(8,128)(2,1)S(1)} %slice.38), channel_id=1, source_target_pairs={{128,0},{129,1},{130,2},{131,3},{132,4},{133,5},{134,6},{135,7},{1... | collective-permute-start | bytes 2359304 | tf_op jit(solution)/shard_map/ppermute | solution.py:27
  203.8 1.8 collective-permute-done.4
  205.7 1.0 copy.19
  206.7 10.3 %all-to-all-start.3 = ((bf16[128,24,128]{2,1,0:T(8,128)(2,1)}), bf16[128,24,128]{2,1,0:T(8,128)(2,1)}, u32[]{:S(2)}, u32[]{:S(2)}) async-start(bf16[128,24,128]{2,1,0:T(8,128)(2,1)} %bitcast.99), calls=%async_computation.3 | async-start | bytes 1572864 | tf_op jit(solution)/shard_map/all_to_all | solution.py:12
  217.1 24.7 %all-to-all-done.3 = bf16[128,24,128]{2,1,0:T(8,128)(2,1)} async-done(((bf16[128,24,128]{2,1,0:T(8,128)(2,1)}), bf16[128,24,128]{2,1,0:T(8,128)(2,1)}, u32[]{:S(2)}, u32[]{:S(2)}) %all-to-all-start.3) | async-done | bytes 786464 | tf_op jit(solution)/shard_map/all_to_all | solution.py:12
  241.7 1.3 convert_reduce_fusion.1
  243.1 29.4 %all_to_all.31 = bf16[128,24,128]{2,1,0:T(8,128)(2,1)S(1)} all-to-all(bf16[128,24,128]{2,1,0:T(8,128)(2,1)S(1)} %broadcast_in_dim.51), channel_id=1, replica_groups=mesh['segment'=2,'et'=128] {'et'}, dimensions={0} | all-to-all | bytes 1572864 | tf_op jit(solution)/shard_map/all_to_all | solution.py:12
  272.7 6.1 %collective-permute-start.6 = (bf16[128,3072]{1,0:T(8,128)(2,1)S(1)}, bf16[128,3072]{1,0:T(8,128)(2,1)S(1)}, u32[]{:S(2)}, u32[]{:S(2)}) collective-permute-start(bf16[128,3072]{1,0:T(8,128)(2,1)S(1)} %bitcast.102), channel_id=1, source_target_pairs={{128,0},{129,1},{130,2},{131,3},{132,4},{133,5},{134,6},{135,7},{1... | collective-permute-start | bytes 2359304 | tf_op jit(solution)/shard_map/ppermute | solution.py:27
  278.8 1.6 collective-permute-done.6
  280.4 1.5 multiply_convert_fusion
  281.9 0.6 multiply_convert_fusion.3
  283.1 0.6 fusion.21
  283.6 0.8 copy-done.3
  284.5 0.6 fusion.2
  285.0 0.7 fusion.30
  285.7 1.5 copy.21
  287.2 7.3 %all-to-all-start.5 = ((bf16[128,48,128]{2,1,0:T(8,128)(2,1)}), bf16[128,48,128]{2,1,0:T(8,128)(2,1)}, u32[]{:S(2)}, u32[]{:S(2)}) async-start(bf16[128,48,128]{2,1,0:T(8,128)(2,1)} %bitcast.98), calls=%async_computation.5 | async-start | bytes 3145728 | tf_op jit(solution)/shard_map/all_to_all | solution.py:12
  294.9 0.8 collective-permute-done.2
  296.2 0.8 collective-permute-done.5
  297.1 3.2 fusion.7
  300.2 1.8 fusion.6
  302.0 1.8 fusion.5
  303.7 32.6 %all-to-all-done.5 = bf16[128,48,128]{2,1,0:T(8,128)(2,1)} async-done(((bf16[128,48,128]{2,1,0:T(8,128)(2,1)}), bf16[128,48,128]{2,1,0:T(8,128)(2,1)}, u32[]{:S(2)}, u32[]{:S(2)}) %all-to-all-start.5) | async-done | bytes 1572896 | tf_op jit(solution)/shard_map/all_to_all | solution.py:12
  336.3 1.7 convert_reduce_fusion
  338.0 0.7 broadcast_select_fusion
  (52 shorter events, 4.2 us)
Async XLA Ops:
  7.2 50.8 %copy-start = (bf16[1,6144,128]{2,1,0:T(8,128)(2,1)S(1)}, bf16[1,6144,128]{2,1,0:T(8,128)(2,1)}, u32[]{:S(2)}) copy-start(bf16[1,6144,128]{2,1,0:T(8,128)(2,1)} %param.11) | copy-start | bytes 4718596
  7.2 19.7 %copy-start.11 = (f32[1,1,128]{2,1,0:T(1,128)S(1)}, f32[1,1,128]{2,1,0:T(1,128)}, u32[]{:S(2)}) copy-start(f32[1,1,128]{2,1,0:T(1,128)} %param.16) | copy-start | bytes 1540
  9.1 45.9 %copy-start.12 = (s32[1,1,128]{2,1,0:T(1,128)S(1)}, s32[1,1,128]{2,1,0:T(1,128)}, u32[]{:S(2)}) copy-start(s32[1,1,128]{2,1,0:T(1,128)} %param.14) | copy-start | bytes 1540
  9.1 41.2 %all-to-all-start = ((bf16[128,24,128]{2,1,0:T(8,128)(2,1)}), bf16[128,24,128]{2,1,0:T(8,128)(2,1)S(1)}, u32[]{:S(2)}, u32[]{:S(2)}) async-start(bf16[128,24,128]{2,1,0:T(8,128)(2,1)} %broadcast_in_dim.49), calls=%async_computation | async-start | bytes 1572864 | tf_op jit(solution)/shard_map/all_to_all | solution.py:12
  50.2 4.7 %copy-start.8 = (bf16[128,24,128]{2,1,0:T(8,128)(2,1)}, bf16[128,24,128]{2,1,0:T(8,128)(2,1)S(1)}, u32[]{:S(2)}) copy-start(bf16[128,24,128]{2,1,0:T(8,128)(2,1)S(1)} %all-to-all-done) | copy-start | bytes 2359300
  50.4 6.4 %collective-permute-start = (bf16[128,3072]{1,0:T(8,128)(2,1)S(1)}, bf16[128,3072]{1,0:T(8,128)(2,1)S(1)}, u32[]{:S(2)}, u32[]{:S(2)}) collective-permute-start(bf16[128,3072]{1,0:T(8,128)(2,1)S(1)} %bitcast.104), channel_id=1, source_target_pairs={{128,0},{129,1},{130,2},{131,3},{132,4},{133,5},{134,6},{135,7},{1... | collective-permute-start | bytes 2359304 | tf_op jit(solution)/shard_map/ppermute | solution.py:27
  55.1 1.8 copy-start.1
  56.8 1.1 copy-start.4
  61.0 4.2 %collective-permute-start.1 = (bf16[128,3072]{1,0:T(8,128)(2,1)S(1)}, bf16[128,3072]{1,0:T(8,128)(2,1)S(1)}, u32[]{:S(2)}, u32[]{:S(2)}) collective-permute-start(bf16[128,3072]{1,0:T(8,128)(2,1)S(1)} %slice.37), channel_id=1, source_target_pairs={{0,128},{1,129},{2,130},{3,131},{4,132},{5,133},{6,134},{7,135},{8... | collective-permute-start | bytes 2359304 | tf_op jit(solution)/shard_map/ppermute | solution.py:27
  66.3 31.8 %all-to-all-start.1 = ((bf16[128,24,128]{2,1,0:T(8,128)(2,1)}), bf16[128,24,128]{2,1,0:T(8,128)(2,1)S(1)}, u32[]{:S(2)}, u32[]{:S(2)}) async-start(bf16[128,24,128]{2,1,0:T(8,128)(2,1)} %bitcast.17), calls=%async_computation.1 | async-start | bytes 1572864 | tf_op jit(solution)/shard_map/all_to_all | solution.py:12
  72.5 116.8 %all-gather.3.cloned.1.call-start = ((), (), s32[]{:S(2)}) async-start(), calls=%async_computation.6 | async-start | bytes 3170304 | tf_op jit(solution)/shard_map/all_gather | solution.py:65
  98.4 90.9 %copy-start.5 = (bf16[1,128,6144]{2,1,0:T(8,128)(2,1)S(1)}, bf16[1,128,6144]{2,1,0:T(8,128)(2,1)}, u32[]{:S(2)}) copy-start(bf16[1,128,6144]{2,1,0:T(8,128)(2,1)} %param.13) | copy-start | bytes 4718596
  129.1 63.3 %collective-permute-start.3 = (bf16[128,3072]{1,0:T(8,128)(2,1)}, bf16[128,3072]{1,0:T(8,128)(2,1)}, u32[]{:S(2)}, u32[]{:S(2)}) collective-permute-start(bf16[128,3072]{1,0:T(8,128)(2,1)} %bitcast.93), channel_id=1, source_target_pairs={{0,128},{1,129},{2,130},{3,131},{4,132},{5,133},{6,134},{7,135},{8... | collective-permute-start | bytes 2359304 | tf_op jit(solution)/shard_map/ppermute | solution.py:27
  192.3 1.9 copy-start.2
  196.6 9.0 %collective-permute-start.4 = (bf16[128,3072]{1,0:T(8,128)(2,1)S(1)}, bf16[128,3072]{1,0:T(8,128)(2,1)S(1)}, u32[]{:S(2)}, u32[]{:S(2)}) collective-permute-start(bf16[128,3072]{1,0:T(8,128)(2,1)S(1)} %slice.38), channel_id=1, source_target_pairs={{128,0},{129,1},{130,2},{131,3},{132,4},{133,5},{134,6},{135,7},{1... | collective-permute-start | bytes 2359304 | tf_op jit(solution)/shard_map/ppermute | solution.py:27
  205.7 11.4 %copy-start.10 = (bf16[1,1,6144]{2,1,0:T(2,128)(2,1)S(1)}, bf16[1,1,6144]{2,1,0:T(2,128)(2,1)}, u32[]{:S(2)}) copy-start(bf16[1,1,6144]{2,1,0:T(2,128)(2,1)} %param.10) | copy-start | bytes 36868
  206.7 35.0 %all-to-all-start.3 = ((bf16[128,24,128]{2,1,0:T(8,128)(2,1)}), bf16[128,24,128]{2,1,0:T(8,128)(2,1)}, u32[]{:S(2)}, u32[]{:S(2)}) async-start(bf16[128,24,128]{2,1,0:T(8,128)(2,1)} %bitcast.99), calls=%async_computation.3 | async-start | bytes 1572864 | tf_op jit(solution)/shard_map/all_to_all | solution.py:12
  243.1 37.3 %copy-start.9 = (bf16[128,1,6144]{2,1,0:T(2,128)(2,1)S(1)}, bf16[128,1,6144]{2,1,0:T(2,128)(2,1)}, u32[]{:S(2)}) copy-start(bf16[128,1,6144]{2,1,0:T(2,128)(2,1)} %all-gather.3.cloned.1.call-done) | copy-start | bytes 4718596
  272.7 9.2 %copy-start.6 = (bf16[1,128,6144]{2,1,0:T(8,128)(2,1)S(1)}, bf16[1,128,6144]{2,1,0:T(8,128)(2,1)}, u32[]{:S(2)}) copy-start(bf16[1,128,6144]{2,1,0:T(8,128)(2,1)} %param.13) | copy-start | bytes 4718596
  272.7 7.7 %collective-permute-start.6 = (bf16[128,3072]{1,0:T(8,128)(2,1)S(1)}, bf16[128,3072]{1,0:T(8,128)(2,1)S(1)}, u32[]{:S(2)}, u32[]{:S(2)}) collective-permute-start(bf16[128,3072]{1,0:T(8,128)(2,1)S(1)} %bitcast.102), channel_id=1, source_target_pairs={{128,0},{129,1},{130,2},{131,3},{132,4},{133,5},{134,6},{135,7},{1... | collective-permute-start | bytes 2359304 | tf_op jit(solution)/shard_map/ppermute | solution.py:27
  281.9 1.1 copy-start.7
  283.0 1.4 copy-start.3
  287.2 49.1 %all-to-all-start.5 = ((bf16[128,48,128]{2,1,0:T(8,128)(2,1)}), bf16[128,48,128]{2,1,0:T(8,128)(2,1)}, u32[]{:S(2)}, u32[]{:S(2)}) async-start(bf16[128,48,128]{2,1,0:T(8,128)(2,1)} %bitcast.98), calls=%async_computation.5 | async-start | bytes 3145728 | tf_op jit(solution)/shard_map/all_to_all | solution.py:12
  294.5 1.3 collective-permute-start.2
  295.8 1.3 collective-permute-start.5
Sparse Core Ops, SparseCore 0:
  77.0 112.2 all-gather.2

commit v2 on v1

v2 whole, which is shorter than its diff:
```python
import jax
import jax.numpy as jnp
from jax import lax
from jax.sharding import Mesh
from jax.sharding import PartitionSpec as P

LANES = 128
PLANE = ("x", "y")
LINE = "z"
ET = ("x", "y", "z")
SIZES = (4, 4, 8)
CONTRACT_LAST = (((1,), (1,)), ((), ()))
CONTRACT_FIRST = (((0,), (0,)), ((), ()))


def exchange(value, axes):
    return lax.all_to_all(value, axes, 0, 0, tiled=True)


def copies(value, count):
    return jnp.broadcast_to(value[None], (count, *value.shape))


def add_bf16(a, b):
    return (a.astype(jnp.float32) + b.astype(jnp.float32)).astype(jnp.bfloat16)


def dot_f32(a, b):
    return jnp.dot(a, b, preferred_element_type=jnp.float32)


def dot_last(a, b):
    return lax.dot_general(a, b, CONTRACT_LAST, preferred_element_type=jnp.float32)


def dot_first(a, b):
    return lax.dot_general(a, b, CONTRACT_FIRST, preferred_element_type=jnp.float32)


def plane_sum(parts, line):
    plane = parts.shape[0] // line
    blocks = exchange(parts.reshape(plane, line, parts.shape[1]), PLANE)
    return jnp.sum(blocks.astype(jnp.float32), axis=0).astype(jnp.bfloat16)


def line_sum(block):
    blocks = exchange(copies(block, lax.axis_size(LINE)), LINE)
    return jnp.sum(blocks.reshape(-1, *block.shape).astype(jnp.float32), axis=0)


def line_sum_steps(block):
    line = lax.axis_size(LINE)
    total = block.astype(jnp.float32)
    stride = 1
    while stride < line:
        pairs = [(i, i ^ stride) for i in range(line)]
        block = total.astype(jnp.bfloat16)
        total = block.astype(jnp.float32) + lax.ppermute(block, LINE, pairs).astype(jnp.float32)
        stride *= 2
    return total


def plane_spread(block, plane):
    return exchange(copies(block, plane), PLANE).reshape(-1, block.shape[1])


def across(value, pairs):
    return lax.ppermute(value, "segment", pairs)


def per_device(
    inputs,
    cotangent,
    gate_weight,
    up_weight,
    down_weight,
    route_rows,
    route_count,
    route_weight,
    width_mask,
):
    width = inputs.shape[2]
    half = width // 2
    line = lax.axis_size(LINE)
    plane = lax.axis_size("x") * lax.axis_size("y")
    tokens = plane * line
    first = lax.axis_index("segment") == 0
    gate_w = gate_weight[0]
    up_w = up_weight[0]
    down_w = down_weight[0]
    keep = width_mask[0, 0].astype(jnp.float32)
    to_one, to_zero, both = [(0, 1)], [(1, 0)], [(0, 1), (1, 0)]

    slots = route_rows.shape[2]
    live = jnp.arange(slots, dtype=jnp.int32) < route_count[0, 0]
    slot_scale = jnp.where(live, route_weight[0, 0], 0.0)
    chosen = route_rows[0, 0][None, :] == jnp.arange(tokens, dtype=jnp.int32)[:, None]
    scale = jnp.sum(jnp.where(chosen, slot_scale[None, :], 0.0), axis=1, keepdims=True)

    def expert_inputs(low, high):
        gate_value = dot_f32(low, gate_w[:half]) + dot_f32(high, gate_w[half:])
        up_value = dot_f32(low, up_w[:half]) + dot_f32(high, up_w[half:])
        return gate_value, up_value

    def scaled(rows):
        return (scale * rows.astype(jnp.float32)).astype(jnp.bfloat16)

    def hidden_of(gate_value, up_value):
        return (gate_value * jax.nn.sigmoid(gate_value) * up_value * keep).astype(jnp.bfloat16)

    def slot_gradient(gate_delta, up_delta, columns):
        return (
            dot_last(gate_delta, gate_w[columns]) + dot_last(up_delta, up_w[columns])
        ).astype(jnp.bfloat16)

    in_row = inputs[0].reshape(2, half // LANES, LANES)
    in_half = jnp.where(first, in_row[0], in_row[1])
    cot_row = cotangent[0].reshape(width // LANES, LANES)
    rows = jnp.concatenate([in_half, cot_row], axis=0)
    rows = exchange(copies(rows, line), LINE)
    in_block = rows[:, : half // LANES].reshape(line, half)
    cot_block = rows[:, half // LANES :].reshape(line, width)
    cot_half = jnp.where(first, cot_block[:, :half], cot_block[:, half:])

    in_mine = plane_spread(in_block, plane)
    in_other = across(in_mine, to_zero)
    gate_zero, up_zero = expert_inputs(in_mine, in_other)
    hidden = hidden_of(gate_zero, up_zero)
    out_high = (scale * dot_f32(hidden, down_w[:, half:])).astype(jnp.bfloat16)
    received = across(out_high, to_one)
    out_low = (scale * dot_f32(hidden, down_w[:, :half])).astype(jnp.bfloat16)
    partial = jnp.where(first, out_low, received)
    partial, cot_part = lax.optimization_barrier((plane_sum(partial, line), cot_half))
    cot_mine = plane_spread(cot_part, plane)
    mid_block = add_bf16(in_block, line_sum_steps(partial))
    mid_block, cot_mine = lax.optimization_barrier((mid_block, cot_mine))
    cot_other = across(cot_mine, to_one)
    mid_mine = plane_spread(mid_block, plane)
    mid_other = across(mid_mine, to_one)

    cot_low, cot_high = scaled(cot_other), scaled(cot_mine)
    delta_one = dot_last(cot_low, down_w[:, :half]) + dot_last(cot_high, down_w[:, half:])
    gate_one, up_one = expert_inputs(mid_other, mid_mine)
    gate_value = jnp.where(first, gate_zero, gate_one)
    up_value = jnp.where(first, up_zero, up_one)
    sig = jax.nn.sigmoid(gate_value)
    gate_slope = keep * up_value * sig * (1.0 + gate_value * (1.0 - sig))
    up_slope = keep * gate_value * sig
    gate_delta = (delta_one * gate_slope).astype(jnp.bfloat16)
    up_delta = (delta_one * up_slope).astype(jnp.bfloat16)
    low, high = slice(0, half), slice(half, width)
    grad_low = slot_gradient(gate_delta, up_delta, low)
    received = across(grad_low, to_zero)
    grad_high = slot_gradient(gate_delta, up_delta, high)
    total = line_sum(plane_sum(jnp.where(first, received, grad_high), line))
    back_block = add_bf16(cot_half, total)
    hidden = hidden_of(gate_value, up_value)
    outcome = (scale * dot_f32(hidden, down_w)).astype(jnp.bfloat16)
    back_mine = plane_spread(back_block, plane)
    back_other = across(back_mine, to_zero)

    back_low, back_high = scaled(back_mine), scaled(back_other)
    delta_zero = dot_last(back_low, down_w[:, :half]) + dot_last(back_high, down_w[:, half:])
    delta = jnp.where(first, delta_zero, delta_one)
    gate_delta = (delta * gate_slope).astype(jnp.bfloat16)
    up_delta = (delta * up_slope).astype(jnp.bfloat16)
    slot_grad = slot_gradient(gate_delta, up_delta, slice(0, width))
    block = plane_sum(jnp.where(first, slot_grad, outcome), line)
    parts = exchange(block.reshape(line, width // LANES, LANES), LINE)
    total = jnp.sum(parts.astype(jnp.float32), axis=0).reshape(width)

    place = lax.axis_index(LINE)
    mine = jnp.stack([mid_block, back_block], axis=1)[place]
    other = across(mine, both)
    whole = jnp.concatenate(
        [jnp.where(first, mine, other), jnp.where(first, other, mine)], axis=1
    )
    mid_row, back_row = whole[0], whole[1]
    last = (jnp.where(first, back_row, mid_row).astype(jnp.float32) + total).astype(jnp.bfloat16)
    section_output = jnp.where(first, mid_row, last)
    grad_input = jnp.where(first, last, back_row)

    picked_low = jnp.where(first, in_mine, mid_other)
    picked_high = jnp.where(first, in_other, mid_mine)
    picked = jnp.concatenate([picked_low, picked_high], axis=1)
    slot_low = jnp.where(first, back_low, cot_low)
    slot_high = jnp.where(first, back_high, cot_high)
    slot_grad_in = jnp.concatenate([slot_low, slot_high], axis=1)
    grad_gate = dot_first(picked, gate_delta)
    grad_up = dot_first(picked, up_delta)
    grad_down = dot_first(hidden, slot_grad_in)
    return (
        section_output.reshape(1, 1, 1, width),
        grad_input.reshape(1, 1, 1, width),
        grad_gate.astype(jnp.bfloat16)[None],
        grad_up.astype(jnp.bfloat16)[None],
        grad_down.astype(jnp.bfloat16)[None],
    )


def solution(mesh):
    torus = Mesh(mesh.devices.reshape(-1, *SIZES), ("segment", *ET))
    return jax.shard_map(
        per_device,
        mesh=torus,
        in_specs=(
            P(None, ET, None),
            P(None, ET, None),
            P("segment", None, ET),
            P("segment", None, ET),
            P("segment", ET, None),
            P("segment", None, None),
            P("segment", None),
            P("segment", None, None),
            P("segment", ET),
        ),
        out_specs=(
            P("segment", None, ET, None),
            P("segment", None, ET, None),
            P("segment", None, ET),
            P("segment", None, ET),
            P("segment", ET, None),
        ),
        check_vma=False,
    )
```

time: 346 us -> 237 us (0.68)
  waiting for transfers between devices: 173 us -> 80.9 us
  between operations: 15.7 us -> 2.48 us
  blocking collectives: 59 us -> 49.3 us
  matrix products: 17.9 us -> 24.6 us
  local copies, waits for them, and re-layouts: 9.64 us -> 5.54 us
  other arithmetic: 8.39 us -> 12.2 us
    all_gather x1 -> x0, waiting for transfers between devices: 58.8 us -> none  [per_device(): cot_all = lax.all_gather(cotangent[0], 'et', axis=0, tiled=True)]
    all_to_all x4 -> x7, waiting for transfers between devices: 105 us -> 68.1 us  [exchange(): return lax.all_to_all(value, axes, 0, 0, tiled=True)]
    all_to_all x2 -> x3, blocking collectives: 59 us -> 49.3 us  [exchange(): return lax.all_to_all(value, axes, 0, 0, tiled=True)]
    all_to_all x4 -> x7, starting transfers between devices: 40.2 us -> 32 us  [exchange(): return lax.all_to_all(value, axes, 0, 0, tiled=True)]
    unnamed x33 -> x38, local copies, waits for them, and re-layouts: 8.25 us -> 1.67 us
    dot_general x5 -> x11, matrix products: 5.36 us -> 11.4 us  [dot_f32(): return jnp.dot(a, b, preferred_element_type=jnp.float32)]
    ppermute x0 -> x3, waiting for transfers between devices: none -> 5.87 us  [line_sum_steps(): lax.ppermute(block, LINE, pairs).astype(jnp.float32)]
    select_n x4 -> x6, other arithmetic: 2.76 us -> 7.55 us  [the longest x1 2.35 us: per_device(): picked_low = jnp.where(first, in_mine, mid_other)]
  transfers between devices with their start and end apart: 12 -> 17, of which waited for: 11 -> 12; matrix products, arithmetic and copies ran while one was open for 4% -> 12% of each run, Pallas kernels for 0% -> 0%
where the time goes in v2:
time: 237 us; the launch traced here: 234 us
  waiting for transfers between devices  80.9 us (34%)
  starting transfers between devices  59.3 us (25%)
  blocking collectives  49.3 us (21%)
  matrix products  24.6 us (10%)
  other arithmetic  12.2 us (5%)
  local copies, waits for them, and re-layouts  5.54 us (2%)
  between operations  2.48 us (1%)
    all_to_all x7, waiting for transfers between devices, exchange(): return lax.all_to_all(value, axes, 0, 0, tiled=True)  68.1 us
    all_to_all x3, blocking collectives, exchange(): return lax.all_to_all(value, axes, 0, 0, tiled=True)  49.3 us
    all_to_all x7, starting transfers between devices, exchange(): return lax.all_to_all(value, axes, 0, 0, tiled=True)  32 us
    ppermute x7, starting transfers between devices, across(): return lax.ppermute(value, 'segment', pairs)  23.1 us
    dot_general x11, matrix products, dot_f32(): return jnp.dot(a, b, preferred_element_type=jnp.float32)  11.4 us
    dot_general x10, matrix products, dot_last(): lax.dot_general(a, b, CONTRACT_LAST, preferred_element_type=jnp.float32)  8 us
    ppermute x7, waiting for transfers between devices, across(): return lax.ppermute(value, 'segment', pairs)  6.91 us
    ppermute x3, waiting for transfers between devices, line_sum_steps(): lax.ppermute(block, LINE, pairs).astype(jnp.float32)  5.87 us
  transfers between devices with their start and end apart: 17, of which 12 were waited for; matrix products, arithmetic and copies ran while one was open for 12% of the time, Pallas kernels for 0%

profile of v2, /device:TPU:1, one launch (start us, length us, event | category | flops | bytes accessed | tf_op | source)
XLA Modules:
  0.0 234.4 jit_solution(14820708106319398689)
XLA Ops:
  2.4 16.7 %all_to_all.50 = bf16[8,72,128]{2,1,0:T(8,128)(2,1)S(1)} all-to-all(bf16[8,72,128]{2,1,0:T(8,128)(2,1)S(1)} %broadcast_in_dim.34), channel_id=1, replica_groups=mesh['segment'=2,'x'=4,'y'=4,'z'=8] {'z'}, dimensions={0} | all-to-all | bytes 294912 | tf_op jit(solution)/shard_map/all_to_all | solution.py:17
  19.2 1.0 broadcast_in_dim.38
  20.1 6.9 %all-to-all-start.1 = ((bf16[16,8,3072]{2,1,0:T(8,128)(2,1)}), bf16[16,8,3072]{2,1,0:T(8,128)(2,1)}, u32[]{:S(2)}, u32[]{:S(2)}) async-start(bf16[16,8,3072]{2,1,0:T(8,128)(2,1)} %broadcast_in_dim.38), calls=%async_computation.1 | async-start | bytes 1572864 | tf_op jit(solution)/shard_map/all_to_all | solution.py:17
  28.4 9.3 %all-to-all-done.1 = bf16[16,8,3072]{2,1,0:T(8,128)(2,1)} async-done(((bf16[16,8,3072]{2,1,0:T(8,128)(2,1)}), bf16[16,8,3072]{2,1,0:T(8,128)(2,1)}, u32[]{:S(2)}, u32[]{:S(2)}) %all-to-all-start.1) | async-done | bytes 786464 | tf_op jit(solution)/shard_map/all_to_all | solution.py:17
  37.7 6.7 %collective-permute-start = (bf16[128,3072]{1,0:T(8,128)(2,1)}, bf16[128,3072]{1,0:T(8,128)(2,1)S(1)}, u32[]{:S(2)}, u32[]{:S(2)}) collective-permute-start(bf16[128,3072]{1,0:T(8,128)(2,1)} %bitcast.3), channel_id=1, source_target_pairs={{128,0},{129,1},{130,2},{131,3},{132,4},{133,5},{134,6},{135,7},{1... | collective-permute-start | bytes 2359304 | tf_op jit(solution)/shard_map/ppermute | solution.py:68
  44.5 1.5 fusion.40
  46.0 1.5 fusion.30
  47.9 1.0 multiply_convert_fusion.13
  49.5 1.3 collective-permute-start.1
  50.9 2.9 %collective-permute-done.1 = bf16[128,3072]{1,0:T(8,128)(2,1)S(1)} collective-permute-done((bf16[128,3072]{1,0:T(8,128)(2,1)S(1)}, bf16[128,3072]{1,0:T(8,128)(2,1)S(1)}, u32[]{:S(2)}, u32[]{:S(2)}) %collective-permute-start.1) | collective-permute-done | bytes 786464 | tf_op jit(solution)/shard_map/ppermute | solution.py:68
  53.7 1.2 fusion.13
  55.0 4.3 %all-to-all-start.2 = ((bf16[16,8,3072]{2,1,0:T(8,128)(2,1)}), bf16[16,8,3072]{2,1,0:T(8,128)(2,1)}, u32[]{:S(2)}, u32[]{:S(2)}) async-start(bf16[16,8,3072]{2,1,0:T(8,128)(2,1)} %fusion.13), calls=%async_computation.2 | async-start | bytes 1572864 | tf_op jit(solution)/shard_map/all_to_all | solution.py:17
  59.3 13.9 %all-to-all-done.2 = bf16[16,8,3072]{2,1,0:T(8,128)(2,1)} async-done(((bf16[16,8,3072]{2,1,0:T(8,128)(2,1)}), bf16[16,8,3072]{2,1,0:T(8,128)(2,1)}, u32[]{:S(2)}, u32[]{:S(2)}) %all-to-all-start.2) | async-done | bytes 786464 | tf_op jit(solution)/shard_map/all_to_all | solution.py:17
  73.3 1.2 reduce_sum.64
  75.3 2.3 collective-permute-done.2
  78.6 4.3 %all-to-all-start.3 = ((bf16[16,8,3072]{2,1,0:T(8,128)(2,1)}), bf16[16,8,3072]{2,1,0:T(8,128)(2,1)}, u32[]{:S(2)}, u32[]{:S(2)}) async-start(bf16[16,8,3072]{2,1,0:T(8,128)(2,1)} %broadcast_in_dim.68), calls=%async_computation.3 | async-start | bytes 1572864 | tf_op jit(solution)/shard_map/all_to_all | solution.py:17
  82.9 3.4 %collective-permute-start.4 = (bf16[8,3072]{1,0:T(8,128)(2,1)S(1)}, bf16[8,3072]{1,0:T(8,128)(2,1)S(1)}, u32[]{:S(2)}, u32[]{:S(2)}) collective-permute-start(bf16[8,3072]{1,0:T(8,128)(2,1)S(1)} %add_convert_fusion.2), channel_id=1, source_target_pairs={{0,4},{1,5},{2,6},{3,7},{4,0},{5,1},{6,2},{7,3},{8,12},{9,13},{10,... | collective-permute-start | bytes 147464 | tf_op jit(solution)/shard_map/ppermute | solution.py:58
  86.3 3.6 %collective-permute-done.4 = bf16[8,3072]{1,0:T(8,128)(2,1)S(1)} collective-permute-done((bf16[8,3072]{1,0:T(8,128)(2,1)S(1)}, bf16[8,3072]{1,0:T(8,128)(2,1)S(1)}, u32[]{:S(2)}, u32[]{:S(2)}) %collective-permute-start.4) | collective-permute-done | bytes 49184 | tf_op jit(solution)/shard_map/ppermute | solution.py:58
  89.9 3.9 %all-to-all-done.3 = bf16[16,8,3072]{2,1,0:T(8,128)(2,1)} async-done(((bf16[16,8,3072]{2,1,0:T(8,128)(2,1)}), bf16[16,8,3072]{2,1,0:T(8,128)(2,1)}, u32[]{:S(2)}, u32[]{:S(2)}) %all-to-all-start.3) | async-done | bytes 786464 | tf_op jit(solution)/shard_map/all_to_all | solution.py:17
  94.7 4.3 %all-to-all-start.4 = ((bf16[16,8,3072]{2,1,0:T(8,128)(2,1)}), bf16[16,8,3072]{2,1,0:T(8,128)(2,1)}, u32[]{:S(2)}, u32[]{:S(2)}) async-start(bf16[16,8,3072]{2,1,0:T(8,128)(2,1)} %broadcast_in_dim.69), calls=%async_computation.4 | async-start | bytes 1572864 | tf_op jit(solution)/shard_map/all_to_all | solution.py:17
  99.0 1.3 collective-permute-start.5
  100.3 9.2 %all-to-all-done.4 = bf16[16,8,3072]{2,1,0:T(8,128)(2,1)} async-done(((bf16[16,8,3072]{2,1,0:T(8,128)(2,1)}), bf16[16,8,3072]{2,1,0:T(8,128)(2,1)}, u32[]{:S(2)}, u32[]{:S(2)}) %all-to-all-start.4) | async-done | bytes 786464 | tf_op jit(solution)/shard_map/all_to_all | solution.py:17
  109.5 1.3 collective-permute-start.6
  110.8 1.8 fusion.43
  112.6 1.5 fusion.25
  114.1 1.5 fusion.34
  115.6 2.5 %collective-permute-done.6 = bf16[128,3072]{1,0:T(8,128)(2,1)S(1)} collective-permute-done((bf16[128,3072]{1,0:T(8,128)(2,1)}, bf16[128,3072]{1,0:T(8,128)(2,1)S(1)}, u32[]{:S(2)}, u32[]{:S(2)}) %collective-permute-start.6) | collective-permute-done | bytes 786464 | tf_op jit(solution)/shard_map/ppermute | solution.py:68
  119.1 1.6 multiply_convert_fusion.11
  121.4 5.6 %collective-permute-start.7 = (bf16[128,3072]{1,0:T(8,128)(2,1)S(1)}, bf16[128,3072]{1,0:T(8,128)(2,1)S(1)}, u32[]{:S(2)}, u32[]{:S(2)}) collective-permute-start(bf16[128,3072]{1,0:T(8,128)(2,1)S(1)} %fusion.9), channel_id=1, source_target_pairs={{128,0},{129,1},{130,2},{131,3},{132,4},{133,5},{134,6},{135,7},{1... | collective-permute-start | bytes 2359304 | tf_op jit(solution)/shard_map/ppermute | solution.py:68
  127.4 1.5 collective-permute-done.7
  129.3 16.6 %all_to_all.51 = bf16[16,8,3072]{2,1,0:T(8,128)(2,1)} all-to-all(bf16[16,8,3072]{2,1,0:T(8,128)(2,1)S(1)} %fusion.14), channel_id=1, replica_groups=mesh['segment'=2,'x'=4,'y'=4,'z'=8] {'x','y'}, dimensions={0} | all-to-all | bytes 1572864 | tf_op jit(solution)/shard_map/all_to_all | solution.py:17
  145.9 1.2 reduce_sum.65
  147.2 16.0 %all_to_all.52 = bf16[8,8,3072]{2,1,0:T(8,128)(2,1)S(1)} all-to-all(bf16[8,8,3072]{2,1,0:T(8,128)(2,1)S(1)} %broadcast_in_dim.70), channel_id=1, replica_groups=mesh['segment'=2,'x'=4,'y'=4,'z'=8] {'z'}, dimensions={0} | all-to-all | bytes 786432 | tf_op jit(solution)/shard_map/all_to_all | solution.py:17
  164.2 4.7 %all-to-all-start.7 = ((bf16[16,8,3072]{2,1,0:T(8,128)(2,1)}), bf16[16,8,3072]{2,1,0:T(8,128)(2,1)}, u32[]{:S(2)}, u32[]{:S(2)}) async-start(bf16[16,8,3072]{2,1,0:T(8,128)(2,1)} %broadcast_in_dim.71), calls=%async_computation.7 | async-start | bytes 1572864 | tf_op jit(solution)/shard_map/all_to_all | solution.py:17
  168.9 2.1 broadcast_select_fusion.2
  171.0 8.6 %all-to-all-done.7 = bf16[16,8,3072]{2,1,0:T(8,128)(2,1)} async-done(((bf16[16,8,3072]{2,1,0:T(8,128)(2,1)}), bf16[16,8,3072]{2,1,0:T(8,128)(2,1)}, u32[]{:S(2)}, u32[]{:S(2)}) %all-to-all-start.7) | async-done | bytes 786464 | tf_op jit(solution)/shard_map/all_to_all | solution.py:17
  179.7 6.7 %collective-permute-start.9 = (bf16[128,3072]{1,0:T(8,128)(2,1)}, bf16[128,3072]{1,0:T(8,128)(2,1)S(1)}, u32[]{:S(2)}, u32[]{:S(2)}) collective-permute-start(bf16[128,3072]{1,0:T(8,128)(2,1)} %bitcast.18), channel_id=1, source_target_pairs={{128,0},{129,1},{130,2},{131,3},{132,4},{133,5},{134,6},{135,7},{1... | collective-permute-start | bytes 2359304 | tf_op jit(solution)/shard_map/ppermute | solution.py:68
  186.3 2.3 %broadcast_select_fusion.3 = bf16[128,3072]{1,0:T(8,128)(2,1)} fusion(bf16[128,3072]{1,0:T(8,128)(2,1)} %copy-done.3, pred[]{:T(512)S(6)} %eq.18, bf16[16,8,3072]{2,1,0:T(8,128)(2,1)} %all-to-all-done.1), kind=kLoop, calls=%fused_computation.66 | loop fusion | flops 393216 | bytes 2359297 | tf_op jit(solution)/shard_map/jit(_where)/select_n | solution.py:183
  189.0 1.6 fusion.46
  192.7 1.7 fusion.3
  194.4 3.8 %all-to-all-start.8 = ((bf16[16,8,6144]{2,1,0:T(8,128)(2,1)}), bf16[16,8,6144]{2,1,0:T(8,128)(2,1)S(1)}, u32[]{:S(2)}, u32[]{:S(2)}) async-start(bf16[16,8,6144]{2,1,0:T(8,128)(2,1)} %fusion.3), calls=%async_computation.8 | async-start | bytes 3145728 | tf_op jit(solution)/shard_map/all_to_all | solution.py:17
  198.3 2.3 broadcast_select_fusion.1
  200.6 1.7 fusion.6
  202.4 1.8 fusion.4
  204.1 17.3 %all-to-all-done.8 = bf16[16,8,6144]{2,1,0:T(8,128)(2,1)S(1)} async-done(((bf16[16,8,6144]{2,1,0:T(8,128)(2,1)}), bf16[16,8,6144]{2,1,0:T(8,128)(2,1)S(1)}, u32[]{:S(2)}, u32[]{:S(2)}) %all-to-all-start.8) | async-done | bytes 1572896 | tf_op jit(solution)/shard_map/all_to_all | solution.py:17
  222.3 3.7 %all-to-all-start.9 = ((bf16[8,48,128]{2,1,0:T(8,128)(2,1)}), bf16[8,48,128]{2,1,0:T(8,128)(2,1)S(1)}, u32[]{:S(2)}, u32[]{:S(2)}) async-start(bf16[8,48,128]{2,1,0:T(8,128)(2,1)} %bitcast.125), calls=%async_computation.9 | async-start | bytes 196608 | tf_op jit(solution)/shard_map/all_to_all | solution.py:17
  226.0 1.8 fusion.5
  227.7 5.9 %all-to-all-done.9 = bf16[8,48,128]{2,1,0:T(8,128)(2,1)S(1)} async-done(((bf16[8,48,128]{2,1,0:T(8,128)(2,1)}), bf16[8,48,128]{2,1,0:T(8,128)(2,1)S(1)}, u32[]{:S(2)}, u32[]{:S(2)}) %all-to-all-start.9) | async-done | bytes 98336 | tf_op jit(solution)/shard_map/all_to_all | solution.py:17
  (78 shorter events, 13.2 us)
Async XLA Ops:
  1.4 42.9 %copy-start.14 = (f32[1,1,128]{2,1,0:T(1,128)S(1)}, f32[1,1,128]{2,1,0:T(1,128)}, u32[]{:S(2)}) copy-start(f32[1,1,128]{2,1,0:T(1,128)} %param.16) | copy-start | bytes 1540
  1.4 42.9 %copy-start.15 = (s32[1,1,128]{2,1,0:T(1,128)S(1)}, s32[1,1,128]{2,1,0:T(1,128)}, u32[]{:S(2)}) copy-start(s32[1,1,128]{2,1,0:T(1,128)} %param.14) | copy-start | bytes 1540
  1.4 43.0 %copy-start = (bf16[1,6144,128]{2,1,0:T(8,128)(2,1)S(1)}, bf16[1,6144,128]{2,1,0:T(8,128)(2,1)}, u32[]{:S(2)}) copy-start(bf16[1,6144,128]{2,1,0:T(8,128)(2,1)} %param.11) | copy-start | bytes 4718596
  20.1 25.9 %copy-start.1 = (bf16[1,6144,128]{2,1,0:T(8,128)(2,1)S(1)}, bf16[1,6144,128]{2,1,0:T(8,128)(2,1)}, u32[]{:S(2)}) copy-start(bf16[1,6144,128]{2,1,0:T(8,128)(2,1)} %param.12) | copy-start | bytes 4718596
  20.1 17.5 %all-to-all-start.1 = ((bf16[16,8,3072]{2,1,0:T(8,128)(2,1)}), bf16[16,8,3072]{2,1,0:T(8,128)(2,1)}, u32[]{:S(2)}, u32[]{:S(2)}) async-start(bf16[16,8,3072]{2,1,0:T(8,128)(2,1)} %broadcast_in_dim.38), calls=%async_computation.1 | async-start | bytes 1572864 | tf_op jit(solution)/shard_map/all_to_all | solution.py:17
  37.7 9.8 %collective-permute-start = (bf16[128,3072]{1,0:T(8,128)(2,1)}, bf16[128,3072]{1,0:T(8,128)(2,1)S(1)}, u32[]{:S(2)}, u32[]{:S(2)}) collective-permute-start(bf16[128,3072]{1,0:T(8,128)(2,1)} %bitcast.3), channel_id=1, source_target_pairs={{128,0},{129,1},{130,2},{131,3},{132,4},{133,5},{134,6},{135,7},{1... | collective-permute-start | bytes 2359304 | tf_op jit(solution)/shard_map/ppermute | solution.py:68
  44.5 9.2 %copy-start.12 = (f32[128]{0:T(128)}, f32[128]{0:T(128)S(1)}, u32[]{:S(2)}) copy-start(f32[128]{0:T(128)S(1)} %select_reduce_fusion) | copy-start | bytes 1540
  47.5 1.7 copy-start.5
  47.5 1.4 copy-start.8
  49.5 4.2 %collective-permute-start.1 = (bf16[128,3072]{1,0:T(8,128)(2,1)S(1)}, bf16[128,3072]{1,0:T(8,128)(2,1)S(1)}, u32[]{:S(2)}, u32[]{:S(2)}) collective-permute-start(bf16[128,3072]{1,0:T(8,128)(2,1)S(1)} %fusion.8), channel_id=1, source_target_pairs={{0,128},{1,129},{2,130},{3,131},{4,132},{5,133},{6,134},{7,135},{8... | collective-permute-start | bytes 2359304 | tf_op jit(solution)/shard_map/ppermute | solution.py:68
  55.0 18.3 %all-to-all-start.2 = ((bf16[16,8,3072]{2,1,0:T(8,128)(2,1)}), bf16[16,8,3072]{2,1,0:T(8,128)(2,1)}, u32[]{:S(2)}, u32[]{:S(2)}) async-start(bf16[16,8,3072]{2,1,0:T(8,128)(2,1)} %fusion.13), calls=%async_computation.2 | async-start | bytes 1572864 | tf_op jit(solution)/shard_map/all_to_all | solution.py:17
  74.5 3.0 %collective-permute-start.2 = (bf16[8,3072]{1,0:T(8,128)(2,1)S(1)}, bf16[8,3072]{1,0:T(8,128)(2,1)S(1)}, u32[]{:S(2)}, u32[]{:S(2)}) collective-permute-start(bf16[8,3072]{1,0:T(8,128)(2,1)S(1)} %reduce_sum.64), channel_id=1, source_target_pairs={{0,1},{1,0},{2,3},{3,2},{4,5},{5,4},{6,7},{7,6},{8,9},{9,8},{10,11... | collective-permute-start | bytes 147464 | tf_op jit(solution)/shard_map/ppermute | solution.py:58
  77.6 5.4 %collective-permute-start.3 = (bf16[8,3072]{1,0:T(8,128)(2,1)S(1)}, bf16[8,3072]{1,0:T(8,128)(2,1)S(1)}, u32[]{:S(2)}, u32[]{:S(2)}) collective-permute-start(bf16[8,3072]{1,0:T(8,128)(2,1)S(1)} %add_convert_fusion.3), channel_id=1, source_target_pairs={{0,2},{1,3},{2,0},{3,1},{4,6},{5,7},{6,4},{7,5},{8,10},{9,11},{10,... | collective-permute-start | bytes 147464 | tf_op jit(solution)/shard_map/ppermute | solution.py:58
  78.6 15.2 %all-to-all-start.3 = ((bf16[16,8,3072]{2,1,0:T(8,128)(2,1)}), bf16[16,8,3072]{2,1,0:T(8,128)(2,1)}, u32[]{:S(2)}, u32[]{:S(2)}) async-start(bf16[16,8,3072]{2,1,0:T(8,128)(2,1)} %broadcast_in_dim.68), calls=%async_computation.3 | async-start | bytes 1572864 | tf_op jit(solution)/shard_map/all_to_all | solution.py:17
  82.9 7.0 %collective-permute-start.4 = (bf16[8,3072]{1,0:T(8,128)(2,1)S(1)}, bf16[8,3072]{1,0:T(8,128)(2,1)S(1)}, u32[]{:S(2)}, u32[]{:S(2)}) collective-permute-start(bf16[8,3072]{1,0:T(8,128)(2,1)S(1)} %add_convert_fusion.2), channel_id=1, source_target_pairs={{0,4},{1,5},{2,6},{3,7},{4,0},{5,1},{6,2},{7,3},{8,12},{9,13},{10,... | collective-permute-start | bytes 147464 | tf_op jit(solution)/shard_map/ppermute | solution.py:58
  94.7 14.8 %all-to-all-start.4 = ((bf16[16,8,3072]{2,1,0:T(8,128)(2,1)}), bf16[16,8,3072]{2,1,0:T(8,128)(2,1)}, u32[]{:S(2)}, u32[]{:S(2)}) async-start(bf16[16,8,3072]{2,1,0:T(8,128)(2,1)} %broadcast_in_dim.69), calls=%async_computation.4 | async-start | bytes 1572864 | tf_op jit(solution)/shard_map/all_to_all | solution.py:17
  99.0 20.1 %collective-permute-start.5 = (bf16[128,3072]{1,0:T(8,128)(2,1)}, bf16[128,3072]{1,0:T(8,128)(2,1)}, u32[]{:S(2)}, u32[]{:S(2)}) collective-permute-start(bf16[128,3072]{1,0:T(8,128)(2,1)} %bitcast.11), channel_id=1, source_target_pairs={{0,128},{1,129},{2,130},{3,131},{4,132},{5,133},{6,134},{7,135},{8... | collective-permute-start | bytes 2359304 | tf_op jit(solution)/shard_map/ppermute | solution.py:68
  109.5 8.7 %collective-permute-start.6 = (bf16[128,3072]{1,0:T(8,128)(2,1)}, bf16[128,3072]{1,0:T(8,128)(2,1)S(1)}, u32[]{:S(2)}, u32[]{:S(2)}) collective-permute-start(bf16[128,3072]{1,0:T(8,128)(2,1)} %bitcast.13), channel_id=1, source_target_pairs={{0,128},{1,129},{2,130},{3,131},{4,132},{5,133},{6,134},{7,135},{8... | collective-permute-start | bytes 2359304 | tf_op jit(solution)/shard_map/ppermute | solution.py:68
  114.1 4.5 %copy-start.11 = (f32[128,128]{1,0:T(8,128)S(1)}, f32[128,128]{1,0:T(8,128)}, u32[]{:S(2)}) copy-start(f32[128,128]{1,0:T(8,128)} %get-tuple-element.25) | copy-start | bytes 196612
  115.6 3.5 %copy-start.6 = (bf16[1,128,6144]{2,1,0:T(8,128)(2,1)S(1)}, bf16[1,128,6144]{2,1,0:T(8,128)(2,1)}, u32[]{:S(2)}) copy-start(bf16[1,128,6144]{2,1,0:T(8,128)(2,1)} %param.13) | copy-start | bytes 4718596
  115.6 3.5 %copy-start.13 = (f32[128]{0:T(128)S(1)}, f32[128]{0:T(128)}, u32[]{:S(2)}) copy-start(f32[128]{0:T(128)} %copy-done.12) | copy-start | bytes 1540
  118.2 0.9 copy-start.3
  121.4 7.5 %collective-permute-start.7 = (bf16[128,3072]{1,0:T(8,128)(2,1)S(1)}, bf16[128,3072]{1,0:T(8,128)(2,1)S(1)}, u32[]{:S(2)}, u32[]{:S(2)}) collective-permute-start(bf16[128,3072]{1,0:T(8,128)(2,1)S(1)} %fusion.9), channel_id=1, source_target_pairs={{128,0},{129,1},{130,2},{131,3},{132,4},{133,5},{134,6},{135,7},{1... | collective-permute-start | bytes 2359304 | tf_op jit(solution)/shard_map/ppermute | solution.py:68
  164.2 15.4 %all-to-all-start.7 = ((bf16[16,8,3072]{2,1,0:T(8,128)(2,1)}), bf16[16,8,3072]{2,1,0:T(8,128)(2,1)}, u32[]{:S(2)}, u32[]{:S(2)}) async-start(bf16[16,8,3072]{2,1,0:T(8,128)(2,1)} %broadcast_in_dim.71), calls=%async_computation.7 | async-start | bytes 1572864 | tf_op jit(solution)/shard_map/all_to_all | solution.py:17
  179.7 9.4 %copy-start.7 = (bf16[1,128,6144]{2,1,0:T(8,128)(2,1)S(1)}, bf16[1,128,6144]{2,1,0:T(8,128)(2,1)}, u32[]{:S(2)}) copy-start(bf16[1,128,6144]{2,1,0:T(8,128)(2,1)} %param.13) | copy-start | bytes 4718596
  179.7 10.9 %collective-permute-start.9 = (bf16[128,3072]{1,0:T(8,128)(2,1)}, bf16[128,3072]{1,0:T(8,128)(2,1)S(1)}, u32[]{:S(2)}, u32[]{:S(2)}) collective-permute-start(bf16[128,3072]{1,0:T(8,128)(2,1)} %bitcast.18), channel_id=1, source_target_pairs={{128,0},{129,1},{130,2},{131,3},{132,4},{133,5},{134,6},{135,7},{1... | collective-permute-start | bytes 2359304 | tf_op jit(solution)/shard_map/ppermute | solution.py:68
  188.7 9.5 %collective-permute-start.8 = (bf16[2,3072]{1,0:T(2,128)(2,1)S(1)}, bf16[2,3072]{1,0:T(2,128)(2,1)S(1)}, u32[]{:S(2)}, u32[]{:S(2)}) collective-permute-start(bf16[2,3072]{1,0:T(2,128)(2,1)S(1)} %bitcast.145), channel_id=1, source_target_pairs={{0,128},{128,0},{1,129},{129,1},{2,130},{130,2},{3,131},{131,3},{4... | collective-permute-start | bytes 36872 | tf_op jit(solution)/shard_map/ppermute | solution.py:68
  190.6 0.9 copy-start.9
  194.4 3.9 %copy-start.10 = (bf16[128,3072]{1,0:T(8,128)(2,1)S(1)}, bf16[128,3072]{1,0:T(8,128)(2,1)}, u32[]{:S(2)}) copy-start(bf16[128,3072]{1,0:T(8,128)(2,1)} %copy-done.9) | copy-start | bytes 2359300
  194.4 27.0 %all-to-all-start.8 = ((bf16[16,8,6144]{2,1,0:T(8,128)(2,1)}), bf16[16,8,6144]{2,1,0:T(8,128)(2,1)S(1)}, u32[]{:S(2)}, u32[]{:S(2)}) async-start(bf16[16,8,6144]{2,1,0:T(8,128)(2,1)} %fusion.3), calls=%async_computation.8 | async-start | bytes 3145728 | tf_op jit(solution)/shard_map/all_to_all | solution.py:17
  200.6 1.8 copy-start.2
  200.6 1.8 copy-start.4
  222.3 11.3 %all-to-all-start.9 = ((bf16[8,48,128]{2,1,0:T(8,128)(2,1)}), bf16[8,48,128]{2,1,0:T(8,128)(2,1)S(1)}, u32[]{:S(2)}, u32[]{:S(2)}) async-start(bf16[8,48,128]{2,1,0:T(8,128)(2,1)} %bitcast.125), calls=%async_computation.9 | async-start | bytes 196608 | tf_op jit(solution)/shard_map/all_to_all | solution.py:17

commit v3 on v2

v3 whole, which is shorter than its diff:
```python
import jax
import jax.numpy as jnp
from jax import lax
from jax.sharding import Mesh
from jax.sharding import PartitionSpec as P

LANES = 128
PLANE = ("x", "y")
LINE = "z"
ET = ("x", "y", "z")
SIZES = (4, 4, 8)
CONTRACT_LAST = (((1,), (1,)), ((), ()))
CONTRACT_FIRST = (((0,), (0,)), ((), ()))


def exchange(value, axes):
    return lax.all_to_all(value, axes, 0, 0, tiled=True)


def copies(value, count):
    return jnp.broadcast_to(value[None], (count, *value.shape))


def add_bf16(a, b):
    return (a.astype(jnp.float32) + b.astype(jnp.float32)).astype(jnp.bfloat16)


def dot_f32(a, b):
    return jnp.dot(a, b, preferred_element_type=jnp.float32)


def dot_last(a, b):
    return lax.dot_general(a, b, CONTRACT_LAST, preferred_element_type=jnp.float32)


def dot_first(a, b):
    return lax.dot_general(a, b, CONTRACT_FIRST, preferred_element_type=jnp.float32)


def plane_sum(parts, line):
    plane = parts.shape[0] // line
    blocks = exchange(parts.reshape(plane, line, parts.shape[1]), PLANE)
    return jnp.sum(blocks.astype(jnp.float32), axis=0).astype(jnp.bfloat16)


def line_sum_steps(block):
    line = lax.axis_size(LINE)
    total = block.astype(jnp.float32)
    stride = 1
    while stride < line:
        pairs = [(i, i ^ stride) for i in range(line)]
        block = total.astype(jnp.bfloat16)
        total = block.astype(jnp.float32) + lax.ppermute(block, LINE, pairs).astype(jnp.float32)
        stride *= 2
    return total


def plane_spread(block, plane):
    return exchange(copies(block, plane), PLANE).reshape(-1, block.shape[1])


def swap(value):
    return lax.ppermute(value, "segment", [(0, 1), (1, 0)])


def per_device(
    inputs,
    cotangent,
    gate_weight,
    up_weight,
    down_weight,
    route_rows,
    route_count,
    route_weight,
    width_mask,
):
    width = inputs.shape[2]
    half = width // 2
    units = gate_weight.shape[2]
    line = lax.axis_size(LINE)
    plane = lax.axis_size("x") * lax.axis_size("y")
    tokens = plane * line
    first = lax.axis_index("segment") == 0

    def pick(a, b):
        return jnp.where(first, a, b)

    def by_section(own):
        other = swap(own)
        return pick(own, other), pick(other, own)

    slots = route_rows.shape[2]
    live = jnp.arange(slots, dtype=jnp.int32) < route_count[0, 0]
    slot_scale = jnp.where(live, route_weight[0, 0], 0.0)
    chosen = route_rows[0, 0][None, :] == jnp.arange(tokens, dtype=jnp.int32)[:, None]
    scale = jnp.sum(jnp.where(chosen, slot_scale[None, :], 0.0), axis=1)
    keep = jnp.broadcast_to(width_mask[0, 0].astype(jnp.float32), (tokens,))
    small = by_section(jnp.stack([scale, keep]))
    scales = [part[0][:, None] for part in small]
    keeps = [part[1][:, None] for part in small]

    def halves(own, axis):
        low = lax.slice_in_dim(own, 0, half, axis=axis)
        high = lax.slice_in_dim(own, half, width, axis=axis)
        mine, other = pick(low, high), swap(pick(high, low))
        return pick(mine, other), pick(other, mine)

    ins = halves(jnp.concatenate([gate_weight[0], up_weight[0]], axis=1), 0)
    downs = halves(down_weight[0], 1)

    def scaled(rows, section):
        return (scales[section] * rows.astype(jnp.float32)).astype(jnp.bfloat16)

    def total_of(part):
        return part + swap(part)

    def forward(rows, section):
        both = total_of(dot_f32(rows, ins[section]))
        gate_value, up_value = both[:, :units], both[:, units:]
        sig = jax.nn.sigmoid(gate_value)
        hidden = (gate_value * sig * up_value * keeps[section]).astype(jnp.bfloat16)
        gate_slope = keeps[section] * up_value * sig * (1.0 + gate_value * (1.0 - sig))
        up_slope = keeps[section] * gate_value * sig
        return hidden, jnp.concatenate([gate_slope, up_slope], axis=1)

    def outcome(hidden, section):
        return (scales[section] * dot_f32(hidden, downs[section])).astype(jnp.bfloat16)

    def hidden_delta(rows, section):
        return total_of(dot_last(rows, downs[section]))

    def deltas_of(delta, slopes):
        return (jnp.concatenate([delta, delta], axis=1) * slopes).astype(jnp.bfloat16)

    def slot_gradient(deltas, section):
        return dot_last(deltas, ins[section]).astype(jnp.bfloat16)

    parts = half // LANES
    in_row = inputs[0].reshape(2, parts, LANES)
    cot_row = cotangent[0].reshape(2, parts, LANES)
    rows = jnp.concatenate([pick(in_row[0], in_row[1]), pick(cot_row[0], cot_row[1])], axis=0)
    rows = exchange(copies(rows, line), LINE)
    in_block = rows[:, :parts].reshape(line, half)
    cot_block = rows[:, parts:].reshape(line, half)

    in_rows = plane_spread(in_block, plane)
    hidden_zero, slopes_zero = forward(in_rows, 0)
    partial = plane_sum(outcome(hidden_zero, 0), line)
    partial, cot_part = lax.optimization_barrier((partial, cot_block))
    cot_rows = plane_spread(cot_part, plane)
    mid_block = add_bf16(in_block, line_sum_steps(partial))
    mid_block, cot_rows = lax.optimization_barrier((mid_block, cot_rows))
    mid_rows = plane_spread(mid_block, plane)

    cot_scaled = scaled(cot_rows, 1)
    delta_one = hidden_delta(cot_scaled, 1)
    hidden_one, slopes_one = forward(mid_rows, 1)
    deltas_one = deltas_of(delta_one, slopes_one)
    partial = plane_sum(slot_gradient(deltas_one, 1), line)
    outcome_one = outcome(hidden_one, 1)
    partial, outcome_one = lax.optimization_barrier((partial, outcome_one))
    out_partial = plane_sum(outcome_one, line)
    back_block = add_bf16(cot_block, line_sum_steps(partial))
    back_block, out_partial = lax.optimization_barrier((back_block, out_partial))
    back_rows = plane_spread(back_block, plane)

    back_scaled = scaled(back_rows, 0)
    deltas_zero = deltas_of(hidden_delta(back_scaled, 0), slopes_zero)
    partial = plane_sum(slot_gradient(deltas_zero, 0), line)
    ends = jnp.stack(
        [partial.reshape(line, parts, LANES), out_partial.reshape(line, parts, LANES)], axis=1
    )
    ends = jnp.sum(exchange(ends, LINE).astype(jnp.float32), axis=0)

    place = lax.axis_index(LINE)
    mid_row = mid_block[place].reshape(parts, LANES)
    back_row = back_block[place].reshape(parts, LANES)
    early = swap(pick(back_row, mid_row))
    last_grad = add_bf16(back_row, ends[0])
    last_out = add_bf16(mid_row, ends[1])
    late = swap(pick(last_out, last_grad))
    section_output = jnp.concatenate([pick(mid_row, late), pick(early, last_out)], axis=0)
    grad_input = jnp.concatenate([pick(last_grad, early), pick(late, back_row)], axis=0)

    other = swap(pick(mid_rows, in_rows))
    picked = jnp.concatenate([pick(in_rows, other), pick(other, mid_rows)], axis=1)
    other = swap(pick(cot_scaled, back_scaled))
    slot_grad_in = jnp.concatenate([pick(back_scaled, other), pick(other, cot_scaled)], axis=1)
    deltas = pick(deltas_zero, deltas_one)
    grad_gate = dot_first(picked, deltas[:, :units])
    grad_up = dot_first(picked, deltas[:, units:])
    grad_down = dot_first(pick(hidden_zero, hidden_one), slot_grad_in)
    return (
        section_output.reshape(1, 1, 1, width),
        grad_input.reshape(1, 1, 1, width),
        grad_gate.astype(jnp.bfloat16)[None],
        grad_up.astype(jnp.bfloat16)[None],
        grad_down.astype(jnp.bfloat16)[None],
    )


def solution(mesh):
    torus = Mesh(mesh.devices.reshape(-1, *SIZES), ("segment", *ET))
    return jax.shard_map(
        per_device,
        mesh=torus,
        in_specs=(
            P(None, ET, None),
            P(None, ET, None),
            P("segment", None, ET),
            P("segment", None, ET),
            P("segment", ET, None),
            P("segment", None, None),
            P("segment", None),
            P("segment", None, None),
            P("segment", ET),
        ),
        out_specs=(
            P("segment", None, ET, None),
            P("segment", None, ET, None),
            P("segment", None, ET),
            P("segment", None, ET),
            P("segment", ET, None),
        ),
        check_vma=False,
    )
```

time: 237 us -> 226 us (0.954)
  blocking collectives: 49.3 us -> 0 us
  starting transfers between devices: 59.3 us -> 78.7 us
  other arithmetic: 12.2 us -> 24.5 us
  waiting for transfers between devices: 80.9 us -> 90.6 us
  matrix products: 24.6 us -> 18.2 us
  local copies, waits for them, and re-layouts: 5.54 us -> 9.57 us
    all_to_all x3 -> x0, blocking collectives: 49.3 us -> none  [exchange(): return lax.all_to_all(value, axes, 0, 0, tiled=True)]
    all_to_all x7 -> x10, starting transfers between devices: 32 us -> 45.6 us  [exchange(): return lax.all_to_all(value, axes, 0, 0, tiled=True)]
    ppermute x3 -> x6, waiting for transfers between devices: 5.87 us -> 16.2 us  [line_sum_steps(): lax.ppermute(block, LINE, pairs).astype(jnp.float32)]
    select_n x7 -> x13, other arithmetic: 8.24 us -> 18.3 us  [pick(): return jnp.where(first, a, b)]
    ppermute x7 -> x11, waiting for transfers between devices: 6.91 us -> 2 us  [swap(): return lax.ppermute(value, 'segment', [(0, 1), (1, 0)])]
    dot_general x11 -> x4, matrix products: 11.4 us -> 6.81 us  [dot_f32(): return jnp.dot(a, b, preferred_element_type=jnp.float32)]
    all_to_all x7 -> x10, waiting for transfers between devices: 68.1 us -> 72.4 us  [exchange(): return lax.all_to_all(value, axes, 0, 0, tiled=True)]
    ppermute x7 -> x11, starting transfers between devices: 23.1 us -> 26.1 us  [swap(): return lax.ppermute(value, 'segment', [(0, 1), (1, 0)])]
  transfers between devices with their start and end apart: 17 -> 27, of which waited for: 12 -> 16; matrix products, arithmetic and copies ran while one was open for 12% -> 15% of each run, Pallas kernels for 0% -> 0%
where the time goes in v3:
time: 226 us; the launch traced here: 224 us
  waiting for transfers between devices  90.6 us (40%)
  starting transfers between devices  78.7 us (35%)
  other arithmetic  24.5 us (11%)
  matrix products  18.2 us (8%)
  local copies, waits for them, and re-layouts  9.57 us (4%)
  between operations  2.49 us (1%)
    all_to_all x10, waiting for transfers between devices, exchange(): return lax.all_to_all(value, axes, 0, 0, tiled=True)  72.4 us
    all_to_all x10, starting transfers between devices, exchange(): return lax.all_to_all(value, axes, 0, 0, tiled=True)  45.6 us
    ppermute x11, starting transfers between devices, swap(): return lax.ppermute(value, 'segment', [(0, 1), (1, 0)])  26.1 us
    select_n x13, other arithmetic, pick(): return jnp.where(first, a, b)  18.3 us
    ppermute x6, waiting for transfers between devices, line_sum_steps(): lax.ppermute(block, LINE, pairs).astype(jnp.float32)  16.2 us
    ppermute x6, starting transfers between devices, line_sum_steps(): lax.ppermute(block, LINE, pairs).astype(jnp.float32)  6.9 us
    dot_general x4, matrix products, dot_f32(): return jnp.dot(a, b, preferred_element_type=jnp.float32)  6.81 us
    dot_general x4, matrix products, dot_last(): lax.dot_general(a, b, CONTRACT_LAST, preferred_element_type=jnp.float32)  6.15 us
  transfers between devices with their start and end apart: 27, of which 16 were waited for; matrix products, arithmetic and copies ran while one was open for 15% of the time, Pallas kernels for 0%

profile of v3, /device:TPU:1, one launch (start us, length us, event | category | flops | bytes accessed | tf_op | source)
XLA Modules:
  0.0 224.0 jit_solution(7126497658456477438)
XLA Ops:
  0.7 2.4 %broadcast_select_fusion.2 = bf16[3072,256]{1,0:T(8,128)(2,1)S(1)} fusion(pred[]{:T(512)S(6)} %eq.18, bf16[6144,128]{1,0:T(8,128)(2,1)} %bitcast.118, bf16[6144,128]{1,0:T(8,128)(2,1)} %bitcast.120), kind=kLoop, calls=%fused_computation.28 | loop fusion | flops 7077888 | bytes 4718593 | tf_op jit(solution)/shard_map/jit(_where)/select_n | solution.py:86
  3.1 3.3 %collective-permute-start.1 = (bf16[3072,256]{1,0:T(8,128)(2,1)S(1)}, bf16[3072,256]{1,0:T(8,128)(2,1)}, u32[]{:S(2)}, u32[]{:S(2)}) collective-permute-start(bf16[3072,256]{1,0:T(8,128)(2,1)S(1)} %broadcast_select_fusion.2), channel_id=1, source_target_pairs={{0,128},{128,0},{1,129},{129,1},{2,130},{130,2},{3,131},{131,3},{4... | collective-permute-start | bytes 4718600 | tf_op jit(solution)/shard_map/ppermute | solution.py:63
  8.8 6.5 %all-to-all-start = ((bf16[8,48,128]{2,1,0:T(8,128)(2,1)}), bf16[8,48,128]{2,1,0:T(8,128)(2,1)S(1)}, u32[]{:S(2)}, u32[]{:S(2)}) async-start(bf16[8,48,128]{2,1,0:T(8,128)(2,1)} %broadcast_in_dim.32), calls=%async_computation | async-start | bytes 196608 | tf_op jit(solution)/shard_map/all_to_all | solution.py:17
  17.2 5.4 %all-to-all-done = bf16[8,48,128]{2,1,0:T(8,128)(2,1)S(1)} async-done(((bf16[8,48,128]{2,1,0:T(8,128)(2,1)}), bf16[8,48,128]{2,1,0:T(8,128)(2,1)S(1)}, u32[]{:S(2)}, u32[]{:S(2)}) %all-to-all-start) | async-done | bytes 98336 | tf_op jit(solution)/shard_map/all_to_all | solution.py:17
  23.7 6.8 %all-to-all-start.1 = ((bf16[16,8,3072]{2,1,0:T(8,128)(2,1)}), bf16[16,8,3072]{2,1,0:T(8,128)(2,1)}, u32[]{:S(2)}, u32[]{:S(2)}) async-start(bf16[16,8,3072]{2,1,0:T(8,128)(2,1)} %broadcast_in_dim.60), calls=%async_computation.1 | async-start | bytes 1572864 | tf_op jit(solution)/shard_map/all_to_all | solution.py:17
  30.5 3.8 %broadcast_select_fusion.1 = (bf16[3072,256]{1,0:T(8,128)(2,1)S(1)}, bf16[3072,256]{1,0:T(8,128)(2,1)S(1)}) fusion(bf16[3072,256]{1,0:T(8,128)(2,1)} %collective-permute-done.1, pred[]{:T(512)S(6)} %eq.18, bf16[6144,128]{1,0:T(8,128)(2,1)} %bitcast.119, bf16[6144,128]{1,0:T(8,128)(2,1)} %bitcast.121), kind=kLoop, calls=%fused_computation.27 | loop fusion | flops 12582912 | bytes 7864321 | tf_op jit(solution)/shard_map/jit(_where)/select_n | solution.py:86
  34.3 6.8 %all-to-all-done.1 = bf16[16,8,3072]{2,1,0:T(8,128)(2,1)} async-done(((bf16[16,8,3072]{2,1,0:T(8,128)(2,1)}), bf16[16,8,3072]{2,1,0:T(8,128)(2,1)}, u32[]{:S(2)}, u32[]{:S(2)}) %all-to-all-start.1) | async-done | bytes 786464 | tf_op jit(solution)/shard_map/all_to_all | solution.py:17
  41.1 1.6 fusion.15
  42.7 4.8 %collective-permute-start.2 = (f32[128,256]{1,0:T(8,128)S(1)}, f32[128,256]{1,0:T(8,128)S(1)}, u32[]{:S(2)}, u32[]{:S(2)}) collective-permute-start(f32[128,256]{1,0:T(8,128)S(1)} %fusion.15), channel_id=1, source_target_pairs={{0,128},{128,0},{1,129},{129,1},{2,130},{130,2},{3,131},{131,3},{4... | collective-permute-start | bytes 393224 | tf_op jit(solution)/shard_map/ppermute | solution.py:63
  49.2 2.4 %fusion.7 = bf16[16,8,3072]{2,1,0:T(8,128)(2,1)} fusion(bf16[128,128]{1,0:T(8,128)(2,1)S(1)} %get-tuple-element.30, f32[128]{0:T(128)S(1)} %get-tuple-element.46, bf16[128,3072]{1,0:T(8,128)(2,1)S(1)} %copy-done.1, bf16[128,3072]{1,0:T(8,128)(2,1)} %collective-permute-done.3, pred[]{:T(512)S(6)} %eq.18), kind=kOutput, calls=%fused_computation.14 | convolution fusion | flops 101842944 | bytes 2392577 | tf_op jit(solution)/shard_map/dot_general | solution.py:29
  51.6 4.3 %all-to-all-start.2 = ((bf16[16,8,3072]{2,1,0:T(8,128)(2,1)}), bf16[16,8,3072]{2,1,0:T(8,128)(2,1)}, u32[]{:S(2)}, u32[]{:S(2)}) async-start(bf16[16,8,3072]{2,1,0:T(8,128)(2,1)} %fusion.7), calls=%async_computation.2 | async-start | bytes 1572864 | tf_op jit(solution)/shard_map/all_to_all | solution.py:17
  55.9 14.7 %all-to-all-done.2 = bf16[16,8,3072]{2,1,0:T(8,128)(2,1)} async-done(((bf16[16,8,3072]{2,1,0:T(8,128)(2,1)}), bf16[16,8,3072]{2,1,0:T(8,128)(2,1)}, u32[]{:S(2)}, u32[]{:S(2)}) %all-to-all-start.2) | async-done | bytes 786464 | tf_op jit(solution)/shard_map/all_to_all | solution.py:17
  72.4 2.5 %collective-permute-done.4 = bf16[8,3072]{1,0:T(8,128)(2,1)S(1)} collective-permute-done((bf16[8,3072]{1,0:T(8,128)(2,1)S(1)}, bf16[8,3072]{1,0:T(8,128)(2,1)S(1)}, u32[]{:S(2)}, u32[]{:S(2)}) %collective-permute-start.4) | collective-permute-done | bytes 49184 | tf_op jit(solution)/shard_map/ppermute | solution.py:53
  76.1 4.3 %all-to-all-start.3 = ((bf16[16,8,3072]{2,1,0:T(8,128)(2,1)}), bf16[16,8,3072]{2,1,0:T(8,128)(2,1)}, u32[]{:S(2)}, u32[]{:S(2)}) async-start(bf16[16,8,3072]{2,1,0:T(8,128)(2,1)} %broadcast_in_dim.61), calls=%async_computation.3 | async-start | bytes 1572864 | tf_op jit(solution)/shard_map/all_to_all | solution.py:17
  80.4 2.5 %collective-permute-start.6 = (bf16[8,3072]{1,0:T(8,128)(2,1)S(1)}, bf16[8,3072]{1,0:T(8,128)(2,1)S(1)}, u32[]{:S(2)}, u32[]{:S(2)}) collective-permute-start(bf16[8,3072]{1,0:T(8,128)(2,1)S(1)} %add_convert_fusion.4), channel_id=1, source_target_pairs={{0,4},{1,5},{2,6},{3,7},{4,0},{5,1},{6,2},{7,3},{8,12},{9,13},{10,... | collective-permute-start | bytes 147464 | tf_op jit(solution)/shard_map/ppermute | solution.py:53
  82.9 4.5 %collective-permute-done.6 = bf16[8,3072]{1,0:T(8,128)(2,1)S(1)} collective-permute-done((bf16[8,3072]{1,0:T(8,128)(2,1)S(1)}, bf16[8,3072]{1,0:T(8,128)(2,1)S(1)}, u32[]{:S(2)}, u32[]{:S(2)}) %collective-permute-start.6) | collective-permute-done | bytes 49184 | tf_op jit(solution)/shard_map/ppermute | solution.py:53
  87.4 5.5 %all-to-all-done.3 = bf16[16,8,3072]{2,1,0:T(8,128)(2,1)} async-done(((bf16[16,8,3072]{2,1,0:T(8,128)(2,1)}), bf16[16,8,3072]{2,1,0:T(8,128)(2,1)}, u32[]{:S(2)}, u32[]{:S(2)}) %all-to-all-start.3) | async-done | bytes 786464 | tf_op jit(solution)/shard_map/all_to_all | solution.py:17
  93.8 4.3 %all-to-all-start.4 = ((bf16[16,8,3072]{2,1,0:T(8,128)(2,1)}), bf16[16,8,3072]{2,1,0:T(8,128)(2,1)}, u32[]{:S(2)}, u32[]{:S(2)}) async-start(bf16[16,8,3072]{2,1,0:T(8,128)(2,1)} %broadcast_in_dim.62), calls=%async_computation.4 | async-start | bytes 1572864 | tf_op jit(solution)/shard_map/all_to_all | solution.py:17
  98.2 10.7 %all-to-all-done.4 = bf16[16,8,3072]{2,1,0:T(8,128)(2,1)} async-done(((bf16[16,8,3072]{2,1,0:T(8,128)(2,1)}), bf16[16,8,3072]{2,1,0:T(8,128)(2,1)}, u32[]{:S(2)}, u32[]{:S(2)}) %all-to-all-start.4) | async-done | bytes 786464 | tf_op jit(solution)/shard_map/all_to_all | solution.py:17
  108.9 1.6 fusion.13
  110.5 4.6 %collective-permute-start.8 = (f32[128,256]{1,0:T(8,128)S(1)}, f32[128,256]{1,0:T(8,128)S(1)}, u32[]{:S(2)}, u32[]{:S(2)}) collective-permute-start(f32[128,256]{1,0:T(8,128)S(1)} %fusion.13), channel_id=1, source_target_pairs={{0,128},{128,0},{1,129},{129,1},{2,130},{130,2},{3,131},{131,3},{4... | collective-permute-start | bytes 393224 | tf_op jit(solution)/shard_map/ppermute | solution.py:63
  115.1 1.6 fusion.18
  118.1 1.5 fusion.5
  119.7 3.7 %all-to-all-start.5 = ((bf16[16,8,3072]{2,1,0:T(8,128)(2,1)}), bf16[16,8,3072]{2,1,0:T(8,128)(2,1)S(1)}, u32[]{:S(2)}, u32[]{:S(2)}) async-start(bf16[16,8,3072]{2,1,0:T(8,128)(2,1)} %fusion.5), calls=%async_computation.5 | async-start | bytes 1572864 | tf_op jit(solution)/shard_map/all_to_all | solution.py:17
  124.7 12.2 %all-to-all-done.5 = bf16[16,8,3072]{2,1,0:T(8,128)(2,1)S(1)} async-done(((bf16[16,8,3072]{2,1,0:T(8,128)(2,1)}), bf16[16,8,3072]{2,1,0:T(8,128)(2,1)S(1)}, u32[]{:S(2)}, u32[]{:S(2)}) %all-to-all-start.5) | async-done | bytes 786464 | tf_op jit(solution)/shard_map/all_to_all | solution.py:17
  138.2 2.6 %collective-permute-done.9 = bf16[8,3072]{1,0:T(8,128)(2,1)S(1)} collective-permute-done((bf16[8,3072]{1,0:T(8,128)(2,1)}, bf16[8,3072]{1,0:T(8,128)(2,1)S(1)}, u32[]{:S(2)}, u32[]{:S(2)}) %collective-permute-start.9) | collective-permute-done | bytes 49184 | tf_op jit(solution)/shard_map/ppermute | solution.py:53
  142.2 2.3 %collective-permute-start.10 = (bf16[8,3072]{1,0:T(8,128)(2,1)}, bf16[8,3072]{1,0:T(8,128)(2,1)}, u32[]{:S(2)}, u32[]{:S(2)}) collective-permute-start(bf16[8,3072]{1,0:T(8,128)(2,1)} %add_convert_fusion.2), channel_id=1, source_target_pairs={{0,2},{1,3},{2,0},{3,1},{4,6},{5,7},{6,4},{7,5},{8,10},{9,11},{10,... | collective-permute-start | bytes 147464 | tf_op jit(solution)/shard_map/ppermute | solution.py:53
  144.5 4.1 %all-to-all-start.6 = ((bf16[16,8,3072]{2,1,0:T(8,128)(2,1)}), bf16[16,8,3072]{2,1,0:T(8,128)(2,1)S(1)}, u32[]{:S(2)}, u32[]{:S(2)}) async-start(bf16[16,8,3072]{2,1,0:T(8,128)(2,1)} %bitcast.122), calls=%async_computation.6 | async-start | bytes 1572864 | tf_op jit(solution)/shard_map/all_to_all | solution.py:17
  150.4 6.5 %collective-permute-done.11 = bf16[8,3072]{1,0:T(8,128)(2,1)S(1)} collective-permute-done((bf16[8,3072]{1,0:T(8,128)(2,1)S(1)}, bf16[8,3072]{1,0:T(8,128)(2,1)S(1)}, u32[]{:S(2)}, u32[]{:S(2)}) %collective-permute-start.11) | collective-permute-done | bytes 49184 | tf_op jit(solution)/shard_map/ppermute | solution.py:53
  157.5 1.8 all-to-all-done.6
  159.5 1.8 broadcast_in_dim.63
  161.2 4.7 %all-to-all-start.7 = ((bf16[16,8,3072]{2,1,0:T(8,128)(2,1)}), bf16[16,8,3072]{2,1,0:T(8,128)(2,1)S(1)}, u32[]{:S(2)}, u32[]{:S(2)}) async-start(bf16[16,8,3072]{2,1,0:T(8,128)(2,1)} %broadcast_in_dim.63), calls=%async_computation.7 | async-start | bytes 1572864 | tf_op jit(solution)/shard_map/all_to_all | solution.py:17
  166.0 2.3 %bitcast_select_fusion.1 = bf16[128,3072]{1,0:T(8,128)(2,1)} fusion(bf16[16,8,3072]{2,1,0:T(8,128)(2,1)} %all-to-all-done.4, bf16[16,8,3072]{2,1,0:T(8,128)(2,1)} %all-to-all-done.1, pred[]{:T(512)S(6)} %eq.18), kind=kLoop, calls=%fused_computation.31 | loop fusion | flops 393216 | bytes 2359297 | tf_op jit(solution)/shard_map/jit(_where)/select_n | solution.py:86
  168.3 4.6 %collective-permute-start.15 = (bf16[128,3072]{1,0:T(8,128)(2,1)}, bf16[128,3072]{1,0:T(8,128)(2,1)}, u32[]{:S(2)}, u32[]{:S(2)}) collective-permute-start(bf16[128,3072]{1,0:T(8,128)(2,1)} %bitcast_select_fusion.1), channel_id=1, source_target_pairs={{0,128},{128,0},{1,129},{129,1},{2,130},{130,2},{3,131},{131,3},{4... | collective-permute-start | bytes 2359304 | tf_op jit(solution)/shard_map/ppermute | solution.py:63
  173.8 2.7 %all-to-all-done.7 = bf16[16,8,3072]{2,1,0:T(8,128)(2,1)S(1)} async-done(((bf16[16,8,3072]{2,1,0:T(8,128)(2,1)}), bf16[16,8,3072]{2,1,0:T(8,128)(2,1)S(1)}, u32[]{:S(2)}, u32[]{:S(2)}) %all-to-all-start.7) | async-done | bytes 786464 | tf_op jit(solution)/shard_map/all_to_all | solution.py:17
  176.4 1.5 fusion.17
  178.0 4.6 %collective-permute-start.12 = (f32[128,128]{1,0:T(8,128)S(1)}, f32[128,128]{1,0:T(8,128)S(1)}, u32[]{:S(2)}, u32[]{:S(2)}) collective-permute-start(f32[128,128]{1,0:T(8,128)S(1)} %fusion.17), channel_id=1, source_target_pairs={{0,128},{128,0},{1,129},{129,1},{2,130},{130,2},{3,131},{131,3},{4... | collective-permute-start | bytes 196616 | tf_op jit(solution)/shard_map/ppermute | solution.py:63
  182.6 2.6 %bitcast_select_fusion.2 = (bf16[128,3072]{1,0:T(8,128)(2,1)S(1)}, bf16[128,3072]{1,0:T(8,128)(2,1)}) fusion(bf16[128,3072]{1,0:T(8,128)(2,1)} %collective-permute-done.15, bf16[16,8,3072]{2,1,0:T(8,128)(2,1)} %all-to-all-done.1, pred[]{:T(512)S(6)} %eq.18, bf16[16,8,3072]{2,1,0:T(8,128)(2,1)} %all-to-all-done.4), kind=kLoop, calls=%fused_computation.34 | loop fusion | flops 786432 | bytes 3932161 | tf_op jit(solution)/shard_map/jit(_where)/select_n | solution.py:86
  188.2 3.6 %all-to-all-start.8 = ((bf16[16,8,3072]{2,1,0:T(8,128)(2,1)}), bf16[16,8,3072]{2,1,0:T(8,128)(2,1)S(1)}, u32[]{:S(2)}, u32[]{:S(2)}) async-start(bf16[16,8,3072]{2,1,0:T(8,128)(2,1)} %fusion.6), calls=%async_computation.8 | async-start | bytes 1572864 | tf_op jit(solution)/shard_map/all_to_all | solution.py:17
  191.9 2.5 %broadcast_select_fusion.6 = bf16[128,3072]{1,0:T(8,128)(2,1)} fusion(pred[]{:T(512)S(6)} %eq.18, bf16[128,3072]{1,0:T(8,128)(2,1)} %bitcast.12, f32[128]{0:T(128)} %copy-done.17, bf16[16,8,3072]{2,1,0:T(8,128)(2,1)S(1)} %all-to-all-done.7, f32[128]{0:T(128)} %copy-done.15), kind=kLoop, calls=%fused_computation.39 | loop fusion | flops 2752512 | bytes 2360321 | tf_op jit(solution)/shard_map/jit(_where)/select_n | solution.py:86
  195.5 1.8 fusion.1
  197.3 1.8 fusion
  199.0 7.2 %all-to-all-done.8 = bf16[16,8,3072]{2,1,0:T(8,128)(2,1)S(1)} async-done(((bf16[16,8,3072]{2,1,0:T(8,128)(2,1)}), bf16[16,8,3072]{2,1,0:T(8,128)(2,1)S(1)}, u32[]{:S(2)}, u32[]{:S(2)}) %all-to-all-start.8) | async-done | bytes 786464 | tf_op jit(solution)/shard_map/all_to_all | solution.py:17
  207.0 3.4 %all-to-all-start.9 = ((bf16[8,2,24,128]{3,2,1,0:T(8,128)(2,1)}), bf16[8,2,24,128]{3,2,1,0:T(8,128)(2,1)S(1)}, u32[]{:S(2)}, u32[]{:S(2)}) async-start(bf16[8,2,24,128]{3,2,1,0:T(8,128)(2,1)} %pad_maximum_fusion.4), calls=%async_computation.9 | async-start | bytes 196608 | tf_op jit(solution)/shard_map/all_to_all | solution.py:17
  210.4 2.0 broadcast_select_fusion.5
  212.5 5.4 %all-to-all-done.9 = bf16[8,2,24,128]{3,2,1,0:T(8,128)(2,1)S(1)} async-done(((bf16[8,2,24,128]{3,2,1,0:T(8,128)(2,1)}), bf16[8,2,24,128]{3,2,1,0:T(8,128)(2,1)S(1)}, u32[]{:S(2)}, u32[]{:S(2)}) %all-to-all-start.9) | async-done | bytes 98336 | tf_op jit(solution)/shard_map/all_to_all | solution.py:17
  218.6 2.4 %collective-permute-start.13 = (bf16[24,128]{1,0:T(8,128)(2,1)S(1)}, bf16[24,128]{1,0:T(8,128)(2,1)S(1)}, u32[]{:S(2)}, u32[]{:S(2)}) collective-permute-start(bf16[24,128]{1,0:T(8,128)(2,1)S(1)} %get-tuple-element.38), channel_id=1, source_target_pairs={{0,128},{128,0},{1,129},{129,1},{2,130},{130,2},{3,131},{131,3},{4... | collective-permute-start | bytes 18440 | tf_op jit(solution)/shard_map/ppermute | solution.py:63
  221.0 1.7 fusion.2
  (112 shorter events, 25.3 us)
Async XLA Ops:
  0.6 6.5 %copy-start.19 = (f32[1,1,128]{2,1,0:T(1,128)S(1)}, f32[1,1,128]{2,1,0:T(1,128)}, u32[]{:S(2)}) copy-start(f32[1,1,128]{2,1,0:T(1,128)} %param.16) | copy-start | bytes 1540
  0.6 7.1 %copy-start.20 = (s32[1,1,128]{2,1,0:T(1,128)S(1)}, s32[1,1,128]{2,1,0:T(1,128)}, u32[]{:S(2)}) copy-start(s32[1,1,128]{2,1,0:T(1,128)} %param.14) | copy-start | bytes 1540
  0.7 7.3 %copy-start.13 = (bf16[1,1,6144]{2,1,0:T(2,128)(2,1)S(1)}, bf16[1,1,6144]{2,1,0:T(2,128)(2,1)}, u32[]{:S(2)}) copy-start(bf16[1,1,6144]{2,1,0:T(2,128)(2,1)} %param.9) | copy-start | bytes 36868
  0.7 7.3 %copy-start.14 = (bf16[1,1,6144]{2,1,0:T(2,128)(2,1)S(1)}, bf16[1,1,6144]{2,1,0:T(2,128)(2,1)}, u32[]{:S(2)}) copy-start(bf16[1,1,6144]{2,1,0:T(2,128)(2,1)} %param.10) | copy-start | bytes 36868
  0.7 14.6 %copy-start.4 = (bf16[1,128,6144]{2,1,0:T(8,128)(2,1)S(1)}, bf16[1,128,6144]{2,1,0:T(8,128)(2,1)}, u32[]{:S(2)}) copy-start(bf16[1,128,6144]{2,1,0:T(8,128)(2,1)} %param.13) | copy-start | bytes 4718596
  3.1 27.4 %collective-permute-start.1 = (bf16[3072,256]{1,0:T(8,128)(2,1)S(1)}, bf16[3072,256]{1,0:T(8,128)(2,1)}, u32[]{:S(2)}, u32[]{:S(2)}) collective-permute-start(bf16[3072,256]{1,0:T(8,128)(2,1)S(1)} %broadcast_select_fusion.2), channel_id=1, source_target_pairs={{0,128},{128,0},{1,129},{129,1},{2,130},{130,2},{3,131},{131,3},{4... | collective-permute-start | bytes 4718600 | tf_op jit(solution)/shard_map/ppermute | solution.py:63
  7.9 9.3 %collective-permute-start = (f32[2,128]{1,0:T(2,128)S(1)}, f32[2,128]{1,0:T(2,128)S(1)}, u32[]{:S(2)}, u32[]{:S(2)}) collective-permute-start(f32[2,128]{1,0:T(2,128)S(1)} %stack.10), channel_id=1, source_target_pairs={{0,128},{128,0},{1,129},{129,1},{2,130},{130,2},{3,131},{131,3},{4... | collective-permute-start | bytes 3080 | tf_op jit(solution)/shard_map/ppermute | solution.py:63
  8.8 13.9 %all-to-all-start = ((bf16[8,48,128]{2,1,0:T(8,128)(2,1)}), bf16[8,48,128]{2,1,0:T(8,128)(2,1)S(1)}, u32[]{:S(2)}, u32[]{:S(2)}) async-start(bf16[8,48,128]{2,1,0:T(8,128)(2,1)} %broadcast_in_dim.32), calls=%async_computation | async-start | bytes 196608 | tf_op jit(solution)/shard_map/all_to_all | solution.py:17
  16.5 32.1 %collective-permute-start.3 = (bf16[128,3072]{1,0:T(8,128)(2,1)}, bf16[128,3072]{1,0:T(8,128)(2,1)}, u32[]{:S(2)}, u32[]{:S(2)}) collective-permute-start(bf16[128,3072]{1,0:T(8,128)(2,1)} %get-tuple-element.24), channel_id=1, source_target_pairs={{0,128},{128,0},{1,129},{129,1},{2,130},{130,2},{3,131},{131,3},{4... | collective-permute-start | bytes 2359304 | tf_op jit(solution)/shard_map/ppermute | solution.py:63
  22.7 33.2 %copy-start.5 = (bf16[1,8,24,128]{3,2,1,0:T(8,128)(2,1)}, bf16[1,8,24,128]{3,2,1,0:T(8,128)(2,1)S(1)}, u32[]{:S(2)}) copy-start(bf16[1,8,24,128]{3,2,1,0:T(8,128)(2,1)S(1)} %get-tuple-element.35) | copy-start | bytes 147460
  23.7 17.4 %all-to-all-start.1 = ((bf16[16,8,3072]{2,1,0:T(8,128)(2,1)}), bf16[16,8,3072]{2,1,0:T(8,128)(2,1)}, u32[]{:S(2)}, u32[]{:S(2)}) async-start(bf16[16,8,3072]{2,1,0:T(8,128)(2,1)} %broadcast_in_dim.60), calls=%async_computation.1 | async-start | bytes 1572864 | tf_op jit(solution)/shard_map/all_to_all | solution.py:17
  41.1 8.1 %copy-start.1 = (bf16[128,3072]{1,0:T(8,128)(2,1)S(1)}, bf16[128,3072]{1,0:T(8,128)(2,1)}, u32[]{:S(2)}) copy-start(bf16[128,3072]{1,0:T(8,128)(2,1)} %get-tuple-element.23) | copy-start | bytes 2359300
  42.7 5.8 %collective-permute-start.2 = (f32[128,256]{1,0:T(8,128)S(1)}, f32[128,256]{1,0:T(8,128)S(1)}, u32[]{:S(2)}, u32[]{:S(2)}) collective-permute-start(f32[128,256]{1,0:T(8,128)S(1)} %fusion.15), channel_id=1, source_target_pairs={{0,128},{128,0},{1,129},{129,1},{2,130},{130,2},{3,131},{131,3},{4... | collective-permute-start | bytes 393224 | tf_op jit(solution)/shard_map/ppermute | solution.py:63
  47.5 128.9 %copy-start.15 = (f32[128]{0:T(128)}, f32[128]{0:T(128)S(1)}, u32[]{:S(2)}) copy-start(f32[128]{0:T(128)S(1)} %get-tuple-element.46) | copy-start | bytes 1540
  48.6 0.6 copy-start.7
  51.6 19.0 %all-to-all-start.2 = ((bf16[16,8,3072]{2,1,0:T(8,128)(2,1)}), bf16[16,8,3072]{2,1,0:T(8,128)(2,1)}, u32[]{:S(2)}, u32[]{:S(2)}) async-start(bf16[16,8,3072]{2,1,0:T(8,128)(2,1)} %fusion.7), calls=%async_computation.2 | async-start | bytes 1572864 | tf_op jit(solution)/shard_map/all_to_all | solution.py:17
  71.9 3.0 %collective-permute-start.4 = (bf16[8,3072]{1,0:T(8,128)(2,1)S(1)}, bf16[8,3072]{1,0:T(8,128)(2,1)S(1)}, u32[]{:S(2)}, u32[]{:S(2)}) collective-permute-start(bf16[8,3072]{1,0:T(8,128)(2,1)S(1)} %reduce_sum.67), channel_id=1, source_target_pairs={{0,1},{1,0},{2,3},{3,2},{4,5},{5,4},{6,7},{7,6},{8,9},{9,8},{10,11... | collective-permute-start | bytes 147464 | tf_op jit(solution)/shard_map/ppermute | solution.py:53
  74.9 5.5 %collective-permute-start.5 = (bf16[8,3072]{1,0:T(8,128)(2,1)S(1)}, bf16[8,3072]{1,0:T(8,128)(2,1)S(1)}, u32[]{:S(2)}, u32[]{:S(2)}) collective-permute-start(bf16[8,3072]{1,0:T(8,128)(2,1)S(1)} %add_convert_fusion.5), channel_id=1, source_target_pairs={{0,2},{1,3},{2,0},{3,1},{4,6},{5,7},{6,4},{7,5},{8,10},{9,11},{10,... | collective-permute-start | bytes 147464 | tf_op jit(solution)/shard_map/ppermute | solution.py:53
  76.1 16.8 %all-to-all-start.3 = ((bf16[16,8,3072]{2,1,0:T(8,128)(2,1)}), bf16[16,8,3072]{2,1,0:T(8,128)(2,1)}, u32[]{:S(2)}, u32[]{:S(2)}) async-start(bf16[16,8,3072]{2,1,0:T(8,128)(2,1)} %broadcast_in_dim.61), calls=%async_computation.3 | async-start | bytes 1572864 | tf_op jit(solution)/shard_map/all_to_all | solution.py:17
  80.4 7.0 %collective-permute-start.6 = (bf16[8,3072]{1,0:T(8,128)(2,1)S(1)}, bf16[8,3072]{1,0:T(8,128)(2,1)S(1)}, u32[]{:S(2)}, u32[]{:S(2)}) collective-permute-start(bf16[8,3072]{1,0:T(8,128)(2,1)S(1)} %add_convert_fusion.4), channel_id=1, source_target_pairs={{0,4},{1,5},{2,6},{3,7},{4,0},{5,1},{6,2},{7,3},{8,12},{9,13},{10,... | collective-permute-start | bytes 147464 | tf_op jit(solution)/shard_map/ppermute | solution.py:53
  87.4 23.1 %copy-start.11 = (bf16[8,3072]{1,0:T(8,128)(2,1)}, bf16[8,3072]{1,0:T(8,128)(2,1)S(1)}, u32[]{:S(2)}) copy-start(bf16[8,3072]{1,0:T(8,128)(2,1)S(1)} %add_convert_fusion.3) | copy-start | bytes 147460
  93.8 15.0 %all-to-all-start.4 = ((bf16[16,8,3072]{2,1,0:T(8,128)(2,1)}), bf16[16,8,3072]{2,1,0:T(8,128)(2,1)}, u32[]{:S(2)}, u32[]{:S(2)}) async-start(bf16[16,8,3072]{2,1,0:T(8,128)(2,1)} %broadcast_in_dim.62), calls=%async_computation.4 | async-start | bytes 1572864 | tf_op jit(solution)/shard_map/all_to_all | solution.py:17
  98.2 25.3 %copy-start.17 = (f32[128]{0:T(128)}, f32[128]{0:T(128)S(1)}, u32[]{:S(2)}) copy-start(f32[128]{0:T(128)S(1)} %get-tuple-element.45) | copy-start | bytes 1540
  108.9 6.2 %copy-start.2 = (bf16[128,3072]{1,0:T(8,128)(2,1)S(1)}, bf16[128,3072]{1,0:T(8,128)(2,1)}, u32[]{:S(2)}) copy-start(bf16[128,3072]{1,0:T(8,128)(2,1)} %get-tuple-element.23) | copy-start | bytes 2359300
  110.5 7.5 %collective-permute-start.8 = (f32[128,256]{1,0:T(8,128)S(1)}, f32[128,256]{1,0:T(8,128)S(1)}, u32[]{:S(2)}, u32[]{:S(2)}) collective-permute-start(f32[128,256]{1,0:T(8,128)S(1)} %fusion.13), channel_id=1, source_target_pairs={{0,128},{128,0},{1,129},{129,1},{2,130},{130,2},{3,131},{131,3},{4... | collective-permute-start | bytes 393224 | tf_op jit(solution)/shard_map/ppermute | solution.py:63
  116.7 1.3 collective-permute-start.7
  118.1 5.3 %copy-start.9 = (bf16[128,128]{1,0:T(8,128)(2,1)}, bf16[128,128]{1,0:T(8,128)(2,1)S(1)}, u32[]{:S(2)}) copy-start(bf16[128,128]{1,0:T(8,128)(2,1)S(1)} %get-tuple-element.32) | copy-start | bytes 98308
  119.7 3.8 %copy-start.3 = (bf16[128,3072]{1,0:T(8,128)(2,1)S(1)}, bf16[128,3072]{1,0:T(8,128)(2,1)}, u32[]{:S(2)}) copy-start(bf16[128,3072]{1,0:T(8,128)(2,1)} %get-tuple-element.23) | copy-start | bytes 2359300
  119.7 17.2 %all-to-all-start.5 = ((bf16[16,8,3072]{2,1,0:T(8,128)(2,1)}), bf16[16,8,3072]{2,1,0:T(8,128)(2,1)S(1)}, u32[]{:S(2)}, u32[]{:S(2)}) async-start(bf16[16,8,3072]{2,1,0:T(8,128)(2,1)} %fusion.5), calls=%async_computation.5 | async-start | bytes 1572864 | tf_op jit(solution)/shard_map/all_to_all | solution.py:17
  124.7 32.2 %copy-start.6 = (bf16[1,8,24,128]{3,2,1,0:T(8,128)(2,1)S(1)}, bf16[1,8,24,128]{3,2,1,0:T(8,128)(2,1)}, u32[]{:S(2)}) copy-start(bf16[1,8,24,128]{3,2,1,0:T(8,128)(2,1)} %copy-done.5) | copy-start | bytes 147460
  137.6 3.2 %collective-permute-start.9 = (bf16[8,3072]{1,0:T(8,128)(2,1)}, bf16[8,3072]{1,0:T(8,128)(2,1)S(1)}, u32[]{:S(2)}, u32[]{:S(2)}) collective-permute-start(bf16[8,3072]{1,0:T(8,128)(2,1)} %reduce_sum.68), channel_id=1, source_target_pairs={{0,1},{1,0},{2,3},{3,2},{4,5},{5,4},{6,7},{7,6},{8,9},{9,8},{10,11... | collective-permute-start | bytes 147464 | tf_op jit(solution)/shard_map/ppermute | solution.py:53
  142.2 6.3 %collective-permute-start.10 = (bf16[8,3072]{1,0:T(8,128)(2,1)}, bf16[8,3072]{1,0:T(8,128)(2,1)}, u32[]{:S(2)}, u32[]{:S(2)}) collective-permute-start(bf16[8,3072]{1,0:T(8,128)(2,1)} %add_convert_fusion.2), channel_id=1, source_target_pairs={{0,2},{1,3},{2,0},{3,1},{4,6},{5,7},{6,4},{7,5},{8,10},{9,11},{10,... | collective-permute-start | bytes 147464 | tf_op jit(solution)/shard_map/ppermute | solution.py:53
  144.5 14.9 %all-to-all-start.6 = ((bf16[16,8,3072]{2,1,0:T(8,128)(2,1)}), bf16[16,8,3072]{2,1,0:T(8,128)(2,1)S(1)}, u32[]{:S(2)}, u32[]{:S(2)}) async-start(bf16[16,8,3072]{2,1,0:T(8,128)(2,1)} %bitcast.122), calls=%async_computation.6 | async-start | bytes 1572864 | tf_op jit(solution)/shard_map/all_to_all | solution.py:17
  149.4 7.5 %collective-permute-start.11 = (bf16[8,3072]{1,0:T(8,128)(2,1)S(1)}, bf16[8,3072]{1,0:T(8,128)(2,1)S(1)}, u32[]{:S(2)}, u32[]{:S(2)}) collective-permute-start(bf16[8,3072]{1,0:T(8,128)(2,1)S(1)} %add_convert_fusion.1), channel_id=1, source_target_pairs={{0,4},{1,5},{2,6},{3,7},{4,0},{5,1},{6,2},{7,3},{8,12},{9,13},{10,... | collective-permute-start | bytes 147464 | tf_op jit(solution)/shard_map/ppermute | solution.py:53
  161.2 15.2 %all-to-all-start.7 = ((bf16[16,8,3072]{2,1,0:T(8,128)(2,1)}), bf16[16,8,3072]{2,1,0:T(8,128)(2,1)S(1)}, u32[]{:S(2)}, u32[]{:S(2)}) async-start(bf16[16,8,3072]{2,1,0:T(8,128)(2,1)} %broadcast_in_dim.63), calls=%async_computation.7 | async-start | bytes 1572864 | tf_op jit(solution)/shard_map/all_to_all | solution.py:17
  168.3 14.3 %collective-permute-start.15 = (bf16[128,3072]{1,0:T(8,128)(2,1)}, bf16[128,3072]{1,0:T(8,128)(2,1)}, u32[]{:S(2)}, u32[]{:S(2)}) collective-permute-start(bf16[128,3072]{1,0:T(8,128)(2,1)} %bitcast_select_fusion.1), channel_id=1, source_target_pairs={{0,128},{128,0},{1,129},{129,1},{2,130},{130,2},{3,131},{131,3},{4... | collective-permute-start | bytes 2359304 | tf_op jit(solution)/shard_map/ppermute | solution.py:63
  178.0 8.7 %collective-permute-start.12 = (f32[128,128]{1,0:T(8,128)S(1)}, f32[128,128]{1,0:T(8,128)S(1)}, u32[]{:S(2)}, u32[]{:S(2)}) collective-permute-start(f32[128,128]{1,0:T(8,128)S(1)} %fusion.17), channel_id=1, source_target_pairs={{0,128},{128,0},{1,129},{129,1},{2,130},{130,2},{3,131},{131,3},{4... | collective-permute-start | bytes 196616 | tf_op jit(solution)/shard_map/ppermute | solution.py:63
  188.2 18.0 %all-to-all-start.8 = ((bf16[16,8,3072]{2,1,0:T(8,128)(2,1)}), bf16[16,8,3072]{2,1,0:T(8,128)(2,1)S(1)}, u32[]{:S(2)}, u32[]{:S(2)}) async-start(bf16[16,8,3072]{2,1,0:T(8,128)(2,1)} %fusion.6), calls=%async_computation.8 | async-start | bytes 1572864 | tf_op jit(solution)/shard_map/all_to_all | solution.py:17
  191.9 3.6 %copy-start = (bf16[128,3072]{1,0:T(8,128)(2,1)S(1)}, bf16[128,3072]{1,0:T(8,128)(2,1)}, u32[]{:S(2)}) copy-start(bf16[128,3072]{1,0:T(8,128)(2,1)} %get-tuple-element.28) | copy-start | bytes 2359300
  194.4 16.0 %collective-permute-start.16 = (bf16[128,3072]{1,0:T(8,128)(2,1)}, bf16[128,3072]{1,0:T(8,128)(2,1)}, u32[]{:S(2)}, u32[]{:S(2)}) collective-permute-start(bf16[128,3072]{1,0:T(8,128)(2,1)} %broadcast_select_fusion.6), channel_id=1, source_target_pairs={{0,128},{128,0},{1,129},{129,1},{2,130},{130,2},{3,131},{131,3},{4... | collective-permute-start | bytes 2359304 | tf_op jit(solution)/shard_map/ppermute | solution.py:63
  195.0 22.9 %collective-permute-start.14 = (bf16[24,128]{1,0:T(8,128)(2,1)}, bf16[24,128]{1,0:T(8,128)(2,1)}, u32[]{:S(2)}, u32[]{:S(2)}) collective-permute-start(bf16[24,128]{1,0:T(8,128)(2,1)} %bitcast_select_fusion.4), channel_id=1, source_target_pairs={{0,128},{128,0},{1,129},{129,1},{2,130},{130,2},{3,131},{131,3},{4... | collective-permute-start | bytes 18440 | tf_op jit(solution)/shard_map/ppermute | solution.py:63
  197.3 9.1 %copy-start.12 = (bf16[1,8,24,128]{3,2,1,0:T(8,128)(2,1)S(1)}, bf16[1,8,24,128]{3,2,1,0:T(8,128)(2,1)}, u32[]{:S(2)}) copy-start(bf16[1,8,24,128]{3,2,1,0:T(8,128)(2,1)} %copy.40) | copy-start | bytes 147460
  197.3 13.2 %copy-start.16 = (f32[128]{0:T(128)S(1)}, f32[128]{0:T(128)}, u32[]{:S(2)}) copy-start(f32[128]{0:T(128)} %copy-done.15) | copy-start | bytes 1540
  197.3 13.2 %copy-start.18 = (f32[128]{0:T(128)S(1)}, f32[128]{0:T(128)}, u32[]{:S(2)}) copy-start(f32[128]{0:T(128)} %copy-done.17) | copy-start | bytes 1540
  207.0 10.9 %all-to-all-start.9 = ((bf16[8,2,24,128]{3,2,1,0:T(8,128)(2,1)}), bf16[8,2,24,128]{3,2,1,0:T(8,128)(2,1)S(1)}, u32[]{:S(2)}, u32[]{:S(2)}) async-start(bf16[8,2,24,128]{3,2,1,0:T(8,128)(2,1)} %pad_maximum_fusion.4), calls=%async_computation.9 | async-start | bytes 196608 | tf_op jit(solution)/shard_map/all_to_all | solution.py:17
  210.4 10.6 %copy-start.8 = (bf16[128,128]{1,0:T(8,128)(2,1)S(1)}, bf16[128,128]{1,0:T(8,128)(2,1)}, u32[]{:S(2)}) copy-start(bf16[128,128]{1,0:T(8,128)(2,1)} %copy-done.7) | copy-start | bytes 98308
  210.4 10.6 %copy-start.10 = (bf16[128,128]{1,0:T(8,128)(2,1)S(1)}, bf16[128,128]{1,0:T(8,128)(2,1)}, u32[]{:S(2)}) copy-start(bf16[128,128]{1,0:T(8,128)(2,1)} %copy-done.9) | copy-start | bytes 98308
  218.6 4.1 %collective-permute-start.13 = (bf16[24,128]{1,0:T(8,128)(2,1)S(1)}, bf16[24,128]{1,0:T(8,128)(2,1)S(1)}, u32[]{:S(2)}, u32[]{:S(2)}) collective-permute-start(bf16[24,128]{1,0:T(8,128)(2,1)S(1)} %get-tuple-element.38), channel_id=1, source_target_pairs={{0,128},{128,0},{1,129},{129,1},{2,130},{130,2},{3,131},{131,3},{4... | collective-permute-start | bytes 18440 | tf_op jit(solution)/shard_map/ppermute | solution.py:63

commit v4 on v3

--- a/solution.py
+++ b/solution.py
@@ -41,6 +41,11 @@
     plane = parts.shape[0] // line
     blocks = exchange(parts.reshape(plane, line, parts.shape[1]), PLANE)
     return jnp.sum(blocks.astype(jnp.float32), axis=0).astype(jnp.bfloat16)
+
+
+def line_sum(block):
+    blocks = exchange(copies(block, lax.axis_size(LINE)), LINE)
+    return jnp.sum(blocks.reshape(-1, *block.shape).astype(jnp.float32), axis=0)
 
 
 def line_sum_steps(block):
@@ -158,15 +163,19 @@
     deltas_one = deltas_of(delta_one, slopes_one)
     partial = plane_sum(slot_gradient(deltas_one, 1), line)
     outcome_one = outcome(hidden_one, 1)
-    partial, outcome_one = lax.optimization_barrier((partial, outcome_one))
-    out_partial = plane_sum(outcome_one, line)
-    back_block = add_bf16(cot_block, line_sum_steps(partial))
+    out_partial = lax.psum_scatter(outcome_one, "x", scatter_dimension=0, tiled=True)
+    back_block = add_bf16(cot_block, line_sum(partial))
     back_block, out_partial = lax.optimization_barrier((back_block, out_partial))
+    out_partial = lax.psum_scatter(out_partial, "y", scatter_dimension=0, tiled=True)
     back_rows = plane_spread(back_block, plane)
 
     back_scaled = scaled(back_rows, 0)
     deltas_zero = deltas_of(hidden_delta(back_scaled, 0), slopes_zero)
-    partial = plane_sum(slot_gradient(deltas_zero, 0), line)
+    shared = swap(pick(mid_rows, in_rows))
+    grad_zero, shared, back_scaled, mid_block, back_block = lax.optimization_barrier(
+        (slot_gradient(deltas_zero, 0), shared, back_scaled, mid_block, back_block)
+    )
+    partial, out_partial = lax.optimization_barrier((plane_sum(grad_zero, line), out_partial))
     ends = jnp.stack(
         [partial.reshape(line, parts, LANES), out_partial.reshape(line, parts, LANES)], axis=1
     )
@@ -182,8 +191,7 @@
     section_output = jnp.concatenate([pick(mid_row, late), pick(early, last_out)], axis=0)
     grad_input = jnp.concatenate([pick(last_grad, early), pick(late, back_row)], axis=0)
 
-    other = swap(pick(mid_rows, in_rows))
-    picked = jnp.concatenate([pick(in_rows, other), pick(other, mid_rows)], axis=1)
+    picked = jnp.concatenate([pick(in_rows, shared), pick(shared, mid_rows)], axis=1)
     other = swap(pick(cot_scaled, back_scaled))
     slot_grad_in = jnp.concatenate([pick(back_scaled, other), pick(other, cot_scaled)], axis=1)
     deltas = pick(deltas_zero, deltas_one)

time: 226 us -> 236 us (1.044)
  blocking collectives: 0 us -> 15 us
  between operations: 2.49 us -> 15.8 us
  waiting for transfers between devices: 90.6 us -> 79.3 us
  starting transfers between devices: 78.7 us -> 70.6 us
    all_to_all x0 -> x1, blocking collectives: none -> 15 us  [exchange(): return lax.all_to_all(value, axes, 0, 0, tiled=True)]
    ppermute x6 -> x3, waiting for transfers between devices: 16.2 us -> 7.02 us  [line_sum_steps(): lax.ppermute(block, LINE, pairs).astype(jnp.float32)]
    ppermute x6 -> x3, starting transfers between devices: 6.9 us -> 3.07 us  [line_sum_steps(): lax.ppermute(block, LINE, pairs).astype(jnp.float32)]
    all_to_all x10 -> x9, waiting for transfers between devices: 72.4 us -> 69.1 us  [exchange(): return lax.all_to_all(value, axes, 0, 0, tiled=True)]
    all_to_all x10 -> x9, starting transfers between devices: 45.6 us -> 42.6 us  [exchange(): return lax.all_to_all(value, axes, 0, 0, tiled=True)]
    broadcast_in_dim x5 -> x6, local copies, waits for them, and re-layouts: 5.28 us -> 5.3 us  [copies(): return jnp.broadcast_to(value[None], (count, *value.shape))]
  transfers between devices with their start and end apart: 27 -> 25, of which waited for: 16 -> 14; matrix products, arithmetic and copies ran while one was open for 15% -> 17% of each run, Pallas kernels for 0% -> 0%
where the time goes in v4:
time: 236 us; the launch traced here: 234 us
  waiting for transfers between devices  79.3 us (34%)
  starting transfers between devices  70.6 us (30%)
  other arithmetic  23.7 us (10%)
  matrix products  19.6 us (8%)
  between operations  15.8 us (7%)
  blocking collectives  15 us (6%)
  local copies, waits for them, and re-layouts  9.68 us (4%)
    all_to_all x9, waiting for transfers between devices, exchange(): return lax.all_to_all(value, axes, 0, 0, tiled=True)  69.1 us
    all_to_all x9, starting transfers between devices, exchange(): return lax.all_to_all(value, axes, 0, 0, tiled=True)  42.6 us
    ppermute x11, starting transfers between devices, swap(): return lax.ppermute(value, 'segment', [(0, 1), (1, 0)])  24.9 us
    select_n x13, other arithmetic, pick(): return jnp.where(first, a, b)  16.2 us
    all_to_all x1, blocking collectives, exchange(): return lax.all_to_all(value, axes, 0, 0, tiled=True)  15 us
    dot_general x4, matrix products, dot_f32(): return jnp.dot(a, b, preferred_element_type=jnp.float32)  7.59 us
    ppermute x3, waiting for transfers between devices, line_sum_steps(): lax.ppermute(block, LINE, pairs).astype(jnp.float32)  7.02 us
    dot_general x4, matrix products, dot_last(): lax.dot_general(a, b, CONTRACT_LAST, preferred_element_type=jnp.float32)  6.76 us
  transfers between devices with their start and end apart: 25, of which 14 were waited for; matrix products, arithmetic and copies ran while one was open for 17% of the time, Pallas kernels for 0%

profile of v4, /device:TPU:1, one launch (start us, length us, event | category | flops | bytes accessed | tf_op | source)
XLA Modules:
  0.0 233.7 jit_solution(13598779012822130911)
XLA Ops:
  7.2 2.4 %broadcast_select_fusion.2 = bf16[3072,256]{1,0:T(8,128)(2,1)S(1)} fusion(pred[]{:T(512)S(6)} %eq.18, bf16[6144,128]{1,0:T(8,128)(2,1)} %bitcast.108, bf16[6144,128]{1,0:T(8,128)(2,1)} %bitcast.110), kind=kLoop, calls=%fused_computation.27 | loop fusion | flops 7077888 | bytes 4718593 | tf_op jit(solution)/shard_map/jit(_where)/select_n | solution.py:91
  9.6 3.3 %collective-permute-start.1 = (bf16[3072,256]{1,0:T(8,128)(2,1)S(1)}, bf16[3072,256]{1,0:T(8,128)(2,1)}, u32[]{:S(2)}, u32[]{:S(2)}) collective-permute-start(bf16[3072,256]{1,0:T(8,128)(2,1)S(1)} %broadcast_select_fusion.2), channel_id=1, source_target_pairs={{0,128},{128,0},{1,129},{129,1},{2,130},{130,2},{3,131},{131,3},{4... | collective-permute-start | bytes 4718600 | tf_op jit(solution)/shard_map/ppermute | solution.py:68
  15.3 6.5 %all-to-all-start = ((bf16[8,48,128]{2,1,0:T(8,128)(2,1)}), bf16[8,48,128]{2,1,0:T(8,128)(2,1)S(1)}, u32[]{:S(2)}, u32[]{:S(2)}) async-start(bf16[8,48,128]{2,1,0:T(8,128)(2,1)} %broadcast_in_dim.37), calls=%async_computation | async-start | bytes 196608 | tf_op jit(solution)/shard_map/all_to_all | solution.py:17
  21.8 1.2 broadcast_select_fusion.10
  23.8 5.4 %all-to-all-done = bf16[8,48,128]{2,1,0:T(8,128)(2,1)S(1)} async-done(((bf16[8,48,128]{2,1,0:T(8,128)(2,1)}), bf16[8,48,128]{2,1,0:T(8,128)(2,1)S(1)}, u32[]{:S(2)}, u32[]{:S(2)}) %all-to-all-start) | async-done | bytes 98336 | tf_op jit(solution)/shard_map/all_to_all | solution.py:17
  30.2 6.8 %all-to-all-start.1 = ((bf16[16,8,3072]{2,1,0:T(8,128)(2,1)}), bf16[16,8,3072]{2,1,0:T(8,128)(2,1)}, u32[]{:S(2)}, u32[]{:S(2)}) async-start(bf16[16,8,3072]{2,1,0:T(8,128)(2,1)} %broadcast_in_dim.66), calls=%async_computation.1 | async-start | bytes 1572864 | tf_op jit(solution)/shard_map/all_to_all | solution.py:17
  37.0 3.7 %broadcast_select_fusion = (bf16[3072,256]{1,0:T(8,128)(2,1)S(1)}, bf16[3072,256]{1,0:T(8,128)(2,1)S(1)}) fusion(bf16[3072,256]{1,0:T(8,128)(2,1)} %collective-permute-done.1, pred[]{:T(512)S(6)} %eq.18, bf16[6144,128]{1,0:T(8,128)(2,1)} %bitcast.109, bf16[6144,128]{1,0:T(8,128)(2,1)} %bitcast.111), kind=kLoop, calls=%fused_computation.25 | loop fusion | flops 12582912 | bytes 7864321 | tf_op jit(solution)/shard_map/jit(_where)/select_n | solution.py:91
  40.7 6.8 %all-to-all-done.1 = bf16[16,8,3072]{2,1,0:T(8,128)(2,1)} async-done(((bf16[16,8,3072]{2,1,0:T(8,128)(2,1)}), bf16[16,8,3072]{2,1,0:T(8,128)(2,1)}, u32[]{:S(2)}, u32[]{:S(2)}) %all-to-all-start.1) | async-done | bytes 786464 | tf_op jit(solution)/shard_map/all_to_all | solution.py:17
  47.6 1.6 fusion.14
  49.2 4.8 %collective-permute-start.2 = (f32[128,256]{1,0:T(8,128)S(1)}, f32[128,256]{1,0:T(8,128)S(1)}, u32[]{:S(2)}, u32[]{:S(2)}) collective-permute-start(f32[128,256]{1,0:T(8,128)S(1)} %fusion.14), channel_id=1, source_target_pairs={{0,128},{128,0},{1,129},{129,1},{2,130},{130,2},{3,131},{131,3},{4... | collective-permute-start | bytes 393224 | tf_op jit(solution)/shard_map/ppermute | solution.py:68
  55.1 2.4 %fusion.6 = bf16[16,8,3072]{2,1,0:T(8,128)(2,1)} fusion(bf16[128,128]{1,0:T(8,128)(2,1)S(1)} %get-tuple-element.40, f32[128]{0:T(128)S(1)} %get-tuple-element.56, bf16[128,3072]{1,0:T(8,128)(2,1)S(1)} %copy-done, bf16[128,3072]{1,0:T(8,128)(2,1)} %collective-permute-done.3, pred[]{:T(512)S(6)} %eq.18), kind=kOutput, calls=%fused_computation.13 | convolution fusion | flops 101842944 | bytes 2392577 | tf_op jit(solution)/shard_map/dot_general | solution.py:29
  57.5 4.3 %all-to-all-start.2 = ((bf16[16,8,3072]{2,1,0:T(8,128)(2,1)}), bf16[16,8,3072]{2,1,0:T(8,128)(2,1)}, u32[]{:S(2)}, u32[]{:S(2)}) async-start(bf16[16,8,3072]{2,1,0:T(8,128)(2,1)} %fusion.6), calls=%async_computation.2 | async-start | bytes 1572864 | tf_op jit(solution)/shard_map/all_to_all | solution.py:17
  61.9 14.7 %all-to-all-done.2 = bf16[16,8,3072]{2,1,0:T(8,128)(2,1)} async-done(((bf16[16,8,3072]{2,1,0:T(8,128)(2,1)}), bf16[16,8,3072]{2,1,0:T(8,128)(2,1)}, u32[]{:S(2)}, u32[]{:S(2)}) %all-to-all-start.2) | async-done | bytes 786464 | tf_op jit(solution)/shard_map/all_to_all | solution.py:17
  76.6 1.2 reduce_sum.64
  78.3 2.5 %collective-permute-done.4 = bf16[8,3072]{1,0:T(8,128)(2,1)S(1)} collective-permute-done((bf16[8,3072]{1,0:T(8,128)(2,1)S(1)}, bf16[8,3072]{1,0:T(8,128)(2,1)S(1)}, u32[]{:S(2)}, u32[]{:S(2)}) %collective-permute-start.4) | collective-permute-done | bytes 49184 | tf_op jit(solution)/shard_map/ppermute | solution.py:58
  82.5 4.3 %all-to-all-start.3 = ((bf16[16,8,3072]{2,1,0:T(8,128)(2,1)}), bf16[16,8,3072]{2,1,0:T(8,128)(2,1)}, u32[]{:S(2)}, u32[]{:S(2)}) async-start(bf16[16,8,3072]{2,1,0:T(8,128)(2,1)} %broadcast_in_dim.67), calls=%async_computation.3 | async-start | bytes 1572864 | tf_op jit(solution)/shard_map/all_to_all | solution.py:17
  87.7 2.5 %collective-permute-start.6 = (bf16[8,3072]{1,0:T(8,128)(2,1)S(1)}, bf16[8,3072]{1,0:T(8,128)(2,1)S(1)}, u32[]{:S(2)}, u32[]{:S(2)}) collective-permute-start(bf16[8,3072]{1,0:T(8,128)(2,1)S(1)} %add_convert_fusion.2), channel_id=1, source_target_pairs={{0,4},{1,5},{2,6},{3,7},{4,0},{5,1},{6,2},{7,3},{8,12},{9,13},{10,... | collective-permute-start | bytes 147464 | tf_op jit(solution)/shard_map/ppermute | solution.py:58
  90.2 4.5 %collective-permute-done.6 = bf16[8,3072]{1,0:T(8,128)(2,1)S(1)} collective-permute-done((bf16[8,3072]{1,0:T(8,128)(2,1)S(1)}, bf16[8,3072]{1,0:T(8,128)(2,1)S(1)}, u32[]{:S(2)}, u32[]{:S(2)}) %collective-permute-start.6) | collective-permute-done | bytes 49184 | tf_op jit(solution)/shard_map/ppermute | solution.py:58
  94.7 4.7 %all-to-all-done.3 = bf16[16,8,3072]{2,1,0:T(8,128)(2,1)} async-done(((bf16[16,8,3072]{2,1,0:T(8,128)(2,1)}), bf16[16,8,3072]{2,1,0:T(8,128)(2,1)}, u32[]{:S(2)}, u32[]{:S(2)}) %all-to-all-start.3) | async-done | bytes 786464 | tf_op jit(solution)/shard_map/all_to_all | solution.py:17
  100.3 4.3 %all-to-all-start.4 = ((bf16[16,8,3072]{2,1,0:T(8,128)(2,1)}), bf16[16,8,3072]{2,1,0:T(8,128)(2,1)}, u32[]{:S(2)}, u32[]{:S(2)}) async-start(bf16[16,8,3072]{2,1,0:T(8,128)(2,1)} %broadcast_in_dim.68), calls=%async_computation.4 | async-start | bytes 1572864 | tf_op jit(solution)/shard_map/all_to_all | solution.py:17
  105.1 10.2 %all-to-all-done.4 = bf16[16,8,3072]{2,1,0:T(8,128)(2,1)} async-done(((bf16[16,8,3072]{2,1,0:T(8,128)(2,1)}), bf16[16,8,3072]{2,1,0:T(8,128)(2,1)}, u32[]{:S(2)}, u32[]{:S(2)}) %all-to-all-start.4) | async-done | bytes 786464 | tf_op jit(solution)/shard_map/all_to_all | solution.py:17
  115.3 1.6 fusion.12
  116.9 4.6 %collective-permute-start.8 = (f32[128,256]{1,0:T(8,128)S(1)}, f32[128,256]{1,0:T(8,128)S(1)}, u32[]{:S(2)}, u32[]{:S(2)}) collective-permute-start(f32[128,256]{1,0:T(8,128)S(1)} %fusion.12), channel_id=1, source_target_pairs={{0,128},{128,0},{1,129},{129,1},{2,130},{130,2},{3,131},{131,3},{4... | collective-permute-start | bytes 393224 | tf_op jit(solution)/shard_map/ppermute | solution.py:68
  121.6 1.6 fusion.17
  125.3 1.5 fusion.5
  126.8 3.7 %all-to-all-start.5 = ((bf16[16,8,3072]{2,1,0:T(8,128)(2,1)}), bf16[16,8,3072]{2,1,0:T(8,128)(2,1)S(1)}, u32[]{:S(2)}, u32[]{:S(2)}) async-start(bf16[16,8,3072]{2,1,0:T(8,128)(2,1)} %fusion.5), calls=%async_computation.5 | async-start | bytes 1572864 | tf_op jit(solution)/shard_map/all_to_all | solution.py:17
  130.6 2.0 fusion.4
  132.6 11.3 %all-to-all-done.5 = bf16[16,8,3072]{2,1,0:T(8,128)(2,1)S(1)} async-done(((bf16[16,8,3072]{2,1,0:T(8,128)(2,1)}), bf16[16,8,3072]{2,1,0:T(8,128)(2,1)S(1)}, u32[]{:S(2)}, u32[]{:S(2)}) %all-to-all-start.5) | async-done | bytes 786464 | tf_op jit(solution)/shard_map/all_to_all | solution.py:17
  145.5 15.0 %all_to_all.50 = bf16[8,8,3072]{2,1,0:T(8,128)(2,1)S(1)} all-to-all(bf16[8,8,3072]{2,1,0:T(8,128)(2,1)S(1)} %broadcast_in_dim.69), channel_id=1, replica_groups=mesh['segment'=2,'x'=4,'y'=4,'z'=8] {'z'}, dimensions={0} | all-to-all | bytes 786432 | tf_op jit(solution)/shard_map/all_to_all | solution.py:17
  161.7 5.7 %all-to-all-start.7 = ((bf16[16,8,3072]{2,1,0:T(8,128)(2,1)}), bf16[16,8,3072]{2,1,0:T(8,128)(2,1)}, u32[]{:S(2)}, u32[]{:S(2)}) async-start(bf16[16,8,3072]{2,1,0:T(8,128)(2,1)} %broadcast_in_dim.70), calls=%async_computation.8 | async-start | bytes 1572864 | tf_op jit(solution)/shard_map/all_to_all | solution.py:17
  167.5 2.3 bitcast_select_fusion.1
  169.8 2.8 %collective-permute-start.10 = (bf16[128,3072]{1,0:T(8,128)(2,1)}, bf16[128,3072]{1,0:T(8,128)(2,1)}, u32[]{:S(2)}, u32[]{:S(2)}) collective-permute-start(bf16[128,3072]{1,0:T(8,128)(2,1)} %bitcast_select_fusion.1), channel_id=1, source_target_pairs={{0,128},{128,0},{1,129},{129,1},{2,130},{130,2},{3,131},{131,3},{4... | collective-permute-start | bytes 2359304 | tf_op jit(solution)/shard_map/ppermute | solution.py:68
  172.6 5.5 %all-to-all-done.7 = bf16[16,8,3072]{2,1,0:T(8,128)(2,1)} async-done(((bf16[16,8,3072]{2,1,0:T(8,128)(2,1)}), bf16[16,8,3072]{2,1,0:T(8,128)(2,1)}, u32[]{:S(2)}, u32[]{:S(2)}) %all-to-all-start.7) | async-done | bytes 786464 | tf_op jit(solution)/shard_map/all_to_all | solution.py:17
  178.1 1.3 fusion.11
  179.4 2.2 fusion.16
  181.6 3.5 %collective-permute-start.9 = (f32[128,128]{1,0:T(8,128)}, f32[128,128]{1,0:T(8,128)S(1)}, u32[]{:S(2)}, u32[]{:S(2)}) collective-permute-start(f32[128,128]{1,0:T(8,128)} %fusion.16), channel_id=1, source_target_pairs={{0,128},{128,0},{1,129},{129,1},{2,130},{130,2},{3,131},{131,3},{4... | collective-permute-start | bytes 196616 | tf_op jit(solution)/shard_map/ppermute | solution.py:68
  187.7 1.5 convolution_convert_fusion.3
  190.9 3.6 %all-to-all-start.8 = ((bf16[16,8,3072]{2,1,0:T(8,128)(2,1)}), bf16[16,8,3072]{2,1,0:T(8,128)(2,1)S(1)}, u32[]{:S(2)}, u32[]{:S(2)}) async-start(bf16[16,8,3072]{2,1,0:T(8,128)(2,1)} %bitcast.18), calls=%async_computation.9 | async-start | bytes 1572864 | tf_op jit(solution)/shard_map/all_to_all | solution.py:17
  195.0 2.3 %broadcast_select_fusion.6 = bf16[128,3072]{1,0:T(8,128)(2,1)} fusion(bf16[128,3072]{1,0:T(8,128)(2,1)S(1)} %fusion.11, pred[]{:T(512)S(6)} %eq.18, bf16[128,3072]{1,0:T(8,128)(2,1)} %bitcast.13, f32[128]{0:T(128)S(1)} %copy-done.11), kind=kLoop, calls=%fused_computation.39 | loop fusion | flops 1572864 | bytes 2359809 | tf_op jit(solution)/shard_map/jit(_where)/select_n | solution.py:91
  197.5 1.7 bitcast_select_fusion.2
  199.3 1.8 fusion.1
  201.0 1.8 fusion
  202.8 4.6 %all-to-all-done.8 = bf16[16,8,3072]{2,1,0:T(8,128)(2,1)S(1)} async-done(((bf16[16,8,3072]{2,1,0:T(8,128)(2,1)}), bf16[16,8,3072]{2,1,0:T(8,128)(2,1)S(1)}, u32[]{:S(2)}, u32[]{:S(2)}) %all-to-all-start.8) | async-done | bytes 786464 | tf_op jit(solution)/shard_map/all_to_all | solution.py:17
  209.0 3.4 %all-to-all-start.9 = ((bf16[8,2,24,128]{3,2,1,0:T(8,128)(2,1)}), bf16[8,2,24,128]{3,2,1,0:T(8,128)(2,1)S(1)}, u32[]{:S(2)}, u32[]{:S(2)}) async-start(bf16[8,2,24,128]{3,2,1,0:T(8,128)(2,1)} %pad_maximum_fusion.4), calls=%async_computation.11 | async-start | bytes 196608 | tf_op jit(solution)/shard_map/all_to_all | solution.py:17
  212.4 1.7 broadcast_select_fusion.5
  214.0 5.8 %all-to-all-done.9 = bf16[8,2,24,128]{3,2,1,0:T(8,128)(2,1)S(1)} async-done(((bf16[8,2,24,128]{3,2,1,0:T(8,128)(2,1)}), bf16[8,2,24,128]{3,2,1,0:T(8,128)(2,1)S(1)}, u32[]{:S(2)}, u32[]{:S(2)}) %all-to-all-start.9) | async-done | bytes 98336 | tf_op jit(solution)/shard_map/all_to_all | solution.py:17
  219.9 4.0 %collective-permute-start.11 = (bf16[24,128]{1,0:T(8,128)(2,1)S(1)}, bf16[24,128]{1,0:T(8,128)(2,1)S(1)}, u32[]{:S(2)}, u32[]{:S(2)}) collective-permute-start(bf16[24,128]{1,0:T(8,128)(2,1)S(1)} %get-tuple-element.48), channel_id=1, source_target_pairs={{0,128},{128,0},{1,129},{129,1},{2,130},{130,2},{3,131},{131,3},{4... | collective-permute-start | bytes 18440 | tf_op jit(solution)/shard_map/ppermute | solution.py:68
  223.8 1.7 fusion.2
  (103 shorter events, 21.0 us)
Async XLA Ops:
  7.2 6.5 %copy-start.15 = (f32[1,1,128]{2,1,0:T(1,128)S(1)}, f32[1,1,128]{2,1,0:T(1,128)}, u32[]{:S(2)}) copy-start(f32[1,1,128]{2,1,0:T(1,128)} %param.16) | copy-start | bytes 1540
  7.2 7.1 %copy-start.16 = (s32[1,1,128]{2,1,0:T(1,128)S(1)}, s32[1,1,128]{2,1,0:T(1,128)}, u32[]{:S(2)}) copy-start(s32[1,1,128]{2,1,0:T(1,128)} %param.14) | copy-start | bytes 1540
  7.2 7.3 %copy-start.8 = (bf16[1,1,6144]{2,1,0:T(2,128)(2,1)S(1)}, bf16[1,1,6144]{2,1,0:T(2,128)(2,1)}, u32[]{:S(2)}) copy-start(bf16[1,1,6144]{2,1,0:T(2,128)(2,1)} %param.9) | copy-start | bytes 36868
  7.2 7.3 %copy-start.9 = (bf16[1,1,6144]{2,1,0:T(2,128)(2,1)S(1)}, bf16[1,1,6144]{2,1,0:T(2,128)(2,1)}, u32[]{:S(2)}) copy-start(bf16[1,1,6144]{2,1,0:T(2,128)(2,1)} %param.10) | copy-start | bytes 36868
  7.2 14.6 %copy-start.3 = (bf16[1,128,6144]{2,1,0:T(8,128)(2,1)S(1)}, bf16[1,128,6144]{2,1,0:T(8,128)(2,1)}, u32[]{:S(2)}) copy-start(bf16[1,128,6144]{2,1,0:T(8,128)(2,1)} %param.13) | copy-start | bytes 4718596
  9.6 27.4 %collective-permute-start.1 = (bf16[3072,256]{1,0:T(8,128)(2,1)S(1)}, bf16[3072,256]{1,0:T(8,128)(2,1)}, u32[]{:S(2)}, u32[]{:S(2)}) collective-permute-start(bf16[3072,256]{1,0:T(8,128)(2,1)S(1)} %broadcast_select_fusion.2), channel_id=1, source_target_pairs={{0,128},{128,0},{1,129},{129,1},{2,130},{130,2},{3,131},{131,3},{4... | collective-permute-start | bytes 4718600 | tf_op jit(solution)/shard_map/ppermute | solution.py:68
  14.4 9.3 %collective-permute-start = (f32[2,128]{1,0:T(2,128)S(1)}, f32[2,128]{1,0:T(2,128)S(1)}, u32[]{:S(2)}, u32[]{:S(2)}) collective-permute-start(f32[2,128]{1,0:T(2,128)S(1)} %stack.10), channel_id=1, source_target_pairs={{0,128},{128,0},{1,129},{129,1},{2,130},{130,2},{3,131},{131,3},{4... | collective-permute-start | bytes 3080 | tf_op jit(solution)/shard_map/ppermute | solution.py:68
  15.3 13.9 %all-to-all-start = ((bf16[8,48,128]{2,1,0:T(8,128)(2,1)}), bf16[8,48,128]{2,1,0:T(8,128)(2,1)S(1)}, u32[]{:S(2)}, u32[]{:S(2)}) async-start(bf16[8,48,128]{2,1,0:T(8,128)(2,1)} %broadcast_in_dim.37), calls=%async_computation | async-start | bytes 196608 | tf_op jit(solution)/shard_map/all_to_all | solution.py:17
  23.0 32.1 %collective-permute-start.3 = (bf16[128,3072]{1,0:T(8,128)(2,1)}, bf16[128,3072]{1,0:T(8,128)(2,1)}, u32[]{:S(2)}, u32[]{:S(2)}) collective-permute-start(bf16[128,3072]{1,0:T(8,128)(2,1)} %get-tuple-element.34), channel_id=1, source_target_pairs={{0,128},{128,0},{1,129},{129,1},{2,130},{130,2},{3,131},{131,3},{4... | collective-permute-start | bytes 2359304 | tf_op jit(solution)/shard_map/ppermute | solution.py:68
  30.2 17.4 %all-to-all-start.1 = ((bf16[16,8,3072]{2,1,0:T(8,128)(2,1)}), bf16[16,8,3072]{2,1,0:T(8,128)(2,1)}, u32[]{:S(2)}, u32[]{:S(2)}) async-start(bf16[16,8,3072]{2,1,0:T(8,128)(2,1)} %broadcast_in_dim.66), calls=%async_computation.1 | async-start | bytes 1572864 | tf_op jit(solution)/shard_map/all_to_all | solution.py:17
  47.6 7.5 %copy-start = (bf16[128,3072]{1,0:T(8,128)(2,1)S(1)}, bf16[128,3072]{1,0:T(8,128)(2,1)}, u32[]{:S(2)}) copy-start(bf16[128,3072]{1,0:T(8,128)(2,1)} %get-tuple-element.33) | copy-start | bytes 2359300
  49.2 5.8 %collective-permute-start.2 = (f32[128,256]{1,0:T(8,128)S(1)}, f32[128,256]{1,0:T(8,128)S(1)}, u32[]{:S(2)}, u32[]{:S(2)}) collective-permute-start(f32[128,256]{1,0:T(8,128)S(1)} %fusion.14), channel_id=1, source_target_pairs={{0,128},{128,0},{1,129},{129,1},{2,130},{130,2},{3,131},{131,3},{4... | collective-permute-start | bytes 393224 | tf_op jit(solution)/shard_map/ppermute | solution.py:68
  54.0 3.5 %copy-start.12 = (f32[128]{0:T(128)}, f32[128]{0:T(128)S(1)}, u32[]{:S(2)}) copy-start(f32[128]{0:T(128)S(1)} %get-tuple-element.56) | copy-start | bytes 1540
  57.5 19.0 %all-to-all-start.2 = ((bf16[16,8,3072]{2,1,0:T(8,128)(2,1)}), bf16[16,8,3072]{2,1,0:T(8,128)(2,1)}, u32[]{:S(2)}, u32[]{:S(2)}) async-start(bf16[16,8,3072]{2,1,0:T(8,128)(2,1)} %fusion.6), calls=%async_computation.2 | async-start | bytes 1572864 | tf_op jit(solution)/shard_map/all_to_all | solution.py:17
  77.8 3.0 %collective-permute-start.4 = (bf16[8,3072]{1,0:T(8,128)(2,1)S(1)}, bf16[8,3072]{1,0:T(8,128)(2,1)S(1)}, u32[]{:S(2)}, u32[]{:S(2)}) collective-permute-start(bf16[8,3072]{1,0:T(8,128)(2,1)S(1)} %reduce_sum.64), channel_id=1, source_target_pairs={{0,1},{1,0},{2,3},{3,2},{4,5},{5,4},{6,7},{7,6},{8,9},{9,8},{10,11... | collective-permute-start | bytes 147464 | tf_op jit(solution)/shard_map/ppermute | solution.py:58
  81.5 5.4 %collective-permute-start.5 = (bf16[8,3072]{1,0:T(8,128)(2,1)}, bf16[8,3072]{1,0:T(8,128)(2,1)}, u32[]{:S(2)}, u32[]{:S(2)}) collective-permute-start(bf16[8,3072]{1,0:T(8,128)(2,1)} %add_convert_fusion.3), channel_id=1, source_target_pairs={{0,2},{1,3},{2,0},{3,1},{4,6},{5,7},{6,4},{7,5},{8,10},{9,11},{10,... | collective-permute-start | bytes 147464 | tf_op jit(solution)/shard_map/ppermute | solution.py:58
  82.5 16.8 %all-to-all-start.3 = ((bf16[16,8,3072]{2,1,0:T(8,128)(2,1)}), bf16[16,8,3072]{2,1,0:T(8,128)(2,1)}, u32[]{:S(2)}, u32[]{:S(2)}) async-start(bf16[16,8,3072]{2,1,0:T(8,128)(2,1)} %broadcast_in_dim.67), calls=%async_computation.3 | async-start | bytes 1572864 | tf_op jit(solution)/shard_map/all_to_all | solution.py:17
  87.7 7.0 %collective-permute-start.6 = (bf16[8,3072]{1,0:T(8,128)(2,1)S(1)}, bf16[8,3072]{1,0:T(8,128)(2,1)S(1)}, u32[]{:S(2)}, u32[]{:S(2)}) collective-permute-start(bf16[8,3072]{1,0:T(8,128)(2,1)S(1)} %add_convert_fusion.2), channel_id=1, source_target_pairs={{0,4},{1,5},{2,6},{3,7},{4,0},{5,1},{6,2},{7,3},{8,12},{9,13},{10,... | collective-permute-start | bytes 147464 | tf_op jit(solution)/shard_map/ppermute | solution.py:58
  94.7 22.3 %copy-start.6 = (bf16[8,3072]{1,0:T(8,128)(2,1)}, bf16[8,3072]{1,0:T(8,128)(2,1)S(1)}, u32[]{:S(2)}) copy-start(bf16[8,3072]{1,0:T(8,128)(2,1)S(1)} %add_convert_fusion.1) | copy-start | bytes 147460
  100.3 15.0 %all-to-all-start.4 = ((bf16[16,8,3072]{2,1,0:T(8,128)(2,1)}), bf16[16,8,3072]{2,1,0:T(8,128)(2,1)}, u32[]{:S(2)}, u32[]{:S(2)}) async-start(bf16[16,8,3072]{2,1,0:T(8,128)(2,1)} %broadcast_in_dim.68), calls=%async_computation.4 | async-start | bytes 1572864 | tf_op jit(solution)/shard_map/all_to_all | solution.py:17
  105.1 18.0 %copy-start.10 = (f32[128]{0:T(128)}, f32[128]{0:T(128)S(1)}, u32[]{:S(2)}) copy-start(f32[128]{0:T(128)S(1)} %get-tuple-element.55) | copy-start | bytes 1540
  115.3 6.2 %copy-start.1 = (bf16[128,3072]{1,0:T(8,128)(2,1)S(1)}, bf16[128,3072]{1,0:T(8,128)(2,1)}, u32[]{:S(2)}) copy-start(bf16[128,3072]{1,0:T(8,128)(2,1)} %get-tuple-element.33) | copy-start | bytes 2359300
  116.9 7.6 %collective-permute-start.8 = (f32[128,256]{1,0:T(8,128)S(1)}, f32[128,256]{1,0:T(8,128)S(1)}, u32[]{:S(2)}, u32[]{:S(2)}) collective-permute-start(f32[128,256]{1,0:T(8,128)S(1)} %fusion.12), channel_id=1, source_target_pairs={{0,128},{128,0},{1,129},{129,1},{2,130},{130,2},{3,131},{131,3},{4... | collective-permute-start | bytes 393224 | tf_op jit(solution)/shard_map/ppermute | solution.py:68
  121.6 3.0 %copy-start.14 = (f32[128]{0:T(128)S(1)}, f32[128]{0:T(128)}, u32[]{:S(2)}) copy-start(f32[128]{0:T(128)} %get-tuple-element.54) | copy-start | bytes 1540
  123.1 1.3 collective-permute-start.7
  126.8 3.8 %copy-start.2 = (bf16[128,3072]{1,0:T(8,128)(2,1)S(1)}, bf16[128,3072]{1,0:T(8,128)(2,1)}, u32[]{:S(2)}) copy-start(bf16[128,3072]{1,0:T(8,128)(2,1)} %get-tuple-element.33) | copy-start | bytes 2359300
  126.8 17.2 %all-to-all-start.5 = ((bf16[16,8,3072]{2,1,0:T(8,128)(2,1)}), bf16[16,8,3072]{2,1,0:T(8,128)(2,1)S(1)}, u32[]{:S(2)}, u32[]{:S(2)}) async-start(bf16[16,8,3072]{2,1,0:T(8,128)(2,1)} %fusion.5), calls=%async_computation.5 | async-start | bytes 1572864 | tf_op jit(solution)/shard_map/all_to_all | solution.py:17
  130.5 30.2 %reduce-scatter.3.cloned.1.call-start = ((), (), s32[]{:S(2)}) async-start(), calls=%async_computation.12 | async-start | bytes 983040 | tf_op jit(solution)/shard_map/reduce_scatter | solution.py:166
  160.7 9.1 %copy-start.7 = (bf16[8,3072]{1,0:T(8,128)(2,1)}, bf16[8,3072]{1,0:T(8,128)(2,1)S(1)}, u32[]{:S(2)}) copy-start(bf16[8,3072]{1,0:T(8,128)(2,1)S(1)} %add_convert_fusion) | copy-start | bytes 147460
  161.7 16.4 %all-to-all-start.7 = ((bf16[16,8,3072]{2,1,0:T(8,128)(2,1)}), bf16[16,8,3072]{2,1,0:T(8,128)(2,1)}, u32[]{:S(2)}, u32[]{:S(2)}) async-start(bf16[16,8,3072]{2,1,0:T(8,128)(2,1)} %broadcast_in_dim.70), calls=%async_computation.8 | async-start | bytes 1572864 | tf_op jit(solution)/shard_map/all_to_all | solution.py:17
  167.4 10.7 %copy-start.13 = (f32[128]{0:T(128)S(1)}, f32[128]{0:T(128)}, u32[]{:S(2)}) copy-start(f32[128]{0:T(128)} %copy-done.12) | copy-start | bytes 1540
  167.4 40.1 %reduce-scatter.5.cloned.1.call-start = ((), (), s32[]{:S(2)}) async-start(), calls=%async_computation.13 | async-start | bytes 245760 | tf_op jit(solution)/shard_map/reduce_scatter | solution.py:169
  169.8 19.4 %collective-permute-start.10 = (bf16[128,3072]{1,0:T(8,128)(2,1)}, bf16[128,3072]{1,0:T(8,128)(2,1)}, u32[]{:S(2)}, u32[]{:S(2)}) collective-permute-start(bf16[128,3072]{1,0:T(8,128)(2,1)} %bitcast_select_fusion.1), channel_id=1, source_target_pairs={{0,128},{128,0},{1,129},{129,1},{2,130},{130,2},{3,131},{131,3},{4... | collective-permute-start | bytes 2359304 | tf_op jit(solution)/shard_map/ppermute | solution.py:68
  181.6 4.6 %collective-permute-start.9 = (f32[128,128]{1,0:T(8,128)}, f32[128,128]{1,0:T(8,128)S(1)}, u32[]{:S(2)}, u32[]{:S(2)}) collective-permute-start(f32[128,128]{1,0:T(8,128)} %fusion.16), channel_id=1, source_target_pairs={{0,128},{128,0},{1,129},{129,1},{2,130},{130,2},{3,131},{131,3},{4... | collective-permute-start | bytes 196616 | tf_op jit(solution)/shard_map/ppermute | solution.py:68
  187.7 7.3 %copy-start.11 = (f32[128]{0:T(128)S(1)}, f32[128]{0:T(128)}, u32[]{:S(2)}) copy-start(f32[128]{0:T(128)} %copy-done.10) | copy-start | bytes 1540
  190.9 16.4 %all-to-all-start.8 = ((bf16[16,8,3072]{2,1,0:T(8,128)(2,1)}), bf16[16,8,3072]{2,1,0:T(8,128)(2,1)S(1)}, u32[]{:S(2)}, u32[]{:S(2)}) async-start(bf16[16,8,3072]{2,1,0:T(8,128)(2,1)} %bitcast.18), calls=%async_computation.9 | async-start | bytes 1572864 | tf_op jit(solution)/shard_map/all_to_all | solution.py:17
  194.6 25.3 %collective-permute-start.12 = (bf16[24,128]{1,0:T(8,128)(2,1)S(1)}, bf16[24,128]{1,0:T(8,128)(2,1)S(1)}, u32[]{:S(2)}, u32[]{:S(2)}) collective-permute-start(bf16[24,128]{1,0:T(8,128)(2,1)S(1)} %bitcast_select_fusion.4), channel_id=1, source_target_pairs={{0,128},{128,0},{1,129},{129,1},{2,130},{130,2},{3,131},{131,3},{4... | collective-permute-start | bytes 18440 | tf_op jit(solution)/shard_map/ppermute | solution.py:68
  197.4 1.9 copy-start.5
  197.4 15.0 %collective-permute-start.13 = (bf16[128,3072]{1,0:T(8,128)(2,1)}, bf16[128,3072]{1,0:T(8,128)(2,1)S(1)}, u32[]{:S(2)}, u32[]{:S(2)}) collective-permute-start(bf16[128,3072]{1,0:T(8,128)(2,1)} %broadcast_select_fusion.6), channel_id=1, source_target_pairs={{0,128},{128,0},{1,129},{129,1},{2,130},{130,2},{3,131},{131,3},{4... | collective-permute-start | bytes 2359304 | tf_op jit(solution)/shard_map/ppermute | solution.py:68
  209.0 10.9 %all-to-all-start.9 = ((bf16[8,2,24,128]{3,2,1,0:T(8,128)(2,1)}), bf16[8,2,24,128]{3,2,1,0:T(8,128)(2,1)S(1)}, u32[]{:S(2)}, u32[]{:S(2)}) async-start(bf16[8,2,24,128]{3,2,1,0:T(8,128)(2,1)} %pad_maximum_fusion.4), calls=%async_computation.11 | async-start | bytes 196608 | tf_op jit(solution)/shard_map/all_to_all | solution.py:17
  212.4 11.5 %copy-start.4 = (bf16[128,128]{1,0:T(8,128)(2,1)S(1)}, bf16[128,128]{1,0:T(8,128)(2,1)}, u32[]{:S(2)}) copy-start(bf16[128,128]{1,0:T(8,128)(2,1)} %get-tuple-element.42) | copy-start | bytes 98308
  219.9 5.7 %collective-permute-start.11 = (bf16[24,128]{1,0:T(8,128)(2,1)S(1)}, bf16[24,128]{1,0:T(8,128)(2,1)S(1)}, u32[]{:S(2)}, u32[]{:S(2)}) collective-permute-start(bf16[24,128]{1,0:T(8,128)(2,1)S(1)} %get-tuple-element.48), channel_id=1, source_target_pairs={{0,128},{128,0},{1,129},{129,1},{2,130},{130,2},{3,131},{131,3},{4... | collective-permute-start | bytes 18440 | tf_op jit(solution)/shard_map/ppermute | solution.py:68
Sparse Core Ops, SparseCore 0:
  134.5 22.1 reduce-scatter.2
  185.2 15.0 reduce-scatter.4

commit v5 on v3

--- a/solution.py
+++ b/solution.py
@@ -85,17 +85,15 @@
     def pick(a, b):
         return jnp.where(first, a, b)
 
-    def by_section(own):
-        other = swap(own)
-        return pick(own, other), pick(other, own)
-
     slots = route_rows.shape[2]
     live = jnp.arange(slots, dtype=jnp.int32) < route_count[0, 0]
     slot_scale = jnp.where(live, route_weight[0, 0], 0.0)
     chosen = route_rows[0, 0][None, :] == jnp.arange(tokens, dtype=jnp.int32)[:, None]
     scale = jnp.sum(jnp.where(chosen, slot_scale[None, :], 0.0), axis=1)
     keep = jnp.broadcast_to(width_mask[0, 0].astype(jnp.float32), (tokens,))
-    small = by_section(jnp.stack([scale, keep]))
+    own = jnp.stack([scale, keep])
+    other = swap(own)
+    small = pick(own, other), pick(other, own)
     scales = [part[0][:, None] for part in small]
     keeps = [part[1][:, None] for part in small]
 
@@ -154,6 +152,7 @@
 
     cot_scaled = scaled(cot_rows, 1)
     delta_one = hidden_delta(cot_scaled, 1)
+    mid_rows, delta_one = lax.optimization_barrier((mid_rows, delta_one))
     hidden_one, slopes_one = forward(mid_rows, 1)
     deltas_one = deltas_of(delta_one, slopes_one)
     partial = plane_sum(slot_gradient(deltas_one, 1), line)
@@ -167,20 +166,17 @@
     back_scaled = scaled(back_rows, 0)
     deltas_zero = deltas_of(hidden_delta(back_scaled, 0), slopes_zero)
     partial = plane_sum(slot_gradient(deltas_zero, 0), line)
-    ends = jnp.stack(
-        [partial.reshape(line, parts, LANES), out_partial.reshape(line, parts, LANES)], axis=1
-    )
-    ends = jnp.sum(exchange(ends, LINE).astype(jnp.float32), axis=0)
+    ends = jnp.concatenate([partial, out_partial], axis=0).reshape(-1, parts, LANES)
+    ends = exchange(ends, ("segment", LINE)).reshape(2, line, parts, LANES)
+    ends = jnp.sum(ends.astype(jnp.float32), axis=1).reshape(2 * parts, LANES)
 
     place = lax.axis_index(LINE)
-    mid_row = mid_block[place].reshape(parts, LANES)
-    back_row = back_block[place].reshape(parts, LANES)
-    early = swap(pick(back_row, mid_row))
-    last_grad = add_bf16(back_row, ends[0])
-    last_out = add_bf16(mid_row, ends[1])
-    late = swap(pick(last_out, last_grad))
-    section_output = jnp.concatenate([pick(mid_row, late), pick(early, last_out)], axis=0)
-    grad_input = jnp.concatenate([pick(last_grad, early), pick(late, back_row)], axis=0)
+    own = jnp.stack([mid_block[place], back_block[place]]).reshape(2, parts, LANES)
+    other = swap(own)
+    mid_row, back_row = jnp.concatenate([pick(own, other), pick(other, own)], axis=1)
+    last = (pick(back_row, mid_row).astype(jnp.float32) + ends).astype(jnp.bfloat16)
+    section_output = pick(mid_row, last)
+    grad_input = pick(last, back_row)
 
     other = swap(pick(mid_rows, in_rows))
     picked = jnp.concatenate([pick(in_rows, other), pick(other, mid_rows)], axis=1)

time: 226 us -> 225 us (level)
    all_to_all x10, waiting for transfers between devices: 72.4 us -> 69.9 us  [exchange(): return lax.all_to_all(value, axes, 0, 0, tiled=True)]
    ppermute x11 -> x10, starting transfers between devices: 26.1 us -> 25 us  [swap(): return lax.ppermute(value, 'segment', [(0, 1), (1, 0)])]
    select_n x13 -> x12, other arithmetic: 18.3 us -> 17.2 us  [pick(): return jnp.where(first, a, b)]
  transfers between devices with their start and end apart: 27 -> 26, of which waited for: 16 -> 17; matrix products, arithmetic and copies ran while one was open for 15% -> 18% of each run, Pallas kernels for 0% -> 0%
where the time goes in v5:
time: 225 us; the launch traced here: 223 us
  waiting for transfers between devices  88.6 us (39%)
  starting transfers between devices  78.3 us (35%)
  other arithmetic  24 us (11%)
  matrix products  19.1 us (8%)
  local copies, waits for them, and re-layouts  10.8 us (5%)
  between operations  2.44 us (1%)
    all_to_all x10, waiting for transfers between devices, exchange(): return lax.all_to_all(value, axes, 0, 0, tiled=True)  69.9 us
    all_to_all x10, starting transfers between devices, exchange(): return lax.all_to_all(value, axes, 0, 0, tiled=True)  47 us
    ppermute x10, starting transfers between devices, swap(): return lax.ppermute(value, 'segment', [(0, 1), (1, 0)])  25 us
    select_n x12, other arithmetic, pick(): return jnp.where(first, a, b)  17.2 us
    ppermute x6, waiting for transfers between devices, line_sum_steps(): lax.ppermute(block, LINE, pairs).astype(jnp.float32)  15.8 us
    dot_general x4, matrix products, dot_f32(): return jnp.dot(a, b, preferred_element_type=jnp.float32)  7.47 us
    ppermute x6, starting transfers between devices, line_sum_steps(): lax.ppermute(block, LINE, pairs).astype(jnp.float32)  6.4 us
    dot_general x4, matrix products, dot_last(): lax.dot_general(a, b, CONTRACT_LAST, preferred_element_type=jnp.float32)  6.39 us
  transfers between devices with their start and end apart: 26, of which 17 were waited for; matrix products, arithmetic and copies ran while one was open for 18% of the time, Pallas kernels for 0%

profile of v5, /device:TPU:1, one launch (start us, length us, event | category | flops | bytes accessed | tf_op | source)
XLA Modules:
  0.0 223.3 jit_solution(541778468028828404)
XLA Ops:
  0.7 2.4 %broadcast_select_fusion.2 = bf16[3072,256]{1,0:T(8,128)(2,1)S(1)} fusion(pred[]{:T(512)S(6)} %eq.18, bf16[6144,128]{1,0:T(8,128)(2,1)} %bitcast.85, bf16[6144,128]{1,0:T(8,128)(2,1)} %bitcast.87), kind=kLoop, calls=%fused_computation.28 | loop fusion | flops 7077888 | bytes 4718593 | tf_op jit(solution)/shard_map/jit(_where)/select_n | solution.py:86
  3.1 3.3 %collective-permute-start.1 = (bf16[3072,256]{1,0:T(8,128)(2,1)S(1)}, bf16[3072,256]{1,0:T(8,128)(2,1)}, u32[]{:S(2)}, u32[]{:S(2)}) collective-permute-start(bf16[3072,256]{1,0:T(8,128)(2,1)S(1)} %broadcast_select_fusion.2), channel_id=1, source_target_pairs={{0,128},{128,0},{1,129},{129,1},{2,130},{130,2},{3,131},{131,3},{4... | collective-permute-start | bytes 4718600 | tf_op jit(solution)/shard_map/ppermute | solution.py:63
  8.8 6.5 %all-to-all-start = ((bf16[8,48,128]{2,1,0:T(8,128)(2,1)}), bf16[8,48,128]{2,1,0:T(8,128)(2,1)S(1)}, u32[]{:S(2)}, u32[]{:S(2)}) async-start(bf16[8,48,128]{2,1,0:T(8,128)(2,1)} %broadcast_in_dim.32), calls=%async_computation | async-start | bytes 196608 | tf_op jit(solution)/shard_map/all_to_all | solution.py:17
  17.2 5.4 %all-to-all-done = bf16[8,48,128]{2,1,0:T(8,128)(2,1)S(1)} async-done(((bf16[8,48,128]{2,1,0:T(8,128)(2,1)}), bf16[8,48,128]{2,1,0:T(8,128)(2,1)S(1)}, u32[]{:S(2)}, u32[]{:S(2)}) %all-to-all-start) | async-done | bytes 98336 | tf_op jit(solution)/shard_map/all_to_all | solution.py:17
  23.7 6.8 %all-to-all-start.1 = ((bf16[16,8,3072]{2,1,0:T(8,128)(2,1)}), bf16[16,8,3072]{2,1,0:T(8,128)(2,1)}, u32[]{:S(2)}, u32[]{:S(2)}) async-start(bf16[16,8,3072]{2,1,0:T(8,128)(2,1)} %broadcast_in_dim.60), calls=%async_computation.1 | async-start | bytes 1572864 | tf_op jit(solution)/shard_map/all_to_all | solution.py:17
  30.5 3.8 %broadcast_select_fusion.1 = (bf16[3072,256]{1,0:T(8,128)(2,1)S(1)}, bf16[3072,256]{1,0:T(8,128)(2,1)S(1)}) fusion(bf16[3072,256]{1,0:T(8,128)(2,1)} %collective-permute-done.1, pred[]{:T(512)S(6)} %eq.18, bf16[6144,128]{1,0:T(8,128)(2,1)} %bitcast.86, bf16[6144,128]{1,0:T(8,128)(2,1)} %bitcast.88), kind=kLoop, calls=%fused_computation.27 | loop fusion | flops 12582912 | bytes 7864321 | tf_op jit(solution)/shard_map/jit(_where)/select_n | solution.py:86
  34.3 6.8 %all-to-all-done.1 = bf16[16,8,3072]{2,1,0:T(8,128)(2,1)} async-done(((bf16[16,8,3072]{2,1,0:T(8,128)(2,1)}), bf16[16,8,3072]{2,1,0:T(8,128)(2,1)}, u32[]{:S(2)}, u32[]{:S(2)}) %all-to-all-start.1) | async-done | bytes 786464 | tf_op jit(solution)/shard_map/all_to_all | solution.py:17
  41.1 1.6 fusion.13
  42.6 4.8 %collective-permute-start.2 = (f32[128,256]{1,0:T(8,128)S(1)}, f32[128,256]{1,0:T(8,128)S(1)}, u32[]{:S(2)}, u32[]{:S(2)}) collective-permute-start(f32[128,256]{1,0:T(8,128)S(1)} %fusion.13), channel_id=1, source_target_pairs={{0,128},{128,0},{1,129},{129,1},{2,130},{130,2},{3,131},{131,3},{4... | collective-permute-start | bytes 393224 | tf_op jit(solution)/shard_map/ppermute | solution.py:63
  49.2 2.4 %fusion.7 = bf16[16,8,3072]{2,1,0:T(8,128)(2,1)} fusion(bf16[128,128]{1,0:T(8,128)(2,1)S(1)} %get-tuple-element.34, f32[128]{0:T(128)S(1)} %get-tuple-element.51, bf16[128,3072]{1,0:T(8,128)(2,1)S(1)} %copy-done.1, bf16[128,3072]{1,0:T(8,128)(2,1)} %collective-permute-done.3, pred[]{:T(512)S(6)} %eq.18), kind=kOutput, calls=%fused_computation.14 | convolution fusion | flops 101842944 | bytes 2392577 | tf_op jit(solution)/shard_map/dot_general | solution.py:29
  51.6 4.3 %all-to-all-start.2 = ((bf16[16,8,3072]{2,1,0:T(8,128)(2,1)}), bf16[16,8,3072]{2,1,0:T(8,128)(2,1)}, u32[]{:S(2)}, u32[]{:S(2)}) async-start(bf16[16,8,3072]{2,1,0:T(8,128)(2,1)} %fusion.7), calls=%async_computation.2 | async-start | bytes 1572864 | tf_op jit(solution)/shard_map/all_to_all | solution.py:17
  55.9 14.7 %all-to-all-done.2 = bf16[16,8,3072]{2,1,0:T(8,128)(2,1)} async-done(((bf16[16,8,3072]{2,1,0:T(8,128)(2,1)}), bf16[16,8,3072]{2,1,0:T(8,128)(2,1)}, u32[]{:S(2)}, u32[]{:S(2)}) %all-to-all-start.2) | async-done | bytes 786464 | tf_op jit(solution)/shard_map/all_to_all | solution.py:17
  72.3 2.5 %collective-permute-done.4 = bf16[8,3072]{1,0:T(8,128)(2,1)S(1)} collective-permute-done((bf16[8,3072]{1,0:T(8,128)(2,1)S(1)}, bf16[8,3072]{1,0:T(8,128)(2,1)S(1)}, u32[]{:S(2)}, u32[]{:S(2)}) %collective-permute-start.4) | collective-permute-done | bytes 49184 | tf_op jit(solution)/shard_map/ppermute | solution.py:53
  76.1 4.3 %all-to-all-start.3 = ((bf16[16,8,3072]{2,1,0:T(8,128)(2,1)}), bf16[16,8,3072]{2,1,0:T(8,128)(2,1)}, u32[]{:S(2)}, u32[]{:S(2)}) async-start(bf16[16,8,3072]{2,1,0:T(8,128)(2,1)} %broadcast_in_dim.61), calls=%async_computation.3 | async-start | bytes 1572864 | tf_op jit(solution)/shard_map/all_to_all | solution.py:17
  81.2 2.5 %collective-permute-start.6 = (bf16[8,3072]{1,0:T(8,128)(2,1)S(1)}, bf16[8,3072]{1,0:T(8,128)(2,1)S(1)}, u32[]{:S(2)}, u32[]{:S(2)}) collective-permute-start(bf16[8,3072]{1,0:T(8,128)(2,1)S(1)} %add_convert_fusion.4), channel_id=1, source_target_pairs={{0,4},{1,5},{2,6},{3,7},{4,0},{5,1},{6,2},{7,3},{8,12},{9,13},{10,... | collective-permute-start | bytes 147464 | tf_op jit(solution)/shard_map/ppermute | solution.py:53
  83.7 4.5 %collective-permute-done.6 = bf16[8,3072]{1,0:T(8,128)(2,1)S(1)} collective-permute-done((bf16[8,3072]{1,0:T(8,128)(2,1)S(1)}, bf16[8,3072]{1,0:T(8,128)(2,1)S(1)}, u32[]{:S(2)}, u32[]{:S(2)}) %collective-permute-start.6) | collective-permute-done | bytes 49184 | tf_op jit(solution)/shard_map/ppermute | solution.py:53
  88.2 4.7 %all-to-all-done.3 = bf16[16,8,3072]{2,1,0:T(8,128)(2,1)} async-done(((bf16[16,8,3072]{2,1,0:T(8,128)(2,1)}), bf16[16,8,3072]{2,1,0:T(8,128)(2,1)}, u32[]{:S(2)}, u32[]{:S(2)}) %all-to-all-start.3) | async-done | bytes 786464 | tf_op jit(solution)/shard_map/all_to_all | solution.py:17
  93.8 4.3 %all-to-all-start.4 = ((bf16[16,8,3072]{2,1,0:T(8,128)(2,1)}), bf16[16,8,3072]{2,1,0:T(8,128)(2,1)}, u32[]{:S(2)}, u32[]{:S(2)}) async-start(bf16[16,8,3072]{2,1,0:T(8,128)(2,1)} %broadcast_in_dim.62), calls=%async_computation.4 | async-start | bytes 1572864 | tf_op jit(solution)/shard_map/all_to_all | solution.py:17
  98.1 1.8 fusion.16
  99.9 2.8 %collective-permute-start.7 = (f32[128,128]{1,0:T(8,128)S(1)}, f32[128,128]{1,0:T(8,128)S(1)}, u32[]{:S(2)}, u32[]{:S(2)}) collective-permute-start(f32[128,128]{1,0:T(8,128)S(1)} %fusion.16), channel_id=1, source_target_pairs={{0,128},{128,0},{1,129},{129,1},{2,130},{130,2},{3,131},{131,3},{4... | collective-permute-start | bytes 196616 | tf_op jit(solution)/shard_map/ppermute | solution.py:63
  103.7 5.2 %all-to-all-done.4 = bf16[16,8,3072]{2,1,0:T(8,128)(2,1)} async-done(((bf16[16,8,3072]{2,1,0:T(8,128)(2,1)}), bf16[16,8,3072]{2,1,0:T(8,128)(2,1)}, u32[]{:S(2)}, u32[]{:S(2)}) %all-to-all-start.4) | async-done | bytes 786464 | tf_op jit(solution)/shard_map/all_to_all | solution.py:17
  110.4 4.6 %collective-permute-start.8 = (f32[128,256]{1,0:T(8,128)S(1)}, f32[128,256]{1,0:T(8,128)S(1)}, u32[]{:S(2)}, u32[]{:S(2)}) collective-permute-start(f32[128,256]{1,0:T(8,128)S(1)} %fusion.35), channel_id=1, source_target_pairs={{0,128},{128,0},{1,129},{129,1},{2,130},{130,2},{3,131},{131,3},{4... | collective-permute-start | bytes 393224 | tf_op jit(solution)/shard_map/ppermute | solution.py:63
  116.7 1.5 fusion.5
  118.2 3.7 %all-to-all-start.5 = ((bf16[16,8,3072]{2,1,0:T(8,128)(2,1)}), bf16[16,8,3072]{2,1,0:T(8,128)(2,1)S(1)}, u32[]{:S(2)}, u32[]{:S(2)}) async-start(bf16[16,8,3072]{2,1,0:T(8,128)(2,1)} %fusion.5), calls=%async_computation.5 | async-start | bytes 1572864 | tf_op jit(solution)/shard_map/all_to_all | solution.py:17
  122.0 2.0 fusion.4
  124.0 10.8 %all-to-all-done.5 = bf16[16,8,3072]{2,1,0:T(8,128)(2,1)S(1)} async-done(((bf16[16,8,3072]{2,1,0:T(8,128)(2,1)}), bf16[16,8,3072]{2,1,0:T(8,128)(2,1)S(1)}, u32[]{:S(2)}, u32[]{:S(2)}) %all-to-all-start.5) | async-done | bytes 786464 | tf_op jit(solution)/shard_map/all_to_all | solution.py:17
  135.4 2.4 %collective-permute-done.9 = bf16[8,3072]{1,0:T(8,128)(2,1)S(1)} collective-permute-done((bf16[8,3072]{1,0:T(8,128)(2,1)S(1)}, bf16[8,3072]{1,0:T(8,128)(2,1)S(1)}, u32[]{:S(2)}, u32[]{:S(2)}) %collective-permute-start.9) | collective-permute-done | bytes 49184 | tf_op jit(solution)/shard_map/ppermute | solution.py:53
  138.5 2.3 %collective-permute-start.10 = (bf16[8,3072]{1,0:T(8,128)(2,1)}, bf16[8,3072]{1,0:T(8,128)(2,1)}, u32[]{:S(2)}, u32[]{:S(2)}) collective-permute-start(bf16[8,3072]{1,0:T(8,128)(2,1)} %add_convert_fusion.2), channel_id=1, source_target_pairs={{0,2},{1,3},{2,0},{3,1},{4,6},{5,7},{6,4},{7,5},{8,10},{9,11},{10,... | collective-permute-start | bytes 147464 | tf_op jit(solution)/shard_map/ppermute | solution.py:53
  142.0 5.0 %collective-permute-start.14 = (bf16[128,3072]{1,0:T(8,128)(2,1)S(1)}, bf16[128,3072]{1,0:T(8,128)(2,1)}, u32[]{:S(2)}, u32[]{:S(2)}) collective-permute-start(bf16[128,3072]{1,0:T(8,128)(2,1)S(1)} %bitcast_select_fusion.1), channel_id=1, source_target_pairs={{0,128},{128,0},{1,129},{129,1},{2,130},{130,2},{3,131},{131,3},{4... | collective-permute-start | bytes 2359304 | tf_op jit(solution)/shard_map/ppermute | solution.py:63
  146.9 3.6 %all-to-all-start.6 = ((bf16[16,8,3072]{2,1,0:T(8,128)(2,1)}), bf16[16,8,3072]{2,1,0:T(8,128)(2,1)S(1)}, u32[]{:S(2)}, u32[]{:S(2)}) async-start(bf16[16,8,3072]{2,1,0:T(8,128)(2,1)} %bitcast.17), calls=%async_computation.6 | async-start | bytes 1572864 | tf_op jit(solution)/shard_map/all_to_all | solution.py:17
  152.6 6.4 %collective-permute-done.11 = bf16[8,3072]{1,0:T(8,128)(2,1)S(1)} collective-permute-done((bf16[8,3072]{1,0:T(8,128)(2,1)S(1)}, bf16[8,3072]{1,0:T(8,128)(2,1)S(1)}, u32[]{:S(2)}, u32[]{:S(2)}) %collective-permute-start.11) | collective-permute-done | bytes 49184 | tf_op jit(solution)/shard_map/ppermute | solution.py:53
  159.6 5.3 %all-to-all-done.6 = bf16[16,8,3072]{2,1,0:T(8,128)(2,1)S(1)} async-done(((bf16[16,8,3072]{2,1,0:T(8,128)(2,1)}), bf16[16,8,3072]{2,1,0:T(8,128)(2,1)S(1)}, u32[]{:S(2)}, u32[]{:S(2)}) %all-to-all-start.6) | async-done | bytes 786464 | tf_op jit(solution)/shard_map/all_to_all | solution.py:17
  165.6 1.8 broadcast_in_dim.63
  167.4 3.6 %all-to-all-start.7 = ((bf16[16,8,3072]{2,1,0:T(8,128)(2,1)}), bf16[16,8,3072]{2,1,0:T(8,128)(2,1)S(1)}, u32[]{:S(2)}, u32[]{:S(2)}) async-start(bf16[16,8,3072]{2,1,0:T(8,128)(2,1)} %broadcast_in_dim.63), calls=%async_computation.7 | async-start | bytes 1572864 | tf_op jit(solution)/shard_map/all_to_all | solution.py:17
  171.0 2.6 %bitcast_select_fusion = (bf16[128,3072]{1,0:T(8,128)(2,1)S(1)}, bf16[128,3072]{1,0:T(8,128)(2,1)}) fusion(bf16[128,3072]{1,0:T(8,128)(2,1)} %collective-permute-done.14, bf16[16,8,3072]{2,1,0:T(8,128)(2,1)} %all-to-all-done.1, pred[]{:T(512)S(6)} %eq.18, bf16[128,3072]{1,0:T(8,128)(2,1)} %bitcast.13), kind=kLoop, calls=%fused_computation.30 | loop fusion | flops 786432 | bytes 3932161 | tf_op jit(solution)/shard_map/jit(_where)/select_n | solution.py:86
  176.1 7.7 %all-to-all-done.7 = bf16[16,8,3072]{2,1,0:T(8,128)(2,1)S(1)} async-done(((bf16[16,8,3072]{2,1,0:T(8,128)(2,1)}), bf16[16,8,3072]{2,1,0:T(8,128)(2,1)S(1)}, u32[]{:S(2)}, u32[]{:S(2)}) %all-to-all-start.7) | async-done | bytes 786464 | tf_op jit(solution)/shard_map/all_to_all | solution.py:17
  183.8 1.6 fusion.15
  185.3 2.5 %collective-permute-start.13 = (f32[128,128]{1,0:T(8,128)S(1)}, f32[128,128]{1,0:T(8,128)S(1)}, u32[]{:S(2)}, u32[]{:S(2)}) collective-permute-start(f32[128,128]{1,0:T(8,128)S(1)} %fusion.15), channel_id=1, source_target_pairs={{0,128},{128,0},{1,129},{129,1},{2,130},{130,2},{3,131},{131,3},{4... | collective-permute-start | bytes 196616 | tf_op jit(solution)/shard_map/ppermute | solution.py:63
  187.9 2.4 %broadcast_select_fusion.6 = bf16[128,3072]{1,0:T(8,128)(2,1)} fusion(pred[]{:T(512)S(6)} %eq.18, bf16[128,3072]{1,0:T(8,128)(2,1)} %bitcast.12, f32[128]{0:T(128)S(1)} %get-tuple-element.50, bf16[16,8,3072]{2,1,0:T(8,128)(2,1)S(1)} %all-to-all-done.7, f32[128]{0:T(128)S(1)} %get-tuple-element.51), kind=kLoop, calls=%fused_computation.36 | loop fusion | flops 2752512 | bytes 2360321 | tf_op jit(solution)/shard_map/jit(_where)/select_n | solution.py:86
  190.3 1.5 fusion.6
  191.8 3.7 %all-to-all-start.8 = ((bf16[16,8,3072]{2,1,0:T(8,128)(2,1)}), bf16[16,8,3072]{2,1,0:T(8,128)(2,1)S(1)}, u32[]{:S(2)}, u32[]{:S(2)}) async-start(bf16[16,8,3072]{2,1,0:T(8,128)(2,1)} %fusion.6), calls=%async_computation.8 | async-start | bytes 1572864 | tf_op jit(solution)/shard_map/all_to_all | solution.py:17
  198.9 1.7 fusion.1
  200.7 1.8 fusion
  202.4 5.9 %all-to-all-done.8 = bf16[16,8,3072]{2,1,0:T(8,128)(2,1)S(1)} async-done(((bf16[16,8,3072]{2,1,0:T(8,128)(2,1)}), bf16[16,8,3072]{2,1,0:T(8,128)(2,1)S(1)}, u32[]{:S(2)}, u32[]{:S(2)}) %all-to-all-start.8) | async-done | bytes 786464 | tf_op jit(solution)/shard_map/all_to_all | solution.py:17
  209.1 6.1 %all-to-all-start.9 = ((bf16[16,24,128]{2,1,0:T(8,128)(2,1)}), bf16[16,24,128]{2,1,0:T(8,128)(2,1)S(1)}, u32[]{:S(2)}, u32[]{:S(2)}) async-start(bf16[16,24,128]{2,1,0:T(8,128)(2,1)} %bitcast.36), calls=%async_computation.9 | async-start | bytes 196608 | tf_op jit(solution)/shard_map/all_to_all | solution.py:17
  215.3 2.0 broadcast_select_fusion.5
  217.3 1.8 fusion.2
  219.1 3.5 %all-to-all-done.9 = bf16[16,24,128]{2,1,0:T(8,128)(2,1)S(1)} async-done(((bf16[16,24,128]{2,1,0:T(8,128)(2,1)}), bf16[16,24,128]{2,1,0:T(8,128)(2,1)S(1)}, u32[]{:S(2)}, u32[]{:S(2)}) %all-to-all-start.9) | async-done | bytes 98336 | tf_op jit(solution)/shard_map/all_to_all | solution.py:17
  (101 shorter events, 27.7 us)
Async XLA Ops:
  0.6 6.5 %copy-start.15 = (f32[1,1,128]{2,1,0:T(1,128)S(1)}, f32[1,1,128]{2,1,0:T(1,128)}, u32[]{:S(2)}) copy-start(f32[1,1,128]{2,1,0:T(1,128)} %param.16) | copy-start | bytes 1540
  0.6 7.1 %copy-start.16 = (s32[1,1,128]{2,1,0:T(1,128)S(1)}, s32[1,1,128]{2,1,0:T(1,128)}, u32[]{:S(2)}) copy-start(s32[1,1,128]{2,1,0:T(1,128)} %param.14) | copy-start | bytes 1540
  0.7 7.3 %copy-start.11 = (bf16[1,1,6144]{2,1,0:T(2,128)(2,1)S(1)}, bf16[1,1,6144]{2,1,0:T(2,128)(2,1)}, u32[]{:S(2)}) copy-start(bf16[1,1,6144]{2,1,0:T(2,128)(2,1)} %param.9) | copy-start | bytes 36868
  0.7 7.3 %copy-start.12 = (bf16[1,1,6144]{2,1,0:T(2,128)(2,1)S(1)}, bf16[1,1,6144]{2,1,0:T(2,128)(2,1)}, u32[]{:S(2)}) copy-start(bf16[1,1,6144]{2,1,0:T(2,128)(2,1)} %param.10) | copy-start | bytes 36868
  0.7 14.6 %copy-start.3 = (bf16[1,128,6144]{2,1,0:T(8,128)(2,1)S(1)}, bf16[1,128,6144]{2,1,0:T(8,128)(2,1)}, u32[]{:S(2)}) copy-start(bf16[1,128,6144]{2,1,0:T(8,128)(2,1)} %param.13) | copy-start | bytes 4718596
  3.1 27.4 %collective-permute-start.1 = (bf16[3072,256]{1,0:T(8,128)(2,1)S(1)}, bf16[3072,256]{1,0:T(8,128)(2,1)}, u32[]{:S(2)}, u32[]{:S(2)}) collective-permute-start(bf16[3072,256]{1,0:T(8,128)(2,1)S(1)} %broadcast_select_fusion.2), channel_id=1, source_target_pairs={{0,128},{128,0},{1,129},{129,1},{2,130},{130,2},{3,131},{131,3},{4... | collective-permute-start | bytes 4718600 | tf_op jit(solution)/shard_map/ppermute | solution.py:63
  7.9 9.3 %collective-permute-start = (f32[2,128]{1,0:T(2,128)S(1)}, f32[2,128]{1,0:T(2,128)S(1)}, u32[]{:S(2)}, u32[]{:S(2)}) collective-permute-start(f32[2,128]{1,0:T(2,128)S(1)} %stack.10), channel_id=1, source_target_pairs={{0,128},{128,0},{1,129},{129,1},{2,130},{130,2},{3,131},{131,3},{4... | collective-permute-start | bytes 3080 | tf_op jit(solution)/shard_map/ppermute | solution.py:63
  8.8 13.9 %all-to-all-start = ((bf16[8,48,128]{2,1,0:T(8,128)(2,1)}), bf16[8,48,128]{2,1,0:T(8,128)(2,1)S(1)}, u32[]{:S(2)}, u32[]{:S(2)}) async-start(bf16[8,48,128]{2,1,0:T(8,128)(2,1)} %broadcast_in_dim.32), calls=%async_computation | async-start | bytes 196608 | tf_op jit(solution)/shard_map/all_to_all | solution.py:17
  16.5 32.1 %collective-permute-start.3 = (bf16[128,3072]{1,0:T(8,128)(2,1)}, bf16[128,3072]{1,0:T(8,128)(2,1)}, u32[]{:S(2)}, u32[]{:S(2)}) collective-permute-start(bf16[128,3072]{1,0:T(8,128)(2,1)} %get-tuple-element.27), channel_id=1, source_target_pairs={{0,128},{128,0},{1,129},{129,1},{2,130},{130,2},{3,131},{131,3},{4... | collective-permute-start | bytes 2359304 | tf_op jit(solution)/shard_map/ppermute | solution.py:63
  23.7 17.4 %all-to-all-start.1 = ((bf16[16,8,3072]{2,1,0:T(8,128)(2,1)}), bf16[16,8,3072]{2,1,0:T(8,128)(2,1)}, u32[]{:S(2)}, u32[]{:S(2)}) async-start(bf16[16,8,3072]{2,1,0:T(8,128)(2,1)} %broadcast_in_dim.60), calls=%async_computation.1 | async-start | bytes 1572864 | tf_op jit(solution)/shard_map/all_to_all | solution.py:17
  41.1 8.1 %copy-start.1 = (bf16[128,3072]{1,0:T(8,128)(2,1)S(1)}, bf16[128,3072]{1,0:T(8,128)(2,1)}, u32[]{:S(2)}) copy-start(bf16[128,3072]{1,0:T(8,128)(2,1)} %get-tuple-element.28) | copy-start | bytes 2359300
  42.6 5.8 %collective-permute-start.2 = (f32[128,256]{1,0:T(8,128)S(1)}, f32[128,256]{1,0:T(8,128)S(1)}, u32[]{:S(2)}, u32[]{:S(2)}) collective-permute-start(f32[128,256]{1,0:T(8,128)S(1)} %fusion.13), channel_id=1, source_target_pairs={{0,128},{128,0},{1,129},{129,1},{2,130},{130,2},{3,131},{131,3},{4... | collective-permute-start | bytes 393224 | tf_op jit(solution)/shard_map/ppermute | solution.py:63
  47.5 140.4 %copy-start.13 = (f32[128]{0:T(128)}, f32[128]{0:T(128)S(1)}, u32[]{:S(2)}) copy-start(f32[128]{0:T(128)S(1)} %get-tuple-element.51) | copy-start | bytes 1540
  48.6 0.6 copy-start.4
  51.6 19.0 %all-to-all-start.2 = ((bf16[16,8,3072]{2,1,0:T(8,128)(2,1)}), bf16[16,8,3072]{2,1,0:T(8,128)(2,1)}, u32[]{:S(2)}, u32[]{:S(2)}) async-start(bf16[16,8,3072]{2,1,0:T(8,128)(2,1)} %fusion.7), calls=%async_computation.2 | async-start | bytes 1572864 | tf_op jit(solution)/shard_map/all_to_all | solution.py:17
  71.9 3.0 %collective-permute-start.4 = (bf16[8,3072]{1,0:T(8,128)(2,1)S(1)}, bf16[8,3072]{1,0:T(8,128)(2,1)S(1)}, u32[]{:S(2)}, u32[]{:S(2)}) collective-permute-start(bf16[8,3072]{1,0:T(8,128)(2,1)S(1)} %reduce_sum.67), channel_id=1, source_target_pairs={{0,1},{1,0},{2,3},{3,2},{4,5},{5,4},{6,7},{7,6},{8,9},{9,8},{10,11... | collective-permute-start | bytes 147464 | tf_op jit(solution)/shard_map/ppermute | solution.py:53
  74.9 5.5 %collective-permute-start.5 = (bf16[8,3072]{1,0:T(8,128)(2,1)S(1)}, bf16[8,3072]{1,0:T(8,128)(2,1)}, u32[]{:S(2)}, u32[]{:S(2)}) collective-permute-start(bf16[8,3072]{1,0:T(8,128)(2,1)S(1)} %add_convert_fusion.5), channel_id=1, source_target_pairs={{0,2},{1,3},{2,0},{3,1},{4,6},{5,7},{6,4},{7,5},{8,10},{9,11},{10,... | collective-permute-start | bytes 147464 | tf_op jit(solution)/shard_map/ppermute | solution.py:53
  76.1 16.8 %all-to-all-start.3 = ((bf16[16,8,3072]{2,1,0:T(8,128)(2,1)}), bf16[16,8,3072]{2,1,0:T(8,128)(2,1)}, u32[]{:S(2)}, u32[]{:S(2)}) async-start(bf16[16,8,3072]{2,1,0:T(8,128)(2,1)} %broadcast_in_dim.61), calls=%async_computation.3 | async-start | bytes 1572864 | tf_op jit(solution)/shard_map/all_to_all | solution.py:17
  81.2 7.0 %collective-permute-start.6 = (bf16[8,3072]{1,0:T(8,128)(2,1)S(1)}, bf16[8,3072]{1,0:T(8,128)(2,1)S(1)}, u32[]{:S(2)}, u32[]{:S(2)}) collective-permute-start(bf16[8,3072]{1,0:T(8,128)(2,1)S(1)} %add_convert_fusion.4), channel_id=1, source_target_pairs={{0,4},{1,5},{2,6},{3,7},{4,0},{5,1},{6,2},{7,3},{8,12},{9,13},{10,... | collective-permute-start | bytes 147464 | tf_op jit(solution)/shard_map/ppermute | solution.py:53
  88.2 11.8 %copy-start.7 = (bf16[8,3072]{1,0:T(8,128)(2,1)}, bf16[8,3072]{1,0:T(8,128)(2,1)S(1)}, u32[]{:S(2)}) copy-start(bf16[8,3072]{1,0:T(8,128)(2,1)S(1)} %add_convert_fusion.3) | copy-start | bytes 147460
  93.8 15.0 %all-to-all-start.4 = ((bf16[16,8,3072]{2,1,0:T(8,128)(2,1)}), bf16[16,8,3072]{2,1,0:T(8,128)(2,1)}, u32[]{:S(2)}, u32[]{:S(2)}) async-start(bf16[16,8,3072]{2,1,0:T(8,128)(2,1)} %broadcast_in_dim.62), calls=%async_computation.4 | async-start | bytes 1572864 | tf_op jit(solution)/shard_map/all_to_all | solution.py:17
  99.9 3.7 %collective-permute-start.7 = (f32[128,128]{1,0:T(8,128)S(1)}, f32[128,128]{1,0:T(8,128)S(1)}, u32[]{:S(2)}, u32[]{:S(2)}) collective-permute-start(f32[128,128]{1,0:T(8,128)S(1)} %fusion.16), channel_id=1, source_target_pairs={{0,128},{128,0},{1,129},{129,1},{2,130},{130,2},{3,131},{131,3},{4... | collective-permute-start | bytes 196616 | tf_op jit(solution)/shard_map/ppermute | solution.py:63
  110.4 5.6 %collective-permute-start.8 = (f32[128,256]{1,0:T(8,128)S(1)}, f32[128,256]{1,0:T(8,128)S(1)}, u32[]{:S(2)}, u32[]{:S(2)}) collective-permute-start(f32[128,256]{1,0:T(8,128)S(1)} %fusion.35), channel_id=1, source_target_pairs={{0,128},{128,0},{1,129},{129,1},{2,130},{130,2},{3,131},{131,3},{4... | collective-permute-start | bytes 393224 | tf_op jit(solution)/shard_map/ppermute | solution.py:63
  118.2 3.8 %copy-start.2 = (bf16[128,3072]{1,0:T(8,128)(2,1)S(1)}, bf16[128,3072]{1,0:T(8,128)(2,1)}, u32[]{:S(2)}) copy-start(bf16[128,3072]{1,0:T(8,128)(2,1)} %get-tuple-element.28) | copy-start | bytes 2359300
  118.2 16.5 %all-to-all-start.5 = ((bf16[16,8,3072]{2,1,0:T(8,128)(2,1)}), bf16[16,8,3072]{2,1,0:T(8,128)(2,1)S(1)}, u32[]{:S(2)}, u32[]{:S(2)}) async-start(bf16[16,8,3072]{2,1,0:T(8,128)(2,1)} %fusion.5), calls=%async_computation.5 | async-start | bytes 1572864 | tf_op jit(solution)/shard_map/all_to_all | solution.py:17
  134.8 3.0 %collective-permute-start.9 = (bf16[8,3072]{1,0:T(8,128)(2,1)S(1)}, bf16[8,3072]{1,0:T(8,128)(2,1)S(1)}, u32[]{:S(2)}, u32[]{:S(2)}) collective-permute-start(bf16[8,3072]{1,0:T(8,128)(2,1)S(1)} %reduce_sum.68), channel_id=1, source_target_pairs={{0,1},{1,0},{2,3},{3,2},{4,5},{5,4},{6,7},{7,6},{8,9},{9,8},{10,11... | collective-permute-start | bytes 147464 | tf_op jit(solution)/shard_map/ppermute | solution.py:53
  138.5 12.1 %collective-permute-start.10 = (bf16[8,3072]{1,0:T(8,128)(2,1)}, bf16[8,3072]{1,0:T(8,128)(2,1)}, u32[]{:S(2)}, u32[]{:S(2)}) collective-permute-start(bf16[8,3072]{1,0:T(8,128)(2,1)} %add_convert_fusion.2), channel_id=1, source_target_pairs={{0,2},{1,3},{2,0},{3,1},{4,6},{5,7},{6,4},{7,5},{8,10},{9,11},{10,... | collective-permute-start | bytes 147464 | tf_op jit(solution)/shard_map/ppermute | solution.py:53
  142.0 29.1 %collective-permute-start.14 = (bf16[128,3072]{1,0:T(8,128)(2,1)S(1)}, bf16[128,3072]{1,0:T(8,128)(2,1)}, u32[]{:S(2)}, u32[]{:S(2)}) collective-permute-start(bf16[128,3072]{1,0:T(8,128)(2,1)S(1)} %bitcast_select_fusion.1), channel_id=1, source_target_pairs={{0,128},{128,0},{1,129},{129,1},{2,130},{130,2},{3,131},{131,3},{4... | collective-permute-start | bytes 2359304 | tf_op jit(solution)/shard_map/ppermute | solution.py:63
  146.9 18.0 %all-to-all-start.6 = ((bf16[16,8,3072]{2,1,0:T(8,128)(2,1)}), bf16[16,8,3072]{2,1,0:T(8,128)(2,1)S(1)}, u32[]{:S(2)}, u32[]{:S(2)}) async-start(bf16[16,8,3072]{2,1,0:T(8,128)(2,1)} %bitcast.17), calls=%async_computation.6 | async-start | bytes 1572864 | tf_op jit(solution)/shard_map/all_to_all | solution.py:17
  151.4 7.5 %collective-permute-start.11 = (bf16[8,3072]{1,0:T(8,128)(2,1)S(1)}, bf16[8,3072]{1,0:T(8,128)(2,1)S(1)}, u32[]{:S(2)}, u32[]{:S(2)}) collective-permute-start(bf16[8,3072]{1,0:T(8,128)(2,1)S(1)} %add_convert_fusion.1), channel_id=1, source_target_pairs={{0,4},{1,5},{2,6},{3,7},{4,0},{5,1},{6,2},{7,3},{8,12},{9,13},{10,... | collective-permute-start | bytes 147464 | tf_op jit(solution)/shard_map/ppermute | solution.py:53
  167.4 16.4 %all-to-all-start.7 = ((bf16[16,8,3072]{2,1,0:T(8,128)(2,1)}), bf16[16,8,3072]{2,1,0:T(8,128)(2,1)S(1)}, u32[]{:S(2)}, u32[]{:S(2)}) async-start(bf16[16,8,3072]{2,1,0:T(8,128)(2,1)} %broadcast_in_dim.63), calls=%async_computation.7 | async-start | bytes 1572864 | tf_op jit(solution)/shard_map/all_to_all | solution.py:17
  175.1 20.5 %collective-permute-start.12 = (bf16[2,24,128]{2,1,0:T(8,128)(2,1)}, bf16[2,24,128]{2,1,0:T(8,128)(2,1)}, u32[]{:S(2)}, u32[]{:S(2)}) collective-permute-start(bf16[2,24,128]{2,1,0:T(8,128)(2,1)} %bitcast.83), channel_id=1, source_target_pairs={{0,128},{128,0},{1,129},{129,1},{2,130},{130,2},{3,131},{131,3},{4... | collective-permute-start | bytes 36872 | tf_op jit(solution)/shard_map/ppermute | solution.py:63
  185.3 5.0 %collective-permute-start.13 = (f32[128,128]{1,0:T(8,128)S(1)}, f32[128,128]{1,0:T(8,128)S(1)}, u32[]{:S(2)}, u32[]{:S(2)}) collective-permute-start(f32[128,128]{1,0:T(8,128)S(1)} %fusion.15), channel_id=1, source_target_pairs={{0,128},{128,0},{1,129},{129,1},{2,130},{130,2},{3,131},{131,3},{4... | collective-permute-start | bytes 196616 | tf_op jit(solution)/shard_map/ppermute | solution.py:63
  190.3 25.0 %collective-permute-start.15 = (bf16[128,3072]{1,0:T(8,128)(2,1)}, bf16[128,3072]{1,0:T(8,128)(2,1)}, u32[]{:S(2)}, u32[]{:S(2)}) collective-permute-start(bf16[128,3072]{1,0:T(8,128)(2,1)} %broadcast_select_fusion.6), channel_id=1, source_target_pairs={{0,128},{128,0},{1,129},{129,1},{2,130},{130,2},{3,131},{131,3},{4... | collective-permute-start | bytes 2359304 | tf_op jit(solution)/shard_map/ppermute | solution.py:63
  191.8 7.1 %copy-start = (bf16[128,3072]{1,0:T(8,128)(2,1)S(1)}, bf16[128,3072]{1,0:T(8,128)(2,1)}, u32[]{:S(2)}) copy-start(bf16[128,3072]{1,0:T(8,128)(2,1)} %get-tuple-element.32) | copy-start | bytes 2359300
  191.8 16.5 %all-to-all-start.8 = ((bf16[16,8,3072]{2,1,0:T(8,128)(2,1)}), bf16[16,8,3072]{2,1,0:T(8,128)(2,1)S(1)}, u32[]{:S(2)}, u32[]{:S(2)}) async-start(bf16[16,8,3072]{2,1,0:T(8,128)(2,1)} %fusion.6), calls=%async_computation.8 | async-start | bytes 1572864 | tf_op jit(solution)/shard_map/all_to_all | solution.py:17
  200.7 7.8 %copy-start.8 = (bf16[8,3072]{1,0:T(8,128)(2,1)S(1)}, bf16[8,3072]{1,0:T(8,128)(2,1)}, u32[]{:S(2)}) copy-start(bf16[8,3072]{1,0:T(8,128)(2,1)} %reduce_sum.69) | copy-start | bytes 147460
  200.7 14.6 %copy-start.14 = (f32[128]{0:T(128)S(1)}, f32[128]{0:T(128)}, u32[]{:S(2)}) copy-start(f32[128]{0:T(128)} %copy-done.13) | copy-start | bytes 1540
  209.1 13.4 %all-to-all-start.9 = ((bf16[16,24,128]{2,1,0:T(8,128)(2,1)}), bf16[16,24,128]{2,1,0:T(8,128)(2,1)S(1)}, u32[]{:S(2)}, u32[]{:S(2)}) async-start(bf16[16,24,128]{2,1,0:T(8,128)(2,1)} %bitcast.36), calls=%async_computation.9 | async-start | bytes 196608 | tf_op jit(solution)/shard_map/all_to_all | solution.py:17
  215.2 2.0 copy-start.5
  215.3 2.1 copy-start.6
  217.3 5.3 %copy-start.9 = (bf16[1,1,1,6144]{3,2,1,0:T(2,128)(2,1)S(1)}, bf16[1,1,1,6144]{3,2,1,0:T(2,128)(2,1)}, u32[]{:S(2)}) copy-start(bf16[1,1,1,6144]{3,2,1,0:T(2,128)(2,1)} %unstack.15) | copy-start | bytes 36868
  217.3 5.3 %copy-start.10 = (bf16[1,1,1,6144]{3,2,1,0:T(2,128)(2,1)S(1)}, bf16[1,1,1,6144]{3,2,1,0:T(2,128)(2,1)}, u32[]{:S(2)}) copy-start(bf16[1,1,1,6144]{3,2,1,0:T(2,128)(2,1)} %unstack.13) | copy-start | bytes 36868

commit v6 on v5

--- a/solution.py
+++ b/solution.py
@@ -43,24 +43,21 @@
     return jnp.sum(blocks.astype(jnp.float32), axis=0).astype(jnp.bfloat16)
 
 
-def line_sum_steps(block):
-    line = lax.axis_size(LINE)
-    total = block.astype(jnp.float32)
-    stride = 1
-    while stride < line:
-        pairs = [(i, i ^ stride) for i in range(line)]
-        block = total.astype(jnp.bfloat16)
-        total = block.astype(jnp.float32) + lax.ppermute(block, LINE, pairs).astype(jnp.float32)
-        stride *= 2
-    return total
+def line_sum(block):
+    blocks = exchange(copies(block, lax.axis_size(LINE)), LINE)
+    return jnp.sum(blocks.reshape(-1, *block.shape).astype(jnp.float32), axis=0)
 
 
 def plane_spread(block, plane):
     return exchange(copies(block, plane), PLANE).reshape(-1, block.shape[1])
 
 
+def across(value, pairs):
+    return lax.ppermute(value, "segment", pairs)
+
+
 def swap(value):
-    return lax.ppermute(value, "segment", [(0, 1), (1, 0)])
+    return across(value, [(0, 1), (1, 0)])
 
 
 def per_device(
@@ -141,13 +138,11 @@
     in_block = rows[:, :parts].reshape(line, half)
     cot_block = rows[:, parts:].reshape(line, half)
 
-    in_rows = plane_spread(in_block, plane)
+    all_rows = plane_spread(jnp.concatenate([in_block, cot_block], axis=1), plane)
+    in_rows, cot_rows = all_rows[:, :half], all_rows[:, half:]
     hidden_zero, slopes_zero = forward(in_rows, 0)
     partial = plane_sum(outcome(hidden_zero, 0), line)
-    partial, cot_part = lax.optimization_barrier((partial, cot_block))
-    cot_rows = plane_spread(cot_part, plane)
-    mid_block = add_bf16(in_block, line_sum_steps(partial))
-    mid_block, cot_rows = lax.optimization_barrier((mid_block, cot_rows))
+    mid_block = add_bf16(in_block, line_sum(partial))
     mid_rows = plane_spread(mid_block, plane)
 
     cot_scaled = scaled(cot_rows, 1)
@@ -157,16 +152,19 @@
     deltas_one = deltas_of(delta_one, slopes_one)
     partial = plane_sum(slot_gradient(deltas_one, 1), line)
     outcome_one = outcome(hidden_one, 1)
-    partial, outcome_one = lax.optimization_barrier((partial, outcome_one))
-    out_partial = plane_sum(outcome_one, line)
-    back_block = add_bf16(cot_block, line_sum_steps(partial))
-    back_block, out_partial = lax.optimization_barrier((back_block, out_partial))
+    back_block = add_bf16(cot_block, line_sum(partial))
     back_rows = plane_spread(back_block, plane)
 
+    in_other, mid_other = across(in_rows, [(1, 0)]), across(mid_rows, [(0, 1)])
+    cot_other = across(cot_scaled, [(0, 1)])
     back_scaled = scaled(back_rows, 0)
+    back_other = across(back_scaled, [(1, 0)])
     deltas_zero = deltas_of(hidden_delta(back_scaled, 0), slopes_zero)
-    partial = plane_sum(slot_gradient(deltas_zero, 0), line)
-    ends = jnp.concatenate([partial, out_partial], axis=0).reshape(-1, parts, LANES)
+    grad_zero, in_other, mid_other, cot_other = lax.optimization_barrier(
+        (slot_gradient(deltas_zero, 0), in_other, mid_other, cot_other)
+    )
+    ends = plane_sum(jnp.concatenate([grad_zero, outcome_one], axis=1), line)
+    ends = ends.reshape(line, 2, parts, LANES).swapaxes(0, 1).reshape(-1, parts, LANES)
     ends = exchange(ends, ("segment", LINE)).reshape(2, line, parts, LANES)
     ends = jnp.sum(ends.astype(jnp.float32), axis=1).reshape(2 * parts, LANES)
 
@@ -178,10 +176,10 @@
     section_output = pick(mid_row, last)
     grad_input = pick(last, back_row)
 
-    other = swap(pick(mid_rows, in_rows))
-    picked = jnp.concatenate([pick(in_rows, other), pick(other, mid_rows)], axis=1)
-    other = swap(pick(cot_scaled, back_scaled))
-    slot_grad_in = jnp.concatenate([pick(back_scaled, other), pick(other, cot_scaled)], axis=1)
+    picked = jnp.concatenate([pick(in_rows, mid_other), pick(in_other, mid_rows)], axis=1)
+    slot_grad_in = jnp.concatenate(
+        [pick(back_scaled, cot_other), pick(back_other, cot_scaled)], axis=1
+    )
     deltas = pick(deltas_zero, deltas_one)
     grad_gate = dot_first(picked, deltas[:, :units])
     grad_up = dot_first(picked, deltas[:, units:])

time: 225 us -> 229 us (1.018)
  blocking collectives: 0 us -> 33.3 us
  waiting for transfers between devices: 88.6 us -> 67.2 us
  starting transfers between devices: 78.3 us -> 73.8 us
  matrix products: 19.1 us -> 16 us
    all_to_all x0 -> x2, blocking collectives: none -> 33.3 us  [exchange(): return lax.all_to_all(value, axes, 0, 0, tiled=True)]
    ppermute x16 -> x12, waiting for transfers between devices: 18.7 us -> 2.89 us  [across(): return lax.ppermute(value, 'segment', pairs)]
    all_to_all x10 -> x8, starting transfers between devices: 47 us -> 37.5 us  [exchange(): return lax.all_to_all(value, axes, 0, 0, tiled=True)]
    all_to_all x10 -> x8, waiting for transfers between devices: 69.9 us -> 64.4 us  [exchange(): return lax.all_to_all(value, axes, 0, 0, tiled=True)]
    ppermute x16 -> x12, starting transfers between devices: 31.4 us -> 36.3 us  [across(): return lax.ppermute(value, 'segment', pairs)]
    select_n x12, other arithmetic: 17.2 us -> 14.7 us  [pick(): return jnp.where(first, a, b)]
    broadcast_in_dim x5 -> x6, local copies, waits for them, and re-layouts: 5.28 us -> 5.44 us  [copies(): return jnp.broadcast_to(value[None], (count, *value.shape))]
  transfers between devices with their start and end apart: 26 -> 20, of which waited for: 17 -> 11; matrix products, arithmetic and copies ran while one was open for 18% -> 15% of each run, Pallas kernels for 0% -> 0%
where the time goes in v6:
time: 229 us; the launch traced here: 227 us
  starting transfers between devices  73.8 us (32%)
  waiting for transfers between devices  67.2 us (29%)
  blocking collectives  33.3 us (15%)
  other arithmetic  24.5 us (11%)
  matrix products  16 us (7%)
  local copies, waits for them, and re-layouts  9.76 us (4%)
  between operations  2.52 us (1%)
    all_to_all x8, waiting for transfers between devices, exchange(): return lax.all_to_all(value, axes, 0, 0, tiled=True)  64.4 us
    all_to_all x8, starting transfers between devices, exchange(): return lax.all_to_all(value, axes, 0, 0, tiled=True)  37.5 us
    ppermute x12, starting transfers between devices, across(): return lax.ppermute(value, 'segment', pairs)  36.3 us
    all_to_all x2, blocking collectives, exchange(): return lax.all_to_all(value, axes, 0, 0, tiled=True)  33.3 us
    select_n x12, other arithmetic, pick(): return jnp.where(first, a, b)  14.7 us
    dot_general x4, matrix products, dot_f32(): return jnp.dot(a, b, preferred_element_type=jnp.float32)  6.18 us
    broadcast_in_dim x6, local copies, waits for them, and re-layouts, copies(): return jnp.broadcast_to(value[None], (count, *value.shape))  5.44 us
    dot_general x3, matrix products, dot_first(): lax.dot_general(a, b, CONTRACT_FIRST, preferred_element_type=jnp.float32)  5.27 us
  transfers between devices with their start and end apart: 20, of which 11 were waited for; matrix products, arithmetic and copies ran while one was open for 15% of the time, Pallas kernels for 0%

profile of v6, /device:TPU:1, one launch (start us, length us, event | category | flops | bytes accessed | tf_op | source)
XLA Modules:
  0.0 227.2 jit_solution(8826506378384543685)
XLA Ops:
  0.7 3.5 %broadcast_select_fusion.2 = bf16[3072,256]{1,0:T(8,128)(2,1)} fusion(pred[]{:T(512)S(6)} %eq.18, bf16[6144,128]{1,0:T(8,128)(2,1)} %bitcast.88, bf16[6144,128]{1,0:T(8,128)(2,1)} %bitcast.90), kind=kLoop, calls=%fused_computation.28 | loop fusion | flops 7077888 | bytes 4718593 | tf_op jit(solution)/shard_map/jit(_where)/select_n | solution.py:83
  4.1 3.2 %collective-permute-start.1 = (bf16[3072,256]{1,0:T(8,128)(2,1)}, bf16[3072,256]{1,0:T(8,128)(2,1)}, u32[]{:S(2)}, u32[]{:S(2)}) collective-permute-start(bf16[3072,256]{1,0:T(8,128)(2,1)} %broadcast_select_fusion.2), channel_id=1, source_target_pairs={{0,128},{128,0},{1,129},{129,1},{2,130},{130,2},{3,131},{131,3},{4... | collective-permute-start | bytes 4718600 | tf_op jit(solution)/shard_map/ppermute | solution.py:56
  8.2 6.4 %all-to-all-start = ((bf16[8,48,128]{2,1,0:T(8,128)(2,1)}), bf16[8,48,128]{2,1,0:T(8,128)(2,1)S(1)}, u32[]{:S(2)}, u32[]{:S(2)}) async-start(bf16[8,48,128]{2,1,0:T(8,128)(2,1)} %broadcast_in_dim.34), calls=%async_computation | async-start | bytes 196608 | tf_op jit(solution)/shard_map/all_to_all | solution.py:17
  16.4 6.0 %all-to-all-done = bf16[8,48,128]{2,1,0:T(8,128)(2,1)S(1)} async-done(((bf16[8,48,128]{2,1,0:T(8,128)(2,1)}), bf16[8,48,128]{2,1,0:T(8,128)(2,1)S(1)}, u32[]{:S(2)}, u32[]{:S(2)}) %all-to-all-start) | async-done | bytes 98336 | tf_op jit(solution)/shard_map/all_to_all | solution.py:17
  22.6 1.3 broadcast_in_dim.38
  23.9 6.8 %all-to-all-start.1 = ((bf16[16,8,6144]{2,1,0:T(8,128)(2,1)}), bf16[16,8,6144]{2,1,0:T(8,128)(2,1)S(1)}, u32[]{:S(2)}, u32[]{:S(2)}) async-start(bf16[16,8,6144]{2,1,0:T(8,128)(2,1)} %broadcast_in_dim.38), calls=%async_computation.1 | async-start | bytes 3145728 | tf_op jit(solution)/shard_map/all_to_all | solution.py:17
  30.7 2.5 %broadcast_select_fusion.10 = (bf16[128,3072]{1,0:T(8,128)(2,1)}, bf16[128,3072]{1,0:T(8,128)(2,1)S(1)}) fusion(pred[]{:T(512)S(6)} %eq.18, bf16[128,6144]{1,0:T(8,128)(2,1)} %bitcast.92), kind=kLoop, calls=%fused_computation.38 | loop fusion | flops 786432 | bytes 3145729 | tf_op jit(solution)/shard_map/jit(_where)/select_n | solution.py:83
  33.2 1.7 collective-permute-start.3
  34.9 3.2 %broadcast_select_fusion.1 = (bf16[3072,256]{1,0:T(8,128)(2,1)}, bf16[3072,256]{1,0:T(8,128)(2,1)}) fusion(bf16[3072,256]{1,0:T(8,128)(2,1)} %collective-permute-done.1, pred[]{:T(512)S(6)} %eq.18, bf16[6144,128]{1,0:T(8,128)(2,1)S(1)} %bitcast.89, bf16[6144,128]{1,0:T(8,128)(2,1)S(1)} %bitcast.91), kind=kLoop, calls=%fused_computation.27 | loop fusion | flops 12582912 | bytes 7864321 | tf_op jit(solution)/shard_map/jit(_where)/select_n | solution.py:83
  38.1 12.9 %all-to-all-done.1 = bf16[16,8,6144]{2,1,0:T(8,128)(2,1)S(1)} async-done(((bf16[16,8,6144]{2,1,0:T(8,128)(2,1)}), bf16[16,8,6144]{2,1,0:T(8,128)(2,1)S(1)}, u32[]{:S(2)}, u32[]{:S(2)}) %all-to-all-start.1) | async-done | bytes 1572896 | tf_op jit(solution)/shard_map/all_to_all | solution.py:17
  51.1 1.8 fusion.31
  52.8 4.4 %collective-permute-start.2 = (f32[128,256]{1,0:T(8,128)S(1)}, f32[128,256]{1,0:T(8,128)S(1)}, u32[]{:S(2)}, u32[]{:S(2)}) collective-permute-start(f32[128,256]{1,0:T(8,128)S(1)} %fusion.31), channel_id=1, source_target_pairs={{0,128},{128,0},{1,129},{129,1},{2,130},{130,2},{3,131},{131,3},{4... | collective-permute-start | bytes 393224 | tf_op jit(solution)/shard_map/ppermute | solution.py:56
  60.0 16.7 %all_to_all.50 = bf16[16,8,3072]{2,1,0:T(8,128)(2,1)} all-to-all(bf16[16,8,3072]{2,1,0:T(8,128)(2,1)S(1)} %fusion.6), channel_id=1, replica_groups=mesh['segment'=2,'x'=4,'y'=4,'z'=8] {'x','y'}, dimensions={0} | all-to-all | bytes 1572864 | tf_op jit(solution)/shard_map/all_to_all | solution.py:17
  76.7 1.2 reduce_sum.73
  78.7 3.5 %all-to-all-start.3 = ((bf16[8,8,3072]{2,1,0:T(8,128)(2,1)}), bf16[8,8,3072]{2,1,0:T(8,128)(2,1)S(1)}, u32[]{:S(2)}, u32[]{:S(2)}) async-start(bf16[8,8,3072]{2,1,0:T(8,128)(2,1)} %broadcast_in_dim.68), calls=%async_computation.3 | async-start | bytes 786432 | tf_op jit(solution)/shard_map/all_to_all | solution.py:17
  82.2 12.4 %all-to-all-done.3 = bf16[8,8,3072]{2,1,0:T(8,128)(2,1)S(1)} async-done(((bf16[8,8,3072]{2,1,0:T(8,128)(2,1)}), bf16[8,8,3072]{2,1,0:T(8,128)(2,1)S(1)}, u32[]{:S(2)}, u32[]{:S(2)}) %all-to-all-start.3) | async-done | bytes 393248 | tf_op jit(solution)/shard_map/all_to_all | solution.py:17
  97.1 4.6 %all-to-all-start.4 = ((bf16[16,8,3072]{2,1,0:T(8,128)(2,1)}), bf16[16,8,3072]{2,1,0:T(8,128)(2,1)}, u32[]{:S(2)}, u32[]{:S(2)}) async-start(bf16[16,8,3072]{2,1,0:T(8,128)(2,1)} %broadcast_in_dim.69), calls=%async_computation.4 | async-start | bytes 1572864 | tf_op jit(solution)/shard_map/all_to_all | solution.py:17
  101.7 1.1 multiply_convert_fusion
  102.8 1.5 fusion.13
  104.3 2.8 %collective-permute-start.4 = (f32[128,128]{1,0:T(8,128)S(1)}, f32[128,128]{1,0:T(8,128)S(1)}, u32[]{:S(2)}, u32[]{:S(2)}) collective-permute-start(f32[128,128]{1,0:T(8,128)S(1)} %fusion.13), channel_id=1, source_target_pairs={{0,128},{128,0},{1,129},{129,1},{2,130},{130,2},{3,131},{131,3},{4... | collective-permute-start | bytes 196616 | tf_op jit(solution)/shard_map/ppermute | solution.py:56
  108.1 4.1 %all-to-all-done.4 = bf16[16,8,3072]{2,1,0:T(8,128)(2,1)} async-done(((bf16[16,8,3072]{2,1,0:T(8,128)(2,1)}), bf16[16,8,3072]{2,1,0:T(8,128)(2,1)}, u32[]{:S(2)}, u32[]{:S(2)}) %all-to-all-start.4) | async-done | bytes 786464 | tf_op jit(solution)/shard_map/all_to_all | solution.py:17
  112.2 2.1 fusion.33
  114.4 4.9 %collective-permute-start.5 = (f32[128,256]{1,0:T(8,128)S(1)}, f32[128,256]{1,0:T(8,128)S(1)}, u32[]{:S(2)}, u32[]{:S(2)}) collective-permute-start(f32[128,256]{1,0:T(8,128)S(1)} %fusion.33), channel_id=1, source_target_pairs={{0,128},{128,0},{1,129},{129,1},{2,130},{130,2},{3,131},{131,3},{4... | collective-permute-start | bytes 393224 | tf_op jit(solution)/shard_map/ppermute | solution.py:56
  121.6 16.6 %all_to_all.51 = bf16[16,8,3072]{2,1,0:T(8,128)(2,1)} all-to-all(bf16[16,8,3072]{2,1,0:T(8,128)(2,1)S(1)} %fusion.5), channel_id=1, replica_groups=mesh['segment'=2,'x'=4,'y'=4,'z'=8] {'x','y'}, dimensions={0} | all-to-all | bytes 1572864 | tf_op jit(solution)/shard_map/all_to_all | solution.py:17
  138.3 1.2 reduce_sum.75
  140.3 3.5 %all-to-all-start.6 = ((bf16[8,8,3072]{2,1,0:T(8,128)(2,1)}), bf16[8,8,3072]{2,1,0:T(8,128)(2,1)S(1)}, u32[]{:S(2)}, u32[]{:S(2)}) async-start(bf16[8,8,3072]{2,1,0:T(8,128)(2,1)} %broadcast_in_dim.70), calls=%async_computation.6 | async-start | bytes 786432 | tf_op jit(solution)/shard_map/all_to_all | solution.py:17
  144.7 1.3 collective-permute-start.10
  146.0 5.4 %collective-permute-start.8 = (bf16[128,3072]{1,0:T(8,128)(2,1)}, bf16[128,3072]{1,0:T(8,128)(2,1)}, u32[]{:S(2)}, u32[]{:S(2)}) collective-permute-start(bf16[128,3072]{1,0:T(8,128)(2,1)} %slice.94), channel_id=1, source_target_pairs={{128,0},{129,1},{130,2},{131,3},{132,4},{133,5},{134,6},{135,7},{1... | collective-permute-start | bytes 2359304 | tf_op jit(solution)/shard_map/ppermute | solution.py:56
  152.2 1.3 collective-permute-start.9
  153.5 2.5 %all-to-all-done.6 = bf16[8,8,3072]{2,1,0:T(8,128)(2,1)S(1)} async-done(((bf16[8,8,3072]{2,1,0:T(8,128)(2,1)}), bf16[8,8,3072]{2,1,0:T(8,128)(2,1)S(1)}, u32[]{:S(2)}, u32[]{:S(2)}) %all-to-all-start.6) | async-done | bytes 393248 | tf_op jit(solution)/shard_map/all_to_all | solution.py:17
  157.8 4.3 %all-to-all-start.7 = ((bf16[16,8,3072]{2,1,0:T(8,128)(2,1)}), bf16[16,8,3072]{2,1,0:T(8,128)(2,1)}, u32[]{:S(2)}, u32[]{:S(2)}) async-start(bf16[16,8,3072]{2,1,0:T(8,128)(2,1)} %broadcast_in_dim.71), calls=%async_computation.7 | async-start | bytes 1572864 | tf_op jit(solution)/shard_map/all_to_all | solution.py:17
  162.2 3.4 %collective-permute-start.6 = (bf16[2,24,128]{2,1,0:T(8,128)(2,1)S(1)}, bf16[2,24,128]{2,1,0:T(8,128)(2,1)S(1)}, u32[]{:S(2)}, u32[]{:S(2)}) collective-permute-start(bf16[2,24,128]{2,1,0:T(8,128)(2,1)S(1)} %bitcast.99), channel_id=1, source_target_pairs={{0,128},{128,0},{1,129},{129,1},{2,130},{130,2},{3,131},{131,3},{4... | collective-permute-start | bytes 36872 | tf_op jit(solution)/shard_map/ppermute | solution.py:56
  165.6 1.9 fusion.4
  167.5 5.4 %all-to-all-done.7 = bf16[16,8,3072]{2,1,0:T(8,128)(2,1)} async-done(((bf16[16,8,3072]{2,1,0:T(8,128)(2,1)}), bf16[16,8,3072]{2,1,0:T(8,128)(2,1)}, u32[]{:S(2)}, u32[]{:S(2)}) %all-to-all-start.7) | async-done | bytes 786464 | tf_op jit(solution)/shard_map/all_to_all | solution.py:17
  172.9 1.3 fusion.11
  175.1 4.6 %collective-permute-start.7 = (f32[128,128]{1,0:T(8,128)S(1)}, f32[128,128]{1,0:T(8,128)S(1)}, u32[]{:S(2)}, u32[]{:S(2)}) collective-permute-start(f32[128,128]{1,0:T(8,128)S(1)} %fusion.12), channel_id=1, source_target_pairs={{0,128},{128,0},{1,129},{129,1},{2,130},{130,2},{3,131},{131,3},{4... | collective-permute-start | bytes 196616 | tf_op jit(solution)/shard_map/ppermute | solution.py:56
  179.7 2.9 %collective-permute-start.11 = (bf16[128,3072]{1,0:T(8,128)(2,1)}, bf16[128,3072]{1,0:T(8,128)(2,1)}, u32[]{:S(2)}, u32[]{:S(2)}) collective-permute-start(bf16[128,3072]{1,0:T(8,128)(2,1)} %copy-done.4), channel_id=1, source_target_pairs={{128,0},{129,1},{130,2},{131,3},{132,4},{133,5},{134,6},{135,7},{1... | collective-permute-start | bytes 2359304 | tf_op jit(solution)/shard_map/ppermute | solution.py:56
  182.7 2.1 convolution_convert_fusion.3
  184.8 1.3 maximum_bitcast_fusion
  186.0 3.7 %all-to-all-start.8 = ((bf16[16,8,6144]{2,1,0:T(8,128)(2,1)}), bf16[16,8,6144]{2,1,0:T(8,128)(2,1)S(1)}, u32[]{:S(2)}, u32[]{:S(2)}) async-start(bf16[16,8,6144]{2,1,0:T(8,128)(2,1)} %maximum_bitcast_fusion), calls=%async_computation.8 | async-start | bytes 3145728 | tf_op jit(solution)/shard_map/all_to_all | solution.py:17
  189.8 3.2 %broadcast_select_fusion.5 = (bf16[128,3072]{1,0:T(8,128)(2,1)}, bf16[128,3072]{1,0:T(8,128)(2,1)S(1)}) fusion(bf16[128,3072]{1,0:T(8,128)(2,1)} %collective-permute-done.10, pred[]{:T(512)S(6)} %eq.18, bf16[128,3072]{1,0:T(8,128)(2,1)} %collective-permute-done.8, bf16[128,3072]{1,0:T(8,128)(2,1)} %bitcast.12, bf16[16,8,3072]{2,1,0:T(8,128)(2,1)} %all-to-all-done.7, ...), kind=kLoop, calls=%fused_computation.33 | loop fusion | flops 1966080 | bytes 4719105 | tf_op jit(solution)/shard_map/jit(_where)/select_n | solution.py:83
  193.0 1.2 broadcast_select_fusion.7
  194.2 1.8 fusion
  196.0 1.8 fusion.1
  197.8 15.7 %all-to-all-done.8 = bf16[16,8,6144]{2,1,0:T(8,128)(2,1)S(1)} async-done(((bf16[16,8,6144]{2,1,0:T(8,128)(2,1)}), bf16[16,8,6144]{2,1,0:T(8,128)(2,1)S(1)}, u32[]{:S(2)}, u32[]{:S(2)}) %all-to-all-start.8) | async-done | bytes 1572896 | tf_op jit(solution)/shard_map/all_to_all | solution.py:17
  214.4 4.7 %all-to-all-start.9 = ((bf16[16,24,128]{2,1,0:T(8,128)(2,1)}), bf16[16,24,128]{2,1,0:T(8,128)(2,1)S(1)}, u32[]{:S(2)}, u32[]{:S(2)}) async-start(bf16[16,24,128]{2,1,0:T(8,128)(2,1)} %bitcast.19), calls=%async_computation.9 | async-start | bytes 196608 | tf_op jit(solution)/shard_map/all_to_all | solution.py:17
  219.5 1.7 fusion.2
  221.2 5.2 %all-to-all-done.9 = bf16[16,24,128]{2,1,0:T(8,128)(2,1)S(1)} async-done(((bf16[16,24,128]{2,1,0:T(8,128)(2,1)}), bf16[16,24,128]{2,1,0:T(8,128)(2,1)S(1)}, u32[]{:S(2)}, u32[]{:S(2)}) %all-to-all-start.9) | async-done | bytes 98336 | tf_op jit(solution)/shard_map/all_to_all | solution.py:17
  (111 shorter events, 17.9 us)
Async XLA Ops:
  0.6 6.7 %copy-start.20 = (bf16[1,1,6144]{2,1,0:T(2,128)(2,1)S(1)}, bf16[1,1,6144]{2,1,0:T(2,128)(2,1)}, u32[]{:S(2)}) copy-start(bf16[1,1,6144]{2,1,0:T(2,128)(2,1)} %param.10) | copy-start | bytes 36868
  0.6 6.8 %copy-start.21 = (bf16[1,1,6144]{2,1,0:T(2,128)(2,1)S(1)}, bf16[1,1,6144]{2,1,0:T(2,128)(2,1)}, u32[]{:S(2)}) copy-start(bf16[1,1,6144]{2,1,0:T(2,128)(2,1)} %param.9) | copy-start | bytes 36868
  0.7 14.6 %copy-start.24 = (f32[1,1,128]{2,1,0:T(1,128)S(1)}, f32[1,1,128]{2,1,0:T(1,128)}, u32[]{:S(2)}) copy-start(f32[1,1,128]{2,1,0:T(1,128)} %param.16) | copy-start | bytes 1540
  0.7 15.3 %copy-start.25 = (s32[1,1,128]{2,1,0:T(1,128)S(1)}, s32[1,1,128]{2,1,0:T(1,128)}, u32[]{:S(2)}) copy-start(s32[1,1,128]{2,1,0:T(1,128)} %param.14) | copy-start | bytes 1540
  4.1 30.8 %collective-permute-start.1 = (bf16[3072,256]{1,0:T(8,128)(2,1)}, bf16[3072,256]{1,0:T(8,128)(2,1)}, u32[]{:S(2)}, u32[]{:S(2)}) collective-permute-start(bf16[3072,256]{1,0:T(8,128)(2,1)} %broadcast_select_fusion.2), channel_id=1, source_target_pairs={{0,128},{128,0},{1,129},{129,1},{2,130},{130,2},{3,131},{131,3},{4... | collective-permute-start | bytes 4718600 | tf_op jit(solution)/shard_map/ppermute | solution.py:56
  8.2 14.3 %all-to-all-start = ((bf16[8,48,128]{2,1,0:T(8,128)(2,1)}), bf16[8,48,128]{2,1,0:T(8,128)(2,1)S(1)}, u32[]{:S(2)}, u32[]{:S(2)}) async-start(bf16[8,48,128]{2,1,0:T(8,128)(2,1)} %broadcast_in_dim.34), calls=%async_computation | async-start | bytes 196608 | tf_op jit(solution)/shard_map/all_to_all | solution.py:17
  16.1 18.8 %collective-permute-start = (f32[2,128]{1,0:T(2,128)S(1)}, f32[2,128]{1,0:T(2,128)S(1)}, u32[]{:S(2)}, u32[]{:S(2)}) collective-permute-start(f32[2,128]{1,0:T(2,128)S(1)} %stack.10), channel_id=1, source_target_pairs={{0,128},{128,0},{1,129},{129,1},{2,130},{130,2},{3,131},{131,3},{4... | collective-permute-start | bytes 3080 | tf_op jit(solution)/shard_map/ppermute | solution.py:56
  22.5 1.4 copy-start.14
  22.5 1.4 copy-start.15
  23.9 27.2 %all-to-all-start.1 = ((bf16[16,8,6144]{2,1,0:T(8,128)(2,1)}), bf16[16,8,6144]{2,1,0:T(8,128)(2,1)S(1)}, u32[]{:S(2)}, u32[]{:S(2)}) async-start(bf16[16,8,6144]{2,1,0:T(8,128)(2,1)} %broadcast_in_dim.38), calls=%async_computation.1 | async-start | bytes 3145728 | tf_op jit(solution)/shard_map/all_to_all | solution.py:17
  30.6 4.3 %copy-start.1 = (bf16[1,6144,128]{2,1,0:T(8,128)(2,1)S(1)}, bf16[1,6144,128]{2,1,0:T(8,128)(2,1)}, u32[]{:S(2)}) copy-start(bf16[1,6144,128]{2,1,0:T(8,128)(2,1)} %param.12) | copy-start | bytes 4718596
  30.6 4.3 %copy-start.2 = (bf16[1,6144,128]{2,1,0:T(8,128)(2,1)S(1)}, bf16[1,6144,128]{2,1,0:T(8,128)(2,1)}, u32[]{:S(2)}) copy-start(bf16[1,6144,128]{2,1,0:T(8,128)(2,1)} %param.11) | copy-start | bytes 4718596
  33.2 25.8 %collective-permute-start.3 = (bf16[128,3072]{1,0:T(8,128)(2,1)}, bf16[128,3072]{1,0:T(8,128)(2,1)S(1)}, u32[]{:S(2)}, u32[]{:S(2)}) collective-permute-start(bf16[128,3072]{1,0:T(8,128)(2,1)} %get-tuple-element.19), channel_id=1, source_target_pairs={{0,128},{128,0},{1,129},{129,1},{2,130},{130,2},{3,131},{131,3},{4... | collective-permute-start | bytes 2359304 | tf_op jit(solution)/shard_map/ppermute | solution.py:56
  52.8 5.4 %collective-permute-start.2 = (f32[128,256]{1,0:T(8,128)S(1)}, f32[128,256]{1,0:T(8,128)S(1)}, u32[]{:S(2)}, u32[]{:S(2)}) collective-permute-start(f32[128,256]{1,0:T(8,128)S(1)} %fusion.31), channel_id=1, source_target_pairs={{0,128},{128,0},{1,129},{129,1},{2,130},{130,2},{3,131},{131,3},{4... | collective-permute-start | bytes 393224 | tf_op jit(solution)/shard_map/ppermute | solution.py:56
  59.0 0.6 copy-start.16
  78.7 15.9 %all-to-all-start.3 = ((bf16[8,8,3072]{2,1,0:T(8,128)(2,1)}), bf16[8,8,3072]{2,1,0:T(8,128)(2,1)S(1)}, u32[]{:S(2)}, u32[]{:S(2)}) async-start(bf16[8,8,3072]{2,1,0:T(8,128)(2,1)} %broadcast_in_dim.68), calls=%async_computation.3 | async-start | bytes 786432 | tf_op jit(solution)/shard_map/all_to_all | solution.py:17
  82.2 20.6 %copy-start.22 = (f32[128]{0:T(128)}, f32[128]{0:T(128)S(1)}, u32[]{:S(2)}) copy-start(f32[128]{0:T(128)S(1)} %get-tuple-element.38) | copy-start | bytes 1540
  95.5 0.6 copy-start.19
  97.1 15.2 %all-to-all-start.4 = ((bf16[16,8,3072]{2,1,0:T(8,128)(2,1)}), bf16[16,8,3072]{2,1,0:T(8,128)(2,1)}, u32[]{:S(2)}, u32[]{:S(2)}) async-start(bf16[16,8,3072]{2,1,0:T(8,128)(2,1)} %broadcast_in_dim.69), calls=%async_computation.4 | async-start | bytes 1572864 | tf_op jit(solution)/shard_map/all_to_all | solution.py:17
  104.3 3.8 %collective-permute-start.4 = (f32[128,128]{1,0:T(8,128)S(1)}, f32[128,128]{1,0:T(8,128)S(1)}, u32[]{:S(2)}, u32[]{:S(2)}) collective-permute-start(f32[128,128]{1,0:T(8,128)S(1)} %fusion.13), channel_id=1, source_target_pairs={{0,128},{128,0},{1,129},{129,1},{2,130},{130,2},{3,131},{131,3},{4... | collective-permute-start | bytes 196616 | tf_op jit(solution)/shard_map/ppermute | solution.py:56
  108.1 12.9 %copy-start.6 = (f32[128,128]{1,0:T(8,128)}, f32[128,128]{1,0:T(8,128)S(1)}, u32[]{:S(2)}) copy-start(f32[128,128]{1,0:T(8,128)S(1)} %add.62) | copy-start | bytes 196612
  112.2 8.7 %copy-start = (bf16[3072,256]{1,0:T(8,128)(2,1)S(1)}, bf16[3072,256]{1,0:T(8,128)(2,1)}, u32[]{:S(2)}) copy-start(bf16[3072,256]{1,0:T(8,128)(2,1)} %get-tuple-element.18) | copy-start | bytes 4718596
  114.4 5.9 %collective-permute-start.5 = (f32[128,256]{1,0:T(8,128)S(1)}, f32[128,256]{1,0:T(8,128)S(1)}, u32[]{:S(2)}, u32[]{:S(2)}) collective-permute-start(f32[128,256]{1,0:T(8,128)S(1)} %fusion.33), channel_id=1, source_target_pairs={{0,128},{128,0},{1,129},{129,1},{2,130},{130,2},{3,131},{131,3},{4... | collective-permute-start | bytes 393224 | tf_op jit(solution)/shard_map/ppermute | solution.py:56
  121.0 0.7 copy-start.10
  121.0 0.7 copy-start.12
  140.3 15.7 %all-to-all-start.6 = ((bf16[8,8,3072]{2,1,0:T(8,128)(2,1)}), bf16[8,8,3072]{2,1,0:T(8,128)(2,1)S(1)}, u32[]{:S(2)}, u32[]{:S(2)}) async-start(bf16[8,8,3072]{2,1,0:T(8,128)(2,1)} %broadcast_in_dim.70), calls=%async_computation.6 | async-start | bytes 786432 | tf_op jit(solution)/shard_map/all_to_all | solution.py:17
  144.7 40.0 %collective-permute-start.10 = (bf16[128,3072]{1,0:T(8,128)(2,1)}, bf16[128,3072]{1,0:T(8,128)(2,1)}, u32[]{:S(2)}, u32[]{:S(2)}) collective-permute-start(bf16[128,3072]{1,0:T(8,128)(2,1)} %multiply_convert_fusion), channel_id=1, source_target_pairs={{0,128},{1,129},{2,130},{3,131},{4,132},{5,133},{6,134},{7,135},{8... | collective-permute-start | bytes 2359304 | tf_op jit(solution)/shard_map/ppermute | solution.py:56
  146.0 38.7 %collective-permute-start.8 = (bf16[128,3072]{1,0:T(8,128)(2,1)}, bf16[128,3072]{1,0:T(8,128)(2,1)}, u32[]{:S(2)}, u32[]{:S(2)}) collective-permute-start(bf16[128,3072]{1,0:T(8,128)(2,1)} %slice.94), channel_id=1, source_target_pairs={{128,0},{129,1},{130,2},{131,3},{132,4},{133,5},{134,6},{135,7},{1... | collective-permute-start | bytes 2359304 | tf_op jit(solution)/shard_map/ppermute | solution.py:56
  152.2 32.6 %collective-permute-start.9 = (bf16[128,3072]{1,0:T(8,128)(2,1)}, bf16[128,3072]{1,0:T(8,128)(2,1)}, u32[]{:S(2)}, u32[]{:S(2)}) collective-permute-start(bf16[128,3072]{1,0:T(8,128)(2,1)} %bitcast.12), channel_id=1, source_target_pairs={{0,128},{1,129},{2,130},{3,131},{4,132},{5,133},{6,134},{7,135},{8... | collective-permute-start | bytes 2359304 | tf_op jit(solution)/shard_map/ppermute | solution.py:56
  156.1 9.5 %copy-start.18 = (bf16[128,128]{1,0:T(8,128)(2,1)S(1)}, bf16[128,128]{1,0:T(8,128)(2,1)}, u32[]{:S(2)}) copy-start(bf16[128,128]{1,0:T(8,128)(2,1)} %get-tuple-element.24) | copy-start | bytes 98308
  157.8 15.0 %all-to-all-start.7 = ((bf16[16,8,3072]{2,1,0:T(8,128)(2,1)}), bf16[16,8,3072]{2,1,0:T(8,128)(2,1)}, u32[]{:S(2)}, u32[]{:S(2)}) async-start(bf16[16,8,3072]{2,1,0:T(8,128)(2,1)} %broadcast_in_dim.71), calls=%async_computation.7 | async-start | bytes 1572864 | tf_op jit(solution)/shard_map/all_to_all | solution.py:17
  162.2 5.3 %collective-permute-start.6 = (bf16[2,24,128]{2,1,0:T(8,128)(2,1)S(1)}, bf16[2,24,128]{2,1,0:T(8,128)(2,1)S(1)}, u32[]{:S(2)}, u32[]{:S(2)}) collective-permute-start(bf16[2,24,128]{2,1,0:T(8,128)(2,1)S(1)} %bitcast.99), channel_id=1, source_target_pairs={{0,128},{128,0},{1,129},{129,1},{2,130},{130,2},{3,131},{131,3},{4... | collective-permute-start | bytes 36872 | tf_op jit(solution)/shard_map/ppermute | solution.py:56
  174.2 0.9 copy-start.4
  174.2 8.4 %copy-start.8 = (f32[128,128]{1,0:T(8,128)S(1)}, f32[128,128]{1,0:T(8,128)}, u32[]{:S(2)}) copy-start(f32[128,128]{1,0:T(8,128)} %get-tuple-element.21) | copy-start | bytes 196612
  174.3 8.4 %copy-start.9 = (f32[128,128]{1,0:T(8,128)S(1)}, f32[128,128]{1,0:T(8,128)}, u32[]{:S(2)}) copy-start(f32[128,128]{1,0:T(8,128)} %get-tuple-element.23) | copy-start | bytes 196612
  175.1 9.7 %copy-start.5 = (bf16[128,3072]{1,0:T(8,128)(2,1)S(1)}, bf16[128,3072]{1,0:T(8,128)(2,1)}, u32[]{:S(2)}) copy-start(bf16[128,3072]{1,0:T(8,128)(2,1)} %fusion.4) | copy-start | bytes 2359300
  175.1 7.5 %collective-permute-start.7 = (f32[128,128]{1,0:T(8,128)S(1)}, f32[128,128]{1,0:T(8,128)S(1)}, u32[]{:S(2)}, u32[]{:S(2)}) collective-permute-start(f32[128,128]{1,0:T(8,128)S(1)} %fusion.12), channel_id=1, source_target_pairs={{0,128},{128,0},{1,129},{129,1},{2,130},{130,2},{3,131},{131,3},{4... | collective-permute-start | bytes 196616 | tf_op jit(solution)/shard_map/ppermute | solution.py:56
  179.7 39.4 %collective-permute-start.11 = (bf16[128,3072]{1,0:T(8,128)(2,1)}, bf16[128,3072]{1,0:T(8,128)(2,1)}, u32[]{:S(2)}, u32[]{:S(2)}) collective-permute-start(bf16[128,3072]{1,0:T(8,128)(2,1)} %copy-done.4), channel_id=1, source_target_pairs={{128,0},{129,1},{130,2},{131,3},{132,4},{133,5},{134,6},{135,7},{1... | collective-permute-start | bytes 2359304 | tf_op jit(solution)/shard_map/ppermute | solution.py:56
  186.0 27.4 %all-to-all-start.8 = ((bf16[16,8,6144]{2,1,0:T(8,128)(2,1)}), bf16[16,8,6144]{2,1,0:T(8,128)(2,1)S(1)}, u32[]{:S(2)}, u32[]{:S(2)}) async-start(bf16[16,8,6144]{2,1,0:T(8,128)(2,1)} %maximum_bitcast_fusion), calls=%async_computation.8 | async-start | bytes 3145728 | tf_op jit(solution)/shard_map/all_to_all | solution.py:17
  189.8 3.2 %copy-start.7 = (f32[128,128]{1,0:T(8,128)S(1)}, f32[128,128]{1,0:T(8,128)}, u32[]{:S(2)}) copy-start(f32[128,128]{1,0:T(8,128)} %copy-done.6) | copy-start | bytes 196612
  189.8 3.2 %copy-start.11 = (f32[128,128]{1,0:T(8,128)S(1)}, f32[128,128]{1,0:T(8,128)}, u32[]{:S(2)}) copy-start(f32[128,128]{1,0:T(8,128)} %copy-done.10) | copy-start | bytes 196612
  189.8 3.2 %copy-start.13 = (f32[128,128]{1,0:T(8,128)S(1)}, f32[128,128]{1,0:T(8,128)}, u32[]{:S(2)}) copy-start(f32[128,128]{1,0:T(8,128)} %copy-done.12) | copy-start | bytes 196612
  197.7 21.4 %copy-start.23 = (f32[128]{0:T(128)S(1)}, f32[128]{0:T(128)}, u32[]{:S(2)}) copy-start(f32[128]{0:T(128)} %copy-done.22) | copy-start | bytes 1540
  213.7 5.8 %copy-start.3 = (bf16[128,3072]{1,0:T(8,128)(2,1)S(1)}, bf16[128,3072]{1,0:T(8,128)(2,1)}, u32[]{:S(2)}) copy-start(bf16[128,3072]{1,0:T(8,128)(2,1)} %get-tuple-element.41) | copy-start | bytes 2359300
  213.7 5.8 %copy-start.17 = (bf16[128,128]{1,0:T(8,128)(2,1)S(1)}, bf16[128,128]{1,0:T(8,128)(2,1)}, u32[]{:S(2)}) copy-start(bf16[128,128]{1,0:T(8,128)(2,1)} %copy-done.16) | copy-start | bytes 98308
  214.4 12.1 %all-to-all-start.9 = ((bf16[16,24,128]{2,1,0:T(8,128)(2,1)}), bf16[16,24,128]{2,1,0:T(8,128)(2,1)S(1)}, u32[]{:S(2)}, u32[]{:S(2)}) async-start(bf16[16,24,128]{2,1,0:T(8,128)(2,1)} %bitcast.19), calls=%async_computation.9 | async-start | bytes 196608 | tf_op jit(solution)/shard_map/all_to_all | solution.py:17

commit v7 on v5

--- a/solution.py
+++ b/solution.py
@@ -59,8 +59,12 @@
     return exchange(copies(block, plane), PLANE).reshape(-1, block.shape[1])
 
 
+def across(value, pairs):
+    return lax.ppermute(value, "segment", pairs)
+
+
 def swap(value):
-    return lax.ppermute(value, "segment", [(0, 1), (1, 0)])
+    return across(value, [(0, 1), (1, 0)])
 
 
 def per_device(
@@ -160,12 +164,20 @@
     partial, outcome_one = lax.optimization_barrier((partial, outcome_one))
     out_partial = plane_sum(outcome_one, line)
     back_block = add_bf16(cot_block, line_sum_steps(partial))
-    back_block, out_partial = lax.optimization_barrier((back_block, out_partial))
+    back_block, out_partial, in_late, mid_late, cot_late, mid_block = lax.optimization_barrier(
+        (back_block, out_partial, in_rows, mid_rows, cot_scaled, mid_block)
+    )
     back_rows = plane_spread(back_block, plane)
+    in_other, mid_other = across(in_late, [(1, 0)]), across(mid_late, [(0, 1)])
+    cot_other = across(cot_late, [(0, 1)])
 
     back_scaled = scaled(back_rows, 0)
     deltas_zero = deltas_of(hidden_delta(back_scaled, 0), slopes_zero)
-    partial = plane_sum(slot_gradient(deltas_zero, 0), line)
+    back_other = across(back_scaled, [(1, 0)])
+    grad_zero, in_other, mid_other, cot_other = lax.optimization_barrier(
+        (slot_gradient(deltas_zero, 0), in_other, mid_other, cot_other)
+    )
+    partial = plane_sum(grad_zero, line)
     ends = jnp.concatenate([partial, out_partial], axis=0).reshape(-1, parts, LANES)
     ends = exchange(ends, ("segment", LINE)).reshape(2, line, parts, LANES)
     ends = jnp.sum(ends.astype(jnp.float32), axis=1).reshape(2 * parts, LANES)
@@ -178,10 +190,10 @@
     section_output = pick(mid_row, last)
     grad_input = pick(last, back_row)
 
-    other = swap(pick(mid_rows, in_rows))
-    picked = jnp.concatenate([pick(in_rows, other), pick(other, mid_rows)], axis=1)
-    other = swap(pick(cot_scaled, back_scaled))
-    slot_grad_in = jnp.concatenate([pick(back_scaled, other), pick(other, cot_scaled)], axis=1)
+    picked = jnp.concatenate([pick(in_rows, mid_other), pick(in_other, mid_rows)], axis=1)
+    slot_grad_in = jnp.concatenate(
+        [pick(back_scaled, cot_other), pick(back_other, cot_scaled)], axis=1
+    )
     deltas = pick(deltas_zero, deltas_one)
     grad_gate = dot_first(picked, deltas[:, :units])
     grad_up = dot_first(picked, deltas[:, units:])

time: 225 us -> 224 us (level)
  waiting for transfers between devices: 88.6 us -> 69.4 us
  starting transfers between devices: 78.3 us -> 95 us
  other arithmetic: 24 us -> 29.2 us
  matrix products: 19.1 us -> 15.9 us
    all_to_all x10, waiting for transfers between devices: 69.9 us -> 50.4 us  [exchange(): return lax.all_to_all(value, axes, 0, 0, tiled=True)]
    ppermute x10 -> x12, starting transfers between devices: 25 us -> 38.4 us  [across(): return lax.ppermute(value, 'segment', pairs)]
    reduce_sum x4, other arithmetic: 2.19 us -> 5.09 us  [plane_sum(): return jnp.sum(blocks.astype(jnp.float32), axis=0).astype(jnp.bfloat16)]
    convert_element_type x0 -> x2, other arithmetic: none -> 2.68 us  [scaled(): return (scales[section] * rows.astype(jnp.float32)).astype(jnp.bfloat16)]
    dot_general x4, matrix products: 6.39 us -> 3.81 us  [dot_last(): lax.dot_general(a, b, CONTRACT_LAST, preferred_element_type=jnp.float32)]
    all_to_all x10, starting transfers between devices: 47 us -> 49.4 us  [exchange(): return lax.all_to_all(value, axes, 0, 0, tiled=True)]
  transfers between devices with their start and end apart: 26 -> 28, of which waited for: 17 -> 16; matrix products, arithmetic and copies ran while one was open for 18% -> 16% of each run, Pallas kernels for 0% -> 0%
where the time goes in v7:
time: 224 us; the launch traced here: 222 us
  starting transfers between devices  95 us (42%)
  waiting for transfers between devices  69.4 us (31%)
  other arithmetic  29.2 us (13%)
  matrix products  15.9 us (7%)
  local copies, waits for them, and re-layouts  10.1 us (5%)
  between operations  2.5 us (1%)
    all_to_all x10, waiting for transfers between devices, exchange(): return lax.all_to_all(value, axes, 0, 0, tiled=True)  50.4 us
    all_to_all x10, starting transfers between devices, exchange(): return lax.all_to_all(value, axes, 0, 0, tiled=True)  49.4 us
    ppermute x12, starting transfers between devices, across(): return lax.ppermute(value, 'segment', pairs)  38.4 us
    ppermute x6, waiting for transfers between devices, line_sum_steps(): lax.ppermute(block, LINE, pairs).astype(jnp.float32)  16.1 us
    select_n x12, other arithmetic, pick(): return jnp.where(first, a, b)  15.8 us
    ppermute x6, starting transfers between devices, line_sum_steps(): lax.ppermute(block, LINE, pairs).astype(jnp.float32)  7.27 us
    dot_general x4, matrix products, dot_f32(): return jnp.dot(a, b, preferred_element_type=jnp.float32)  6.88 us
    broadcast_in_dim x5, local copies, waits for them, and re-layouts, copies(): return jnp.broadcast_to(value[None], (count, *value.shape))  5.27 us
  transfers between devices with their start and end apart: 28, of which 16 were waited for; matrix products, arithmetic and copies ran while one was open for 16% of the time, Pallas kernels for 0%

profile of v7, /device:TPU:1, one launch (start us, length us, event | category | flops | bytes accessed | tf_op | source)
XLA Modules:
  0.0 222.1 jit_solution(2371574584238405979)
XLA Ops:
  0.7 2.3 %broadcast_select_fusion.2 = bf16[3072,256]{1,0:T(8,128)(2,1)S(1)} fusion(pred[]{:T(512)S(6)} %eq.18, bf16[6144,128]{1,0:T(8,128)(2,1)} %bitcast.82, bf16[6144,128]{1,0:T(8,128)(2,1)} %bitcast.84), kind=kLoop, calls=%fused_computation.27 | loop fusion | flops 7077888 | bytes 4718593 | tf_op jit(solution)/shard_map/jit(_where)/select_n | solution.py:90
  3.0 3.3 %collective-permute-start.1 = (bf16[3072,256]{1,0:T(8,128)(2,1)S(1)}, bf16[3072,256]{1,0:T(8,128)(2,1)}, u32[]{:S(2)}, u32[]{:S(2)}) collective-permute-start(bf16[3072,256]{1,0:T(8,128)(2,1)S(1)} %broadcast_select_fusion.2), channel_id=1, source_target_pairs={{0,128},{128,0},{1,129},{129,1},{2,130},{130,2},{3,131},{131,3},{4... | collective-permute-start | bytes 4718600 | tf_op jit(solution)/shard_map/ppermute | solution.py:63
  8.7 6.5 %all-to-all-start = ((bf16[8,48,128]{2,1,0:T(8,128)(2,1)}), bf16[8,48,128]{2,1,0:T(8,128)(2,1)S(1)}, u32[]{:S(2)}, u32[]{:S(2)}) async-start(bf16[8,48,128]{2,1,0:T(8,128)(2,1)} %broadcast_in_dim.32), calls=%async_computation | async-start | bytes 196608 | tf_op jit(solution)/shard_map/all_to_all | solution.py:17
  15.1 2.4 %broadcast_select_fusion.10 = (bf16[128,3072]{1,0:T(8,128)(2,1)}, bf16[128,3072]{1,0:T(8,128)(2,1)S(1)}) fusion(pred[]{:T(512)S(6)} %eq.18, bf16[128,6144]{1,0:T(8,128)(2,1)} %bitcast.87), kind=kLoop, calls=%fused_computation.35 | loop fusion | flops 786432 | bytes 3145729 | tf_op jit(solution)/shard_map/jit(_where)/select_n | solution.py:90
  18.3 4.3 %all-to-all-done = bf16[8,48,128]{2,1,0:T(8,128)(2,1)S(1)} async-done(((bf16[8,48,128]{2,1,0:T(8,128)(2,1)}), bf16[8,48,128]{2,1,0:T(8,128)(2,1)S(1)}, u32[]{:S(2)}, u32[]{:S(2)}) %all-to-all-start) | async-done | bytes 98336 | tf_op jit(solution)/shard_map/all_to_all | solution.py:17
  23.6 6.8 %all-to-all-start.1 = ((bf16[16,8,3072]{2,1,0:T(8,128)(2,1)}), bf16[16,8,3072]{2,1,0:T(8,128)(2,1)}, u32[]{:S(2)}, u32[]{:S(2)}) async-start(bf16[16,8,3072]{2,1,0:T(8,128)(2,1)} %broadcast_in_dim.60), calls=%async_computation.1 | async-start | bytes 1572864 | tf_op jit(solution)/shard_map/all_to_all | solution.py:17
  30.4 4.5 %broadcast_select_fusion.1 = (bf16[3072,256]{1,0:T(8,128)(2,1)S(1)}, bf16[3072,256]{1,0:T(8,128)(2,1)}) fusion(bf16[3072,256]{1,0:T(8,128)(2,1)} %collective-permute-done.1, pred[]{:T(512)S(6)} %eq.18, bf16[6144,128]{1,0:T(8,128)(2,1)} %bitcast.83, bf16[6144,128]{1,0:T(8,128)(2,1)} %bitcast.85), kind=kLoop, calls=%fused_computation.26 | loop fusion | flops 12582912 | bytes 7864321 | tf_op jit(solution)/shard_map/jit(_where)/select_n | solution.py:90
  34.9 6.1 %all-to-all-done.1 = bf16[16,8,3072]{2,1,0:T(8,128)(2,1)} async-done(((bf16[16,8,3072]{2,1,0:T(8,128)(2,1)}), bf16[16,8,3072]{2,1,0:T(8,128)(2,1)}, u32[]{:S(2)}, u32[]{:S(2)}) %all-to-all-start.1) | async-done | bytes 786464 | tf_op jit(solution)/shard_map/all_to_all | solution.py:17
  41.0 1.5 fusion.29
  42.5 4.8 %collective-permute-start.2 = (f32[128,256]{1,0:T(8,128)S(1)}, f32[128,256]{1,0:T(8,128)S(1)}, u32[]{:S(2)}, u32[]{:S(2)}) collective-permute-start(f32[128,256]{1,0:T(8,128)S(1)} %fusion.29), channel_id=1, source_target_pairs={{0,128},{128,0},{1,129},{129,1},{2,130},{130,2},{3,131},{131,3},{4... | collective-permute-start | bytes 393224 | tf_op jit(solution)/shard_map/ppermute | solution.py:63
  50.3 4.3 %all-to-all-start.2 = ((bf16[16,8,3072]{2,1,0:T(8,128)(2,1)}), bf16[16,8,3072]{2,1,0:T(8,128)(2,1)}, u32[]{:S(2)}, u32[]{:S(2)}) async-start(bf16[16,8,3072]{2,1,0:T(8,128)(2,1)} %fusion.6), calls=%async_computation.2 | async-start | bytes 1572864 | tf_op jit(solution)/shard_map/all_to_all | solution.py:17
  54.6 12.8 %all-to-all-done.2 = bf16[16,8,3072]{2,1,0:T(8,128)(2,1)} async-done(((bf16[16,8,3072]{2,1,0:T(8,128)(2,1)}), bf16[16,8,3072]{2,1,0:T(8,128)(2,1)}, u32[]{:S(2)}, u32[]{:S(2)}) %all-to-all-start.2) | async-done | bytes 786464 | tf_op jit(solution)/shard_map/all_to_all | solution.py:17
  69.1 2.5 %collective-permute-done.4 = bf16[8,3072]{1,0:T(8,128)(2,1)S(1)} collective-permute-done((bf16[8,3072]{1,0:T(8,128)(2,1)S(1)}, bf16[8,3072]{1,0:T(8,128)(2,1)S(1)}, u32[]{:S(2)}, u32[]{:S(2)}) %collective-permute-start.4) | collective-permute-done | bytes 49184 | tf_op jit(solution)/shard_map/ppermute | solution.py:53
  72.9 4.7 %all-to-all-start.3 = ((bf16[16,8,3072]{2,1,0:T(8,128)(2,1)}), bf16[16,8,3072]{2,1,0:T(8,128)(2,1)}, u32[]{:S(2)}, u32[]{:S(2)}) async-start(bf16[16,8,3072]{2,1,0:T(8,128)(2,1)} %broadcast_in_dim.61), calls=%async_computation.3 | async-start | bytes 1572864 | tf_op jit(solution)/shard_map/all_to_all | solution.py:17
  78.4 2.5 %collective-permute-start.6 = (bf16[8,3072]{1,0:T(8,128)(2,1)S(1)}, bf16[8,3072]{1,0:T(8,128)(2,1)S(1)}, u32[]{:S(2)}, u32[]{:S(2)}) collective-permute-start(bf16[8,3072]{1,0:T(8,128)(2,1)S(1)} %add_convert_fusion.4), channel_id=1, source_target_pairs={{0,4},{1,5},{2,6},{3,7},{4,0},{5,1},{6,2},{7,3},{8,12},{9,13},{10,... | collective-permute-start | bytes 147464 | tf_op jit(solution)/shard_map/ppermute | solution.py:53
  80.9 4.5 %collective-permute-done.6 = bf16[8,3072]{1,0:T(8,128)(2,1)S(1)} collective-permute-done((bf16[8,3072]{1,0:T(8,128)(2,1)S(1)}, bf16[8,3072]{1,0:T(8,128)(2,1)S(1)}, u32[]{:S(2)}, u32[]{:S(2)}) %collective-permute-start.6) | collective-permute-done | bytes 49184 | tf_op jit(solution)/shard_map/ppermute | solution.py:53
  85.4 2.8 %all-to-all-done.3 = bf16[16,8,3072]{2,1,0:T(8,128)(2,1)} async-done(((bf16[16,8,3072]{2,1,0:T(8,128)(2,1)}), bf16[16,8,3072]{2,1,0:T(8,128)(2,1)}, u32[]{:S(2)}, u32[]{:S(2)}) %all-to-all-start.3) | async-done | bytes 786464 | tf_op jit(solution)/shard_map/all_to_all | solution.py:17
  89.2 4.3 %all-to-all-start.4 = ((bf16[16,8,3072]{2,1,0:T(8,128)(2,1)}), bf16[16,8,3072]{2,1,0:T(8,128)(2,1)}, u32[]{:S(2)}, u32[]{:S(2)}) async-start(bf16[16,8,3072]{2,1,0:T(8,128)(2,1)} %broadcast_in_dim.62), calls=%async_computation.4 | async-start | bytes 1572864 | tf_op jit(solution)/shard_map/all_to_all | solution.py:17
  96.1 5.0 %collective-permute-start.7 = (f32[128,128]{1,0:T(8,128)S(1)}, f32[128,128]{1,0:T(8,128)S(1)}, u32[]{:S(2)}, u32[]{:S(2)}) collective-permute-start(f32[128,128]{1,0:T(8,128)S(1)} %fusion.13), channel_id=1, source_target_pairs={{0,128},{128,0},{1,129},{129,1},{2,130},{130,2},{3,131},{131,3},{4... | collective-permute-start | bytes 196616 | tf_op jit(solution)/shard_map/ppermute | solution.py:63
  102.0 1.9 all-to-all-done.4
  104.0 2.1 fusion.33
  106.1 6.1 %collective-permute-start.8 = (f32[128,256]{1,0:T(8,128)S(1)}, f32[128,256]{1,0:T(8,128)S(1)}, u32[]{:S(2)}, u32[]{:S(2)}) collective-permute-start(f32[128,256]{1,0:T(8,128)S(1)} %fusion.33), channel_id=1, source_target_pairs={{0,128},{128,0},{1,129},{129,1},{2,130},{130,2},{3,131},{131,3},{4... | collective-permute-start | bytes 393224 | tf_op jit(solution)/shard_map/ppermute | solution.py:63
  113.9 1.5 fusion.5
  115.4 4.3 %all-to-all-start.5 = ((bf16[16,8,3072]{2,1,0:T(8,128)(2,1)}), bf16[16,8,3072]{2,1,0:T(8,128)(2,1)}, u32[]{:S(2)}, u32[]{:S(2)}) async-start(bf16[16,8,3072]{2,1,0:T(8,128)(2,1)} %fusion.5), calls=%async_computation.5 | async-start | bytes 1572864 | tf_op jit(solution)/shard_map/all_to_all | solution.py:17
  119.7 2.0 fusion.4
  121.7 10.8 %all-to-all-done.5 = bf16[16,8,3072]{2,1,0:T(8,128)(2,1)} async-done(((bf16[16,8,3072]{2,1,0:T(8,128)(2,1)}), bf16[16,8,3072]{2,1,0:T(8,128)(2,1)}, u32[]{:S(2)}, u32[]{:S(2)}) %all-to-all-start.5) | async-done | bytes 786464 | tf_op jit(solution)/shard_map/all_to_all | solution.py:17
  132.6 1.9 reduce_sum.68
  134.9 2.7 %collective-permute-done.9 = bf16[8,3072]{1,0:T(8,128)(2,1)S(1)} collective-permute-done((bf16[8,3072]{1,0:T(8,128)(2,1)}, bf16[8,3072]{1,0:T(8,128)(2,1)S(1)}, u32[]{:S(2)}, u32[]{:S(2)}) %collective-permute-start.9) | collective-permute-done | bytes 49184 | tf_op jit(solution)/shard_map/ppermute | solution.py:53
  139.0 2.6 %collective-permute-start.10 = (bf16[8,3072]{1,0:T(8,128)(2,1)}, bf16[8,3072]{1,0:T(8,128)(2,1)}, u32[]{:S(2)}, u32[]{:S(2)}) collective-permute-start(bf16[8,3072]{1,0:T(8,128)(2,1)} %add_convert_fusion.2), channel_id=1, source_target_pairs={{0,2},{1,3},{2,0},{3,1},{4,6},{5,7},{6,4},{7,5},{8,10},{9,11},{10,... | collective-permute-start | bytes 147464 | tf_op jit(solution)/shard_map/ppermute | solution.py:53
  141.6 4.7 %all-to-all-start.6 = ((bf16[16,8,3072]{2,1,0:T(8,128)(2,1)}), bf16[16,8,3072]{2,1,0:T(8,128)(2,1)}, u32[]{:S(2)}, u32[]{:S(2)}) async-start(bf16[16,8,3072]{2,1,0:T(8,128)(2,1)} %bitcast.86), calls=%async_computation.6 | async-start | bytes 1572864 | tf_op jit(solution)/shard_map/all_to_all | solution.py:17
  148.3 6.4 %collective-permute-done.11 = bf16[8,3072]{1,0:T(8,128)(2,1)S(1)} collective-permute-done((bf16[8,3072]{1,0:T(8,128)(2,1)S(1)}, bf16[8,3072]{1,0:T(8,128)(2,1)S(1)}, u32[]{:S(2)}, u32[]{:S(2)}) %collective-permute-start.11) | collective-permute-done | bytes 49184 | tf_op jit(solution)/shard_map/ppermute | solution.py:53
  155.3 1.6 all-to-all-done.6
  156.9 1.9 reduce_sum.69
  158.8 1.8 broadcast_in_dim.63
  160.6 5.1 %all-to-all-start.7 = ((bf16[16,8,3072]{2,1,0:T(8,128)(2,1)}), bf16[16,8,3072]{2,1,0:T(8,128)(2,1)}, u32[]{:S(2)}, u32[]{:S(2)}) async-start(bf16[16,8,3072]{2,1,0:T(8,128)(2,1)} %broadcast_in_dim.63), calls=%async_computation.7 | async-start | bytes 1572864 | tf_op jit(solution)/shard_map/all_to_all | solution.py:17
  166.6 5.5 %collective-permute-start.12 = (bf16[2,24,128]{2,1,0:T(8,128)(2,1)S(1)}, bf16[2,24,128]{2,1,0:T(8,128)(2,1)S(1)}, u32[]{:S(2)}, u32[]{:S(2)}) collective-permute-start(bf16[2,24,128]{2,1,0:T(8,128)(2,1)S(1)} %bitcast.93), channel_id=1, source_target_pairs={{0,128},{128,0},{1,129},{129,1},{2,130},{130,2},{3,131},{131,3},{4... | collective-permute-start | bytes 36872 | tf_op jit(solution)/shard_map/ppermute | solution.py:63
  172.1 2.8 %collective-permute-start.14 = (bf16[128,3072]{1,0:T(8,128)(2,1)}, bf16[128,3072]{1,0:T(8,128)(2,1)}, u32[]{:S(2)}, u32[]{:S(2)}) collective-permute-start(bf16[128,3072]{1,0:T(8,128)(2,1)} %bitcast.6), channel_id=1, source_target_pairs={{128,0},{129,1},{130,2},{131,3},{132,4},{133,5},{134,6},{135,7},{1... | collective-permute-start | bytes 2359304 | tf_op jit(solution)/shard_map/ppermute | solution.py:63
  180.4 4.5 %collective-permute-start.13 = (f32[128,128]{1,0:T(8,128)S(1)}, f32[128,128]{1,0:T(8,128)S(1)}, u32[]{:S(2)}, u32[]{:S(2)}) collective-permute-start(f32[128,128]{1,0:T(8,128)S(1)} %fusion.12), channel_id=1, source_target_pairs={{0,128},{128,0},{1,129},{129,1},{2,130},{130,2},{3,131},{131,3},{4... | collective-permute-start | bytes 196616 | tf_op jit(solution)/shard_map/ppermute | solution.py:63
  186.2 2.8 %collective-permute-start.17 = (bf16[128,3072]{1,0:T(8,128)(2,1)}, bf16[128,3072]{1,0:T(8,128)(2,1)}, u32[]{:S(2)}, u32[]{:S(2)}) collective-permute-start(bf16[128,3072]{1,0:T(8,128)(2,1)} %copy-done.2), channel_id=1, source_target_pairs={{128,0},{129,1},{130,2},{131,3},{132,4},{133,5},{134,6},{135,7},{1... | collective-permute-start | bytes 2359304 | tf_op jit(solution)/shard_map/ppermute | solution.py:63
  189.8 1.5 convolution_convert_fusion.3
  191.4 5.3 %all-to-all-start.8 = ((bf16[16,8,3072]{2,1,0:T(8,128)(2,1)}), bf16[16,8,3072]{2,1,0:T(8,128)(2,1)S(1)}, u32[]{:S(2)}, u32[]{:S(2)}) async-start(bf16[16,8,3072]{2,1,0:T(8,128)(2,1)} %bitcast.19), calls=%async_computation.8 | async-start | bytes 1572864 | tf_op jit(solution)/shard_map/all_to_all | solution.py:17
  196.6 2.2 %broadcast_select_fusion.5 = (bf16[128,3072]{1,0:T(8,128)(2,1)S(1)}, bf16[128,3072]{1,0:T(8,128)(2,1)S(1)}) fusion(bf16[128,3072]{1,0:T(8,128)(2,1)} %collective-permute-done.16, pred[]{:T(512)S(6)} %eq.18, bf16[128,3072]{1,0:T(8,128)(2,1)} %collective-permute-done.14, bf16[128,3072]{1,0:T(8,128)(2,1)} %bitcast.13, bf16[16,8,3072]{2,1,0:T(8,128)(2,1)} %all-to-all-done.7, ...), kind=kLoop, calls=%fused_computation.30 | loop fusion | flops 1966080 | bytes 4719105 | tf_op jit(solution)/shard_map/jit(_where)/select_n | solution.py:90
  200.4 1.7 fusion.1
  202.1 1.8 fusion
  203.9 6.9 %all-to-all-done.8 = bf16[16,8,3072]{2,1,0:T(8,128)(2,1)S(1)} async-done(((bf16[16,8,3072]{2,1,0:T(8,128)(2,1)}), bf16[16,8,3072]{2,1,0:T(8,128)(2,1)S(1)}, u32[]{:S(2)}, u32[]{:S(2)}) %all-to-all-start.8) | async-done | bytes 786464 | tf_op jit(solution)/shard_map/all_to_all | solution.py:17
  211.6 3.4 %all-to-all-start.9 = ((bf16[16,24,128]{2,1,0:T(8,128)(2,1)}), bf16[16,24,128]{2,1,0:T(8,128)(2,1)S(1)}, u32[]{:S(2)}, u32[]{:S(2)}) async-start(bf16[16,24,128]{2,1,0:T(8,128)(2,1)} %bitcast.36), calls=%async_computation.9 | async-start | bytes 196608 | tf_op jit(solution)/shard_map/all_to_all | solution.py:17
  216.5 1.7 fusion.2
  218.3 3.1 %all-to-all-done.9 = bf16[16,24,128]{2,1,0:T(8,128)(2,1)S(1)} async-done(((bf16[16,24,128]{2,1,0:T(8,128)(2,1)}), bf16[16,24,128]{2,1,0:T(8,128)(2,1)S(1)}, u32[]{:S(2)}, u32[]{:S(2)}) %all-to-all-start.9) | async-done | bytes 98336 | tf_op jit(solution)/shard_map/all_to_all | solution.py:17
  (108 shorter events, 32.9 us)
Async XLA Ops:
  0.6 6.3 %copy-start.16 = (f32[1,1,128]{2,1,0:T(1,128)S(1)}, f32[1,1,128]{2,1,0:T(1,128)}, u32[]{:S(2)}) copy-start(f32[1,1,128]{2,1,0:T(1,128)} %param.16) | copy-start | bytes 1540
  0.6 6.4 %copy-start.17 = (s32[1,1,128]{2,1,0:T(1,128)S(1)}, s32[1,1,128]{2,1,0:T(1,128)}, u32[]{:S(2)}) copy-start(s32[1,1,128]{2,1,0:T(1,128)} %param.14) | copy-start | bytes 1540
  0.7 7.2 %copy-start.12 = (bf16[1,1,6144]{2,1,0:T(2,128)(2,1)S(1)}, bf16[1,1,6144]{2,1,0:T(2,128)(2,1)}, u32[]{:S(2)}) copy-start(bf16[1,1,6144]{2,1,0:T(2,128)(2,1)} %param.9) | copy-start | bytes 36868
  0.7 7.3 %copy-start.13 = (bf16[1,1,6144]{2,1,0:T(2,128)(2,1)S(1)}, bf16[1,1,6144]{2,1,0:T(2,128)(2,1)}, u32[]{:S(2)}) copy-start(bf16[1,1,6144]{2,1,0:T(2,128)(2,1)} %param.10) | copy-start | bytes 36868
  3.0 27.4 %collective-permute-start.1 = (bf16[3072,256]{1,0:T(8,128)(2,1)S(1)}, bf16[3072,256]{1,0:T(8,128)(2,1)}, u32[]{:S(2)}, u32[]{:S(2)}) collective-permute-start(bf16[3072,256]{1,0:T(8,128)(2,1)S(1)} %broadcast_select_fusion.2), channel_id=1, source_target_pairs={{0,128},{128,0},{1,129},{129,1},{2,130},{130,2},{3,131},{131,3},{4... | collective-permute-start | bytes 4718600 | tf_op jit(solution)/shard_map/ppermute | solution.py:63
  7.8 10.5 %collective-permute-start = (f32[2,128]{1,0:T(2,128)S(1)}, f32[2,128]{1,0:T(2,128)S(1)}, u32[]{:S(2)}, u32[]{:S(2)}) collective-permute-start(f32[2,128]{1,0:T(2,128)S(1)} %stack.10), channel_id=1, source_target_pairs={{0,128},{128,0},{1,129},{129,1},{2,130},{130,2},{3,131},{131,3},{4... | collective-permute-start | bytes 3080 | tf_op jit(solution)/shard_map/ppermute | solution.py:63
  8.7 13.9 %all-to-all-start = ((bf16[8,48,128]{2,1,0:T(8,128)(2,1)}), bf16[8,48,128]{2,1,0:T(8,128)(2,1)S(1)}, u32[]{:S(2)}, u32[]{:S(2)}) async-start(bf16[8,48,128]{2,1,0:T(8,128)(2,1)} %broadcast_in_dim.32), calls=%async_computation | async-start | bytes 196608 | tf_op jit(solution)/shard_map/all_to_all | solution.py:17
  17.5 30.9 %collective-permute-start.3 = (bf16[128,3072]{1,0:T(8,128)(2,1)}, bf16[128,3072]{1,0:T(8,128)(2,1)S(1)}, u32[]{:S(2)}, u32[]{:S(2)}) collective-permute-start(bf16[128,3072]{1,0:T(8,128)(2,1)} %get-tuple-element.43), channel_id=1, source_target_pairs={{0,128},{128,0},{1,129},{129,1},{2,130},{130,2},{3,131},{131,3},{4... | collective-permute-start | bytes 2359304 | tf_op jit(solution)/shard_map/ppermute | solution.py:63
  23.6 17.4 %all-to-all-start.1 = ((bf16[16,8,3072]{2,1,0:T(8,128)(2,1)}), bf16[16,8,3072]{2,1,0:T(8,128)(2,1)}, u32[]{:S(2)}, u32[]{:S(2)}) async-start(bf16[16,8,3072]{2,1,0:T(8,128)(2,1)} %broadcast_in_dim.60), calls=%async_computation.1 | async-start | bytes 1572864 | tf_op jit(solution)/shard_map/all_to_all | solution.py:17
  42.5 5.8 %collective-permute-start.2 = (f32[128,256]{1,0:T(8,128)S(1)}, f32[128,256]{1,0:T(8,128)S(1)}, u32[]{:S(2)}, u32[]{:S(2)}) collective-permute-start(f32[128,256]{1,0:T(8,128)S(1)} %fusion.29), channel_id=1, source_target_pairs={{0,128},{128,0},{1,129},{129,1},{2,130},{130,2},{3,131},{131,3},{4... | collective-permute-start | bytes 393224 | tf_op jit(solution)/shard_map/ppermute | solution.py:63
  47.3 130.8 %copy-start.14 = (f32[128]{0:T(128)}, f32[128]{0:T(128)S(1)}, u32[]{:S(2)}) copy-start(f32[128]{0:T(128)S(1)} %get-tuple-element.63) | copy-start | bytes 1540
  48.4 0.6 copy-start.3
  50.3 17.1 %all-to-all-start.2 = ((bf16[16,8,3072]{2,1,0:T(8,128)(2,1)}), bf16[16,8,3072]{2,1,0:T(8,128)(2,1)}, u32[]{:S(2)}, u32[]{:S(2)}) async-start(bf16[16,8,3072]{2,1,0:T(8,128)(2,1)} %fusion.6), calls=%async_computation.2 | async-start | bytes 1572864 | tf_op jit(solution)/shard_map/all_to_all | solution.py:17
  68.6 3.0 %collective-permute-start.4 = (bf16[8,3072]{1,0:T(8,128)(2,1)S(1)}, bf16[8,3072]{1,0:T(8,128)(2,1)S(1)}, u32[]{:S(2)}, u32[]{:S(2)}) collective-permute-start(bf16[8,3072]{1,0:T(8,128)(2,1)S(1)} %reduce_sum.67), channel_id=1, source_target_pairs={{0,1},{1,0},{2,3},{3,2},{4,5},{5,4},{6,7},{7,6},{8,9},{9,8},{10,11... | collective-permute-start | bytes 147464 | tf_op jit(solution)/shard_map/ppermute | solution.py:53
  71.7 5.9 %collective-permute-start.5 = (bf16[8,3072]{1,0:T(8,128)(2,1)S(1)}, bf16[8,3072]{1,0:T(8,128)(2,1)}, u32[]{:S(2)}, u32[]{:S(2)}) collective-permute-start(bf16[8,3072]{1,0:T(8,128)(2,1)S(1)} %add_convert_fusion.5), channel_id=1, source_target_pairs={{0,2},{1,3},{2,0},{3,1},{4,6},{5,7},{6,4},{7,5},{8,10},{9,11},{10,... | collective-permute-start | bytes 147464 | tf_op jit(solution)/shard_map/ppermute | solution.py:53
  72.9 15.4 %all-to-all-start.3 = ((bf16[16,8,3072]{2,1,0:T(8,128)(2,1)}), bf16[16,8,3072]{2,1,0:T(8,128)(2,1)}, u32[]{:S(2)}, u32[]{:S(2)}) async-start(bf16[16,8,3072]{2,1,0:T(8,128)(2,1)} %broadcast_in_dim.61), calls=%async_computation.3 | async-start | bytes 1572864 | tf_op jit(solution)/shard_map/all_to_all | solution.py:17
  78.4 7.0 %collective-permute-start.6 = (bf16[8,3072]{1,0:T(8,128)(2,1)S(1)}, bf16[8,3072]{1,0:T(8,128)(2,1)S(1)}, u32[]{:S(2)}, u32[]{:S(2)}) collective-permute-start(bf16[8,3072]{1,0:T(8,128)(2,1)S(1)} %add_convert_fusion.4), channel_id=1, source_target_pairs={{0,4},{1,5},{2,6},{3,7},{4,0},{5,1},{6,2},{7,3},{8,12},{9,13},{10,... | collective-permute-start | bytes 147464 | tf_op jit(solution)/shard_map/ppermute | solution.py:53
  85.4 9.4 %copy-start.7 = (bf16[8,3072]{1,0:T(8,128)(2,1)}, bf16[8,3072]{1,0:T(8,128)(2,1)S(1)}, u32[]{:S(2)}) copy-start(bf16[8,3072]{1,0:T(8,128)(2,1)S(1)} %add_convert_fusion.3) | copy-start | bytes 147460
  89.2 14.8 %all-to-all-start.4 = ((bf16[16,8,3072]{2,1,0:T(8,128)(2,1)}), bf16[16,8,3072]{2,1,0:T(8,128)(2,1)}, u32[]{:S(2)}, u32[]{:S(2)}) async-start(bf16[16,8,3072]{2,1,0:T(8,128)(2,1)} %broadcast_in_dim.62), calls=%async_computation.4 | async-start | bytes 1572864 | tf_op jit(solution)/shard_map/all_to_all | solution.py:17
  94.9 0.9 copy-start.1
  96.1 5.9 %collective-permute-start.7 = (f32[128,128]{1,0:T(8,128)S(1)}, f32[128,128]{1,0:T(8,128)S(1)}, u32[]{:S(2)}, u32[]{:S(2)}) collective-permute-start(f32[128,128]{1,0:T(8,128)S(1)} %fusion.13), channel_id=1, source_target_pairs={{0,128},{128,0},{1,129},{129,1},{2,130},{130,2},{3,131},{131,3},{4... | collective-permute-start | bytes 196616 | tf_op jit(solution)/shard_map/ppermute | solution.py:63
  104.0 9.9 %copy-start = (bf16[3072,256]{1,0:T(8,128)(2,1)S(1)}, bf16[3072,256]{1,0:T(8,128)(2,1)}, u32[]{:S(2)}) copy-start(bf16[3072,256]{1,0:T(8,128)(2,1)} %get-tuple-element.42) | copy-start | bytes 4718596
  106.1 7.1 %collective-permute-start.8 = (f32[128,256]{1,0:T(8,128)S(1)}, f32[128,256]{1,0:T(8,128)S(1)}, u32[]{:S(2)}, u32[]{:S(2)}) collective-permute-start(f32[128,256]{1,0:T(8,128)S(1)} %fusion.33), channel_id=1, source_target_pairs={{0,128},{128,0},{1,129},{129,1},{2,130},{130,2},{3,131},{131,3},{4... | collective-permute-start | bytes 393224 | tf_op jit(solution)/shard_map/ppermute | solution.py:63
  115.4 17.1 %all-to-all-start.5 = ((bf16[16,8,3072]{2,1,0:T(8,128)(2,1)}), bf16[16,8,3072]{2,1,0:T(8,128)(2,1)}, u32[]{:S(2)}, u32[]{:S(2)}) async-start(bf16[16,8,3072]{2,1,0:T(8,128)(2,1)} %fusion.5), calls=%async_computation.5 | async-start | bytes 1572864 | tf_op jit(solution)/shard_map/all_to_all | solution.py:17
  134.5 3.2 %collective-permute-start.9 = (bf16[8,3072]{1,0:T(8,128)(2,1)}, bf16[8,3072]{1,0:T(8,128)(2,1)S(1)}, u32[]{:S(2)}, u32[]{:S(2)}) collective-permute-start(bf16[8,3072]{1,0:T(8,128)(2,1)} %reduce_sum.68), channel_id=1, source_target_pairs={{0,1},{1,0},{2,3},{3,2},{4,5},{5,4},{6,7},{7,6},{8,9},{9,8},{10,11... | collective-permute-start | bytes 147464 | tf_op jit(solution)/shard_map/ppermute | solution.py:53
  139.0 7.3 %collective-permute-start.10 = (bf16[8,3072]{1,0:T(8,128)(2,1)}, bf16[8,3072]{1,0:T(8,128)(2,1)}, u32[]{:S(2)}, u32[]{:S(2)}) collective-permute-start(bf16[8,3072]{1,0:T(8,128)(2,1)} %add_convert_fusion.2), channel_id=1, source_target_pairs={{0,2},{1,3},{2,0},{3,1},{4,6},{5,7},{6,4},{7,5},{8,10},{9,11},{10,... | collective-permute-start | bytes 147464 | tf_op jit(solution)/shard_map/ppermute | solution.py:53
  141.6 15.3 %all-to-all-start.6 = ((bf16[16,8,3072]{2,1,0:T(8,128)(2,1)}), bf16[16,8,3072]{2,1,0:T(8,128)(2,1)}, u32[]{:S(2)}, u32[]{:S(2)}) async-start(bf16[16,8,3072]{2,1,0:T(8,128)(2,1)} %bitcast.86), calls=%async_computation.6 | async-start | bytes 1572864 | tf_op jit(solution)/shard_map/all_to_all | solution.py:17
  147.2 7.5 %collective-permute-start.11 = (bf16[8,3072]{1,0:T(8,128)(2,1)S(1)}, bf16[8,3072]{1,0:T(8,128)(2,1)S(1)}, u32[]{:S(2)}, u32[]{:S(2)}) collective-permute-start(bf16[8,3072]{1,0:T(8,128)(2,1)S(1)} %add_convert_fusion.1), channel_id=1, source_target_pairs={{0,4},{1,5},{2,6},{3,7},{4,0},{5,1},{6,2},{7,3},{8,12},{9,13},{10,... | collective-permute-start | bytes 147464 | tf_op jit(solution)/shard_map/ppermute | solution.py:53
  160.6 17.6 %all-to-all-start.7 = ((bf16[16,8,3072]{2,1,0:T(8,128)(2,1)}), bf16[16,8,3072]{2,1,0:T(8,128)(2,1)}, u32[]{:S(2)}, u32[]{:S(2)}) async-start(bf16[16,8,3072]{2,1,0:T(8,128)(2,1)} %broadcast_in_dim.63), calls=%async_computation.7 | async-start | bytes 1572864 | tf_op jit(solution)/shard_map/all_to_all | solution.py:17
  166.6 10.9 %collective-permute-start.12 = (bf16[2,24,128]{2,1,0:T(8,128)(2,1)S(1)}, bf16[2,24,128]{2,1,0:T(8,128)(2,1)S(1)}, u32[]{:S(2)}, u32[]{:S(2)}) collective-permute-start(bf16[2,24,128]{2,1,0:T(8,128)(2,1)S(1)} %bitcast.93), channel_id=1, source_target_pairs={{0,128},{128,0},{1,129},{129,1},{2,130},{130,2},{3,131},{131,3},{4... | collective-permute-start | bytes 36872 | tf_op jit(solution)/shard_map/ppermute | solution.py:63
  172.1 19.2 %collective-permute-start.14 = (bf16[128,3072]{1,0:T(8,128)(2,1)}, bf16[128,3072]{1,0:T(8,128)(2,1)}, u32[]{:S(2)}, u32[]{:S(2)}) collective-permute-start(bf16[128,3072]{1,0:T(8,128)(2,1)} %bitcast.6), channel_id=1, source_target_pairs={{128,0},{129,1},{130,2},{131,3},{132,4},{133,5},{134,6},{135,7},{1... | collective-permute-start | bytes 2359304 | tf_op jit(solution)/shard_map/ppermute | solution.py:63
  174.9 16.4 %collective-permute-start.15 = (bf16[128,3072]{1,0:T(8,128)(2,1)}, bf16[128,3072]{1,0:T(8,128)(2,1)}, u32[]{:S(2)}, u32[]{:S(2)}) collective-permute-start(bf16[128,3072]{1,0:T(8,128)(2,1)} %bitcast.13), channel_id=1, source_target_pairs={{0,128},{1,129},{2,130},{3,131},{4,132},{5,133},{6,134},{7,135},{8... | collective-permute-start | bytes 2359304 | tf_op jit(solution)/shard_map/ppermute | solution.py:63
  176.2 15.1 %collective-permute-start.16 = (bf16[128,3072]{1,0:T(8,128)(2,1)}, bf16[128,3072]{1,0:T(8,128)(2,1)}, u32[]{:S(2)}, u32[]{:S(2)}) collective-permute-start(bf16[128,3072]{1,0:T(8,128)(2,1)} %copy-done.1), channel_id=1, source_target_pairs={{0,128},{1,129},{2,130},{3,131},{4,132},{5,133},{6,134},{7,135},{8... | collective-permute-start | bytes 2359304 | tf_op jit(solution)/shard_map/ppermute | solution.py:63
  179.5 0.9 copy-start.2
  179.5 5.4 %copy-start.11 = (bf16[2,24,128]{2,1,0:T(8,128)(2,1)S(1)}, bf16[2,24,128]{2,1,0:T(8,128)(2,1)}, u32[]{:S(2)}) copy-start(bf16[2,24,128]{2,1,0:T(8,128)(2,1)} %get-tuple-element.58) | copy-start | bytes 36868
  180.4 8.6 %copy-start.6 = (f32[128,128]{1,0:T(8,128)}, f32[128,128]{1,0:T(8,128)S(1)}, u32[]{:S(2)}) copy-start(f32[128,128]{1,0:T(8,128)S(1)} %fusion.12) | copy-start | bytes 196612
  180.4 8.6 %collective-permute-start.13 = (f32[128,128]{1,0:T(8,128)S(1)}, f32[128,128]{1,0:T(8,128)S(1)}, u32[]{:S(2)}, u32[]{:S(2)}) collective-permute-start(f32[128,128]{1,0:T(8,128)S(1)} %fusion.12), channel_id=1, source_target_pairs={{0,128},{128,0},{1,129},{129,1},{2,130},{130,2},{3,131},{131,3},{4... | collective-permute-start | bytes 196616 | tf_op jit(solution)/shard_map/ppermute | solution.py:63
  186.2 28.8 %collective-permute-start.17 = (bf16[128,3072]{1,0:T(8,128)(2,1)}, bf16[128,3072]{1,0:T(8,128)(2,1)}, u32[]{:S(2)}, u32[]{:S(2)}) collective-permute-start(bf16[128,3072]{1,0:T(8,128)(2,1)} %copy-done.2), channel_id=1, source_target_pairs={{128,0},{129,1},{130,2},{131,3},{132,4},{133,5},{134,6},{135,7},{1... | collective-permute-start | bytes 2359304 | tf_op jit(solution)/shard_map/ppermute | solution.py:63
  189.8 6.8 %copy-start.15 = (f32[128]{0:T(128)S(1)}, f32[128]{0:T(128)}, u32[]{:S(2)}) copy-start(f32[128]{0:T(128)} %copy-done.14) | copy-start | bytes 1540
  191.4 19.4 %all-to-all-start.8 = ((bf16[16,8,3072]{2,1,0:T(8,128)(2,1)}), bf16[16,8,3072]{2,1,0:T(8,128)(2,1)S(1)}, u32[]{:S(2)}, u32[]{:S(2)}) async-start(bf16[16,8,3072]{2,1,0:T(8,128)(2,1)} %bitcast.19), calls=%async_computation.8 | async-start | bytes 1572864 | tf_op jit(solution)/shard_map/all_to_all | solution.py:17
  202.1 8.8 %copy-start.8 = (bf16[8,3072]{1,0:T(8,128)(2,1)S(1)}, bf16[8,3072]{1,0:T(8,128)(2,1)}, u32[]{:S(2)}) copy-start(bf16[8,3072]{1,0:T(8,128)(2,1)} %reduce_sum.69) | copy-start | bytes 147460
  210.9 5.6 %copy-start.4 = (bf16[128,128]{1,0:T(8,128)(2,1)S(1)}, bf16[128,128]{1,0:T(8,128)(2,1)}, u32[]{:S(2)}) copy-start(bf16[128,128]{1,0:T(8,128)(2,1)} %copy-done.3) | copy-start | bytes 98308
  210.9 5.6 %copy-start.5 = (bf16[128,128]{1,0:T(8,128)(2,1)S(1)}, bf16[128,128]{1,0:T(8,128)(2,1)}, u32[]{:S(2)}) copy-start(bf16[128,128]{1,0:T(8,128)(2,1)} %get-tuple-element.48) | copy-start | bytes 98308
  211.6 9.8 %all-to-all-start.9 = ((bf16[16,24,128]{2,1,0:T(8,128)(2,1)}), bf16[16,24,128]{2,1,0:T(8,128)(2,1)S(1)}, u32[]{:S(2)}, u32[]{:S(2)}) async-start(bf16[16,24,128]{2,1,0:T(8,128)(2,1)} %bitcast.36), calls=%async_computation.9 | async-start | bytes 196608 | tf_op jit(solution)/shard_map/all_to_all | solution.py:17
  216.5 4.9 %copy-start.9 = (bf16[1,1,1,6144]{3,2,1,0:T(2,128)(2,1)S(1)}, bf16[1,1,1,6144]{3,2,1,0:T(2,128)(2,1)}, u32[]{:S(2)}) copy-start(bf16[1,1,1,6144]{3,2,1,0:T(2,128)(2,1)} %unstack.15) | copy-start | bytes 36868
  216.5 4.9 %copy-start.10 = (bf16[1,1,1,6144]{3,2,1,0:T(2,128)(2,1)S(1)}, bf16[1,1,1,6144]{3,2,1,0:T(2,128)(2,1)}, u32[]{:S(2)}) copy-start(bf16[1,1,1,6144]{3,2,1,0:T(2,128)(2,1)} %unstack.13) | copy-start | bytes 36868

commit v8 on v7

--- a/solution.py
+++ b/solution.py
@@ -41,6 +41,11 @@
     plane = parts.shape[0] // line
     blocks = exchange(parts.reshape(plane, line, parts.shape[1]), PLANE)
     return jnp.sum(blocks.astype(jnp.float32), axis=0).astype(jnp.bfloat16)
+
+
+def line_sum(block):
+    blocks = exchange(copies(block, lax.axis_size(LINE)), LINE)
+    return jnp.sum(blocks.reshape(-1, *block.shape).astype(jnp.float32), axis=0)
 
 
 def line_sum_steps(block):
@@ -129,7 +134,7 @@
         return (scales[section] * dot_f32(hidden, downs[section])).astype(jnp.bfloat16)
 
     def hidden_delta(rows, section):
-        return total_of(dot_last(rows, downs[section]))
+        return scales[section] * total_of(dot_last(rows, downs[section]))
 
     def deltas_of(delta, slopes):
         return (jnp.concatenate([delta, delta], axis=1) * slopes).astype(jnp.bfloat16)
@@ -155,30 +160,28 @@
     mid_rows = plane_spread(mid_block, plane)
 
     cot_scaled = scaled(cot_rows, 1)
-    delta_one = hidden_delta(cot_scaled, 1)
+    delta_one = hidden_delta(cot_rows, 1)
     mid_rows, delta_one = lax.optimization_barrier((mid_rows, delta_one))
     hidden_one, slopes_one = forward(mid_rows, 1)
     deltas_one = deltas_of(delta_one, slopes_one)
     partial = plane_sum(slot_gradient(deltas_one, 1), line)
     outcome_one = outcome(hidden_one, 1)
-    partial, outcome_one = lax.optimization_barrier((partial, outcome_one))
-    out_partial = plane_sum(outcome_one, line)
-    back_block = add_bf16(cot_block, line_sum_steps(partial))
-    back_block, out_partial, in_late, mid_late, cot_late, mid_block = lax.optimization_barrier(
-        (back_block, out_partial, in_rows, mid_rows, cot_scaled, mid_block)
+    back_block = add_bf16(cot_block, line_sum(partial))
+    back_block, in_late, mid_late, cot_late, mid_block = lax.optimization_barrier(
+        (back_block, in_rows, mid_rows, cot_scaled, mid_block)
     )
     back_rows = plane_spread(back_block, plane)
     in_other, mid_other = across(in_late, [(1, 0)]), across(mid_late, [(0, 1)])
     cot_other = across(cot_late, [(0, 1)])
 
+    deltas_zero = deltas_of(hidden_delta(back_rows, 0), slopes_zero)
+    grad_zero, in_other, mid_other, cot_other, back_rows = lax.optimization_barrier(
+        (slot_gradient(deltas_zero, 0), in_other, mid_other, cot_other, back_rows)
+    )
     back_scaled = scaled(back_rows, 0)
-    deltas_zero = deltas_of(hidden_delta(back_scaled, 0), slopes_zero)
     back_other = across(back_scaled, [(1, 0)])
-    grad_zero, in_other, mid_other, cot_other = lax.optimization_barrier(
-        (slot_gradient(deltas_zero, 0), in_other, mid_other, cot_other)
-    )
-    partial = plane_sum(grad_zero, line)
-    ends = jnp.concatenate([partial, out_partial], axis=0).reshape(-1, parts, LANES)
+    ends = plane_sum(jnp.concatenate([grad_zero, outcome_one], axis=1), line)
+    ends = ends.reshape(line, 2, parts, LANES).swapaxes(0, 1).reshape(-1, parts, LANES)
     ends = exchange(ends, ("segment", LINE)).reshape(2, line, parts, LANES)
     ends = jnp.sum(ends.astype(jnp.float32), axis=1).reshape(2 * parts, LANES)
 

time: 224 us -> 225 us (level)
  waiting for transfers between devices: 69.4 us -> 79.1 us
  other arithmetic: 29.2 us -> 23.5 us
    all_to_all x10, waiting for transfers between devices: 50.4 us -> 68.3 us  [exchange(): return lax.all_to_all(value, axes, 0, 0, tiled=True)]
    ppermute x6 -> x3, waiting for transfers between devices: 16.1 us -> 7.05 us  [line_sum_steps(): lax.ppermute(block, LINE, pairs).astype(jnp.float32)]
    all_to_all x10, starting transfers between devices: 49.4 us -> 54.1 us  [exchange(): return lax.all_to_all(value, axes, 0, 0, tiled=True)]
    ppermute x6 -> x3, starting transfers between devices: 7.27 us -> 3.18 us  [line_sum_steps(): lax.ppermute(block, LINE, pairs).astype(jnp.float32)]
    convert_element_type x4 -> x2, other arithmetic: 3.1 us -> 0.03 us  [line_sum_steps(): block = total.astype(jnp.bfloat16)]
    reduce_sum x4 -> x3, other arithmetic: 5.09 us -> 2.71 us  [plane_sum(): return jnp.sum(blocks.astype(jnp.float32), axis=0).astype(jnp.bfloat16)]
    broadcast_in_dim x5 -> x6, local copies, waits for them, and re-layouts: 5.27 us -> 5.25 us  [copies(): return jnp.broadcast_to(value[None], (count, *value.shape))]
  transfers between devices with their start and end apart: 28 -> 25, of which waited for: 16 -> 15; matrix products, arithmetic and copies ran while one was open for 16% -> 13% of each run, Pallas kernels for 0% -> 0%
where the time goes in v8:
time: 225 us; the launch traced here: 223 us
  starting transfers between devices  94.1 us (42%)
  waiting for transfers between devices  79.1 us (35%)
  other arithmetic  23.5 us (10%)
  matrix products  15.7 us (7%)
  local copies, waits for them, and re-layouts  8.18 us (4%)
  between operations  2.51 us (1%)
    all_to_all x10, waiting for transfers between devices, exchange(): return lax.all_to_all(value, axes, 0, 0, tiled=True)  68.3 us
    all_to_all x10, starting transfers between devices, exchange(): return lax.all_to_all(value, axes, 0, 0, tiled=True)  54.1 us
    ppermute x12, starting transfers between devices, across(): return lax.ppermute(value, 'segment', pairs)  36.7 us
    select_n x12, other arithmetic, pick(): return jnp.where(first, a, b)  15.1 us
    ppermute x3, waiting for transfers between devices, line_sum_steps(): lax.ppermute(block, LINE, pairs).astype(jnp.float32)  7.05 us
    dot_general x4, matrix products, dot_f32(): return jnp.dot(a, b, preferred_element_type=jnp.float32)  6.13 us
    dot_general x3, matrix products, dot_first(): lax.dot_general(a, b, CONTRACT_FIRST, preferred_element_type=jnp.float32)  5.26 us
    broadcast_in_dim x6, local copies, waits for them, and re-layouts, copies(): return jnp.broadcast_to(value[None], (count, *value.shape))  5.25 us
  transfers between devices with their start and end apart: 25, of which 15 were waited for; matrix products, arithmetic and copies ran while one was open for 13% of the time, Pallas kernels for 0%

profile of v8, /device:TPU:1, one launch (start us, length us, event | category | flops | bytes accessed | tf_op | source)
XLA Modules:
  0.0 223.0 jit_solution(515120192437197708)
XLA Ops:
  0.7 2.3 %broadcast_select_fusion.2 = bf16[3072,256]{1,0:T(8,128)(2,1)S(1)} fusion(pred[]{:T(512)S(6)} %eq.18, bf16[6144,128]{1,0:T(8,128)(2,1)} %bitcast.87, bf16[6144,128]{1,0:T(8,128)(2,1)} %bitcast.89), kind=kLoop, calls=%fused_computation.27 | loop fusion | flops 7077888 | bytes 4718593 | tf_op jit(solution)/shard_map/jit(_where)/select_n | solution.py:95
  3.0 3.3 %collective-permute-start.1 = (bf16[3072,256]{1,0:T(8,128)(2,1)S(1)}, bf16[3072,256]{1,0:T(8,128)(2,1)}, u32[]{:S(2)}, u32[]{:S(2)}) collective-permute-start(bf16[3072,256]{1,0:T(8,128)(2,1)S(1)} %broadcast_select_fusion.2), channel_id=1, source_target_pairs={{0,128},{128,0},{1,129},{129,1},{2,130},{130,2},{3,131},{131,3},{4... | collective-permute-start | bytes 4718600 | tf_op jit(solution)/shard_map/ppermute | solution.py:68
  8.7 6.5 %all-to-all-start = ((bf16[8,48,128]{2,1,0:T(8,128)(2,1)}), bf16[8,48,128]{2,1,0:T(8,128)(2,1)S(1)}, u32[]{:S(2)}, u32[]{:S(2)}) async-start(bf16[8,48,128]{2,1,0:T(8,128)(2,1)} %broadcast_in_dim.34), calls=%async_computation | async-start | bytes 196608 | tf_op jit(solution)/shard_map/all_to_all | solution.py:17
  15.1 2.4 %broadcast_select_fusion.10 = (bf16[128,3072]{1,0:T(8,128)(2,1)}, bf16[128,3072]{1,0:T(8,128)(2,1)S(1)}) fusion(pred[]{:T(512)S(6)} %eq.18, bf16[128,6144]{1,0:T(8,128)(2,1)} %bitcast.91), kind=kLoop, calls=%fused_computation.36 | loop fusion | flops 786432 | bytes 3145729 | tf_op jit(solution)/shard_map/jit(_where)/select_n | solution.py:95
  18.3 4.3 %all-to-all-done = bf16[8,48,128]{2,1,0:T(8,128)(2,1)S(1)} async-done(((bf16[8,48,128]{2,1,0:T(8,128)(2,1)}), bf16[8,48,128]{2,1,0:T(8,128)(2,1)S(1)}, u32[]{:S(2)}, u32[]{:S(2)}) %all-to-all-start) | async-done | bytes 98336 | tf_op jit(solution)/shard_map/all_to_all | solution.py:17
  23.6 6.8 %all-to-all-start.1 = ((bf16[16,8,3072]{2,1,0:T(8,128)(2,1)}), bf16[16,8,3072]{2,1,0:T(8,128)(2,1)}, u32[]{:S(2)}, u32[]{:S(2)}) async-start(bf16[16,8,3072]{2,1,0:T(8,128)(2,1)} %broadcast_in_dim.66), calls=%async_computation.1 | async-start | bytes 1572864 | tf_op jit(solution)/shard_map/all_to_all | solution.py:17
  30.4 4.5 %broadcast_select_fusion.1 = (bf16[3072,256]{1,0:T(8,128)(2,1)S(1)}, bf16[3072,256]{1,0:T(8,128)(2,1)}) fusion(bf16[3072,256]{1,0:T(8,128)(2,1)} %collective-permute-done.1, pred[]{:T(512)S(6)} %eq.18, bf16[6144,128]{1,0:T(8,128)(2,1)} %bitcast.88, bf16[6144,128]{1,0:T(8,128)(2,1)} %bitcast.90), kind=kLoop, calls=%fused_computation.26 | loop fusion | flops 12582912 | bytes 7864321 | tf_op jit(solution)/shard_map/jit(_where)/select_n | solution.py:95
  34.9 6.0 %all-to-all-done.1 = bf16[16,8,3072]{2,1,0:T(8,128)(2,1)} async-done(((bf16[16,8,3072]{2,1,0:T(8,128)(2,1)}), bf16[16,8,3072]{2,1,0:T(8,128)(2,1)}, u32[]{:S(2)}, u32[]{:S(2)}) %all-to-all-start.1) | async-done | bytes 786464 | tf_op jit(solution)/shard_map/all_to_all | solution.py:17
  41.0 1.5 fusion.29
  42.5 4.8 %collective-permute-start.2 = (f32[128,256]{1,0:T(8,128)S(1)}, f32[128,256]{1,0:T(8,128)S(1)}, u32[]{:S(2)}, u32[]{:S(2)}) collective-permute-start(f32[128,256]{1,0:T(8,128)S(1)} %fusion.29), channel_id=1, source_target_pairs={{0,128},{128,0},{1,129},{129,1},{2,130},{130,2},{3,131},{131,3},{4... | collective-permute-start | bytes 393224 | tf_op jit(solution)/shard_map/ppermute | solution.py:68
  50.9 4.3 %all-to-all-start.2 = ((bf16[16,8,3072]{2,1,0:T(8,128)(2,1)}), bf16[16,8,3072]{2,1,0:T(8,128)(2,1)}, u32[]{:S(2)}, u32[]{:S(2)}) async-start(bf16[16,8,3072]{2,1,0:T(8,128)(2,1)} %fusion.6), calls=%async_computation.2 | async-start | bytes 1572864 | tf_op jit(solution)/shard_map/all_to_all | solution.py:17
  55.3 12.8 %all-to-all-done.2 = bf16[16,8,3072]{2,1,0:T(8,128)(2,1)} async-done(((bf16[16,8,3072]{2,1,0:T(8,128)(2,1)}), bf16[16,8,3072]{2,1,0:T(8,128)(2,1)}, u32[]{:S(2)}, u32[]{:S(2)}) %all-to-all-start.2) | async-done | bytes 786464 | tf_op jit(solution)/shard_map/all_to_all | solution.py:17
  68.1 1.2 reduce_sum.64
  69.8 2.5 %collective-permute-done.4 = bf16[8,3072]{1,0:T(8,128)(2,1)S(1)} collective-permute-done((bf16[8,3072]{1,0:T(8,128)(2,1)S(1)}, bf16[8,3072]{1,0:T(8,128)(2,1)S(1)}, u32[]{:S(2)}, u32[]{:S(2)}) %collective-permute-start.4) | collective-permute-done | bytes 49184 | tf_op jit(solution)/shard_map/ppermute | solution.py:58
  73.5 4.7 %all-to-all-start.3 = ((bf16[16,8,3072]{2,1,0:T(8,128)(2,1)}), bf16[16,8,3072]{2,1,0:T(8,128)(2,1)S(1)}, u32[]{:S(2)}, u32[]{:S(2)}) async-start(bf16[16,8,3072]{2,1,0:T(8,128)(2,1)} %broadcast_in_dim.67), calls=%async_computation.3 | async-start | bytes 1572864 | tf_op jit(solution)/shard_map/all_to_all | solution.py:17
  78.3 2.5 %collective-permute-start.6 = (bf16[8,3072]{1,0:T(8,128)(2,1)S(1)}, bf16[8,3072]{1,0:T(8,128)(2,1)S(1)}, u32[]{:S(2)}, u32[]{:S(2)}) collective-permute-start(bf16[8,3072]{1,0:T(8,128)(2,1)S(1)} %add_convert_fusion.2), channel_id=1, source_target_pairs={{0,4},{1,5},{2,6},{3,7},{4,0},{5,1},{6,2},{7,3},{8,12},{9,13},{10,... | collective-permute-start | bytes 147464 | tf_op jit(solution)/shard_map/ppermute | solution.py:58
  80.7 4.5 %collective-permute-done.6 = bf16[8,3072]{1,0:T(8,128)(2,1)S(1)} collective-permute-done((bf16[8,3072]{1,0:T(8,128)(2,1)S(1)}, bf16[8,3072]{1,0:T(8,128)(2,1)S(1)}, u32[]{:S(2)}, u32[]{:S(2)}) %collective-permute-start.6) | collective-permute-done | bytes 49184 | tf_op jit(solution)/shard_map/ppermute | solution.py:58
  85.3 3.7 %all-to-all-done.3 = bf16[16,8,3072]{2,1,0:T(8,128)(2,1)S(1)} async-done(((bf16[16,8,3072]{2,1,0:T(8,128)(2,1)}), bf16[16,8,3072]{2,1,0:T(8,128)(2,1)S(1)}, u32[]{:S(2)}, u32[]{:S(2)}) %all-to-all-start.3) | async-done | bytes 786464 | tf_op jit(solution)/shard_map/all_to_all | solution.py:17
  89.9 4.3 %all-to-all-start.4 = ((bf16[16,8,3072]{2,1,0:T(8,128)(2,1)}), bf16[16,8,3072]{2,1,0:T(8,128)(2,1)}, u32[]{:S(2)}, u32[]{:S(2)}) async-start(bf16[16,8,3072]{2,1,0:T(8,128)(2,1)} %broadcast_in_dim.68), calls=%async_computation.4 | async-start | bytes 1572864 | tf_op jit(solution)/shard_map/all_to_all | solution.py:17
  94.6 5.7 %collective-permute-start.7 = (f32[128,128]{1,0:T(8,128)S(1)}, f32[128,128]{1,0:T(8,128)S(1)}, u32[]{:S(2)}, u32[]{:S(2)}) collective-permute-start(f32[128,128]{1,0:T(8,128)S(1)} %fusion.12), channel_id=1, source_target_pairs={{0,128},{128,0},{1,129},{129,1},{2,130},{130,2},{3,131},{131,3},{4... | collective-permute-start | bytes 196616 | tf_op jit(solution)/shard_map/ppermute | solution.py:68
  101.4 3.3 %all-to-all-done.4 = bf16[16,8,3072]{2,1,0:T(8,128)(2,1)} async-done(((bf16[16,8,3072]{2,1,0:T(8,128)(2,1)}), bf16[16,8,3072]{2,1,0:T(8,128)(2,1)}, u32[]{:S(2)}, u32[]{:S(2)}) %all-to-all-start.4) | async-done | bytes 786464 | tf_op jit(solution)/shard_map/all_to_all | solution.py:17
  104.7 2.1 fusion.33
  106.8 5.7 %collective-permute-start.8 = (f32[128,256]{1,0:T(8,128)S(1)}, f32[128,256]{1,0:T(8,128)S(1)}, u32[]{:S(2)}, u32[]{:S(2)}) collective-permute-start(f32[128,256]{1,0:T(8,128)S(1)} %fusion.33), channel_id=1, source_target_pairs={{0,128},{128,0},{1,129},{129,1},{2,130},{130,2},{3,131},{131,3},{4... | collective-permute-start | bytes 393224 | tf_op jit(solution)/shard_map/ppermute | solution.py:68
  114.9 1.5 fusion.5
  116.4 4.3 %all-to-all-start.5 = ((bf16[16,8,3072]{2,1,0:T(8,128)(2,1)}), bf16[16,8,3072]{2,1,0:T(8,128)(2,1)}, u32[]{:S(2)}, u32[]{:S(2)}) async-start(bf16[16,8,3072]{2,1,0:T(8,128)(2,1)} %fusion.5), calls=%async_computation.5 | async-start | bytes 1572864 | tf_op jit(solution)/shard_map/all_to_all | solution.py:17
  120.7 12.8 %all-to-all-done.5 = bf16[16,8,3072]{2,1,0:T(8,128)(2,1)} async-done(((bf16[16,8,3072]{2,1,0:T(8,128)(2,1)}), bf16[16,8,3072]{2,1,0:T(8,128)(2,1)}, u32[]{:S(2)}, u32[]{:S(2)}) %all-to-all-start.5) | async-done | bytes 786464 | tf_op jit(solution)/shard_map/all_to_all | solution.py:17
  133.5 1.2 reduce_sum.65
  135.5 3.7 %all-to-all-start.6 = ((bf16[8,8,3072]{2,1,0:T(8,128)(2,1)}), bf16[8,8,3072]{2,1,0:T(8,128)(2,1)S(1)}, u32[]{:S(2)}, u32[]{:S(2)}) async-start(bf16[8,8,3072]{2,1,0:T(8,128)(2,1)} %broadcast_in_dim.69), calls=%async_computation.6 | async-start | bytes 786432 | tf_op jit(solution)/shard_map/all_to_all | solution.py:17
  140.3 9.4 %all-to-all-done.6 = bf16[8,8,3072]{2,1,0:T(8,128)(2,1)S(1)} async-done(((bf16[8,8,3072]{2,1,0:T(8,128)(2,1)}), bf16[8,8,3072]{2,1,0:T(8,128)(2,1)S(1)}, u32[]{:S(2)}, u32[]{:S(2)}) %all-to-all-start.6) | async-done | bytes 393248 | tf_op jit(solution)/shard_map/all_to_all | solution.py:17
  151.5 6.8 %all-to-all-start.7 = ((bf16[16,8,3072]{2,1,0:T(8,128)(2,1)}), bf16[16,8,3072]{2,1,0:T(8,128)(2,1)}, u32[]{:S(2)}, u32[]{:S(2)}) async-start(bf16[16,8,3072]{2,1,0:T(8,128)(2,1)} %broadcast_in_dim.70), calls=%async_computation.7 | async-start | bytes 1572864 | tf_op jit(solution)/shard_map/all_to_all | solution.py:17
  159.3 3.4 %collective-permute-start.9 = (bf16[2,24,128]{2,1,0:T(8,128)(2,1)S(1)}, bf16[2,24,128]{2,1,0:T(8,128)(2,1)S(1)}, u32[]{:S(2)}, u32[]{:S(2)}) collective-permute-start(bf16[2,24,128]{2,1,0:T(8,128)(2,1)S(1)} %bitcast.98), channel_id=1, source_target_pairs={{0,128},{128,0},{1,129},{129,1},{2,130},{130,2},{3,131},{131,3},{4... | collective-permute-start | bytes 36872 | tf_op jit(solution)/shard_map/ppermute | solution.py:68
  162.7 1.2 fusion.4
  163.9 4.1 %collective-permute-start.11 = (bf16[128,3072]{1,0:T(8,128)(2,1)}, bf16[128,3072]{1,0:T(8,128)(2,1)}, u32[]{:S(2)}, u32[]{:S(2)}) collective-permute-start(bf16[128,3072]{1,0:T(8,128)(2,1)} %bitcast.6), channel_id=1, source_target_pairs={{128,0},{129,1},{130,2},{131,3},{132,4},{133,5},{134,6},{135,7},{1... | collective-permute-start | bytes 2359304 | tf_op jit(solution)/shard_map/ppermute | solution.py:68
  168.0 1.3 collective-permute-start.12
  169.3 1.3 collective-permute-start.13
  170.6 1.8 fusion.11
  172.4 2.9 %collective-permute-start.10 = (f32[128,128]{1,0:T(8,128)S(1)}, f32[128,128]{1,0:T(8,128)S(1)}, u32[]{:S(2)}, u32[]{:S(2)}) collective-permute-start(f32[128,128]{1,0:T(8,128)S(1)} %fusion.11), channel_id=1, source_target_pairs={{0,128},{128,0},{1,129},{129,1},{2,130},{130,2},{3,131},{131,3},{4... | collective-permute-start | bytes 196616 | tf_op jit(solution)/shard_map/ppermute | solution.py:68
  177.7 1.3 maximum_bitcast_fusion
  178.9 6.8 %all-to-all-start.8 = ((bf16[16,8,6144]{2,1,0:T(8,128)(2,1)}), bf16[16,8,6144]{2,1,0:T(8,128)(2,1)S(1)}, u32[]{:S(2)}, u32[]{:S(2)}) async-start(bf16[16,8,6144]{2,1,0:T(8,128)(2,1)} %maximum_bitcast_fusion), calls=%async_computation.8 | async-start | bytes 3145728 | tf_op jit(solution)/shard_map/all_to_all | solution.py:17
  185.8 2.9 %broadcast_select_fusion.5 = (bf16[128,3072]{1,0:T(8,128)(2,1)}, bf16[128,3072]{1,0:T(8,128)(2,1)}) fusion(bf16[128,3072]{1,0:T(8,128)(2,1)} %collective-permute-done.13, pred[]{:T(512)S(6)} %eq.18, bf16[128,3072]{1,0:T(8,128)(2,1)} %bitcast.17, f32[128]{0:T(128)S(1)} %copy-done.22), kind=kLoop, calls=%fused_computation.31 | loop fusion | flops 1572864 | bytes 3146241 | tf_op jit(solution)/shard_map/jit(_where)/select_n | solution.py:95
  188.7 3.4 %collective-permute-start.14 = (bf16[128,3072]{1,0:T(8,128)(2,1)}, bf16[128,3072]{1,0:T(8,128)(2,1)}, u32[]{:S(2)}, u32[]{:S(2)}) collective-permute-start(bf16[128,3072]{1,0:T(8,128)(2,1)} %get-tuple-element.38), channel_id=1, source_target_pairs={{128,0},{129,1},{130,2},{131,3},{132,4},{133,5},{134,6},{135,7},{1... | collective-permute-start | bytes 2359304 | tf_op jit(solution)/shard_map/ppermute | solution.py:68
  192.1 1.8 broadcast_select_fusion.6
  193.9 1.7 fusion.1
  195.6 1.8 fusion
  197.4 10.7 %all-to-all-done.8 = bf16[16,8,6144]{2,1,0:T(8,128)(2,1)S(1)} async-done(((bf16[16,8,6144]{2,1,0:T(8,128)(2,1)}), bf16[16,8,6144]{2,1,0:T(8,128)(2,1)S(1)}, u32[]{:S(2)}, u32[]{:S(2)}) %all-to-all-start.8) | async-done | bytes 1572896 | tf_op jit(solution)/shard_map/all_to_all | solution.py:17
  209.0 6.0 %all-to-all-start.9 = ((bf16[16,24,128]{2,1,0:T(8,128)(2,1)}), bf16[16,24,128]{2,1,0:T(8,128)(2,1)S(1)}, u32[]{:S(2)}, u32[]{:S(2)}) async-start(bf16[16,24,128]{2,1,0:T(8,128)(2,1)} %bitcast.20), calls=%async_computation.9 | async-start | bytes 196608 | tf_op jit(solution)/shard_map/all_to_all | solution.py:17
  215.4 1.8 fusion.2
  217.2 5.2 %all-to-all-done.9 = bf16[16,24,128]{2,1,0:T(8,128)(2,1)S(1)} async-done(((bf16[16,24,128]{2,1,0:T(8,128)(2,1)}), bf16[16,24,128]{2,1,0:T(8,128)(2,1)S(1)}, u32[]{:S(2)}, u32[]{:S(2)}) %all-to-all-start.9) | async-done | bytes 98336 | tf_op jit(solution)/shard_map/all_to_all | solution.py:17
  (114 shorter events, 21.7 us)
Async XLA Ops:
  0.6 6.3 %copy-start.23 = (f32[1,1,128]{2,1,0:T(1,128)S(1)}, f32[1,1,128]{2,1,0:T(1,128)}, u32[]{:S(2)}) copy-start(f32[1,1,128]{2,1,0:T(1,128)} %param.16) | copy-start | bytes 1540
  0.6 6.4 %copy-start.24 = (s32[1,1,128]{2,1,0:T(1,128)S(1)}, s32[1,1,128]{2,1,0:T(1,128)}, u32[]{:S(2)}) copy-start(s32[1,1,128]{2,1,0:T(1,128)} %param.14) | copy-start | bytes 1540
  0.7 7.2 %copy-start.17 = (bf16[1,1,6144]{2,1,0:T(2,128)(2,1)S(1)}, bf16[1,1,6144]{2,1,0:T(2,128)(2,1)}, u32[]{:S(2)}) copy-start(bf16[1,1,6144]{2,1,0:T(2,128)(2,1)} %param.9) | copy-start | bytes 36868
  0.7 7.3 %copy-start.18 = (bf16[1,1,6144]{2,1,0:T(2,128)(2,1)S(1)}, bf16[1,1,6144]{2,1,0:T(2,128)(2,1)}, u32[]{:S(2)}) copy-start(bf16[1,1,6144]{2,1,0:T(2,128)(2,1)} %param.10) | copy-start | bytes 36868
  3.0 27.4 %collective-permute-start.1 = (bf16[3072,256]{1,0:T(8,128)(2,1)S(1)}, bf16[3072,256]{1,0:T(8,128)(2,1)}, u32[]{:S(2)}, u32[]{:S(2)}) collective-permute-start(bf16[3072,256]{1,0:T(8,128)(2,1)S(1)} %broadcast_select_fusion.2), channel_id=1, source_target_pairs={{0,128},{128,0},{1,129},{129,1},{2,130},{130,2},{3,131},{131,3},{4... | collective-permute-start | bytes 4718600 | tf_op jit(solution)/shard_map/ppermute | solution.py:68
  7.8 10.5 %collective-permute-start = (f32[2,128]{1,0:T(2,128)S(1)}, f32[2,128]{1,0:T(2,128)S(1)}, u32[]{:S(2)}, u32[]{:S(2)}) collective-permute-start(f32[2,128]{1,0:T(2,128)S(1)} %stack.10), channel_id=1, source_target_pairs={{0,128},{128,0},{1,129},{129,1},{2,130},{130,2},{3,131},{131,3},{4... | collective-permute-start | bytes 3080 | tf_op jit(solution)/shard_map/ppermute | solution.py:68
  8.7 13.9 %all-to-all-start = ((bf16[8,48,128]{2,1,0:T(8,128)(2,1)}), bf16[8,48,128]{2,1,0:T(8,128)(2,1)S(1)}, u32[]{:S(2)}, u32[]{:S(2)}) async-start(bf16[8,48,128]{2,1,0:T(8,128)(2,1)} %broadcast_in_dim.34), calls=%async_computation | async-start | bytes 196608 | tf_op jit(solution)/shard_map/all_to_all | solution.py:17
  17.5 31.6 %collective-permute-start.3 = (bf16[128,3072]{1,0:T(8,128)(2,1)}, bf16[128,3072]{1,0:T(8,128)(2,1)S(1)}, u32[]{:S(2)}, u32[]{:S(2)}) collective-permute-start(bf16[128,3072]{1,0:T(8,128)(2,1)} %get-tuple-element.41), channel_id=1, source_target_pairs={{0,128},{128,0},{1,129},{129,1},{2,130},{130,2},{3,131},{131,3},{4... | collective-permute-start | bytes 2359304 | tf_op jit(solution)/shard_map/ppermute | solution.py:68
  22.6 32.6 %copy-start.12 = (bf16[1,8,24,128]{3,2,1,0:T(8,128)(2,1)}, bf16[1,8,24,128]{3,2,1,0:T(8,128)(2,1)S(1)}, u32[]{:S(2)}) copy-start(bf16[1,8,24,128]{3,2,1,0:T(8,128)(2,1)S(1)} %get-tuple-element.49) | copy-start | bytes 147460
  23.6 17.4 %all-to-all-start.1 = ((bf16[16,8,3072]{2,1,0:T(8,128)(2,1)}), bf16[16,8,3072]{2,1,0:T(8,128)(2,1)}, u32[]{:S(2)}, u32[]{:S(2)}) async-start(bf16[16,8,3072]{2,1,0:T(8,128)(2,1)} %broadcast_in_dim.66), calls=%async_computation.1 | async-start | bytes 1572864 | tf_op jit(solution)/shard_map/all_to_all | solution.py:17
  42.5 5.8 %collective-permute-start.2 = (f32[128,256]{1,0:T(8,128)S(1)}, f32[128,256]{1,0:T(8,128)S(1)}, u32[]{:S(2)}, u32[]{:S(2)}) collective-permute-start(f32[128,256]{1,0:T(8,128)S(1)} %fusion.29), channel_id=1, source_target_pairs={{0,128},{128,0},{1,129},{129,1},{2,130},{130,2},{3,131},{131,3},{4... | collective-permute-start | bytes 393224 | tf_op jit(solution)/shard_map/ppermute | solution.py:68
  47.3 1.8 copy-start.21
  49.1 1.9 copy-start.1
  50.9 17.1 %all-to-all-start.2 = ((bf16[16,8,3072]{2,1,0:T(8,128)(2,1)}), bf16[16,8,3072]{2,1,0:T(8,128)(2,1)}, u32[]{:S(2)}, u32[]{:S(2)}) async-start(bf16[16,8,3072]{2,1,0:T(8,128)(2,1)} %fusion.6), calls=%async_computation.2 | async-start | bytes 1572864 | tf_op jit(solution)/shard_map/all_to_all | solution.py:17
  69.3 3.0 %collective-permute-start.4 = (bf16[8,3072]{1,0:T(8,128)(2,1)S(1)}, bf16[8,3072]{1,0:T(8,128)(2,1)S(1)}, u32[]{:S(2)}, u32[]{:S(2)}) collective-permute-start(bf16[8,3072]{1,0:T(8,128)(2,1)S(1)} %reduce_sum.64), channel_id=1, source_target_pairs={{0,1},{1,0},{2,3},{3,2},{4,5},{5,4},{6,7},{7,6},{8,9},{9,8},{10,11... | collective-permute-start | bytes 147464 | tf_op jit(solution)/shard_map/ppermute | solution.py:58
  72.4 5.9 %collective-permute-start.5 = (bf16[8,3072]{1,0:T(8,128)(2,1)S(1)}, bf16[8,3072]{1,0:T(8,128)(2,1)S(1)}, u32[]{:S(2)}, u32[]{:S(2)}) collective-permute-start(bf16[8,3072]{1,0:T(8,128)(2,1)S(1)} %add_convert_fusion.3), channel_id=1, source_target_pairs={{0,2},{1,3},{2,0},{3,1},{4,6},{5,7},{6,4},{7,5},{8,10},{9,11},{10,... | collective-permute-start | bytes 147464 | tf_op jit(solution)/shard_map/ppermute | solution.py:58
  73.5 15.4 %all-to-all-start.3 = ((bf16[16,8,3072]{2,1,0:T(8,128)(2,1)}), bf16[16,8,3072]{2,1,0:T(8,128)(2,1)S(1)}, u32[]{:S(2)}, u32[]{:S(2)}) async-start(bf16[16,8,3072]{2,1,0:T(8,128)(2,1)} %broadcast_in_dim.67), calls=%async_computation.3 | async-start | bytes 1572864 | tf_op jit(solution)/shard_map/all_to_all | solution.py:17
  78.3 7.0 %collective-permute-start.6 = (bf16[8,3072]{1,0:T(8,128)(2,1)S(1)}, bf16[8,3072]{1,0:T(8,128)(2,1)S(1)}, u32[]{:S(2)}, u32[]{:S(2)}) collective-permute-start(bf16[8,3072]{1,0:T(8,128)(2,1)S(1)} %add_convert_fusion.2), channel_id=1, source_target_pairs={{0,4},{1,5},{2,6},{3,7},{4,0},{5,1},{6,2},{7,3},{8,12},{9,13},{10,... | collective-permute-start | bytes 147464 | tf_op jit(solution)/shard_map/ppermute | solution.py:58
  85.3 9.4 %copy-start.16 = (bf16[8,3072]{1,0:T(8,128)(2,1)}, bf16[8,3072]{1,0:T(8,128)(2,1)S(1)}, u32[]{:S(2)}) copy-start(bf16[8,3072]{1,0:T(8,128)(2,1)S(1)} %add_convert_fusion.1) | copy-start | bytes 147460
  89.9 14.8 %all-to-all-start.4 = ((bf16[16,8,3072]{2,1,0:T(8,128)(2,1)}), bf16[16,8,3072]{2,1,0:T(8,128)(2,1)}, u32[]{:S(2)}, u32[]{:S(2)}) async-start(bf16[16,8,3072]{2,1,0:T(8,128)(2,1)} %broadcast_in_dim.68), calls=%async_computation.4 | async-start | bytes 1572864 | tf_op jit(solution)/shard_map/all_to_all | solution.py:17
  94.6 6.6 %collective-permute-start.7 = (f32[128,128]{1,0:T(8,128)S(1)}, f32[128,128]{1,0:T(8,128)S(1)}, u32[]{:S(2)}, u32[]{:S(2)}) collective-permute-start(f32[128,128]{1,0:T(8,128)S(1)} %fusion.12), channel_id=1, source_target_pairs={{0,128},{128,0},{1,129},{129,1},{2,130},{130,2},{3,131},{131,3},{4... | collective-permute-start | bytes 196616 | tf_op jit(solution)/shard_map/ppermute | solution.py:68
  100.4 62.3 %copy-start.19 = (f32[128]{0:T(128)}, f32[128]{0:T(128)S(1)}, u32[]{:S(2)}) copy-start(f32[128]{0:T(128)S(1)} %get-tuple-element.60) | copy-start | bytes 1540
  101.4 12.8 %copy-start.4 = (f32[128,128]{1,0:T(8,128)}, f32[128,128]{1,0:T(8,128)S(1)}, u32[]{:S(2)}) copy-start(f32[128,128]{1,0:T(8,128)S(1)} %add_multiply_fusion.3) | copy-start | bytes 196612
  104.7 10.2 %copy-start = (bf16[3072,256]{1,0:T(8,128)(2,1)S(1)}, bf16[3072,256]{1,0:T(8,128)(2,1)}, u32[]{:S(2)}) copy-start(bf16[3072,256]{1,0:T(8,128)(2,1)} %get-tuple-element.40) | copy-start | bytes 4718596
  106.8 6.6 %collective-permute-start.8 = (f32[128,256]{1,0:T(8,128)S(1)}, f32[128,256]{1,0:T(8,128)S(1)}, u32[]{:S(2)}, u32[]{:S(2)}) collective-permute-start(f32[128,256]{1,0:T(8,128)S(1)} %fusion.33), channel_id=1, source_target_pairs={{0,128},{128,0},{1,129},{129,1},{2,130},{130,2},{3,131},{131,3},{4... | collective-permute-start | bytes 393224 | tf_op jit(solution)/shard_map/ppermute | solution.py:68
  114.2 0.7 copy-start.10
  116.4 17.1 %all-to-all-start.5 = ((bf16[16,8,3072]{2,1,0:T(8,128)(2,1)}), bf16[16,8,3072]{2,1,0:T(8,128)(2,1)}, u32[]{:S(2)}, u32[]{:S(2)}) async-start(bf16[16,8,3072]{2,1,0:T(8,128)(2,1)} %fusion.5), calls=%async_computation.5 | async-start | bytes 1572864 | tf_op jit(solution)/shard_map/all_to_all | solution.py:17
  135.5 14.2 %all-to-all-start.6 = ((bf16[8,8,3072]{2,1,0:T(8,128)(2,1)}), bf16[8,8,3072]{2,1,0:T(8,128)(2,1)S(1)}, u32[]{:S(2)}, u32[]{:S(2)}) async-start(bf16[8,8,3072]{2,1,0:T(8,128)(2,1)} %broadcast_in_dim.69), calls=%async_computation.6 | async-start | bytes 786432 | tf_op jit(solution)/shard_map/all_to_all | solution.py:17
  149.8 12.9 %copy-start.15 = (bf16[128,128]{1,0:T(8,128)(2,1)S(1)}, bf16[128,128]{1,0:T(8,128)(2,1)}, u32[]{:S(2)}) copy-start(bf16[128,128]{1,0:T(8,128)(2,1)} %get-tuple-element.46) | copy-start | bytes 98308
  151.5 19.1 %all-to-all-start.7 = ((bf16[16,8,3072]{2,1,0:T(8,128)(2,1)}), bf16[16,8,3072]{2,1,0:T(8,128)(2,1)}, u32[]{:S(2)}, u32[]{:S(2)}) async-start(bf16[16,8,3072]{2,1,0:T(8,128)(2,1)} %broadcast_in_dim.70), calls=%async_computation.7 | async-start | bytes 1572864 | tf_op jit(solution)/shard_map/all_to_all | solution.py:17
  159.3 11.3 %collective-permute-start.9 = (bf16[2,24,128]{2,1,0:T(8,128)(2,1)S(1)}, bf16[2,24,128]{2,1,0:T(8,128)(2,1)S(1)}, u32[]{:S(2)}, u32[]{:S(2)}) collective-permute-start(bf16[2,24,128]{2,1,0:T(8,128)(2,1)S(1)} %bitcast.98), channel_id=1, source_target_pairs={{0,128},{128,0},{1,129},{129,1},{2,130},{130,2},{3,131},{131,3},{4... | collective-permute-start | bytes 36872 | tf_op jit(solution)/shard_map/ppermute | solution.py:68
  163.9 13.0 %copy-start.6 = (f32[128,128]{1,0:T(8,128)S(1)}, f32[128,128]{1,0:T(8,128)}, u32[]{:S(2)}) copy-start(f32[128,128]{1,0:T(8,128)} %get-tuple-element.43) | copy-start | bytes 196612
  163.9 13.0 %copy-start.7 = (f32[128,128]{1,0:T(8,128)S(1)}, f32[128,128]{1,0:T(8,128)}, u32[]{:S(2)}) copy-start(f32[128,128]{1,0:T(8,128)} %get-tuple-element.45) | copy-start | bytes 196612
  163.9 13.7 %collective-permute-start.11 = (bf16[128,3072]{1,0:T(8,128)(2,1)}, bf16[128,3072]{1,0:T(8,128)(2,1)}, u32[]{:S(2)}, u32[]{:S(2)}) collective-permute-start(bf16[128,3072]{1,0:T(8,128)(2,1)} %bitcast.6), channel_id=1, source_target_pairs={{128,0},{129,1},{130,2},{131,3},{132,4},{133,5},{134,6},{135,7},{1... | collective-permute-start | bytes 2359304 | tf_op jit(solution)/shard_map/ppermute | solution.py:68
  168.0 9.6 %collective-permute-start.12 = (bf16[128,3072]{1,0:T(8,128)(2,1)}, bf16[128,3072]{1,0:T(8,128)(2,1)}, u32[]{:S(2)}, u32[]{:S(2)}) collective-permute-start(bf16[128,3072]{1,0:T(8,128)(2,1)} %bitcast.13), channel_id=1, source_target_pairs={{0,128},{1,129},{2,130},{3,131},{4,132},{5,133},{6,134},{7,135},{8... | collective-permute-start | bytes 2359304 | tf_op jit(solution)/shard_map/ppermute | solution.py:68
  169.3 8.4 %collective-permute-start.13 = (bf16[128,3072]{1,0:T(8,128)(2,1)}, bf16[128,3072]{1,0:T(8,128)(2,1)}, u32[]{:S(2)}, u32[]{:S(2)}) collective-permute-start(bf16[128,3072]{1,0:T(8,128)(2,1)} %multiply_convert_fusion.1), channel_id=1, source_target_pairs={{0,128},{1,129},{2,130},{3,131},{4,132},{5,133},{6,134},{7,135},{8... | collective-permute-start | bytes 2359304 | tf_op jit(solution)/shard_map/ppermute | solution.py:68
  172.4 5.3 %copy-start.2 = (bf16[128,3072]{1,0:T(8,128)(2,1)S(1)}, bf16[128,3072]{1,0:T(8,128)(2,1)}, u32[]{:S(2)}) copy-start(bf16[128,3072]{1,0:T(8,128)(2,1)} %fusion.4) | copy-start | bytes 2359300
  172.4 3.8 %collective-permute-start.10 = (f32[128,128]{1,0:T(8,128)S(1)}, f32[128,128]{1,0:T(8,128)S(1)}, u32[]{:S(2)}, u32[]{:S(2)}) collective-permute-start(f32[128,128]{1,0:T(8,128)S(1)} %fusion.11), channel_id=1, source_target_pairs={{0,128},{128,0},{1,129},{129,1},{2,130},{130,2},{3,131},{131,3},{4... | collective-permute-start | bytes 196616 | tf_op jit(solution)/shard_map/ppermute | solution.py:68
  178.9 6.8 %copy-start.22 = (f32[128]{0:T(128)S(1)}, f32[128]{0:T(128)}, u32[]{:S(2)}) copy-start(f32[128]{0:T(128)} %copy-done.21) | copy-start | bytes 1540
  178.9 29.2 %all-to-all-start.8 = ((bf16[16,8,6144]{2,1,0:T(8,128)(2,1)}), bf16[16,8,6144]{2,1,0:T(8,128)(2,1)S(1)}, u32[]{:S(2)}, u32[]{:S(2)}) async-start(bf16[16,8,6144]{2,1,0:T(8,128)(2,1)} %maximum_bitcast_fusion), calls=%async_computation.8 | async-start | bytes 3145728 | tf_op jit(solution)/shard_map/all_to_all | solution.py:17
  188.7 5.1 %copy-start.5 = (f32[128,128]{1,0:T(8,128)S(1)}, f32[128,128]{1,0:T(8,128)}, u32[]{:S(2)}) copy-start(f32[128,128]{1,0:T(8,128)} %copy-done.4) | copy-start | bytes 196612
  188.7 5.2 %copy-start.9 = (f32[128,128]{1,0:T(8,128)S(1)}, f32[128,128]{1,0:T(8,128)}, u32[]{:S(2)}) copy-start(f32[128,128]{1,0:T(8,128)} %copy-done.8) | copy-start | bytes 196612
  188.7 5.2 %copy-start.11 = (f32[128,128]{1,0:T(8,128)S(1)}, f32[128,128]{1,0:T(8,128)}, u32[]{:S(2)}) copy-start(f32[128,128]{1,0:T(8,128)} %copy-done.10) | copy-start | bytes 196612
  188.7 26.3 %collective-permute-start.14 = (bf16[128,3072]{1,0:T(8,128)(2,1)}, bf16[128,3072]{1,0:T(8,128)(2,1)}, u32[]{:S(2)}, u32[]{:S(2)}) collective-permute-start(bf16[128,3072]{1,0:T(8,128)(2,1)} %get-tuple-element.38), channel_id=1, source_target_pairs={{128,0},{129,1},{130,2},{131,3},{132,4},{133,5},{134,6},{135,7},{1... | collective-permute-start | bytes 2359304 | tf_op jit(solution)/shard_map/ppermute | solution.py:68
  197.4 17.6 %copy-start.20 = (f32[128]{0:T(128)S(1)}, f32[128]{0:T(128)}, u32[]{:S(2)}) copy-start(f32[128]{0:T(128)} %copy-done.19) | copy-start | bytes 1540
  208.3 7.1 %copy-start.3 = (bf16[128,3072]{1,0:T(8,128)(2,1)S(1)}, bf16[128,3072]{1,0:T(8,128)(2,1)}, u32[]{:S(2)}) copy-start(bf16[128,3072]{1,0:T(8,128)(2,1)} %get-tuple-element.37) | copy-start | bytes 2359300
  208.3 7.1 %copy-start.14 = (bf16[128,128]{1,0:T(8,128)(2,1)S(1)}, bf16[128,128]{1,0:T(8,128)(2,1)}, u32[]{:S(2)}) copy-start(bf16[128,128]{1,0:T(8,128)(2,1)} %copy-done.13) | copy-start | bytes 98308
  209.0 13.3 %all-to-all-start.9 = ((bf16[16,24,128]{2,1,0:T(8,128)(2,1)}), bf16[16,24,128]{2,1,0:T(8,128)(2,1)S(1)}, u32[]{:S(2)}, u32[]{:S(2)}) async-start(bf16[16,24,128]{2,1,0:T(8,128)(2,1)} %bitcast.20), calls=%async_computation.9 | async-start | bytes 196608 | tf_op jit(solution)/shard_map/all_to_all | solution.py:17
  (2 other events, 1.2 us)

commit v9 on v7

--- a/solution.py
+++ b/solution.py
@@ -129,7 +129,7 @@
         return (scales[section] * dot_f32(hidden, downs[section])).astype(jnp.bfloat16)
 
     def hidden_delta(rows, section):
-        return total_of(dot_last(rows, downs[section]))
+        return scales[section] * total_of(dot_last(rows, downs[section]))
 
     def deltas_of(delta, slopes):
         return (jnp.concatenate([delta, delta], axis=1) * slopes).astype(jnp.bfloat16)
@@ -155,7 +155,7 @@
     mid_rows = plane_spread(mid_block, plane)
 
     cot_scaled = scaled(cot_rows, 1)
-    delta_one = hidden_delta(cot_scaled, 1)
+    delta_one = hidden_delta(cot_rows, 1)
     mid_rows, delta_one = lax.optimization_barrier((mid_rows, delta_one))
     hidden_one, slopes_one = forward(mid_rows, 1)
     deltas_one = deltas_of(delta_one, slopes_one)
@@ -171,12 +171,12 @@
     in_other, mid_other = across(in_late, [(1, 0)]), across(mid_late, [(0, 1)])
     cot_other = across(cot_late, [(0, 1)])
 
+    deltas_zero = deltas_of(hidden_delta(back_rows, 0), slopes_zero)
+    grad_zero, in_other, mid_other, cot_other, back_rows = lax.optimization_barrier(
+        (slot_gradient(deltas_zero, 0), in_other, mid_other, cot_other, back_rows)
+    )
     back_scaled = scaled(back_rows, 0)
-    deltas_zero = deltas_of(hidden_delta(back_scaled, 0), slopes_zero)
     back_other = across(back_scaled, [(1, 0)])
-    grad_zero, in_other, mid_other, cot_other = lax.optimization_barrier(
-        (slot_gradient(deltas_zero, 0), in_other, mid_other, cot_other)
-    )
     partial = plane_sum(grad_zero, line)
     ends = jnp.concatenate([partial, out_partial], axis=0).reshape(-1, parts, LANES)
     ends = exchange(ends, ("segment", LINE)).reshape(2, line, parts, LANES)

time: 224 us -> 221 us (0.987)
  waiting for transfers between devices: 69.4 us -> 66.8 us
  other arithmetic: 29.2 us -> 26.8 us
    ppermute x6, waiting for transfers between devices: 16.1 us -> 12.6 us  [line_sum_steps(): lax.ppermute(block, LINE, pairs).astype(jnp.float32)]
where the time goes in v9:
time: 221 us; the launch traced here: 219 us
  starting transfers between devices  96.9 us (44%)
  waiting for transfers between devices  66.8 us (30%)
  other arithmetic  26.8 us (12%)
  matrix products  17.4 us (8%)
  local copies, waits for them, and re-layouts  8.72 us (4%)
  between operations  2.48 us (1%)
    all_to_all x10, starting transfers between devices, exchange(): return lax.all_to_all(value, axes, 0, 0, tiled=True)  51.5 us
    all_to_all x10, waiting for transfers between devices, exchange(): return lax.all_to_all(value, axes, 0, 0, tiled=True)  51.3 us
    ppermute x12, starting transfers between devices, across(): return lax.ppermute(value, 'segment', pairs)  36.4 us
    select_n x12, other arithmetic, pick(): return jnp.where(first, a, b)  15.7 us
    ppermute x6, waiting for transfers between devices, line_sum_steps(): lax.ppermute(block, LINE, pairs).astype(jnp.float32)  12.6 us
    ppermute x6, starting transfers between devices, line_sum_steps(): lax.ppermute(block, LINE, pairs).astype(jnp.float32)  9.02 us
    dot_general x4, matrix products, dot_f32(): return jnp.dot(a, b, preferred_element_type=jnp.float32)  6.9 us
    broadcast_in_dim x5, local copies, waits for them, and re-layouts, copies(): return jnp.broadcast_to(value[None], (count, *value.shape))  5.28 us
  transfers between devices with their start and end apart: 28, of which 16 were waited for; matrix products, arithmetic and copies ran while one was open for 16% of the time, Pallas kernels for 0%

profile of v9, /device:TPU:1, one launch (start us, length us, event | category | flops | bytes accessed | tf_op | source)
XLA Modules:
  0.0 219.1 jit_solution(1294293370555247216)
XLA Ops:
  0.7 2.3 %broadcast_select_fusion.2 = bf16[3072,256]{1,0:T(8,128)(2,1)S(1)} fusion(pred[]{:T(512)S(6)} %eq.18, bf16[6144,128]{1,0:T(8,128)(2,1)} %bitcast.82, bf16[6144,128]{1,0:T(8,128)(2,1)} %bitcast.84), kind=kLoop, calls=%fused_computation.26 | loop fusion | flops 7077888 | bytes 4718593 | tf_op jit(solution)/shard_map/jit(_where)/select_n | solution.py:90
  3.0 3.3 %collective-permute-start.1 = (bf16[3072,256]{1,0:T(8,128)(2,1)S(1)}, bf16[3072,256]{1,0:T(8,128)(2,1)}, u32[]{:S(2)}, u32[]{:S(2)}) collective-permute-start(bf16[3072,256]{1,0:T(8,128)(2,1)S(1)} %broadcast_select_fusion.2), channel_id=1, source_target_pairs={{0,128},{128,0},{1,129},{129,1},{2,130},{130,2},{3,131},{131,3},{4... | collective-permute-start | bytes 4718600 | tf_op jit(solution)/shard_map/ppermute | solution.py:63
  7.1 6.5 %all-to-all-start = ((bf16[8,48,128]{2,1,0:T(8,128)(2,1)}), bf16[8,48,128]{2,1,0:T(8,128)(2,1)S(1)}, u32[]{:S(2)}, u32[]{:S(2)}) async-start(bf16[8,48,128]{2,1,0:T(8,128)(2,1)} %broadcast_in_dim.32), calls=%async_computation | async-start | bytes 196608 | tf_op jit(solution)/shard_map/all_to_all | solution.py:17
  15.4 2.4 %broadcast_select_fusion.10 = (bf16[128,3072]{1,0:T(8,128)(2,1)}, bf16[128,3072]{1,0:T(8,128)(2,1)S(1)}) fusion(pred[]{:T(512)S(6)} %eq.18, bf16[128,6144]{1,0:T(8,128)(2,1)} %bitcast.87), kind=kLoop, calls=%fused_computation.34 | loop fusion | flops 786432 | bytes 3145729 | tf_op jit(solution)/shard_map/jit(_where)/select_n | solution.py:90
  18.0 3.4 %all-to-all-done = bf16[8,48,128]{2,1,0:T(8,128)(2,1)S(1)} async-done(((bf16[8,48,128]{2,1,0:T(8,128)(2,1)}), bf16[8,48,128]{2,1,0:T(8,128)(2,1)S(1)}, u32[]{:S(2)}, u32[]{:S(2)}) %all-to-all-start) | async-done | bytes 98336 | tf_op jit(solution)/shard_map/all_to_all | solution.py:17
  22.4 6.8 %all-to-all-start.1 = ((bf16[16,8,3072]{2,1,0:T(8,128)(2,1)}), bf16[16,8,3072]{2,1,0:T(8,128)(2,1)}, u32[]{:S(2)}, u32[]{:S(2)}) async-start(bf16[16,8,3072]{2,1,0:T(8,128)(2,1)} %broadcast_in_dim.60), calls=%async_computation.1 | async-start | bytes 1572864 | tf_op jit(solution)/shard_map/all_to_all | solution.py:17
  29.2 4.5 %broadcast_select_fusion.1 = (bf16[3072,256]{1,0:T(8,128)(2,1)S(1)}, bf16[3072,256]{1,0:T(8,128)(2,1)}) fusion(bf16[3072,256]{1,0:T(8,128)(2,1)} %collective-permute-done.1, pred[]{:T(512)S(6)} %eq.18, bf16[6144,128]{1,0:T(8,128)(2,1)} %bitcast.83, bf16[6144,128]{1,0:T(8,128)(2,1)} %bitcast.85), kind=kLoop, calls=%fused_computation.25 | loop fusion | flops 12582912 | bytes 7864321 | tf_op jit(solution)/shard_map/jit(_where)/select_n | solution.py:90
  33.7 8.0 %all-to-all-done.1 = bf16[16,8,3072]{2,1,0:T(8,128)(2,1)} async-done(((bf16[16,8,3072]{2,1,0:T(8,128)(2,1)}), bf16[16,8,3072]{2,1,0:T(8,128)(2,1)}, u32[]{:S(2)}, u32[]{:S(2)}) %all-to-all-start.1) | async-done | bytes 786464 | tf_op jit(solution)/shard_map/all_to_all | solution.py:17
  43.2 2.9 %collective-permute-start.2 = (f32[128,256]{1,0:T(8,128)S(1)}, f32[128,256]{1,0:T(8,128)S(1)}, u32[]{:S(2)}, u32[]{:S(2)}) collective-permute-start(f32[128,256]{1,0:T(8,128)S(1)} %fusion.29), channel_id=1, source_target_pairs={{0,128},{128,0},{1,129},{129,1},{2,130},{130,2},{3,131},{131,3},{4... | collective-permute-start | bytes 393224 | tf_op jit(solution)/shard_map/ppermute | solution.py:63
  49.0 4.3 %all-to-all-start.2 = ((bf16[16,8,3072]{2,1,0:T(8,128)(2,1)}), bf16[16,8,3072]{2,1,0:T(8,128)(2,1)}, u32[]{:S(2)}, u32[]{:S(2)}) async-start(bf16[16,8,3072]{2,1,0:T(8,128)(2,1)} %fusion.6), calls=%async_computation.2 | async-start | bytes 1572864 | tf_op jit(solution)/shard_map/all_to_all | solution.py:17
  53.3 12.8 %all-to-all-done.2 = bf16[16,8,3072]{2,1,0:T(8,128)(2,1)} async-done(((bf16[16,8,3072]{2,1,0:T(8,128)(2,1)}), bf16[16,8,3072]{2,1,0:T(8,128)(2,1)}, u32[]{:S(2)}, u32[]{:S(2)}) %all-to-all-start.2) | async-done | bytes 786464 | tf_op jit(solution)/shard_map/all_to_all | solution.py:17
  67.5 2.9 %collective-permute-done.4 = bf16[8,3072]{1,0:T(8,128)(2,1)S(1)} collective-permute-done((bf16[8,3072]{1,0:T(8,128)(2,1)S(1)}, bf16[8,3072]{1,0:T(8,128)(2,1)S(1)}, u32[]{:S(2)}, u32[]{:S(2)}) %collective-permute-start.4) | collective-permute-done | bytes 49184 | tf_op jit(solution)/shard_map/ppermute | solution.py:53
  71.5 4.7 %all-to-all-start.3 = ((bf16[16,8,3072]{2,1,0:T(8,128)(2,1)}), bf16[16,8,3072]{2,1,0:T(8,128)(2,1)S(1)}, u32[]{:S(2)}, u32[]{:S(2)}) async-start(bf16[16,8,3072]{2,1,0:T(8,128)(2,1)} %broadcast_in_dim.61), calls=%async_computation.3 | async-start | bytes 1572864 | tf_op jit(solution)/shard_map/all_to_all | solution.py:17
  76.2 3.0 %collective-permute-start.6 = (bf16[8,3072]{1,0:T(8,128)(2,1)S(1)}, bf16[8,3072]{1,0:T(8,128)(2,1)S(1)}, u32[]{:S(2)}, u32[]{:S(2)}) collective-permute-start(bf16[8,3072]{1,0:T(8,128)(2,1)S(1)} %add_convert_fusion.4), channel_id=1, source_target_pairs={{0,4},{1,5},{2,6},{3,7},{4,0},{5,1},{6,2},{7,3},{8,12},{9,13},{10,... | collective-permute-start | bytes 147464 | tf_op jit(solution)/shard_map/ppermute | solution.py:53
  79.2 4.0 %collective-permute-done.6 = bf16[8,3072]{1,0:T(8,128)(2,1)S(1)} collective-permute-done((bf16[8,3072]{1,0:T(8,128)(2,1)S(1)}, bf16[8,3072]{1,0:T(8,128)(2,1)S(1)}, u32[]{:S(2)}, u32[]{:S(2)}) %collective-permute-start.6) | collective-permute-done | bytes 49184 | tf_op jit(solution)/shard_map/ppermute | solution.py:53
  83.2 3.5 %all-to-all-done.3 = bf16[16,8,3072]{2,1,0:T(8,128)(2,1)S(1)} async-done(((bf16[16,8,3072]{2,1,0:T(8,128)(2,1)}), bf16[16,8,3072]{2,1,0:T(8,128)(2,1)S(1)}, u32[]{:S(2)}, u32[]{:S(2)}) %all-to-all-start.3) | async-done | bytes 786464 | tf_op jit(solution)/shard_map/all_to_all | solution.py:17
  87.7 4.4 %all-to-all-start.4 = ((bf16[16,8,3072]{2,1,0:T(8,128)(2,1)}), bf16[16,8,3072]{2,1,0:T(8,128)(2,1)}, u32[]{:S(2)}, u32[]{:S(2)}) async-start(bf16[16,8,3072]{2,1,0:T(8,128)(2,1)} %broadcast_in_dim.62), calls=%async_computation.4 | async-start | bytes 1572864 | tf_op jit(solution)/shard_map/all_to_all | solution.py:17
  92.5 5.8 %collective-permute-start.7 = (f32[128,128]{1,0:T(8,128)S(1)}, f32[128,128]{1,0:T(8,128)S(1)}, u32[]{:S(2)}, u32[]{:S(2)}) collective-permute-start(f32[128,128]{1,0:T(8,128)S(1)} %fusion.12), channel_id=1, source_target_pairs={{0,128},{128,0},{1,129},{129,1},{2,130},{130,2},{3,131},{131,3},{4... | collective-permute-start | bytes 196616 | tf_op jit(solution)/shard_map/ppermute | solution.py:63
  99.3 3.3 %all-to-all-done.4 = bf16[16,8,3072]{2,1,0:T(8,128)(2,1)} async-done(((bf16[16,8,3072]{2,1,0:T(8,128)(2,1)}), bf16[16,8,3072]{2,1,0:T(8,128)(2,1)}, u32[]{:S(2)}, u32[]{:S(2)}) %all-to-all-start.4) | async-done | bytes 786464 | tf_op jit(solution)/shard_map/all_to_all | solution.py:17
  102.6 2.1 fusion.33
  104.8 5.7 %collective-permute-start.8 = (f32[128,256]{1,0:T(8,128)S(1)}, f32[128,256]{1,0:T(8,128)S(1)}, u32[]{:S(2)}, u32[]{:S(2)}) collective-permute-start(f32[128,256]{1,0:T(8,128)S(1)} %fusion.33), channel_id=1, source_target_pairs={{0,128},{128,0},{1,129},{129,1},{2,130},{130,2},{3,131},{131,3},{4... | collective-permute-start | bytes 393224 | tf_op jit(solution)/shard_map/ppermute | solution.py:63
  113.7 4.3 %all-to-all-start.5 = ((bf16[16,8,3072]{2,1,0:T(8,128)(2,1)}), bf16[16,8,3072]{2,1,0:T(8,128)(2,1)}, u32[]{:S(2)}, u32[]{:S(2)}) async-start(bf16[16,8,3072]{2,1,0:T(8,128)(2,1)} %fusion.5), calls=%async_computation.5 | async-start | bytes 1572864 | tf_op jit(solution)/shard_map/all_to_all | solution.py:17
  118.0 2.0 fusion.4
  120.0 10.8 %all-to-all-done.5 = bf16[16,8,3072]{2,1,0:T(8,128)(2,1)} async-done(((bf16[16,8,3072]{2,1,0:T(8,128)(2,1)}), bf16[16,8,3072]{2,1,0:T(8,128)(2,1)}, u32[]{:S(2)}, u32[]{:S(2)}) %all-to-all-start.5) | async-done | bytes 786464 | tf_op jit(solution)/shard_map/all_to_all | solution.py:17
  130.8 1.9 reduce_sum.68
  133.6 2.2 collective-permute-done.9
  137.3 2.4 %collective-permute-start.10 = (bf16[8,3072]{1,0:T(8,128)(2,1)}, bf16[8,3072]{1,0:T(8,128)(2,1)}, u32[]{:S(2)}, u32[]{:S(2)}) collective-permute-start(bf16[8,3072]{1,0:T(8,128)(2,1)} %add_convert_fusion.2), channel_id=1, source_target_pairs={{0,2},{1,3},{2,0},{3,1},{4,6},{5,7},{6,4},{7,5},{8,10},{9,11},{10,... | collective-permute-start | bytes 147464 | tf_op jit(solution)/shard_map/ppermute | solution.py:53
  139.6 4.7 %all-to-all-start.6 = ((bf16[16,8,3072]{2,1,0:T(8,128)(2,1)}), bf16[16,8,3072]{2,1,0:T(8,128)(2,1)}, u32[]{:S(2)}, u32[]{:S(2)}) async-start(bf16[16,8,3072]{2,1,0:T(8,128)(2,1)} %bitcast.86), calls=%async_computation.6 | async-start | bytes 1572864 | tf_op jit(solution)/shard_map/all_to_all | solution.py:17
  145.2 2.5 %collective-permute-start.11 = (bf16[8,3072]{1,0:T(8,128)(2,1)S(1)}, bf16[8,3072]{1,0:T(8,128)(2,1)S(1)}, u32[]{:S(2)}, u32[]{:S(2)}) collective-permute-start(bf16[8,3072]{1,0:T(8,128)(2,1)S(1)} %add_convert_fusion.1), channel_id=1, source_target_pairs={{0,4},{1,5},{2,6},{3,7},{4,0},{5,1},{6,2},{7,3},{8,12},{9,13},{10,... | collective-permute-start | bytes 147464 | tf_op jit(solution)/shard_map/ppermute | solution.py:53
  148.8 3.5 %collective-permute-done.11 = bf16[8,3072]{1,0:T(8,128)(2,1)S(1)} collective-permute-done((bf16[8,3072]{1,0:T(8,128)(2,1)S(1)}, bf16[8,3072]{1,0:T(8,128)(2,1)S(1)}, u32[]{:S(2)}, u32[]{:S(2)}) %collective-permute-start.11) | collective-permute-done | bytes 49184 | tf_op jit(solution)/shard_map/ppermute | solution.py:53
  153.0 2.0 all-to-all-done.6
  155.0 1.9 reduce_sum.69
  156.9 1.8 broadcast_in_dim.63
  158.6 4.6 %all-to-all-start.7 = ((bf16[16,8,3072]{2,1,0:T(8,128)(2,1)}), bf16[16,8,3072]{2,1,0:T(8,128)(2,1)}, u32[]{:S(2)}, u32[]{:S(2)}) async-start(bf16[16,8,3072]{2,1,0:T(8,128)(2,1)} %broadcast_in_dim.63), calls=%async_computation.7 | async-start | bytes 1572864 | tf_op jit(solution)/shard_map/all_to_all | solution.py:17
  164.2 5.4 %collective-permute-start.12 = (bf16[2,24,128]{2,1,0:T(8,128)(2,1)S(1)}, bf16[2,24,128]{2,1,0:T(8,128)(2,1)S(1)}, u32[]{:S(2)}, u32[]{:S(2)}) collective-permute-start(bf16[2,24,128]{2,1,0:T(8,128)(2,1)S(1)} %bitcast.93), channel_id=1, source_target_pairs={{0,128},{128,0},{1,129},{129,1},{2,130},{130,2},{3,131},{131,3},{4... | collective-permute-start | bytes 36872 | tf_op jit(solution)/shard_map/ppermute | solution.py:63
  169.6 2.8 %collective-permute-start.14 = (bf16[128,3072]{1,0:T(8,128)(2,1)}, bf16[128,3072]{1,0:T(8,128)(2,1)}, u32[]{:S(2)}, u32[]{:S(2)}) collective-permute-start(bf16[128,3072]{1,0:T(8,128)(2,1)} %bitcast.6), channel_id=1, source_target_pairs={{128,0},{129,1},{130,2},{131,3},{132,4},{133,5},{134,6},{135,7},{1... | collective-permute-start | bytes 2359304 | tf_op jit(solution)/shard_map/ppermute | solution.py:63
  175.6 1.8 fusion.11
  177.4 4.4 %collective-permute-start.13 = (f32[128,128]{1,0:T(8,128)S(1)}, f32[128,128]{1,0:T(8,128)S(1)}, u32[]{:S(2)}, u32[]{:S(2)}) collective-permute-start(f32[128,128]{1,0:T(8,128)S(1)} %fusion.11), channel_id=1, source_target_pairs={{0,128},{128,0},{1,129},{129,1},{2,130},{130,2},{3,131},{131,3},{4... | collective-permute-start | bytes 196616 | tf_op jit(solution)/shard_map/ppermute | solution.py:63
  185.5 5.2 %all-to-all-start.8 = ((bf16[16,8,3072]{2,1,0:T(8,128)(2,1)}), bf16[16,8,3072]{2,1,0:T(8,128)(2,1)S(1)}, u32[]{:S(2)}, u32[]{:S(2)}) async-start(bf16[16,8,3072]{2,1,0:T(8,128)(2,1)} %bitcast.19), calls=%async_computation.8 | async-start | bytes 1572864 | tf_op jit(solution)/shard_map/all_to_all | solution.py:17
  190.8 2.9 %broadcast_select_fusion.5 = (bf16[128,3072]{1,0:T(8,128)(2,1)}, bf16[128,3072]{1,0:T(8,128)(2,1)}) fusion(bf16[128,3072]{1,0:T(8,128)(2,1)} %collective-permute-done.16, pred[]{:T(512)S(6)} %eq.18, bf16[128,3072]{1,0:T(8,128)(2,1)} %bitcast.18, f32[128]{0:T(128)S(1)} %copy-done.15), kind=kLoop, calls=%fused_computation.29 | loop fusion | flops 1572864 | bytes 3146241 | tf_op jit(solution)/shard_map/jit(_where)/select_n | solution.py:90
  193.7 2.9 %collective-permute-start.17 = (bf16[128,3072]{1,0:T(8,128)(2,1)}, bf16[128,3072]{1,0:T(8,128)(2,1)}, u32[]{:S(2)}, u32[]{:S(2)}) collective-permute-start(bf16[128,3072]{1,0:T(8,128)(2,1)} %get-tuple-element.44), channel_id=1, source_target_pairs={{128,0},{129,1},{130,2},{131,3},{132,4},{133,5},{134,6},{135,7},{1... | collective-permute-start | bytes 2359304 | tf_op jit(solution)/shard_map/ppermute | solution.py:63
  196.6 1.8 broadcast_select_fusion.6
  198.4 1.8 fusion
  200.2 1.8 fusion.1
  201.9 2.3 %all-to-all-done.8 = bf16[16,8,3072]{2,1,0:T(8,128)(2,1)S(1)} async-done(((bf16[16,8,3072]{2,1,0:T(8,128)(2,1)}), bf16[16,8,3072]{2,1,0:T(8,128)(2,1)S(1)}, u32[]{:S(2)}, u32[]{:S(2)}) %all-to-all-start.8) | async-done | bytes 786464 | tf_op jit(solution)/shard_map/all_to_all | solution.py:17
  205.0 6.0 %all-to-all-start.9 = ((bf16[16,24,128]{2,1,0:T(8,128)(2,1)}), bf16[16,24,128]{2,1,0:T(8,128)(2,1)S(1)}, u32[]{:S(2)}, u32[]{:S(2)}) async-start(bf16[16,24,128]{2,1,0:T(8,128)(2,1)} %bitcast.35), calls=%async_computation.9 | async-start | bytes 196608 | tf_op jit(solution)/shard_map/all_to_all | solution.py:17
  211.4 1.7 fusion.2
  213.1 5.2 %all-to-all-done.9 = bf16[16,24,128]{2,1,0:T(8,128)(2,1)S(1)} async-done(((bf16[16,24,128]{2,1,0:T(8,128)(2,1)}), bf16[16,24,128]{2,1,0:T(8,128)(2,1)S(1)}, u32[]{:S(2)}, u32[]{:S(2)}) %all-to-all-start.9) | async-done | bytes 98336 | tf_op jit(solution)/shard_map/all_to_all | solution.py:17
  (107 shorter events, 29.6 us)
Async XLA Ops:
  0.6 5.7 %copy-start.12 = (bf16[1,1,6144]{2,1,0:T(2,128)(2,1)S(1)}, bf16[1,1,6144]{2,1,0:T(2,128)(2,1)}, u32[]{:S(2)}) copy-start(bf16[1,1,6144]{2,1,0:T(2,128)(2,1)} %param.10) | copy-start | bytes 36868
  0.6 5.7 %copy-start.13 = (bf16[1,1,6144]{2,1,0:T(2,128)(2,1)S(1)}, bf16[1,1,6144]{2,1,0:T(2,128)(2,1)}, u32[]{:S(2)}) copy-start(bf16[1,1,6144]{2,1,0:T(2,128)(2,1)} %param.9) | copy-start | bytes 36868
  0.7 14.2 %copy-start.16 = (f32[1,1,128]{2,1,0:T(1,128)S(1)}, f32[1,1,128]{2,1,0:T(1,128)}, u32[]{:S(2)}) copy-start(f32[1,1,128]{2,1,0:T(1,128)} %param.16) | copy-start | bytes 1540
  0.7 14.2 %copy-start.17 = (s32[1,1,128]{2,1,0:T(1,128)S(1)}, s32[1,1,128]{2,1,0:T(1,128)}, u32[]{:S(2)}) copy-start(s32[1,1,128]{2,1,0:T(1,128)} %param.14) | copy-start | bytes 1540
  3.0 26.2 %collective-permute-start.1 = (bf16[3072,256]{1,0:T(8,128)(2,1)S(1)}, bf16[3072,256]{1,0:T(8,128)(2,1)}, u32[]{:S(2)}, u32[]{:S(2)}) collective-permute-start(bf16[3072,256]{1,0:T(8,128)(2,1)S(1)} %broadcast_select_fusion.2), channel_id=1, source_target_pairs={{0,128},{128,0},{1,129},{129,1},{2,130},{130,2},{3,131},{131,3},{4... | collective-permute-start | bytes 4718600 | tf_op jit(solution)/shard_map/ppermute | solution.py:63
  7.1 14.3 %all-to-all-start = ((bf16[8,48,128]{2,1,0:T(8,128)(2,1)}), bf16[8,48,128]{2,1,0:T(8,128)(2,1)S(1)}, u32[]{:S(2)}, u32[]{:S(2)}) async-start(bf16[8,48,128]{2,1,0:T(8,128)(2,1)} %broadcast_in_dim.32), calls=%async_computation | async-start | bytes 196608 | tf_op jit(solution)/shard_map/all_to_all | solution.py:17
  15.0 3.0 %collective-permute-start = (f32[2,128]{1,0:T(2,128)S(1)}, f32[2,128]{1,0:T(2,128)S(1)}, u32[]{:S(2)}, u32[]{:S(2)}) collective-permute-start(f32[2,128]{1,0:T(2,128)S(1)} %stack.10), channel_id=1, source_target_pairs={{0,128},{128,0},{1,129},{129,1},{2,130},{130,2},{3,131},{131,3},{4... | collective-permute-start | bytes 3080 | tf_op jit(solution)/shard_map/ppermute | solution.py:63
  17.8 29.4 %collective-permute-start.3 = (bf16[128,3072]{1,0:T(8,128)(2,1)}, bf16[128,3072]{1,0:T(8,128)(2,1)S(1)}, u32[]{:S(2)}, u32[]{:S(2)}) collective-permute-start(bf16[128,3072]{1,0:T(8,128)(2,1)} %get-tuple-element.47), channel_id=1, source_target_pairs={{0,128},{128,0},{1,129},{129,1},{2,130},{130,2},{3,131},{131,3},{4... | collective-permute-start | bytes 2359304 | tf_op jit(solution)/shard_map/ppermute | solution.py:63
  22.4 19.3 %all-to-all-start.1 = ((bf16[16,8,3072]{2,1,0:T(8,128)(2,1)}), bf16[16,8,3072]{2,1,0:T(8,128)(2,1)}, u32[]{:S(2)}, u32[]{:S(2)}) async-start(bf16[16,8,3072]{2,1,0:T(8,128)(2,1)} %broadcast_in_dim.60), calls=%async_computation.1 | async-start | bytes 1572864 | tf_op jit(solution)/shard_map/all_to_all | solution.py:17
  43.2 3.9 %collective-permute-start.2 = (f32[128,256]{1,0:T(8,128)S(1)}, f32[128,256]{1,0:T(8,128)S(1)}, u32[]{:S(2)}, u32[]{:S(2)}) collective-permute-start(f32[128,256]{1,0:T(8,128)S(1)} %fusion.29), channel_id=1, source_target_pairs={{0,128},{128,0},{1,129},{129,1},{2,130},{130,2},{3,131},{131,3},{4... | collective-permute-start | bytes 393224 | tf_op jit(solution)/shard_map/ppermute | solution.py:63
  46.1 2.9 %copy-start.14 = (f32[128]{0:T(128)}, f32[128]{0:T(128)S(1)}, u32[]{:S(2)}) copy-start(f32[128]{0:T(128)S(1)} %get-tuple-element.67) | copy-start | bytes 1540
  47.2 0.6 copy-start.3
  47.2 1.8 copy-start.1
  49.0 17.1 %all-to-all-start.2 = ((bf16[16,8,3072]{2,1,0:T(8,128)(2,1)}), bf16[16,8,3072]{2,1,0:T(8,128)(2,1)}, u32[]{:S(2)}, u32[]{:S(2)}) async-start(bf16[16,8,3072]{2,1,0:T(8,128)(2,1)} %fusion.6), calls=%async_computation.2 | async-start | bytes 1572864 | tf_op jit(solution)/shard_map/all_to_all | solution.py:17
  67.4 3.0 %collective-permute-start.4 = (bf16[8,3072]{1,0:T(8,128)(2,1)S(1)}, bf16[8,3072]{1,0:T(8,128)(2,1)S(1)}, u32[]{:S(2)}, u32[]{:S(2)}) collective-permute-start(bf16[8,3072]{1,0:T(8,128)(2,1)S(1)} %reduce_sum.67), channel_id=1, source_target_pairs={{0,1},{1,0},{2,3},{3,2},{4,5},{5,4},{6,7},{7,6},{8,9},{9,8},{10,11... | collective-permute-start | bytes 147464 | tf_op jit(solution)/shard_map/ppermute | solution.py:53
  70.4 5.8 %collective-permute-start.5 = (bf16[8,3072]{1,0:T(8,128)(2,1)S(1)}, bf16[8,3072]{1,0:T(8,128)(2,1)S(1)}, u32[]{:S(2)}, u32[]{:S(2)}) collective-permute-start(bf16[8,3072]{1,0:T(8,128)(2,1)S(1)} %add_convert_fusion.5), channel_id=1, source_target_pairs={{0,2},{1,3},{2,0},{3,1},{4,6},{5,7},{6,4},{7,5},{8,10},{9,11},{10,... | collective-permute-start | bytes 147464 | tf_op jit(solution)/shard_map/ppermute | solution.py:53
  71.5 15.3 %all-to-all-start.3 = ((bf16[16,8,3072]{2,1,0:T(8,128)(2,1)}), bf16[16,8,3072]{2,1,0:T(8,128)(2,1)S(1)}, u32[]{:S(2)}, u32[]{:S(2)}) async-start(bf16[16,8,3072]{2,1,0:T(8,128)(2,1)} %broadcast_in_dim.61), calls=%async_computation.3 | async-start | bytes 1572864 | tf_op jit(solution)/shard_map/all_to_all | solution.py:17
  76.2 7.0 %collective-permute-start.6 = (bf16[8,3072]{1,0:T(8,128)(2,1)S(1)}, bf16[8,3072]{1,0:T(8,128)(2,1)S(1)}, u32[]{:S(2)}, u32[]{:S(2)}) collective-permute-start(bf16[8,3072]{1,0:T(8,128)(2,1)S(1)} %add_convert_fusion.4), channel_id=1, source_target_pairs={{0,4},{1,5},{2,6},{3,7},{4,0},{5,1},{6,2},{7,3},{8,12},{9,13},{10,... | collective-permute-start | bytes 147464 | tf_op jit(solution)/shard_map/ppermute | solution.py:53
  83.2 9.3 %copy-start.7 = (bf16[8,3072]{1,0:T(8,128)(2,1)}, bf16[8,3072]{1,0:T(8,128)(2,1)S(1)}, u32[]{:S(2)}) copy-start(bf16[8,3072]{1,0:T(8,128)(2,1)S(1)} %add_convert_fusion.3) | copy-start | bytes 147460
  87.7 14.9 %all-to-all-start.4 = ((bf16[16,8,3072]{2,1,0:T(8,128)(2,1)}), bf16[16,8,3072]{2,1,0:T(8,128)(2,1)}, u32[]{:S(2)}, u32[]{:S(2)}) async-start(bf16[16,8,3072]{2,1,0:T(8,128)(2,1)} %broadcast_in_dim.62), calls=%async_computation.4 | async-start | bytes 1572864 | tf_op jit(solution)/shard_map/all_to_all | solution.py:17
  92.5 6.7 %collective-permute-start.7 = (f32[128,128]{1,0:T(8,128)S(1)}, f32[128,128]{1,0:T(8,128)S(1)}, u32[]{:S(2)}, u32[]{:S(2)}) collective-permute-start(f32[128,128]{1,0:T(8,128)S(1)} %fusion.12), channel_id=1, source_target_pairs={{0,128},{128,0},{1,129},{129,1},{2,130},{130,2},{3,131},{131,3},{4... | collective-permute-start | bytes 196616 | tf_op jit(solution)/shard_map/ppermute | solution.py:63
  102.6 9.5 %copy-start = (bf16[3072,256]{1,0:T(8,128)(2,1)S(1)}, bf16[3072,256]{1,0:T(8,128)(2,1)}, u32[]{:S(2)}) copy-start(bf16[3072,256]{1,0:T(8,128)(2,1)} %get-tuple-element.46) | copy-start | bytes 4718596
  104.8 6.7 %collective-permute-start.8 = (f32[128,256]{1,0:T(8,128)S(1)}, f32[128,256]{1,0:T(8,128)S(1)}, u32[]{:S(2)}, u32[]{:S(2)}) collective-permute-start(f32[128,256]{1,0:T(8,128)S(1)} %fusion.33), channel_id=1, source_target_pairs={{0,128},{128,0},{1,129},{129,1},{2,130},{130,2},{3,131},{131,3},{4... | collective-permute-start | bytes 393224 | tf_op jit(solution)/shard_map/ppermute | solution.py:63
  113.7 17.1 %all-to-all-start.5 = ((bf16[16,8,3072]{2,1,0:T(8,128)(2,1)}), bf16[16,8,3072]{2,1,0:T(8,128)(2,1)}, u32[]{:S(2)}, u32[]{:S(2)}) async-start(bf16[16,8,3072]{2,1,0:T(8,128)(2,1)} %fusion.5), calls=%async_computation.5 | async-start | bytes 1572864 | tf_op jit(solution)/shard_map/all_to_all | solution.py:17
  132.7 3.2 %collective-permute-start.9 = (bf16[8,3072]{1,0:T(8,128)(2,1)}, bf16[8,3072]{1,0:T(8,128)(2,1)S(1)}, u32[]{:S(2)}, u32[]{:S(2)}) collective-permute-start(bf16[8,3072]{1,0:T(8,128)(2,1)} %reduce_sum.68), channel_id=1, source_target_pairs={{0,1},{1,0},{2,3},{3,2},{4,5},{5,4},{6,7},{7,6},{8,9},{9,8},{10,11... | collective-permute-start | bytes 147464 | tf_op jit(solution)/shard_map/ppermute | solution.py:53
  137.3 7.1 %collective-permute-start.10 = (bf16[8,3072]{1,0:T(8,128)(2,1)}, bf16[8,3072]{1,0:T(8,128)(2,1)}, u32[]{:S(2)}, u32[]{:S(2)}) collective-permute-start(bf16[8,3072]{1,0:T(8,128)(2,1)} %add_convert_fusion.2), channel_id=1, source_target_pairs={{0,2},{1,3},{2,0},{3,1},{4,6},{5,7},{6,4},{7,5},{8,10},{9,11},{10,... | collective-permute-start | bytes 147464 | tf_op jit(solution)/shard_map/ppermute | solution.py:53
  139.6 15.4 %all-to-all-start.6 = ((bf16[16,8,3072]{2,1,0:T(8,128)(2,1)}), bf16[16,8,3072]{2,1,0:T(8,128)(2,1)}, u32[]{:S(2)}, u32[]{:S(2)}) async-start(bf16[16,8,3072]{2,1,0:T(8,128)(2,1)} %bitcast.86), calls=%async_computation.6 | async-start | bytes 1572864 | tf_op jit(solution)/shard_map/all_to_all | solution.py:17
  145.2 7.1 %collective-permute-start.11 = (bf16[8,3072]{1,0:T(8,128)(2,1)S(1)}, bf16[8,3072]{1,0:T(8,128)(2,1)S(1)}, u32[]{:S(2)}, u32[]{:S(2)}) collective-permute-start(bf16[8,3072]{1,0:T(8,128)(2,1)S(1)} %add_convert_fusion.1), channel_id=1, source_target_pairs={{0,4},{1,5},{2,6},{3,7},{4,0},{5,1},{6,2},{7,3},{8,12},{9,13},{10,... | collective-permute-start | bytes 147464 | tf_op jit(solution)/shard_map/ppermute | solution.py:53
  158.6 17.0 %all-to-all-start.7 = ((bf16[16,8,3072]{2,1,0:T(8,128)(2,1)}), bf16[16,8,3072]{2,1,0:T(8,128)(2,1)}, u32[]{:S(2)}, u32[]{:S(2)}) async-start(bf16[16,8,3072]{2,1,0:T(8,128)(2,1)} %broadcast_in_dim.63), calls=%async_computation.7 | async-start | bytes 1572864 | tf_op jit(solution)/shard_map/all_to_all | solution.py:17
  164.2 10.8 %collective-permute-start.12 = (bf16[2,24,128]{2,1,0:T(8,128)(2,1)S(1)}, bf16[2,24,128]{2,1,0:T(8,128)(2,1)S(1)}, u32[]{:S(2)}, u32[]{:S(2)}) collective-permute-start(bf16[2,24,128]{2,1,0:T(8,128)(2,1)S(1)} %bitcast.93), channel_id=1, source_target_pairs={{0,128},{128,0},{1,129},{129,1},{2,130},{130,2},{3,131},{131,3},{4... | collective-permute-start | bytes 36872 | tf_op jit(solution)/shard_map/ppermute | solution.py:63
  169.6 15.9 %collective-permute-start.14 = (bf16[128,3072]{1,0:T(8,128)(2,1)}, bf16[128,3072]{1,0:T(8,128)(2,1)}, u32[]{:S(2)}, u32[]{:S(2)}) collective-permute-start(bf16[128,3072]{1,0:T(8,128)(2,1)} %bitcast.6), channel_id=1, source_target_pairs={{128,0},{129,1},{130,2},{131,3},{132,4},{133,5},{134,6},{135,7},{1... | collective-permute-start | bytes 2359304 | tf_op jit(solution)/shard_map/ppermute | solution.py:63
  172.4 13.1 %collective-permute-start.15 = (bf16[128,3072]{1,0:T(8,128)(2,1)}, bf16[128,3072]{1,0:T(8,128)(2,1)}, u32[]{:S(2)}, u32[]{:S(2)}) collective-permute-start(bf16[128,3072]{1,0:T(8,128)(2,1)} %bitcast.13), channel_id=1, source_target_pairs={{0,128},{1,129},{2,130},{3,131},{4,132},{5,133},{6,134},{7,135},{8... | collective-permute-start | bytes 2359304 | tf_op jit(solution)/shard_map/ppermute | solution.py:63
  173.7 11.8 %collective-permute-start.16 = (bf16[128,3072]{1,0:T(8,128)(2,1)}, bf16[128,3072]{1,0:T(8,128)(2,1)}, u32[]{:S(2)}, u32[]{:S(2)}) collective-permute-start(bf16[128,3072]{1,0:T(8,128)(2,1)} %multiply_convert_fusion.1), channel_id=1, source_target_pairs={{0,128},{1,129},{2,130},{3,131},{4,132},{5,133},{6,134},{7,135},{8... | collective-permute-start | bytes 2359304 | tf_op jit(solution)/shard_map/ppermute | solution.py:63
  175.6 6.2 %copy-start.11 = (bf16[2,24,128]{2,1,0:T(8,128)(2,1)S(1)}, bf16[2,24,128]{2,1,0:T(8,128)(2,1)}, u32[]{:S(2)}) copy-start(bf16[2,24,128]{2,1,0:T(8,128)(2,1)} %get-tuple-element.62) | copy-start | bytes 36868
  177.4 5.7 %copy-start.6 = (f32[128,128]{1,0:T(8,128)}, f32[128,128]{1,0:T(8,128)S(1)}, u32[]{:S(2)}) copy-start(f32[128,128]{1,0:T(8,128)S(1)} %fusion.11) | copy-start | bytes 196612
  177.4 5.6 %collective-permute-start.13 = (f32[128,128]{1,0:T(8,128)S(1)}, f32[128,128]{1,0:T(8,128)S(1)}, u32[]{:S(2)}, u32[]{:S(2)}) collective-permute-start(f32[128,128]{1,0:T(8,128)S(1)} %fusion.11), channel_id=1, source_target_pairs={{0,128},{128,0},{1,129},{129,1},{2,130},{130,2},{3,131},{131,3},{4... | collective-permute-start | bytes 196616 | tf_op jit(solution)/shard_map/ppermute | solution.py:63
  184.0 6.8 %copy-start.15 = (f32[128]{0:T(128)S(1)}, f32[128]{0:T(128)}, u32[]{:S(2)}) copy-start(f32[128]{0:T(128)} %copy-done.14) | copy-start | bytes 1540
  185.5 18.6 %all-to-all-start.8 = ((bf16[16,8,3072]{2,1,0:T(8,128)(2,1)}), bf16[16,8,3072]{2,1,0:T(8,128)(2,1)S(1)}, u32[]{:S(2)}, u32[]{:S(2)}) async-start(bf16[16,8,3072]{2,1,0:T(8,128)(2,1)} %bitcast.19), calls=%async_computation.8 | async-start | bytes 1572864 | tf_op jit(solution)/shard_map/all_to_all | solution.py:17
  193.7 17.3 %collective-permute-start.17 = (bf16[128,3072]{1,0:T(8,128)(2,1)}, bf16[128,3072]{1,0:T(8,128)(2,1)}, u32[]{:S(2)}, u32[]{:S(2)}) collective-permute-start(bf16[128,3072]{1,0:T(8,128)(2,1)} %get-tuple-element.44), channel_id=1, source_target_pairs={{128,0},{129,1},{130,2},{131,3},{132,4},{133,5},{134,6},{135,7},{1... | collective-permute-start | bytes 2359304 | tf_op jit(solution)/shard_map/ppermute | solution.py:63
  200.2 4.1 %copy-start.8 = (bf16[8,3072]{1,0:T(8,128)(2,1)S(1)}, bf16[8,3072]{1,0:T(8,128)(2,1)}, u32[]{:S(2)}) copy-start(bf16[8,3072]{1,0:T(8,128)(2,1)} %reduce_sum.69) | copy-start | bytes 147460
  204.3 7.0 %copy-start.2 = (bf16[128,3072]{1,0:T(8,128)(2,1)S(1)}, bf16[128,3072]{1,0:T(8,128)(2,1)}, u32[]{:S(2)}) copy-start(bf16[128,3072]{1,0:T(8,128)(2,1)} %get-tuple-element.43) | copy-start | bytes 2359300
  204.3 7.0 %copy-start.4 = (bf16[128,128]{1,0:T(8,128)(2,1)S(1)}, bf16[128,128]{1,0:T(8,128)(2,1)}, u32[]{:S(2)}) copy-start(bf16[128,128]{1,0:T(8,128)(2,1)} %copy-done.3) | copy-start | bytes 98308
  204.3 7.0 %copy-start.5 = (bf16[128,128]{1,0:T(8,128)(2,1)S(1)}, bf16[128,128]{1,0:T(8,128)(2,1)}, u32[]{:S(2)}) copy-start(bf16[128,128]{1,0:T(8,128)(2,1)} %get-tuple-element.52) | copy-start | bytes 98308
  205.0 13.4 %all-to-all-start.9 = ((bf16[16,24,128]{2,1,0:T(8,128)(2,1)}), bf16[16,24,128]{2,1,0:T(8,128)(2,1)S(1)}, u32[]{:S(2)}, u32[]{:S(2)}) async-start(bf16[16,24,128]{2,1,0:T(8,128)(2,1)} %bitcast.35), calls=%async_computation.9 | async-start | bytes 196608 | tf_op jit(solution)/shard_map/all_to_all | solution.py:17
  211.4 7.0 %copy-start.9 = (bf16[1,1,1,6144]{3,2,1,0:T(2,128)(2,1)S(1)}, bf16[1,1,1,6144]{3,2,1,0:T(2,128)(2,1)}, u32[]{:S(2)}) copy-start(bf16[1,1,1,6144]{3,2,1,0:T(2,128)(2,1)} %unstack.15) | copy-start | bytes 36868
  211.4 7.0 %copy-start.10 = (bf16[1,1,1,6144]{3,2,1,0:T(2,128)(2,1)S(1)}, bf16[1,1,1,6144]{3,2,1,0:T(2,128)(2,1)}, u32[]{:S(2)}) copy-start(bf16[1,1,1,6144]{3,2,1,0:T(2,128)(2,1)} %unstack.13) | copy-start | bytes 36868

commit v10 on v9

--- a/solution.py
+++ b/solution.py
@@ -162,12 +162,13 @@
     partial = plane_sum(slot_gradient(deltas_one, 1), line)
     outcome_one = outcome(hidden_one, 1)
     partial, outcome_one = lax.optimization_barrier((partial, outcome_one))
-    out_partial = plane_sum(outcome_one, line)
+    out_blocks = exchange(outcome_one.reshape(plane, line, half), PLANE)
     back_block = add_bf16(cot_block, line_sum_steps(partial))
-    back_block, out_partial, in_late, mid_late, cot_late, mid_block = lax.optimization_barrier(
-        (back_block, out_partial, in_rows, mid_rows, cot_scaled, mid_block)
+    back_block, out_blocks, in_late, mid_late, cot_late, mid_block = lax.optimization_barrier(
+        (back_block, out_blocks, in_rows, mid_rows, cot_scaled, mid_block)
     )
     back_rows = plane_spread(back_block, plane)
+    out_partial = jnp.sum(out_blocks.astype(jnp.float32), axis=0).astype(jnp.bfloat16)
     in_other, mid_other = across(in_late, [(1, 0)]), across(mid_late, [(0, 1)])
     cot_other = across(cot_late, [(0, 1)])
 

time: 221 us -> 221 us (level)
    reduce_sum x4 -> x3, other arithmetic: 5.11 us -> 3.23 us  [plane_sum(): return jnp.sum(blocks.astype(jnp.float32), axis=0).astype(jnp.bfloat16)]
  transfers between devices with their start and end apart: 28 -> 28, of which waited for: 16 -> 16; matrix products, arithmetic and copies ran while one was open for 16% -> 17% of each run, Pallas kernels for 0% -> 0%
where the time goes in v10:
time: 221 us; the launch traced here: 219 us
  starting transfers between devices  96.9 us (44%)
  waiting for transfers between devices  66.8 us (30%)
  other arithmetic  26.9 us (12%)
  matrix products  17.4 us (8%)
  local copies, waits for them, and re-layouts  8.72 us (4%)
  between operations  2.48 us (1%)
    all_to_all x10, starting transfers between devices, exchange(): return lax.all_to_all(value, axes, 0, 0, tiled=True)  53.2 us
    all_to_all x10, waiting for transfers between devices, exchange(): return lax.all_to_all(value, axes, 0, 0, tiled=True)  51.4 us
    ppermute x12, starting transfers between devices, across(): return lax.ppermute(value, 'segment', pairs)  34.7 us
    select_n x12, other arithmetic, pick(): return jnp.where(first, a, b)  15.7 us
    ppermute x6, waiting for transfers between devices, line_sum_steps(): lax.ppermute(block, LINE, pairs).astype(jnp.float32)  12.6 us
    ppermute x6, starting transfers between devices, line_sum_steps(): lax.ppermute(block, LINE, pairs).astype(jnp.float32)  9.02 us
    dot_general x4, matrix products, dot_f32(): return jnp.dot(a, b, preferred_element_type=jnp.float32)  6.9 us
    broadcast_in_dim x5, local copies, waits for them, and re-layouts, copies(): return jnp.broadcast_to(value[None], (count, *value.shape))  5.28 us
  transfers between devices with their start and end apart: 28, of which 16 were waited for; matrix products, arithmetic and copies ran while one was open for 17% of the time, Pallas kernels for 0%

profile of v10, /device:TPU:1, one launch (start us, length us, event | category | flops | bytes accessed | tf_op | source)
XLA Modules:
  0.0 219.1 jit_solution(5021647101141235943)
XLA Ops:
  0.7 2.3 %broadcast_select_fusion.2 = bf16[3072,256]{1,0:T(8,128)(2,1)S(1)} fusion(pred[]{:T(512)S(6)} %eq.18, bf16[6144,128]{1,0:T(8,128)(2,1)} %bitcast.82, bf16[6144,128]{1,0:T(8,128)(2,1)} %bitcast.84), kind=kLoop, calls=%fused_computation.26 | loop fusion | flops 7077888 | bytes 4718593 | tf_op jit(solution)/shard_map/jit(_where)/select_n | solution.py:90
  3.0 3.3 %collective-permute-start.1 = (bf16[3072,256]{1,0:T(8,128)(2,1)S(1)}, bf16[3072,256]{1,0:T(8,128)(2,1)}, u32[]{:S(2)}, u32[]{:S(2)}) collective-permute-start(bf16[3072,256]{1,0:T(8,128)(2,1)S(1)} %broadcast_select_fusion.2), channel_id=1, source_target_pairs={{0,128},{128,0},{1,129},{129,1},{2,130},{130,2},{3,131},{131,3},{4... | collective-permute-start | bytes 4718600 | tf_op jit(solution)/shard_map/ppermute | solution.py:63
  7.1 6.5 %all-to-all-start = ((bf16[8,48,128]{2,1,0:T(8,128)(2,1)}), bf16[8,48,128]{2,1,0:T(8,128)(2,1)S(1)}, u32[]{:S(2)}, u32[]{:S(2)}) async-start(bf16[8,48,128]{2,1,0:T(8,128)(2,1)} %broadcast_in_dim.32), calls=%async_computation | async-start | bytes 196608 | tf_op jit(solution)/shard_map/all_to_all | solution.py:17
  15.4 2.4 %broadcast_select_fusion.10 = (bf16[128,3072]{1,0:T(8,128)(2,1)}, bf16[128,3072]{1,0:T(8,128)(2,1)S(1)}) fusion(pred[]{:T(512)S(6)} %eq.18, bf16[128,6144]{1,0:T(8,128)(2,1)} %bitcast.87), kind=kLoop, calls=%fused_computation.34 | loop fusion | flops 786432 | bytes 3145729 | tf_op jit(solution)/shard_map/jit(_where)/select_n | solution.py:90
  18.0 3.4 %all-to-all-done = bf16[8,48,128]{2,1,0:T(8,128)(2,1)S(1)} async-done(((bf16[8,48,128]{2,1,0:T(8,128)(2,1)}), bf16[8,48,128]{2,1,0:T(8,128)(2,1)S(1)}, u32[]{:S(2)}, u32[]{:S(2)}) %all-to-all-start) | async-done | bytes 98336 | tf_op jit(solution)/shard_map/all_to_all | solution.py:17
  22.4 6.8 %all-to-all-start.1 = ((bf16[16,8,3072]{2,1,0:T(8,128)(2,1)}), bf16[16,8,3072]{2,1,0:T(8,128)(2,1)}, u32[]{:S(2)}, u32[]{:S(2)}) async-start(bf16[16,8,3072]{2,1,0:T(8,128)(2,1)} %broadcast_in_dim.60), calls=%async_computation.1 | async-start | bytes 1572864 | tf_op jit(solution)/shard_map/all_to_all | solution.py:17
  29.2 4.5 %broadcast_select_fusion.1 = (bf16[3072,256]{1,0:T(8,128)(2,1)S(1)}, bf16[3072,256]{1,0:T(8,128)(2,1)}) fusion(bf16[3072,256]{1,0:T(8,128)(2,1)} %collective-permute-done.1, pred[]{:T(512)S(6)} %eq.18, bf16[6144,128]{1,0:T(8,128)(2,1)} %bitcast.83, bf16[6144,128]{1,0:T(8,128)(2,1)} %bitcast.85), kind=kLoop, calls=%fused_computation.25 | loop fusion | flops 12582912 | bytes 7864321 | tf_op jit(solution)/shard_map/jit(_where)/select_n | solution.py:90
  33.7 8.0 %all-to-all-done.1 = bf16[16,8,3072]{2,1,0:T(8,128)(2,1)} async-done(((bf16[16,8,3072]{2,1,0:T(8,128)(2,1)}), bf16[16,8,3072]{2,1,0:T(8,128)(2,1)}, u32[]{:S(2)}, u32[]{:S(2)}) %all-to-all-start.1) | async-done | bytes 786464 | tf_op jit(solution)/shard_map/all_to_all | solution.py:17
  43.2 2.9 %collective-permute-start.2 = (f32[128,256]{1,0:T(8,128)S(1)}, f32[128,256]{1,0:T(8,128)S(1)}, u32[]{:S(2)}, u32[]{:S(2)}) collective-permute-start(f32[128,256]{1,0:T(8,128)S(1)} %fusion.29), channel_id=1, source_target_pairs={{0,128},{128,0},{1,129},{129,1},{2,130},{130,2},{3,131},{131,3},{4... | collective-permute-start | bytes 393224 | tf_op jit(solution)/shard_map/ppermute | solution.py:63
  49.0 4.3 %all-to-all-start.2 = ((bf16[16,8,3072]{2,1,0:T(8,128)(2,1)}), bf16[16,8,3072]{2,1,0:T(8,128)(2,1)}, u32[]{:S(2)}, u32[]{:S(2)}) async-start(bf16[16,8,3072]{2,1,0:T(8,128)(2,1)} %fusion.6), calls=%async_computation.2 | async-start | bytes 1572864 | tf_op jit(solution)/shard_map/all_to_all | solution.py:17
  53.3 12.8 %all-to-all-done.2 = bf16[16,8,3072]{2,1,0:T(8,128)(2,1)} async-done(((bf16[16,8,3072]{2,1,0:T(8,128)(2,1)}), bf16[16,8,3072]{2,1,0:T(8,128)(2,1)}, u32[]{:S(2)}, u32[]{:S(2)}) %all-to-all-start.2) | async-done | bytes 786464 | tf_op jit(solution)/shard_map/all_to_all | solution.py:17
  67.5 2.9 %collective-permute-done.4 = bf16[8,3072]{1,0:T(8,128)(2,1)S(1)} collective-permute-done((bf16[8,3072]{1,0:T(8,128)(2,1)S(1)}, bf16[8,3072]{1,0:T(8,128)(2,1)S(1)}, u32[]{:S(2)}, u32[]{:S(2)}) %collective-permute-start.4) | collective-permute-done | bytes 49184 | tf_op jit(solution)/shard_map/ppermute | solution.py:53
  71.5 4.7 %all-to-all-start.3 = ((bf16[16,8,3072]{2,1,0:T(8,128)(2,1)}), bf16[16,8,3072]{2,1,0:T(8,128)(2,1)S(1)}, u32[]{:S(2)}, u32[]{:S(2)}) async-start(bf16[16,8,3072]{2,1,0:T(8,128)(2,1)} %broadcast_in_dim.61), calls=%async_computation.3 | async-start | bytes 1572864 | tf_op jit(solution)/shard_map/all_to_all | solution.py:17
  76.2 3.0 %collective-permute-start.6 = (bf16[8,3072]{1,0:T(8,128)(2,1)S(1)}, bf16[8,3072]{1,0:T(8,128)(2,1)S(1)}, u32[]{:S(2)}, u32[]{:S(2)}) collective-permute-start(bf16[8,3072]{1,0:T(8,128)(2,1)S(1)} %add_convert_fusion.4), channel_id=1, source_target_pairs={{0,4},{1,5},{2,6},{3,7},{4,0},{5,1},{6,2},{7,3},{8,12},{9,13},{10,... | collective-permute-start | bytes 147464 | tf_op jit(solution)/shard_map/ppermute | solution.py:53
  79.2 4.0 %collective-permute-done.6 = bf16[8,3072]{1,0:T(8,128)(2,1)S(1)} collective-permute-done((bf16[8,3072]{1,0:T(8,128)(2,1)S(1)}, bf16[8,3072]{1,0:T(8,128)(2,1)S(1)}, u32[]{:S(2)}, u32[]{:S(2)}) %collective-permute-start.6) | collective-permute-done | bytes 49184 | tf_op jit(solution)/shard_map/ppermute | solution.py:53
  83.2 3.5 %all-to-all-done.3 = bf16[16,8,3072]{2,1,0:T(8,128)(2,1)S(1)} async-done(((bf16[16,8,3072]{2,1,0:T(8,128)(2,1)}), bf16[16,8,3072]{2,1,0:T(8,128)(2,1)S(1)}, u32[]{:S(2)}, u32[]{:S(2)}) %all-to-all-start.3) | async-done | bytes 786464 | tf_op jit(solution)/shard_map/all_to_all | solution.py:17
  87.7 4.4 %all-to-all-start.4 = ((bf16[16,8,3072]{2,1,0:T(8,128)(2,1)}), bf16[16,8,3072]{2,1,0:T(8,128)(2,1)}, u32[]{:S(2)}, u32[]{:S(2)}) async-start(bf16[16,8,3072]{2,1,0:T(8,128)(2,1)} %broadcast_in_dim.62), calls=%async_computation.4 | async-start | bytes 1572864 | tf_op jit(solution)/shard_map/all_to_all | solution.py:17
  92.5 5.8 %collective-permute-start.7 = (f32[128,128]{1,0:T(8,128)S(1)}, f32[128,128]{1,0:T(8,128)S(1)}, u32[]{:S(2)}, u32[]{:S(2)}) collective-permute-start(f32[128,128]{1,0:T(8,128)S(1)} %fusion.12), channel_id=1, source_target_pairs={{0,128},{128,0},{1,129},{129,1},{2,130},{130,2},{3,131},{131,3},{4... | collective-permute-start | bytes 196616 | tf_op jit(solution)/shard_map/ppermute | solution.py:63
  99.3 3.3 %all-to-all-done.4 = bf16[16,8,3072]{2,1,0:T(8,128)(2,1)} async-done(((bf16[16,8,3072]{2,1,0:T(8,128)(2,1)}), bf16[16,8,3072]{2,1,0:T(8,128)(2,1)}, u32[]{:S(2)}, u32[]{:S(2)}) %all-to-all-start.4) | async-done | bytes 786464 | tf_op jit(solution)/shard_map/all_to_all | solution.py:17
  102.6 2.1 fusion.33
  104.8 5.7 %collective-permute-start.8 = (f32[128,256]{1,0:T(8,128)S(1)}, f32[128,256]{1,0:T(8,128)S(1)}, u32[]{:S(2)}, u32[]{:S(2)}) collective-permute-start(f32[128,256]{1,0:T(8,128)S(1)} %fusion.33), channel_id=1, source_target_pairs={{0,128},{128,0},{1,129},{129,1},{2,130},{130,2},{3,131},{131,3},{4... | collective-permute-start | bytes 393224 | tf_op jit(solution)/shard_map/ppermute | solution.py:63
  113.7 4.3 %all-to-all-start.5 = ((bf16[16,8,3072]{2,1,0:T(8,128)(2,1)}), bf16[16,8,3072]{2,1,0:T(8,128)(2,1)}, u32[]{:S(2)}, u32[]{:S(2)}) async-start(bf16[16,8,3072]{2,1,0:T(8,128)(2,1)} %fusion.5), calls=%async_computation.5 | async-start | bytes 1572864 | tf_op jit(solution)/shard_map/all_to_all | solution.py:17
  118.0 2.0 fusion.4
  120.0 10.8 %all-to-all-done.5 = bf16[16,8,3072]{2,1,0:T(8,128)(2,1)} async-done(((bf16[16,8,3072]{2,1,0:T(8,128)(2,1)}), bf16[16,8,3072]{2,1,0:T(8,128)(2,1)}, u32[]{:S(2)}, u32[]{:S(2)}) %all-to-all-start.5) | async-done | bytes 786464 | tf_op jit(solution)/shard_map/all_to_all | solution.py:17
  130.8 1.9 reduce_sum.68
  133.6 2.2 collective-permute-done.9
  137.3 2.4 %collective-permute-start.10 = (bf16[8,3072]{1,0:T(8,128)(2,1)}, bf16[8,3072]{1,0:T(8,128)(2,1)}, u32[]{:S(2)}, u32[]{:S(2)}) collective-permute-start(bf16[8,3072]{1,0:T(8,128)(2,1)} %add_convert_fusion.2), channel_id=1, source_target_pairs={{0,2},{1,3},{2,0},{3,1},{4,6},{5,7},{6,4},{7,5},{8,10},{9,11},{10,... | collective-permute-start | bytes 147464 | tf_op jit(solution)/shard_map/ppermute | solution.py:53
  139.6 4.7 %all-to-all-start.6 = ((bf16[16,8,3072]{2,1,0:T(8,128)(2,1)}), bf16[16,8,3072]{2,1,0:T(8,128)(2,1)}, u32[]{:S(2)}, u32[]{:S(2)}) async-start(bf16[16,8,3072]{2,1,0:T(8,128)(2,1)} %bitcast.86), calls=%async_computation.6 | async-start | bytes 1572864 | tf_op jit(solution)/shard_map/all_to_all | solution.py:17
  145.2 2.5 %collective-permute-start.11 = (bf16[8,3072]{1,0:T(8,128)(2,1)S(1)}, bf16[8,3072]{1,0:T(8,128)(2,1)S(1)}, u32[]{:S(2)}, u32[]{:S(2)}) collective-permute-start(bf16[8,3072]{1,0:T(8,128)(2,1)S(1)} %add_convert_fusion.1), channel_id=1, source_target_pairs={{0,4},{1,5},{2,6},{3,7},{4,0},{5,1},{6,2},{7,3},{8,12},{9,13},{10,... | collective-permute-start | bytes 147464 | tf_op jit(solution)/shard_map/ppermute | solution.py:53
  148.9 3.5 %collective-permute-done.11 = bf16[8,3072]{1,0:T(8,128)(2,1)S(1)} collective-permute-done((bf16[8,3072]{1,0:T(8,128)(2,1)S(1)}, bf16[8,3072]{1,0:T(8,128)(2,1)S(1)}, u32[]{:S(2)}, u32[]{:S(2)}) %collective-permute-start.11) | collective-permute-done | bytes 49184 | tf_op jit(solution)/shard_map/ppermute | solution.py:53
  153.0 2.0 all-to-all-done.6
  155.0 1.8 broadcast_in_dim.63
  156.8 4.6 %all-to-all-start.7 = ((bf16[16,8,3072]{2,1,0:T(8,128)(2,1)}), bf16[16,8,3072]{2,1,0:T(8,128)(2,1)}, u32[]{:S(2)}, u32[]{:S(2)}) async-start(bf16[16,8,3072]{2,1,0:T(8,128)(2,1)} %broadcast_in_dim.63), calls=%async_computation.7 | async-start | bytes 1572864 | tf_op jit(solution)/shard_map/all_to_all | solution.py:17
  162.3 5.4 %collective-permute-start.12 = (bf16[2,24,128]{2,1,0:T(8,128)(2,1)S(1)}, bf16[2,24,128]{2,1,0:T(8,128)(2,1)S(1)}, u32[]{:S(2)}, u32[]{:S(2)}) collective-permute-start(bf16[2,24,128]{2,1,0:T(8,128)(2,1)S(1)} %bitcast.93), channel_id=1, source_target_pairs={{0,128},{128,0},{1,129},{129,1},{2,130},{130,2},{3,131},{131,3},{4... | collective-permute-start | bytes 36872 | tf_op jit(solution)/shard_map/ppermute | solution.py:63
  167.7 1.9 reduce_sum.70
  169.6 2.8 %collective-permute-start.14 = (bf16[128,3072]{1,0:T(8,128)(2,1)}, bf16[128,3072]{1,0:T(8,128)(2,1)}, u32[]{:S(2)}, u32[]{:S(2)}) collective-permute-start(bf16[128,3072]{1,0:T(8,128)(2,1)} %bitcast.6), channel_id=1, source_target_pairs={{128,0},{129,1},{130,2},{131,3},{132,4},{133,5},{134,6},{135,7},{1... | collective-permute-start | bytes 2359304 | tf_op jit(solution)/shard_map/ppermute | solution.py:63
  175.6 1.8 fusion.11
  177.4 2.7 %collective-permute-start.13 = (f32[128,128]{1,0:T(8,128)S(1)}, f32[128,128]{1,0:T(8,128)S(1)}, u32[]{:S(2)}, u32[]{:S(2)}) collective-permute-start(f32[128,128]{1,0:T(8,128)S(1)} %fusion.11), channel_id=1, source_target_pairs={{0,128},{128,0},{1,129},{129,1},{2,130},{130,2},{3,131},{131,3},{4... | collective-permute-start | bytes 196616 | tf_op jit(solution)/shard_map/ppermute | solution.py:63
  183.9 6.9 %all-to-all-start.8 = ((bf16[16,8,3072]{2,1,0:T(8,128)(2,1)}), bf16[16,8,3072]{2,1,0:T(8,128)(2,1)S(1)}, u32[]{:S(2)}, u32[]{:S(2)}) async-start(bf16[16,8,3072]{2,1,0:T(8,128)(2,1)} %bitcast.19), calls=%async_computation.8 | async-start | bytes 1572864 | tf_op jit(solution)/shard_map/all_to_all | solution.py:17
  190.8 2.9 %broadcast_select_fusion.5 = (bf16[128,3072]{1,0:T(8,128)(2,1)}, bf16[128,3072]{1,0:T(8,128)(2,1)}) fusion(bf16[128,3072]{1,0:T(8,128)(2,1)} %collective-permute-done.16, pred[]{:T(512)S(6)} %eq.18, bf16[128,3072]{1,0:T(8,128)(2,1)} %bitcast.18, f32[128]{0:T(128)S(1)} %copy-done.15), kind=kLoop, calls=%fused_computation.29 | loop fusion | flops 1572864 | bytes 3146241 | tf_op jit(solution)/shard_map/jit(_where)/select_n | solution.py:90
  193.7 2.8 %collective-permute-start.17 = (bf16[128,3072]{1,0:T(8,128)(2,1)}, bf16[128,3072]{1,0:T(8,128)(2,1)}, u32[]{:S(2)}, u32[]{:S(2)}) collective-permute-start(bf16[128,3072]{1,0:T(8,128)(2,1)} %get-tuple-element.44), channel_id=1, source_target_pairs={{128,0},{129,1},{130,2},{131,3},{132,4},{133,5},{134,6},{135,7},{1... | collective-permute-start | bytes 2359304 | tf_op jit(solution)/shard_map/ppermute | solution.py:63
  196.6 1.8 broadcast_select_fusion.6
  198.4 1.8 fusion
  200.1 1.7 fusion.1
  201.9 2.3 %all-to-all-done.8 = bf16[16,8,3072]{2,1,0:T(8,128)(2,1)S(1)} async-done(((bf16[16,8,3072]{2,1,0:T(8,128)(2,1)}), bf16[16,8,3072]{2,1,0:T(8,128)(2,1)S(1)}, u32[]{:S(2)}, u32[]{:S(2)}) %all-to-all-start.8) | async-done | bytes 786464 | tf_op jit(solution)/shard_map/all_to_all | solution.py:17
  205.0 6.0 %all-to-all-start.9 = ((bf16[16,24,128]{2,1,0:T(8,128)(2,1)}), bf16[16,24,128]{2,1,0:T(8,128)(2,1)S(1)}, u32[]{:S(2)}, u32[]{:S(2)}) async-start(bf16[16,24,128]{2,1,0:T(8,128)(2,1)} %bitcast.35), calls=%async_computation.9 | async-start | bytes 196608 | tf_op jit(solution)/shard_map/all_to_all | solution.py:17
  211.4 1.7 fusion.2
  213.1 5.2 %all-to-all-done.9 = bf16[16,24,128]{2,1,0:T(8,128)(2,1)S(1)} async-done(((bf16[16,24,128]{2,1,0:T(8,128)(2,1)}), bf16[16,24,128]{2,1,0:T(8,128)(2,1)S(1)}, u32[]{:S(2)}, u32[]{:S(2)}) %all-to-all-start.9) | async-done | bytes 98336 | tf_op jit(solution)/shard_map/all_to_all | solution.py:17
  (107 shorter events, 29.6 us)
Async XLA Ops:
  0.6 5.7 %copy-start.12 = (bf16[1,1,6144]{2,1,0:T(2,128)(2,1)S(1)}, bf16[1,1,6144]{2,1,0:T(2,128)(2,1)}, u32[]{:S(2)}) copy-start(bf16[1,1,6144]{2,1,0:T(2,128)(2,1)} %param.10) | copy-start | bytes 36868
  0.6 5.7 %copy-start.13 = (bf16[1,1,6144]{2,1,0:T(2,128)(2,1)S(1)}, bf16[1,1,6144]{2,1,0:T(2,128)(2,1)}, u32[]{:S(2)}) copy-start(bf16[1,1,6144]{2,1,0:T(2,128)(2,1)} %param.9) | copy-start | bytes 36868
  0.7 14.2 %copy-start.16 = (f32[1,1,128]{2,1,0:T(1,128)S(1)}, f32[1,1,128]{2,1,0:T(1,128)}, u32[]{:S(2)}) copy-start(f32[1,1,128]{2,1,0:T(1,128)} %param.16) | copy-start | bytes 1540
  0.7 14.2 %copy-start.17 = (s32[1,1,128]{2,1,0:T(1,128)S(1)}, s32[1,1,128]{2,1,0:T(1,128)}, u32[]{:S(2)}) copy-start(s32[1,1,128]{2,1,0:T(1,128)} %param.14) | copy-start | bytes 1540
  3.0 26.2 %collective-permute-start.1 = (bf16[3072,256]{1,0:T(8,128)(2,1)S(1)}, bf16[3072,256]{1,0:T(8,128)(2,1)}, u32[]{:S(2)}, u32[]{:S(2)}) collective-permute-start(bf16[3072,256]{1,0:T(8,128)(2,1)S(1)} %broadcast_select_fusion.2), channel_id=1, source_target_pairs={{0,128},{128,0},{1,129},{129,1},{2,130},{130,2},{3,131},{131,3},{4... | collective-permute-start | bytes 4718600 | tf_op jit(solution)/shard_map/ppermute | solution.py:63
  7.1 14.3 %all-to-all-start = ((bf16[8,48,128]{2,1,0:T(8,128)(2,1)}), bf16[8,48,128]{2,1,0:T(8,128)(2,1)S(1)}, u32[]{:S(2)}, u32[]{:S(2)}) async-start(bf16[8,48,128]{2,1,0:T(8,128)(2,1)} %broadcast_in_dim.32), calls=%async_computation | async-start | bytes 196608 | tf_op jit(solution)/shard_map/all_to_all | solution.py:17
  15.0 3.0 %collective-permute-start = (f32[2,128]{1,0:T(2,128)S(1)}, f32[2,128]{1,0:T(2,128)S(1)}, u32[]{:S(2)}, u32[]{:S(2)}) collective-permute-start(f32[2,128]{1,0:T(2,128)S(1)} %stack.10), channel_id=1, source_target_pairs={{0,128},{128,0},{1,129},{129,1},{2,130},{130,2},{3,131},{131,3},{4... | collective-permute-start | bytes 3080 | tf_op jit(solution)/shard_map/ppermute | solution.py:63
  17.8 29.4 %collective-permute-start.3 = (bf16[128,3072]{1,0:T(8,128)(2,1)}, bf16[128,3072]{1,0:T(8,128)(2,1)S(1)}, u32[]{:S(2)}, u32[]{:S(2)}) collective-permute-start(bf16[128,3072]{1,0:T(8,128)(2,1)} %get-tuple-element.47), channel_id=1, source_target_pairs={{0,128},{128,0},{1,129},{129,1},{2,130},{130,2},{3,131},{131,3},{4... | collective-permute-start | bytes 2359304 | tf_op jit(solution)/shard_map/ppermute | solution.py:63
  22.4 19.3 %all-to-all-start.1 = ((bf16[16,8,3072]{2,1,0:T(8,128)(2,1)}), bf16[16,8,3072]{2,1,0:T(8,128)(2,1)}, u32[]{:S(2)}, u32[]{:S(2)}) async-start(bf16[16,8,3072]{2,1,0:T(8,128)(2,1)} %broadcast_in_dim.60), calls=%async_computation.1 | async-start | bytes 1572864 | tf_op jit(solution)/shard_map/all_to_all | solution.py:17
  43.2 3.9 %collective-permute-start.2 = (f32[128,256]{1,0:T(8,128)S(1)}, f32[128,256]{1,0:T(8,128)S(1)}, u32[]{:S(2)}, u32[]{:S(2)}) collective-permute-start(f32[128,256]{1,0:T(8,128)S(1)} %fusion.29), channel_id=1, source_target_pairs={{0,128},{128,0},{1,129},{129,1},{2,130},{130,2},{3,131},{131,3},{4... | collective-permute-start | bytes 393224 | tf_op jit(solution)/shard_map/ppermute | solution.py:63
  46.1 2.9 %copy-start.14 = (f32[128]{0:T(128)}, f32[128]{0:T(128)S(1)}, u32[]{:S(2)}) copy-start(f32[128]{0:T(128)S(1)} %get-tuple-element.67) | copy-start | bytes 1540
  47.2 0.6 copy-start.3
  47.2 1.8 copy-start.1
  49.0 17.1 %all-to-all-start.2 = ((bf16[16,8,3072]{2,1,0:T(8,128)(2,1)}), bf16[16,8,3072]{2,1,0:T(8,128)(2,1)}, u32[]{:S(2)}, u32[]{:S(2)}) async-start(bf16[16,8,3072]{2,1,0:T(8,128)(2,1)} %fusion.6), calls=%async_computation.2 | async-start | bytes 1572864 | tf_op jit(solution)/shard_map/all_to_all | solution.py:17
  67.4 3.0 %collective-permute-start.4 = (bf16[8,3072]{1,0:T(8,128)(2,1)S(1)}, bf16[8,3072]{1,0:T(8,128)(2,1)S(1)}, u32[]{:S(2)}, u32[]{:S(2)}) collective-permute-start(bf16[8,3072]{1,0:T(8,128)(2,1)S(1)} %reduce_sum.67), channel_id=1, source_target_pairs={{0,1},{1,0},{2,3},{3,2},{4,5},{5,4},{6,7},{7,6},{8,9},{9,8},{10,11... | collective-permute-start | bytes 147464 | tf_op jit(solution)/shard_map/ppermute | solution.py:53
  70.4 5.8 %collective-permute-start.5 = (bf16[8,3072]{1,0:T(8,128)(2,1)S(1)}, bf16[8,3072]{1,0:T(8,128)(2,1)S(1)}, u32[]{:S(2)}, u32[]{:S(2)}) collective-permute-start(bf16[8,3072]{1,0:T(8,128)(2,1)S(1)} %add_convert_fusion.5), channel_id=1, source_target_pairs={{0,2},{1,3},{2,0},{3,1},{4,6},{5,7},{6,4},{7,5},{8,10},{9,11},{10,... | collective-permute-start | bytes 147464 | tf_op jit(solution)/shard_map/ppermute | solution.py:53
  71.5 15.3 %all-to-all-start.3 = ((bf16[16,8,3072]{2,1,0:T(8,128)(2,1)}), bf16[16,8,3072]{2,1,0:T(8,128)(2,1)S(1)}, u32[]{:S(2)}, u32[]{:S(2)}) async-start(bf16[16,8,3072]{2,1,0:T(8,128)(2,1)} %broadcast_in_dim.61), calls=%async_computation.3 | async-start | bytes 1572864 | tf_op jit(solution)/shard_map/all_to_all | solution.py:17
  76.2 7.0 %collective-permute-start.6 = (bf16[8,3072]{1,0:T(8,128)(2,1)S(1)}, bf16[8,3072]{1,0:T(8,128)(2,1)S(1)}, u32[]{:S(2)}, u32[]{:S(2)}) collective-permute-start(bf16[8,3072]{1,0:T(8,128)(2,1)S(1)} %add_convert_fusion.4), channel_id=1, source_target_pairs={{0,4},{1,5},{2,6},{3,7},{4,0},{5,1},{6,2},{7,3},{8,12},{9,13},{10,... | collective-permute-start | bytes 147464 | tf_op jit(solution)/shard_map/ppermute | solution.py:53
  83.2 9.3 %copy-start.7 = (bf16[8,3072]{1,0:T(8,128)(2,1)}, bf16[8,3072]{1,0:T(8,128)(2,1)S(1)}, u32[]{:S(2)}) copy-start(bf16[8,3072]{1,0:T(8,128)(2,1)S(1)} %add_convert_fusion.3) | copy-start | bytes 147460
  87.7 14.9 %all-to-all-start.4 = ((bf16[16,8,3072]{2,1,0:T(8,128)(2,1)}), bf16[16,8,3072]{2,1,0:T(8,128)(2,1)}, u32[]{:S(2)}, u32[]{:S(2)}) async-start(bf16[16,8,3072]{2,1,0:T(8,128)(2,1)} %broadcast_in_dim.62), calls=%async_computation.4 | async-start | bytes 1572864 | tf_op jit(solution)/shard_map/all_to_all | solution.py:17
  92.5 6.7 %collective-permute-start.7 = (f32[128,128]{1,0:T(8,128)S(1)}, f32[128,128]{1,0:T(8,128)S(1)}, u32[]{:S(2)}, u32[]{:S(2)}) collective-permute-start(f32[128,128]{1,0:T(8,128)S(1)} %fusion.12), channel_id=1, source_target_pairs={{0,128},{128,0},{1,129},{129,1},{2,130},{130,2},{3,131},{131,3},{4... | collective-permute-start | bytes 196616 | tf_op jit(solution)/shard_map/ppermute | solution.py:63
  102.6 9.5 %copy-start = (bf16[3072,256]{1,0:T(8,128)(2,1)S(1)}, bf16[3072,256]{1,0:T(8,128)(2,1)}, u32[]{:S(2)}) copy-start(bf16[3072,256]{1,0:T(8,128)(2,1)} %get-tuple-element.46) | copy-start | bytes 4718596
  104.8 6.7 %collective-permute-start.8 = (f32[128,256]{1,0:T(8,128)S(1)}, f32[128,256]{1,0:T(8,128)S(1)}, u32[]{:S(2)}, u32[]{:S(2)}) collective-permute-start(f32[128,256]{1,0:T(8,128)S(1)} %fusion.33), channel_id=1, source_target_pairs={{0,128},{128,0},{1,129},{129,1},{2,130},{130,2},{3,131},{131,3},{4... | collective-permute-start | bytes 393224 | tf_op jit(solution)/shard_map/ppermute | solution.py:63
  113.7 17.1 %all-to-all-start.5 = ((bf16[16,8,3072]{2,1,0:T(8,128)(2,1)}), bf16[16,8,3072]{2,1,0:T(8,128)(2,1)}, u32[]{:S(2)}, u32[]{:S(2)}) async-start(bf16[16,8,3072]{2,1,0:T(8,128)(2,1)} %fusion.5), calls=%async_computation.5 | async-start | bytes 1572864 | tf_op jit(solution)/shard_map/all_to_all | solution.py:17
  132.7 3.2 %collective-permute-start.9 = (bf16[8,3072]{1,0:T(8,128)(2,1)}, bf16[8,3072]{1,0:T(8,128)(2,1)S(1)}, u32[]{:S(2)}, u32[]{:S(2)}) collective-permute-start(bf16[8,3072]{1,0:T(8,128)(2,1)} %reduce_sum.68), channel_id=1, source_target_pairs={{0,1},{1,0},{2,3},{3,2},{4,5},{5,4},{6,7},{7,6},{8,9},{9,8},{10,11... | collective-permute-start | bytes 147464 | tf_op jit(solution)/shard_map/ppermute | solution.py:53
  137.3 7.1 %collective-permute-start.10 = (bf16[8,3072]{1,0:T(8,128)(2,1)}, bf16[8,3072]{1,0:T(8,128)(2,1)}, u32[]{:S(2)}, u32[]{:S(2)}) collective-permute-start(bf16[8,3072]{1,0:T(8,128)(2,1)} %add_convert_fusion.2), channel_id=1, source_target_pairs={{0,2},{1,3},{2,0},{3,1},{4,6},{5,7},{6,4},{7,5},{8,10},{9,11},{10,... | collective-permute-start | bytes 147464 | tf_op jit(solution)/shard_map/ppermute | solution.py:53
  139.6 15.4 %all-to-all-start.6 = ((bf16[16,8,3072]{2,1,0:T(8,128)(2,1)}), bf16[16,8,3072]{2,1,0:T(8,128)(2,1)}, u32[]{:S(2)}, u32[]{:S(2)}) async-start(bf16[16,8,3072]{2,1,0:T(8,128)(2,1)} %bitcast.86), calls=%async_computation.6 | async-start | bytes 1572864 | tf_op jit(solution)/shard_map/all_to_all | solution.py:17
  145.2 7.1 %collective-permute-start.11 = (bf16[8,3072]{1,0:T(8,128)(2,1)S(1)}, bf16[8,3072]{1,0:T(8,128)(2,1)S(1)}, u32[]{:S(2)}, u32[]{:S(2)}) collective-permute-start(bf16[8,3072]{1,0:T(8,128)(2,1)S(1)} %add_convert_fusion.1), channel_id=1, source_target_pairs={{0,4},{1,5},{2,6},{3,7},{4,0},{5,1},{6,2},{7,3},{8,12},{9,13},{10,... | collective-permute-start | bytes 147464 | tf_op jit(solution)/shard_map/ppermute | solution.py:53
  156.8 18.9 %all-to-all-start.7 = ((bf16[16,8,3072]{2,1,0:T(8,128)(2,1)}), bf16[16,8,3072]{2,1,0:T(8,128)(2,1)}, u32[]{:S(2)}, u32[]{:S(2)}) async-start(bf16[16,8,3072]{2,1,0:T(8,128)(2,1)} %broadcast_in_dim.63), calls=%async_computation.7 | async-start | bytes 1572864 | tf_op jit(solution)/shard_map/all_to_all | solution.py:17
  162.3 12.7 %collective-permute-start.12 = (bf16[2,24,128]{2,1,0:T(8,128)(2,1)S(1)}, bf16[2,24,128]{2,1,0:T(8,128)(2,1)S(1)}, u32[]{:S(2)}, u32[]{:S(2)}) collective-permute-start(bf16[2,24,128]{2,1,0:T(8,128)(2,1)S(1)} %bitcast.93), channel_id=1, source_target_pairs={{0,128},{128,0},{1,129},{129,1},{2,130},{130,2},{3,131},{131,3},{4... | collective-permute-start | bytes 36872 | tf_op jit(solution)/shard_map/ppermute | solution.py:63
  169.6 14.2 %collective-permute-start.14 = (bf16[128,3072]{1,0:T(8,128)(2,1)}, bf16[128,3072]{1,0:T(8,128)(2,1)}, u32[]{:S(2)}, u32[]{:S(2)}) collective-permute-start(bf16[128,3072]{1,0:T(8,128)(2,1)} %bitcast.6), channel_id=1, source_target_pairs={{128,0},{129,1},{130,2},{131,3},{132,4},{133,5},{134,6},{135,7},{1... | collective-permute-start | bytes 2359304 | tf_op jit(solution)/shard_map/ppermute | solution.py:63
  172.4 11.4 %collective-permute-start.15 = (bf16[128,3072]{1,0:T(8,128)(2,1)}, bf16[128,3072]{1,0:T(8,128)(2,1)}, u32[]{:S(2)}, u32[]{:S(2)}) collective-permute-start(bf16[128,3072]{1,0:T(8,128)(2,1)} %bitcast.13), channel_id=1, source_target_pairs={{0,128},{1,129},{2,130},{3,131},{4,132},{5,133},{6,134},{7,135},{8... | collective-permute-start | bytes 2359304 | tf_op jit(solution)/shard_map/ppermute | solution.py:63
  173.7 10.1 %collective-permute-start.16 = (bf16[128,3072]{1,0:T(8,128)(2,1)}, bf16[128,3072]{1,0:T(8,128)(2,1)}, u32[]{:S(2)}, u32[]{:S(2)}) collective-permute-start(bf16[128,3072]{1,0:T(8,128)(2,1)} %multiply_convert_fusion.1), channel_id=1, source_target_pairs={{0,128},{1,129},{2,130},{3,131},{4,132},{5,133},{6,134},{7,135},{8... | collective-permute-start | bytes 2359304 | tf_op jit(solution)/shard_map/ppermute | solution.py:63
  175.6 4.5 %copy-start.11 = (bf16[2,24,128]{2,1,0:T(8,128)(2,1)S(1)}, bf16[2,24,128]{2,1,0:T(8,128)(2,1)}, u32[]{:S(2)}) copy-start(bf16[2,24,128]{2,1,0:T(8,128)(2,1)} %get-tuple-element.62) | copy-start | bytes 36868
  177.4 4.0 %copy-start.6 = (f32[128,128]{1,0:T(8,128)}, f32[128,128]{1,0:T(8,128)S(1)}, u32[]{:S(2)}) copy-start(f32[128,128]{1,0:T(8,128)S(1)} %fusion.11) | copy-start | bytes 196612
  177.4 4.0 %collective-permute-start.13 = (f32[128,128]{1,0:T(8,128)S(1)}, f32[128,128]{1,0:T(8,128)S(1)}, u32[]{:S(2)}, u32[]{:S(2)}) collective-permute-start(f32[128,128]{1,0:T(8,128)S(1)} %fusion.11), channel_id=1, source_target_pairs={{0,128},{128,0},{1,129},{129,1},{2,130},{130,2},{3,131},{131,3},{4... | collective-permute-start | bytes 196616 | tf_op jit(solution)/shard_map/ppermute | solution.py:63
  182.3 8.5 %copy-start.15 = (f32[128]{0:T(128)S(1)}, f32[128]{0:T(128)}, u32[]{:S(2)}) copy-start(f32[128]{0:T(128)} %copy-done.14) | copy-start | bytes 1540
  183.9 20.3 %all-to-all-start.8 = ((bf16[16,8,3072]{2,1,0:T(8,128)(2,1)}), bf16[16,8,3072]{2,1,0:T(8,128)(2,1)S(1)}, u32[]{:S(2)}, u32[]{:S(2)}) async-start(bf16[16,8,3072]{2,1,0:T(8,128)(2,1)} %bitcast.19), calls=%async_computation.8 | async-start | bytes 1572864 | tf_op jit(solution)/shard_map/all_to_all | solution.py:17
  193.7 17.3 %collective-permute-start.17 = (bf16[128,3072]{1,0:T(8,128)(2,1)}, bf16[128,3072]{1,0:T(8,128)(2,1)}, u32[]{:S(2)}, u32[]{:S(2)}) collective-permute-start(bf16[128,3072]{1,0:T(8,128)(2,1)} %get-tuple-element.44), channel_id=1, source_target_pairs={{128,0},{129,1},{130,2},{131,3},{132,4},{133,5},{134,6},{135,7},{1... | collective-permute-start | bytes 2359304 | tf_op jit(solution)/shard_map/ppermute | solution.py:63
  200.1 4.2 %copy-start.8 = (bf16[8,3072]{1,0:T(8,128)(2,1)S(1)}, bf16[8,3072]{1,0:T(8,128)(2,1)}, u32[]{:S(2)}) copy-start(bf16[8,3072]{1,0:T(8,128)(2,1)} %reduce_sum.70) | copy-start | bytes 147460
  204.3 7.0 %copy-start.2 = (bf16[128,3072]{1,0:T(8,128)(2,1)S(1)}, bf16[128,3072]{1,0:T(8,128)(2,1)}, u32[]{:S(2)}) copy-start(bf16[128,3072]{1,0:T(8,128)(2,1)} %get-tuple-element.43) | copy-start | bytes 2359300
  204.3 7.0 %copy-start.4 = (bf16[128,128]{1,0:T(8,128)(2,1)S(1)}, bf16[128,128]{1,0:T(8,128)(2,1)}, u32[]{:S(2)}) copy-start(bf16[128,128]{1,0:T(8,128)(2,1)} %copy-done.3) | copy-start | bytes 98308
  204.3 7.0 %copy-start.5 = (bf16[128,128]{1,0:T(8,128)(2,1)S(1)}, bf16[128,128]{1,0:T(8,128)(2,1)}, u32[]{:S(2)}) copy-start(bf16[128,128]{1,0:T(8,128)(2,1)} %get-tuple-element.52) | copy-start | bytes 98308
  205.0 13.4 %all-to-all-start.9 = ((bf16[16,24,128]{2,1,0:T(8,128)(2,1)}), bf16[16,24,128]{2,1,0:T(8,128)(2,1)S(1)}, u32[]{:S(2)}, u32[]{:S(2)}) async-start(bf16[16,24,128]{2,1,0:T(8,128)(2,1)} %bitcast.35), calls=%async_computation.9 | async-start | bytes 196608 | tf_op jit(solution)/shard_map/all_to_all | solution.py:17
  211.4 7.0 %copy-start.9 = (bf16[1,1,1,6144]{3,2,1,0:T(2,128)(2,1)S(1)}, bf16[1,1,1,6144]{3,2,1,0:T(2,128)(2,1)}, u32[]{:S(2)}) copy-start(bf16[1,1,1,6144]{3,2,1,0:T(2,128)(2,1)} %unstack.15) | copy-start | bytes 36868
  211.4 7.0 %copy-start.10 = (bf16[1,1,1,6144]{3,2,1,0:T(2,128)(2,1)S(1)}, bf16[1,1,1,6144]{3,2,1,0:T(2,128)(2,1)}, u32[]{:S(2)}) copy-start(bf16[1,1,1,6144]{3,2,1,0:T(2,128)(2,1)} %unstack.13) | copy-start | bytes 36868
